TPU v7x, 32 devices: a whole 2x2x4 slice. The times are simulated.
32 devices in a mesh: seq: 8 (over z, y), fsdp: 4 (over x, core).
Axes of the slice: x: 2, y: 2, z: 4, core: 2. Of those that a mesh axis runs over, the one named last changes fastest.
Arguments:
- tokens: bfloat16 [4, 16384, 768], P('fsdp', 'seq'), may hold values from -6 to 6
- first_gain: bfloat16 [768], P('fsdp'), may hold values from 0.099609375 to 1.8984375
- first_shift: bfloat16 [768], P('fsdp'), may hold values from -3 to 3
- project_in: bfloat16 [768, 2304], P('fsdp'), may hold values from -0.21875 to 0.21875
- project_out: bfloat16 [768, 768], P('fsdp'), may hold values from -2 to 2
- second_gain: bfloat16 [768], P('fsdp'), may hold values from 0.099609375 to 1.8984375
- second_shift: bfloat16 [768], P('fsdp'), may hold values from -3 to 3
- up_weight: bfloat16 [768, 3072], P('fsdp'), may hold values from -0.21875 to 0.21875
- down_weight: bfloat16 [3072, 768], P('fsdp'), may hold values from -0.15625 to 0.15625
- valid_mask: int32 [4, 16384], P('fsdp', 'seq'), may hold values from 0 to 1, as said below
- cotangent: bfloat16 [4, 16384, 768], P('fsdp', 'seq'), may hold values from -6 to 6
Outputs:
- mixed: bfloat16 [4, 16384, 768], P('fsdp', 'seq')
- tokens_back: float32 [4, 16384, 768], P('fsdp', 'seq')
- first_gain_back: float32 [768], P('fsdp')
- first_shift_back: float32 [768], P('fsdp')
- project_in_back: float32 [768, 2304], P('fsdp')
- project_out_back: float32 [768, 768], P('fsdp')
- second_gain_back: float32 [768], P('fsdp')
- second_shift_back: float32 [768], P('fsdp')
- up_weight_back: float32 [768, 3072], P('fsdp')
- down_weight_back: float32 [3072, 768], P('fsdp')
Inputs may be any that keep to these rules, and one draw needn't show every extreme that they name: `valid_mask`: positions of a stream come in blocks of 16384; each slide covers one or more whole blocks, and its valid positions are a prefix of it that ends inside its last block after 2 * 1024 or more of that block's positions; the last block of every stream ends in padding.
All inputs are finite; a program needn't handle non-finite values.
Results may differ from a plain program's by a relative error of at most 0.014.
Values may be sent and summed in bfloat16 or wider, within the bound.
A program may use at most 384 MiB of HBM per device.

v0:
```python
import jax
import jax.numpy as jnp
from jax import lax
from jax.sharding import PartitionSpec as P

HEADS = 16
HEAD_DIM = 48
SEG = 1024
BRANCHES = 5


EPS = 1e-05
NEG = -1e30
ROOT_HALF = 0.7071067811865476
INV_ROOT_TWO_PI = 0.3989422804014327


def as_sent(shard):

    def short(part):
        return part.astype(jnp.bfloat16) if part.dtype == jnp.float32 else part

    return jax.tree.map(short, shard)


def swapped(shard, axis, stride):
    return lax.ppermute(shard, axis, [(i, i ^ 1 << stride) for i in range(lax.axis_size(axis))])


def normalize(values, gain, shift):
    mean = jnp.mean(values, axis=-1, keepdims=True)
    centred = values - mean
    spread = jnp.mean(centred * centred, axis=-1, keepdims=True)
    inverse = lax.rsqrt(spread + EPS)
    normed = centred * inverse
    return (normed * gain + shift, normed, inverse)


def normalize_back(grad, normed, inverse, gain):
    scaled = grad * gain
    first = jnp.mean(scaled, axis=-1, keepdims=True)
    second = jnp.mean(scaled * normed, axis=-1, keepdims=True)
    return (
        inverse * (scaled - first - normed * second),
        jnp.sum(grad * normed, axis=0),
        jnp.sum(grad, axis=0),
    )


def head_pick(ratio, columns):
    owner = jnp.arange(HEADS * columns, dtype=jnp.int32) // columns
    return jnp.arange(ratio, dtype=jnp.int32)[:, None] == (owner % ratio)[None, :]


def select_rows(array, ratio, columns):
    length = array.shape[0]
    shaped = array.reshape(length // ratio, ratio, array.shape[1])
    return jnp.sum(
        jnp.where(head_pick(ratio, columns)[None], shaped, jnp.zeros((), array.dtype)), axis=1
    )


def spread_rows(chosen, ratio, columns, fill):
    full = jnp.where(
        head_pick(ratio, columns)[None], chosen[:, None, :], jnp.asarray(fill, chosen.dtype)
    )
    return full.reshape(-1, chosen.shape[1])


def ordered(upper, near, far, axis):
    first = jnp.where(upper, far, near)
    second = jnp.where(upper, near, far)
    return jnp.concatenate([first, second], axis=axis)


def gather_group(pieces, bits):
    place = lax.axis_index("seq")
    for bit in range(bits):
        other = jax.tree.map(
            lambda part, own: part.astype(own.dtype), swapped(as_sent(pieces), "seq", bit), pieces
        )
        upper = place // 2**bit % 2 == 1
        pieces = tuple((ordered(upper, near, far, 0) for near, far in zip(pieces, other)))
    return pieces


def reduce_group(pieces, bits):
    place = lax.axis_index("seq")
    for bit in reversed(range(bits)):
        upper = place // 2**bit % 2 == 1
        half = pieces[0].shape[0] // 2
        kept = tuple((jnp.where(upper, piece[half:], piece[:half]) for piece in pieces))
        given = tuple((jnp.where(upper, piece[:half], piece[half:]) for piece in pieces))
        other = jax.tree.map(
            lambda part, own: part.astype(own.dtype), swapped(as_sent(given), "seq", bit), given
        )
        pieces = tuple((mine + theirs for mine, theirs in zip(kept, other)))
    return pieces


def query_block(rows, heads_here):
    size = rows
    while size % 2 == 0 and size * heads_here > 1024:
        size = size // 2
    return size


def attend_forward(queries, keys, values, keeping, scale):
    count, rows, heads_here, depth = queries.shape
    size = query_block(rows, heads_here)
    blocks = queries.reshape(count, rows // size, size, heads_here, depth)

    def segment(item):
        query_all, key_seg, value_seg, mask_seg = item
        mask_cols = mask_seg.T[:, None, :] > 0.5

        def piece(query):
            scores = (
                jnp.einsum("qhd,khd->hqk", query, key_seg, preferred_element_type=jnp.float32)
                * scale
            )
            scores = jnp.where(mask_cols, scores, NEG)
            top = jnp.max(scores, axis=-1, keepdims=True)
            lse = top + jnp.log(jnp.sum(jnp.exp(scores - top), axis=-1, keepdims=True))
            probs = jnp.exp(scores - lse).astype(jnp.bfloat16)
            result = jnp.einsum(
                "hqk,khd->qhd", probs, value_seg, preferred_element_type=jnp.float32
            )
            return (result, lse[..., 0].T)

        return lax.map(piece, query_all)

    result, lse = lax.map(segment, (blocks, keys, values, keeping))
    return (result.reshape(count * rows, heads_here * depth), lse.reshape(count * rows, heads_here))


def attend_backward(queries, keys, values, keeping, lse, grad_out, grad_lse, scale):
    count, rows, heads_here, depth = queries.shape
    size = query_block(rows, heads_here)
    split = rows // size
    query_b = queries.reshape(count, split, size, heads_here, depth)
    lse_b = lse.reshape(count, split, size, heads_here)
    grad_b = grad_out.reshape(count, split, size, heads_here, depth)
    slope_b = grad_lse.reshape(count, split, size, heads_here)

    def segment(item):
        query_all, key_seg, value_seg, mask_seg, lse_all, grad_all, slope_all = item
        mask_cols = mask_seg.T[:, None, :] > 0.5

        def piece(carry, block):
            key_acc, value_acc = carry
            query, lse_blk, grad_blk, slope_blk = block
            scores = (
                jnp.einsum("qhd,khd->hqk", query, key_seg, preferred_element_type=jnp.float32)
                * scale
            )
            scores = jnp.where(mask_cols, scores, NEG)
            probs = jnp.exp(scores - lse_blk.T[:, :, None])
            grad_probs = jnp.einsum(
                "qhd,khd->hqk", grad_blk, value_seg, preferred_element_type=jnp.float32
            )
            delta = jnp.sum(probs * grad_probs, axis=-1, keepdims=True)
            grad_scores = (probs * (grad_probs - delta + slope_blk.T[:, :, None])).astype(
                jnp.bfloat16
            )
            grad_query = (
                jnp.einsum("hqk,khd->qhd", grad_scores, key_seg, preferred_element_type=jnp.float32)
                * scale
            )
            key_acc = (
                key_acc
                + jnp.einsum("hqk,qhd->khd", grad_scores, query, preferred_element_type=jnp.float32)
                * scale
            )
            value_acc = value_acc + jnp.einsum(
                "hqk,qhd->khd",
                probs.astype(jnp.bfloat16),
                grad_blk,
                preferred_element_type=jnp.float32,
            )
            return ((key_acc, value_acc), grad_query)

        start = jnp.zeros(key_seg.shape, jnp.float32)
        (key_acc, value_acc), grad_query = lax.scan(
            piece, (start, start), (query_all, lse_all, grad_all, slope_all)
        )
        return (grad_query, key_acc, value_acc)

    grad_query, grad_key, grad_value = lax.map(
        segment, (query_b, keys, values, keeping, lse_b, grad_b, slope_b)
    )
    width = heads_here * depth
    return (
        grad_query.reshape(-1, width),
        grad_key.reshape(-1, width),
        grad_value.reshape(-1, width),
    )


def per_device(
    tokens,
    first_gain,
    first_shift,
    project_in,
    project_out,
    second_gain,
    second_shift,
    up_weight,
    down_weight,
    valid_mask,
    cotangent,
):
    length = tokens.shape[1]
    width = tokens.shape[2]
    scale = HEAD_DIM ** (-0.5)
    gathered = (
        lax.all_gather(first_gain, "fsdp", axis=0, tiled=True),
        lax.all_gather(first_shift, "fsdp", axis=0, tiled=True),
        lax.all_gather(project_in, "fsdp", axis=0, tiled=True),
        lax.all_gather(project_out, "fsdp", axis=0, tiled=True),
        lax.all_gather(second_gain, "fsdp", axis=0, tiled=True),
        lax.all_gather(second_shift, "fsdp", axis=0, tiled=True),
        lax.all_gather(up_weight, "fsdp", axis=0, tiled=True),
        lax.all_gather(down_weight, "fsdp", axis=0, tiled=True),
    )
    (
        gain_attend,
        shift_attend,
        weight_in,
        weight_out,
        gain_feed,
        shift_feed,
        weight_up,
        weight_down,
    ) = gathered
    stream = tokens[0].astype(jnp.float32)
    keep_row = valid_mask[0].astype(jnp.float32)
    normed_in, unit_first, inverse_first = normalize(
        stream, gain_attend.astype(jnp.float32), shift_attend.astype(jnp.float32)
    )
    inner = normed_in.astype(jnp.bfloat16)
    mixed_qkv = jnp.dot(inner, weight_in, preferred_element_type=jnp.float32).astype(jnp.bfloat16)
    query_all = mixed_qkv[:, :width]
    key_all = mixed_qkv[:, width : 2 * width]
    value_all = mixed_qkv[:, 2 * width :]
    keep_heads = jnp.broadcast_to(valid_mask[0].astype(jnp.bfloat16)[:, None], (length, HEADS))
    saved = []
    outs = []
    lses = []
    for level in range(BRANCHES):
        ratio = 2**level
        span = SEG * ratio
        bits = max(span // length, 1).bit_length() - 1
        count = max(length // span, 1)
        query_sel = select_rows(query_all, ratio, HEAD_DIM)
        key_sel = select_rows(key_all, ratio, HEAD_DIM)
        value_sel = select_rows(value_all, ratio, HEAD_DIM)
        mask_sel = select_rows(keep_heads, ratio, 1)
        key_group, value_group, mask_group = gather_group((key_sel, value_sel, mask_sel), bits)
        rows = query_sel.shape[0] // count
        query_blk = query_sel.reshape(count, rows, HEADS, HEAD_DIM)
        key_blk = key_group.reshape(count, SEG, HEADS, HEAD_DIM)
        value_blk = value_group.reshape(count, SEG, HEADS, HEAD_DIM)
        mask_blk = mask_group.reshape(count, SEG, HEADS)
        out_blk, lse_blk = attend_forward(query_blk, key_blk, value_blk, mask_blk, scale)
        outs.append(spread_rows(out_blk, ratio, HEAD_DIM, 0.0))
        lses.append(spread_rows(lse_blk, ratio, 1, NEG))
        saved.append((query_blk, key_blk, value_blk, mask_blk, lse_blk, bits))
    stacked = jnp.stack(lses)
    top = jnp.max(stacked, axis=0)
    total = top + jnp.log(jnp.sum(jnp.exp(stacked - top), axis=0))
    shares = jnp.exp(stacked - total)
    share_cols = [jnp.repeat(shares[level], HEAD_DIM, axis=1) for level in range(BRANCHES)]
    merged = share_cols[0] * outs[0]
    for level in range(1, BRANCHES):
        merged = merged + share_cols[level] * outs[level]
    attended = (merged * keep_row[:, None]).astype(jnp.bfloat16)
    middle = stream + jnp.dot(attended, weight_out, preferred_element_type=jnp.float32)
    normed_mid, unit_second, inverse_second = normalize(
        middle, gain_feed.astype(jnp.float32), shift_feed.astype(jnp.float32)
    )
    hidden = normed_mid.astype(jnp.bfloat16)
    upper = jnp.dot(hidden, weight_up, preferred_element_type=jnp.float32)
    active = (0.5 * upper * (1.0 + lax.erf(upper * ROOT_HALF))).astype(jnp.bfloat16)
    final = middle + jnp.dot(active, weight_down, preferred_element_type=jnp.float32)
    mixed = final.astype(jnp.bfloat16)[None]
    back_set = (
        lax.all_gather(first_gain, "fsdp", axis=0, tiled=True),
        lax.all_gather(project_in, "fsdp", axis=0, tiled=True),
        lax.all_gather(project_out, "fsdp", axis=0, tiled=True),
        lax.all_gather(second_gain, "fsdp", axis=0, tiled=True),
        lax.all_gather(up_weight, "fsdp", axis=0, tiled=True),
        lax.all_gather(down_weight, "fsdp", axis=0, tiled=True),
    )
    back_gain_attend, back_in, back_out, back_gain_feed, back_up, back_down = back_set
    grad_final = cotangent[0]
    grad_down = jnp.einsum("tf,td->fd", active, grad_final, preferred_element_type=jnp.float32)
    grad_active = jnp.einsum("td,fd->tf", grad_final, back_down, preferred_element_type=jnp.float32)
    slope = (
        0.5 * (1.0 + lax.erf(upper * ROOT_HALF))
        + upper * jnp.exp(-0.5 * upper * upper) * INV_ROOT_TWO_PI
    )
    grad_upper = (grad_active * slope).astype(jnp.bfloat16)
    grad_up = jnp.einsum("td,tf->df", hidden, grad_upper, preferred_element_type=jnp.float32)
    grad_hidden = jnp.einsum("tf,df->td", grad_upper, back_up, preferred_element_type=jnp.float32)
    grad_mid_norm, grad_gain_feed, grad_shift_feed = normalize_back(
        grad_hidden, unit_second, inverse_second, back_gain_feed.astype(jnp.float32)
    )
    grad_middle = grad_final.astype(jnp.float32) + grad_mid_norm
    grad_branch = grad_middle.astype(jnp.bfloat16)
    grad_out_proj = jnp.einsum(
        "tc,td->cd", attended, grad_branch, preferred_element_type=jnp.float32
    )
    grad_attended = jnp.einsum(
        "td,cd->tc", grad_branch, back_out, preferred_element_type=jnp.float32
    ).astype(jnp.bfloat16)
    grad_merged = grad_attended.astype(jnp.float32) * keep_row[:, None]
    along_merged = jnp.sum((grad_merged * merged).reshape(length, HEADS, HEAD_DIM), axis=-1)
    grad_query = jnp.zeros((length, width), jnp.float32)
    grad_key = jnp.zeros((length, width), jnp.float32)
    grad_value = jnp.zeros((length, width), jnp.float32)
    for level in range(BRANCHES):
        ratio = 2**level
        query_blk, key_blk, value_blk, mask_blk, lse_blk, bits = saved[level]
        grad_o_full = share_cols[level] * grad_merged
        along_level = jnp.sum((grad_merged * outs[level]).reshape(length, HEADS, HEAD_DIM), axis=-1)
        grad_lse_full = shares[level] * (along_level - along_merged)
        grad_o_sel = select_rows(grad_o_full, ratio, HEAD_DIM).astype(jnp.bfloat16)
        grad_lse_sel = select_rows(grad_lse_full, ratio, 1)
        query_part, key_part, value_part = attend_backward(
            query_blk, key_blk, value_blk, mask_blk, lse_blk, grad_o_sel, grad_lse_sel, scale
        )
        key_back, value_back = reduce_group((key_part, value_part), bits)
        grad_query = grad_query + spread_rows(query_part, ratio, HEAD_DIM, 0.0)
        grad_key = grad_key + spread_rows(key_back, ratio, HEAD_DIM, 0.0)
        grad_value = grad_value + spread_rows(value_back, ratio, HEAD_DIM, 0.0)
    grad_mixed = jnp.concatenate([grad_query, grad_key, grad_value], axis=1).astype(jnp.bfloat16)
    grad_in = jnp.einsum("tc,te->ce", inner, grad_mixed, preferred_element_type=jnp.float32)
    grad_inner = jnp.einsum("te,ce->tc", grad_mixed, back_in, preferred_element_type=jnp.float32)
    grad_in_norm, grad_gain_attend, grad_shift_attend = normalize_back(
        grad_inner, unit_first, inverse_first, back_gain_attend.astype(jnp.float32)
    )
    tokens_back = (grad_middle + grad_in_norm)[None]
    terms = (
        grad_gain_attend,
        grad_shift_attend,
        grad_in,
        grad_out_proj,
        grad_gain_feed,
        grad_shift_feed,
        grad_up,
        grad_down,
    )
    shards = (
        lax.psum_scatter(
            terms[0].astype(jnp.bfloat16), "fsdp", scatter_dimension=0, tiled=True
        ).astype(jnp.float32),
        lax.psum_scatter(
            terms[1].astype(jnp.bfloat16), "fsdp", scatter_dimension=0, tiled=True
        ).astype(jnp.float32),
        lax.psum_scatter(
            terms[2].astype(jnp.bfloat16), "fsdp", scatter_dimension=0, tiled=True
        ).astype(jnp.float32),
        lax.psum_scatter(
            terms[3].astype(jnp.bfloat16), "fsdp", scatter_dimension=0, tiled=True
        ).astype(jnp.float32),
        lax.psum_scatter(
            terms[4].astype(jnp.bfloat16), "fsdp", scatter_dimension=0, tiled=True
        ).astype(jnp.float32),
        lax.psum_scatter(
            terms[5].astype(jnp.bfloat16), "fsdp", scatter_dimension=0, tiled=True
        ).astype(jnp.float32),
        lax.psum_scatter(
            terms[6].astype(jnp.bfloat16), "fsdp", scatter_dimension=0, tiled=True
        ).astype(jnp.float32),
        lax.psum_scatter(
            terms[7].astype(jnp.bfloat16), "fsdp", scatter_dimension=0, tiled=True
        ).astype(jnp.float32),
    )
    totals = lax.psum(
        (shards[0], shards[1], shards[2], shards[3], shards[4], shards[5], shards[6], shards[7]),
        "seq",
    )
    return (
        mixed,
        tokens_back,
        totals[0],
        totals[1],
        totals[2],
        totals[3],
        totals[4],
        totals[5],
        totals[6],
        totals[7],
    )


def solution(mesh):
    in_specs = (
        P("fsdp", "seq", None),
        P("fsdp"),
        P("fsdp"),
        P("fsdp", None),
        P("fsdp", None),
        P("fsdp"),
        P("fsdp"),
        P("fsdp", None),
        P("fsdp", None),
        P("fsdp", "seq"),
        P("fsdp", "seq", None),
    )
    out_specs = (
        P("fsdp", "seq", None),
        P("fsdp", "seq", None),
        P("fsdp"),
        P("fsdp"),
        P("fsdp", None),
        P("fsdp", None),
        P("fsdp"),
        P("fsdp"),
        P("fsdp", None),
        P("fsdp", None),
    )
    return jax.shard_map(
        per_device, mesh=mesh, in_specs=in_specs, out_specs=out_specs, check_vma=False
    )
```

profile of v0, /device:TPU:0, one launch (start us, length us, event | category | flops | bytes accessed | tf_op | source)
XLA Modules:
  0.0 4590.4 jit_solution(12405066349696650894)
XLA Ops:
  194.3 194.4 %while.242 = (s32[]{:T(128)}, f32[2,16,64,16,48]{2,1,0,4,3:T(8,128)}, f32[2,16,64,16]{2,3,1,0:T(8,128)S(1)}, bf16[2,16,64,16,48]{2,4,3,1,0:T(8,128)(2,1)}, bf16[...) while((s32[]{:T(128)}, ...), condition=%wide.region_7.8_spmd, body=%wide.region_2.7_spmd.sunk | while | flops 212876288 | bytes 51332912 | solution.py:133
  201.6 80.9 %while.253 = (s32[]{:T(128)}, f32[16,64,16,48]{1,3,2,0:T(8,128)}, f32[16,64,16]{1,2,0:T(8,128)S(1)}, pred[16,1,1024]{2,0,1:T(8,128)(4,1)S(1)}, bf16[16,64,16,48]...) while((s32[]{:T(128)}, f32[16,64,16,48]{1,3,2,0:T(8,128)}, ...), condition=%wide.region_6.6_spmd, body=%wide.region_3.5_spmd.sunk | while | flops 212859904 | bytes 16417881 | solution.py:131
  298.6 80.9 %while.253 = (s32[]{:T(128)}, f32[16,64,16,48]{1,3,2,0:T(8,128)}, f32[16,64,16]{1,2,0:T(8,128)S(1)}, pred[16,1,1024]{2,0,1:T(8,128)(4,1)S(1)}, bf16[16,64,16,48]...) while((s32[]{:T(128)}, f32[16,64,16,48]{1,3,2,0:T(8,128)}, ...), condition=%wide.region_6.6_spmd, body=%wide.region_3.5_spmd.sunk | while | flops 212859904 | bytes 16417881 | solution.py:131
  440.3 30.5 fusion.478
  490.9 90.3 %while.243 = (s32[]{:T(128)}, f32[16,64,16,48]{1,3,2,0:T(8,128)}, f32[16,64,16]{1,2,0:T(8,128)}, pred[16,1,1024]{2,0,1:T(8,128)(4,1)S(1)}, bf16[16,64,16,48]{1,3...) while((s32[]{:T(128)}, f32[16,64,16,48]{1,3,2,0:T(8,128)}, ...), condition=%wide.region_15.16_spmd, body=%wide.region_12.15_spmd.sunk | while | flops 212859904 | bytes 16406101 | solution.py:131
  661.2 21.8 collective-permute-done.13
  696.5 45.1 while.244
  783.7 22.5 while.245
  874.9 16.0 fusion.466
  899.6 21.0 multiply_convert_fusion.5
  920.6 21.0 fusion.445
  974.4 38.8 fusion.472
  1070.5 309.6 %while.250 = (s32[]{:T(128)}, f32[1024,16,48]{0,2,1:T(8,128)}, f32[1024,16,48]{0,2,1:T(8,128)}, f32[8,64,16,48]{1,3,2,0:T(8,128)}, bf16[8,64,16,48]{1,3,2,0:T(8,...) while((s32[]{:T(128)}, f32[1024,16,48]{0,2,1:T(8,128)}, ...), condition=%wide.region_63.64_spmd.clone, body=%wide.region_61.63_spmd.clone.sunk | while | flops 534564864 | bytes 64772744 | solution.py:184
  1408.3 154.1 %while.251 = (s32[]{:T(128)}, f32[1024,16,48]{0,2,1:T(8,128)}, f32[1024,16,48]{0,2,1:T(8,128)}, f32[4,64,16,48]{1,3,2,0:T(8,128)}, bf16[4,64,16,48]{1,3,2,0:T(8,...) while((s32[]{:T(128)}, f32[1024,16,48]{0,2,1:T(8,128)}, ...), condition=%wide.region_69.70_spmd.clone, body=%wide.region_67.69_spmd.clone.sunk | while | flops 534564864 | bytes 64772744 | solution.py:184
  1588.1 69.8 %while.252 = (s32[]{:T(128)}, f32[1024,16,48]{0,2,1:T(8,128)}, f32[1024,16,48]{0,2,1:T(8,128)}, f32[2,64,16,48]{1,3,2,0:T(8,128)}, bf16[2,64,16,48]{1,3,2,0:T(8,...) while((s32[]{:T(128)}, f32[1024,16,48]{0,2,1:T(8,128)}, ...), condition=%wide.region_75.76_spmd.clone, body=%wide.region_73.75_spmd.clone.sunk | while | flops 534564864 | bytes 65627880 | solution.py:184
  1708.5 613.5 %while.249 = (s32[]{:T(128)}, f32[1024,16,48]{0,2,1:T(8,128)}, f32[1024,16,48]{0,2,1:T(8,128)}, f32[16,64,16,48]{1,3,2,0:T(8,128)}, bf16[16,64,16,48]{1,3,2,0:T(...) while((s32[]{:T(128)}, f32[1024,16,48]{0,2,1:T(8,128)}, ...), condition=%wide.region_57.58_spmd.clone, body=%wide.region_55.57_spmd.clone.sunk | while | flops 534564864 | bytes 64772744 | solution.py:184
  2344.6 14.1 broadcast_select_fusion.2
  2390.1 1485.1 %while.248 = (s32[]{:T(128)}, f32[2,16,64,16,48]{2,1,0,4,3:T(8,128)}, f32[2,1024,16,48]{1,0,3,2:T(2,128)}, f32[2,1024,16,48]{1,0,3,2:T(2,128)}, bf16[2,16,64,16,...) while((s32[]{:T(128)}, ...), condition=%wide.region_51.52_spmd, body=%wide.region_47.51_spmd.sunk | while | flops 534581248 | bytes 151199280 | solution.py:189
  2404.3 600.3 %while.254 = (s32[]{:T(128)}, f32[1024,16,48]{0,2,1:T(8,128)}, f32[1024,16,48]{0,2,1:T(8,128)S(1)}, f32[16,64,16,48]{1,3,2,0:T(8,128)}, bf16[16,64,16,48]{1,3,2,...) while((s32[]{:T(128)}, f32[1024,16,48]{0,2,1:T(8,128)}, ...), condition=%wide.region_50.50_spmd.clone, body=%wide.region_48.49_spmd.clone.sunk | while | flops 534564864 | bytes 71064224 | solution.py:184
  2573.3 13.6 bitcast_add_fusion.28
  2610.8 13.6 bitcast_add_fusion.28
  2648.4 13.6 bitcast_add_fusion.28
  2761.1 13.6 bitcast_add_fusion.28
  2798.7 13.6 bitcast_add_fusion.28
  2873.9 13.6 bitcast_add_fusion.28
  2911.5 13.7 bitcast_add_fusion.28
  2949.1 13.6 bitcast_add_fusion.28
  2986.7 13.6 bitcast_add_fusion.28
  3018.9 54.3 %dynamic_update_slice.174 = f32[2,1024,16,48]{1,0,3,2:T(2,128)} dynamic-update-slice(f32[2,1024,16,48]{1,0,3,2:T(2,128)} %get-tuple-element.3123, f32[1,1024,16,48]{1,0,3,2:T(1,128)} %copy.972, s32[]{:T(128)} %get-tuple-element.3121, s32[]{:T(128)} %constant.876.clone.1..sunk.1, s32[]{:T(128)} %constant.876.clone.1..sunk.1, s32[]{:T(128)} %constant.876.clone.1..sunk.1) | dynamic-update-slice | bytes 6291460 | tf_op jit(solution)/shard_map/while/body/jit(dynamic_update_index_in_dim)/dynamic_update_slice | solution.py:189
  3078.1 54.4 %dynamic_update_slice.175 = f32[2,1024,16,48]{1,0,3,2:T(2,128)} dynamic-update-slice(f32[2,1024,16,48]{1,0,3,2:T(2,128)} %get-tuple-element.3124, f32[1,1024,16,48]{1,0,3,2:T(1,128)} %copy.973, s32[]{:T(128)} %get-tuple-element.3121, s32[]{:T(128)} %constant.876.clone.1..sunk.1, s32[]{:T(128)} %constant.876.clone.1..sunk.1, s32[]{:T(128)} %constant.876.clone.1..sunk.1) | dynamic-update-slice | bytes 6291460 | tf_op jit(solution)/shard_map/while/body/jit(dynamic_update_index_in_dim)/dynamic_update_slice | solution.py:189
  3146.6 600.3 %while.254 = (s32[]{:T(128)}, f32[1024,16,48]{0,2,1:T(8,128)}, f32[1024,16,48]{0,2,1:T(8,128)S(1)}, f32[16,64,16,48]{1,3,2,0:T(8,128)}, bf16[16,64,16,48]{1,3,2,...) while((s32[]{:T(128)}, f32[1024,16,48]{0,2,1:T(8,128)}, ...), condition=%wide.region_50.50_spmd.clone, body=%wide.region_48.49_spmd.clone.sunk | while | flops 534564864 | bytes 71064224 | solution.py:184
  3315.6 13.6 bitcast_add_fusion.28
  3353.1 13.6 bitcast_add_fusion.28
  3390.7 13.6 bitcast_add_fusion.28
  3503.4 13.6 bitcast_add_fusion.28
  3541.0 13.6 bitcast_add_fusion.28
  3616.2 13.6 bitcast_add_fusion.28
  3653.7 13.7 bitcast_add_fusion.28
  3691.4 13.6 bitcast_add_fusion.28
  3729.0 13.6 bitcast_add_fusion.28
  3761.1 54.3 %dynamic_update_slice.174 = f32[2,1024,16,48]{1,0,3,2:T(2,128)} dynamic-update-slice(f32[2,1024,16,48]{1,0,3,2:T(2,128)} %get-tuple-element.3123, f32[1,1024,16,48]{1,0,3,2:T(1,128)} %copy.972, s32[]{:T(128)} %get-tuple-element.3121, s32[]{:T(128)} %constant.876.clone.1..sunk.1, s32[]{:T(128)} %constant.876.clone.1..sunk.1, s32[]{:T(128)} %constant.876.clone.1..sunk.1) | dynamic-update-slice | bytes 6291460 | tf_op jit(solution)/shard_map/while/body/jit(dynamic_update_index_in_dim)/dynamic_update_slice | solution.py:189
  3820.4 54.4 %dynamic_update_slice.175 = f32[2,1024,16,48]{1,0,3,2:T(2,128)} dynamic-update-slice(f32[2,1024,16,48]{1,0,3,2:T(2,128)} %get-tuple-element.3124, f32[1,1024,16,48]{1,0,3,2:T(1,128)} %copy.973, s32[]{:T(128)} %get-tuple-element.3121, s32[]{:T(128)} %constant.876.clone.1..sunk.1, s32[]{:T(128)} %constant.876.clone.1..sunk.1, s32[]{:T(128)} %constant.876.clone.1..sunk.1) | dynamic-update-slice | bytes 6291460 | tf_op jit(solution)/shard_map/while/body/jit(dynamic_update_index_in_dim)/dynamic_update_slice | solution.py:189
  4114.1 13.8 add_convert_fusion.2
  4164.7 16.9 convolution_convert_fusion.2
  4181.7 15.6 convolution_convert_fusion.1
  4197.9 16.5 fusion.484
  4262.8 41.7 reduce-scatter.11.cloned.1.call-done
  4304.4 278.9 %all-reduce.12 = (f32[192]{0:T(256)}, f32[192]{0:T(256)}, f32[192,2304]{1,0:T(8,128)}, f32[192,768]{1,0:T(8,128)}, f32[192]{0:T(256)}, /*index=5*/f32[192]{0:T(256)}, f32[192,3072]{1,0:T(8,128)}, f32[768,768]{1,0:T(8,128)}) all-reduce(f32[192]{0:T(256)S(1)} %dynamic-slice_convert_fusion.3, ...), channel_id=1, replica_groups=mesh['seq'=8,'fsdp'=4] {'seq'}, use_global_device_ids=true, to_apply=%region_80.81 | all-reduce | flops 1770240 | bytes 10622976 | tf_op jit(solution)/shard_map/psum | solution.py:380
  (1504 shorter events, 3569.6 us)
Async XLA Ops:
  7.2 81.5 %all-gather.5.cloned.1.call-start = ((), (), s32[]{:S(2)}) async-start(), calls=%async_computation.4 | async-start | bytes 4423680 | tf_op jit(solution)/shard_map/all_gather | solution.py:219
  7.9 883.0 %all-gather.7.cloned.1.call-start = ((), (), s32[]{:S(2)}) async-start(), calls=%async_computation.5 | async-start | bytes 1474560 | tf_op jit(solution)/shard_map/all_gather | solution.py:220
  8.7 891.0 %all-gather.9.cloned.1.call-start = ((), (), s32[]{:S(2)}) async-start(), calls=%async_computation.6 | async-start | bytes 5898240 | tf_op jit(solution)/shard_map/all_gather | solution.py:223
  9.4 911.2 %all-gather.11.cloned.1.call-start = ((), (), s32[]{:S(2)}) async-start(), calls=%async_computation.7 | async-start | bytes 5898240 | tf_op jit(solution)/shard_map/all_gather | solution.py:224
  11.2 56.8 %collective-permute-start.9 = (bf16[128,16]{0,1:T(8,128)(2,1)}, bf16[128,16]{0,1:T(8,128)(2,1)}, u32[]{:S(2)}, u32[]{:S(2)}) collective-permute-start(bf16[128,16]{0,1:T(8,128)(2,1)} %select_reduce_fusion.12), channel_id=1, source_target_pairs={{0,4},{4,0},{8,12},{12,8},{16,20},{20,16},{24,28},{28,24},{1,5},{5... | collective-permute-start | bytes 12296 | tf_op jit(solution)/shard_map/ppermute | solution.py:27
  15.4 56.1 %collective-permute-start.3 = (bf16[256,16]{1,0:T(8,128)(2,1)}, bf16[256,16]{1,0:T(8,128)(2,1)}, u32[]{:S(2)}, u32[]{:S(2)}) collective-permute-start(bf16[256,16]{1,0:T(8,128)(2,1)} %select_reduce_fusion.13), channel_id=1, source_target_pairs={{0,4},{4,0},{8,12},{12,8},{16,20},{20,16},{24,28},{28,24},{1,5},{5... | collective-permute-start | bytes 24584 | tf_op jit(solution)/shard_map/ppermute | solution.py:27
  16.6 65.2 %collective-permute-start = (bf16[512,16]{1,0:T(8,128)(2,1)S(1)}, bf16[512,16]{1,0:T(8,128)(2,1)}, u32[]{:S(2)}, u32[]{:S(2)}) collective-permute-start(bf16[512,16]{1,0:T(8,128)(2,1)S(1)} %select_reduce_fusion.14), channel_id=1, source_target_pairs={{0,4},{4,0},{8,12},{12,8},{16,20},{20,16},{24,28},{28,24},{1,5},{5... | collective-permute-start | bytes 49160 | tf_op jit(solution)/shard_map/ppermute | solution.py:27
  18.7 4244.1 %reduce-scatter.7.cloned.1.call-start = ((), (), s32[]{:S(2)}) async-start(), calls=%async_computation.9 | async-start | bytes 1474560 | tf_op jit(solution)/shard_map/reduce_scatter | solution.py:364
  27.4 61.3 %copy-start.16 = (bf16[1,2048,768]{1,2,0:T(8,128)(2,1)}, bf16[1,2048,768]{1,2,0:T(8,128)(2,1)S(1)}, u32[]{:S(2)}) copy-start(bf16[1,2048,768]{1,2,0:T(8,128)(2,1)S(1)} %copy.732) | copy-start | bytes 9437188
  27.9 60.7 %copy-start.116 = (f32[2048]{0:T(1024)}, f32[2048]{0:T(1024)S(1)}, u32[]{:S(2)}) copy-start(f32[2048]{0:T(1024)S(1)} %broadcast_multiply_fusion.5) | copy-start | bytes 24580
  28.8 59.9 %copy-start.127 = (f32[2048]{0:T(1024)}, f32[2048]{0:T(1024)S(1)}, u32[]{:S(2)}) copy-start(f32[2048]{0:T(1024)S(1)} %add_rsqrt_fusion.1) | copy-start | bytes 24580
  69.9 7.9 collective-permute-start.10
  77.4 8.6 collective-permute-start.4
  79.2 8.1 collective-permute-start.11
  397.3 246.1 %collective-permute-start.15 = (bf16[128,768]{1,0:T(8,128)(2,1)}, bf16[128,768]{1,0:T(8,128)(2,1)}, u32[]{:S(2)}, u32[]{:S(2)}) collective-permute-start(bf16[128,768]{1,0:T(8,128)(2,1)} %get-tuple-element.1645), channel_id=1, source_target_pairs={{0,4},{4,0},{8,12},{12,8},{16,20},{20,16},{24,28},{28,24},{1,5},{5... | collective-permute-start | bytes 589832 | tf_op jit(solution)/shard_map/ppermute | solution.py:27
  397.9 247.6 %collective-permute-start.12 = (bf16[128,768]{1,0:T(8,128)(2,1)}, bf16[128,768]{1,0:T(8,128)(2,1)}, u32[]{:S(2)}, u32[]{:S(2)}) collective-permute-start(bf16[128,768]{1,0:T(8,128)(2,1)} %get-tuple-element.1646), channel_id=1, source_target_pairs={{0,4},{4,0},{8,12},{12,8},{16,20},{20,16},{24,28},{28,24},{1,5},{5... | collective-permute-start | bytes 589832 | tf_op jit(solution)/shard_map/ppermute | solution.py:27
  410.2 238.1 %collective-permute-start.7 = (bf16[256,768]{1,0:T(8,128)(2,1)}, bf16[256,768]{1,0:T(8,128)(2,1)}, u32[]{:S(2)}, u32[]{:S(2)}) collective-permute-start(bf16[256,768]{1,0:T(8,128)(2,1)} %get-tuple-element.1648), channel_id=1, source_target_pairs={{0,4},{4,0},{8,12},{12,8},{16,20},{20,16},{24,28},{28,24},{1,5},{5... | collective-permute-start | bytes 1179656 | tf_op jit(solution)/shard_map/ppermute | solution.py:27
  410.9 240.2 %collective-permute-start.5 = (bf16[256,768]{1,0:T(8,128)(2,1)S(1)}, bf16[256,768]{1,0:T(8,128)(2,1)}, u32[]{:S(2)}, u32[]{:S(2)}) collective-permute-start(bf16[256,768]{1,0:T(8,128)(2,1)S(1)} %get-tuple-element.1649), channel_id=1, source_target_pairs={{0,4},{4,0},{8,12},{12,8},{16,20},{20,16},{24,28},{28,24},{1,5},{5... | collective-permute-start | bytes 1179656 | tf_op jit(solution)/shard_map/ppermute | solution.py:27
  430.5 254.3 %collective-permute-start.2 = (bf16[512,768]{1,0:T(8,128)(2,1)}, bf16[512,768]{1,0:T(8,128)(2,1)}, u32[]{:S(2)}, u32[]{:S(2)}) collective-permute-start(bf16[512,768]{1,0:T(8,128)(2,1)} %get-tuple-element.1653), channel_id=1, source_target_pairs={{0,4},{4,0},{8,12},{12,8},{16,20},{20,16},{24,28},{28,24},{1,5},{5... | collective-permute-start | bytes 2359304 | tf_op jit(solution)/shard_map/ppermute | solution.py:27
  643.4 46.7 %collective-permute-start.1 = (bf16[512,768]{1,0:T(8,128)(2,1)}, bf16[512,768]{1,0:T(8,128)(2,1)}, u32[]{:S(2)}, u32[]{:S(2)}) collective-permute-start(bf16[512,768]{1,0:T(8,128)(2,1)} %get-tuple-element.1654), channel_id=1, source_target_pairs={{0,4},{4,0},{8,12},{12,8},{16,20},{20,16},{24,28},{28,24},{1,5},{5... | collective-permute-start | bytes 2359304 | tf_op jit(solution)/shard_map/ppermute | solution.py:27
  645.6 12.1 collective-permute-start.16
  648.3 34.6 collective-permute-start.13
  651.2 124.3 %collective-permute-start.8 = (bf16[512,768]{1,0:T(8,128)(2,1)}, bf16[512,768]{1,0:T(8,128)(2,1)}, u32[]{:S(2)}, u32[]{:S(2)}) collective-permute-start(bf16[512,768]{1,0:T(8,128)(2,1)} %pad_maximum_fusion.10), channel_id=1, source_target_pairs={{0,8},{4,12},{8,0},{12,4},{16,24},{20,28},{24,16},{28,20},{1,9},{5... | collective-permute-start | bytes 2359304 | tf_op jit(solution)/shard_map/ppermute | solution.py:27
  653.8 29.1 copy-start.74
  657.7 120.1 %collective-permute-start.6 = (bf16[512,768]{1,0:T(8,128)(2,1)}, bf16[512,768]{1,0:T(8,128)(2,1)}, u32[]{:S(2)}, u32[]{:S(2)}) collective-permute-start(bf16[512,768]{1,0:T(8,128)(2,1)} %pad_maximum_fusion.9), channel_id=1, source_target_pairs={{0,8},{4,12},{8,0},{12,4},{16,24},{20,28},{24,16},{28,20},{1,9},{5... | collective-permute-start | bytes 2359304 | tf_op jit(solution)/shard_map/ppermute | solution.py:27
  683.0 144.3 %collective-permute-start.17 = (bf16[512,768]{1,0:T(8,128)(2,1)}, bf16[512,768]{1,0:T(8,128)(2,1)}, u32[]{:S(2)}, u32[]{:S(2)}) collective-permute-start(bf16[512,768]{1,0:T(8,128)(2,1)} %pad_maximum_fusion.12), channel_id=1, source_target_pairs={{0,16},{4,20},{8,24},{12,28},{16,0},{20,4},{24,8},{28,12},{1,17},{... | collective-permute-start | bytes 2359304 | tf_op jit(solution)/shard_map/ppermute | solution.py:27
  684.8 144.8 %collective-permute-start.14 = (bf16[512,768]{1,0:T(8,128)(2,1)}, bf16[512,768]{1,0:T(8,128)(2,1)}, u32[]{:S(2)}, u32[]{:S(2)}) collective-permute-start(bf16[512,768]{1,0:T(8,128)(2,1)} %pad_maximum_fusion.11), channel_id=1, source_target_pairs={{0,16},{4,20},{8,24},{12,28},{16,0},{20,4},{24,8},{28,12},{1,17},{... | collective-permute-start | bytes 2359304 | tf_op jit(solution)/shard_map/ppermute | solution.py:27
  896.3 72.4 %copy-start.118 = (f32[2048]{0:T(1024)}, f32[2048]{0:T(1024)S(1)}, u32[]{:S(2)}) copy-start(f32[2048]{0:T(1024)S(1)} %broadcast_multiply_fusion.4) | copy-start | bytes 24580
  899.6 69.1 %copy-start.129 = (f32[2048]{0:T(1024)}, f32[2048]{0:T(1024)S(1)}, u32[]{:S(2)}) copy-start(f32[2048]{0:T(1024)S(1)} %add_rsqrt_fusion) | copy-start | bytes 24580
  920.6 21.0 copy-start.161
  3078.1 54.4 %copy-start.81 = (f32[2,16,64,16]{2,1,0,3:T(8,128)S(1)}, f32[2,16,64,16]{2,1,0,3:T(8,128)}, u32[]{:S(2)}) copy-start(f32[2,16,64,16]{2,1,0,3:T(8,128)} %copy-done.80) | copy-start | bytes 393220 | tf_op jit(solution)/shard_map/while
  3820.4 54.4 %copy-start.81 = (f32[2,16,64,16]{2,1,0,3:T(8,128)S(1)}, f32[2,16,64,16]{2,1,0,3:T(8,128)}, u32[]{:S(2)}) copy-start(f32[2,16,64,16]{2,1,0,3:T(8,128)} %copy-done.80) | copy-start | bytes 393220 | tf_op jit(solution)/shard_map/while
  3888.2 94.4 %collective-permute-start.24 = (bf16[512,768]{1,0:T(8,128)(2,1)}, bf16[512,768]{1,0:T(8,128)(2,1)}, u32[]{:S(2)}, u32[]{:S(2)}) collective-permute-start(bf16[512,768]{1,0:T(8,128)(2,1)} %copy.857), channel_id=1, source_target_pairs={{0,4},{4,0},{8,12},{12,8},{16,20},{20,16},{24,28},{28,24},{1,5},{5... | collective-permute-start | bytes 2359304 | tf_op jit(solution)/shard_map/ppermute | solution.py:27
  3894.7 92.7 %collective-permute-start.18 = (bf16[512,768]{1,0:T(8,128)(2,1)}, bf16[512,768]{1,0:T(8,128)(2,1)}, u32[]{:S(2)}, u32[]{:S(2)}) collective-permute-start(bf16[512,768]{1,0:T(8,128)(2,1)} %copy.845), channel_id=1, source_target_pairs={{0,4},{4,0},{8,12},{12,8},{16,20},{20,16},{24,28},{28,24},{1,5},{5... | collective-permute-start | bytes 2359304 | tf_op jit(solution)/shard_map/ppermute | solution.py:27
  3911.5 99.4 %collective-permute-start.25 = (bf16[512,768]{1,0:T(8,128)(2,1)}, bf16[512,768]{1,0:T(8,128)(2,1)}, u32[]{:S(2)}, u32[]{:S(2)}) collective-permute-start(bf16[512,768]{1,0:T(8,128)(2,1)} %copy.860), channel_id=1, source_target_pairs={{0,8},{4,12},{8,0},{12,4},{16,24},{20,28},{24,16},{28,20},{1,9},{5... | collective-permute-start | bytes 2359304 | tf_op jit(solution)/shard_map/ppermute | solution.py:27
  3914.3 99.8 %collective-permute-start.19 = (bf16[512,768]{1,0:T(8,128)(2,1)}, bf16[512,768]{1,0:T(8,128)(2,1)}, u32[]{:S(2)}, u32[]{:S(2)}) collective-permute-start(bf16[512,768]{1,0:T(8,128)(2,1)} %copy.848), channel_id=1, source_target_pairs={{0,8},{4,12},{8,0},{12,4},{16,24},{20,28},{24,16},{28,20},{1,9},{5... | collective-permute-start | bytes 2359304 | tf_op jit(solution)/shard_map/ppermute | solution.py:27
  3924.7 92.8 %collective-permute-start.27 = (bf16[512,768]{1,0:T(8,128)(2,1)}, bf16[512,768]{1,0:T(8,128)(2,1)}, u32[]{:S(2)}, u32[]{:S(2)}) collective-permute-start(bf16[512,768]{1,0:T(8,128)(2,1)} %copy.863), channel_id=1, source_target_pairs={{0,16},{4,20},{8,24},{12,28},{16,0},{20,4},{24,8},{28,12},{1,17},{... | collective-permute-start | bytes 2359304 | tf_op jit(solution)/shard_map/ppermute | solution.py:27
  3982.6 280.2 %reduce-scatter.5.cloned.1.call-start = ((), (), s32[]{:S(2)}) async-start(), calls=%async_computation.8 | async-start | bytes 4423680 | tf_op jit(solution)/shard_map/reduce_scatter | solution.py:361
  3982.6 37.5 collective-permute-start.21
  4013.2 39.4 collective-permute-start.26
  4016.4 37.4 collective-permute-start.20
  4019.8 49.4 %collective-permute-start.28 = (bf16[256,768]{1,0:T(8,128)(2,1)}, bf16[256,768]{1,0:T(8,128)(2,1)}, u32[]{:S(2)}, u32[]{:S(2)}) collective-permute-start(bf16[256,768]{1,0:T(8,128)(2,1)} %select_convert_fusion.6), channel_id=1, source_target_pairs={{0,8},{4,12},{8,0},{12,4},{16,24},{20,28},{24,16},{28,20},{1,9},{5... | collective-permute-start | bytes 1179656 | tf_op jit(solution)/shard_map/ppermute | solution.py:27
  4022.3 49.0 %collective-permute-start.22 = (bf16[256,768]{1,0:T(8,128)(2,1)}, bf16[256,768]{1,0:T(8,128)(2,1)}, u32[]{:S(2)}, u32[]{:S(2)}) collective-permute-start(bf16[256,768]{1,0:T(8,128)(2,1)} %select_convert_fusion.8), channel_id=1, source_target_pairs={{0,8},{4,12},{8,0},{12,4},{16,24},{20,28},{24,16},{28,20},{1,9},{5... | collective-permute-start | bytes 1179656 | tf_op jit(solution)/shard_map/ppermute | solution.py:27
  4070.3 16.7 collective-permute-start.29
  4072.5 14.6 collective-permute-start.23
  4114.1 25.4 slice-start.6
  4164.6 98.2 %reduce-scatter.9.cloned.1.call-start = ((), (), s32[]{:S(2)}) async-start(), calls=%async_computation.10 | async-start | bytes 5898240 | tf_op jit(solution)/shard_map/reduce_scatter | solution.py:373
  4181.6 122.8 %reduce-scatter.11.cloned.1.call-start = ((), (), s32[]{:S(2)}) async-start(), calls=%async_computation.11 | async-start | bytes 5898240 | tf_op jit(solution)/shard_map/reduce_scatter | solution.py:376
  (205 other events, 1333.1 us)
Sparse Core Ops, SparseCore 0:
  9.6 33.4 all-gather.4
  44.7 17.7 all-gather.6
  64.0 37.4 all-gather.8
  102.9 37.4 all-gather.10
  3982.7 25.7 reduce-scatter.6
  4164.7 38.6 reduce-scatter.4
  4206.0 47.8 reduce-scatter.8
  4256.5 47.8 reduce-scatter.10
where the time goes:
time: 4630 us; the launch traced here: 4590 us
  matrix products  2750 us (59%)
  local copies, waits for them, and re-layouts  979 us (21%)
  other arithmetic  439 us (9%)
  blocking collectives  292 us (6%)
  waiting for transfers between devices  68.5 us (1%)
    dot_general x62, matrix products, piece(): jnp.einsum('hqk,qhd->khd', grad_scores, query, preferred_element_type=jnp...  828 us
    dot_general x62, matrix products, piece(): jnp.einsum('hqk,khd->qhd', grad_scores, key_seg, preferred_element_type=j...  701 us
    dot_general x124, matrix products, piece(): jnp.einsum('qhd,khd->hqk', query, key_seg, preferred_element_type=jnp.flo...  362 us
    dot_general x62, matrix products, piece(): jnp.einsum('hqk,qhd->khd', probs.astype(jnp.bfloat16), grad_blk, preferre...  322 us
    psum x1, blocking collectives, per_device(): lax.psum((shards[0], shards[1], shards[2], shards[3], shards[4], shards[5...  279 us
    dynamic_update_slice x8, local copies, waits for them, and re-layouts, attend_backward(): lax.map(segment, (query_b, keys, values, keeping, lse_b, grad_b, slope_b))  237 us
    dot_general x62, matrix products, piece(): jnp.einsum('qhd,khd->hqk', grad_blk, value_seg, preferred_element_type=jn...  227 us
    select_n x32, local copies, waits for them, and re-layouts, spread_rows(): jnp.where(head_pick(ratio, columns)[None], chosen[:, None, :], jnp.asarra...  185 us
  transfers between devices with their start and end apart: 38, of which 3 were waited for; matrix products, arithmetic and copies ran while one was open for 26% of the time, Pallas kernels for 0%

commit v1 on v0

v1 whole, which is shorter than its diff:
```python
import functools
import math

import jax
import jax.numpy as jnp
import ml_dtypes
import numpy as np
from jax import lax
from jax.experimental import pallas as pl
from jax.experimental.pallas import tpu as pltpu
from jax.sharding import PartitionSpec as P

HEADS = 16
HEAD_DIM = 48
SEG = 1024
BRANCHES = 5
RES = 16
RUN = SEG // RES
D = HEADS * HEAD_DIM

EPS = 1e-05
NEG = -1e30
ROOT_HALF = 0.7071067811865476
INV_ROOT_TWO_PI = 0.3989422804014327
F32 = jnp.float32
BF16 = jnp.bfloat16
QUERY_SCALE = math.log2(math.e) * HEAD_DIM ** (-0.5)
VMEM_LIMIT = 56 * 1024 * 1024


def dotg(left, right, left_dim, right_dim):
    return lax.dot_general(
        left, right, (((left_dim,), (right_dim,)), ((), ())), preferred_element_type=F32
    )


def normalize(values, gain, shift):
    mean = jnp.mean(values, axis=-1, keepdims=True)
    centred = values - mean
    spread = jnp.mean(centred * centred, axis=-1, keepdims=True)
    inverse = lax.rsqrt(spread + EPS)
    normed = centred * inverse
    return (normed * gain + shift, normed, inverse)


def normalize_back(grad, normed, inverse, gain):
    scaled = grad * gain
    first = jnp.mean(scaled, axis=-1, keepdims=True)
    second = jnp.mean(scaled * normed, axis=-1, keepdims=True)
    return (
        inverse * (scaled - first - normed * second),
        jnp.sum(grad * normed, axis=0),
        jnp.sum(grad, axis=0),
    )


def reorder(array):
    rows, cols = array.shape
    split = array.reshape(rows // SEG, RUN, 2, 2, 2, 2, cols)
    return split.transpose(0, 5, 4, 3, 2, 1, 6).reshape(rows, cols)


def restore(array):
    rows, cols = array.shape
    split = array.reshape(rows // SEG, 2, 2, 2, 2, RUN, cols)
    return split.transpose(0, 5, 4, 3, 2, 1, 6).reshape(rows, cols)


def reversed_bits(head):
    return ((head & 1) << 3) | ((head & 2) << 1) | ((head & 4) >> 1) | ((head & 8) >> 3)


def near_class(head, low_bits, length):
    lane = lax.broadcasted_iota(jnp.int32, (1, length), 1)
    rho = lax.rem(lane // RUN, 1 << low_bits)
    return rho ^ (reversed_bits(head) & ((1 << low_bits) - 1))


def class_rows(near, length):
    row = lax.broadcasted_iota(jnp.int32, (16, length), 0)
    step = lax.rem(row + 3, 4) + 1
    bound = jnp.where((row >= 5) & (row <= 12), lax.shift_right_logical(RES, step), 0)
    return row, near < bound


def query_rows(head, length, neg_lse=None):
    near = near_class(head, 4, length)
    row, inside = class_rows(near, length)
    out = jnp.where(inside, 1.0, 0.0)
    out = jnp.where(row == 0, 1.0, out)
    out = jnp.where(row == 4, jnp.where(near < 1, 0.0, NEG), out)
    if neg_lse is not None:
        high = neg_lse.astype(BF16).astype(F32)
        rest = neg_lse - high
        mid = rest.astype(BF16).astype(F32)
        low = rest - mid
        out = jnp.where(row == 1, high, jnp.where(row == 2, mid, jnp.where(row == 3, low, out)))
    return out.astype(BF16)


def weight_of(level, step):
    return math.log2((step - level + 1) / (step - level)) if step > level else 0.0


def key_rows(head, level, low_bits, length, keep):
    near = near_class(head, low_bits, length)
    row, inside = class_rows(near, length)
    weight = jnp.zeros((16, length), F32)
    for step in range(level + 1, BRANCHES):
        value = weight_of(level, step)
        high = float(np.asarray(value, ml_dtypes.bfloat16))
        weight = jnp.where(row == 4 + step, high, weight)
        weight = jnp.where(row == 8 + step, value - high, weight)
    out = jnp.where(inside, weight, 0.0)
    out = jnp.where((row >= 1) & (row <= 3), 1.0, out)
    out = jnp.where(row == 0, jnp.where(keep > 0.5, 0.0, NEG), out)
    if level == BRANCHES - 1:
        out = jnp.where(row == 4, 1.0, out)
    return out.astype(BF16)


def value_rows(length):
    row = lax.broadcasted_iota(jnp.int32, (16, length), 0)
    return jnp.where(row < 2, 1.0, 0.0).astype(BF16)


def join(rows, extra):
    return jnp.concatenate([rows, extra], axis=0)


def kept_start(head, level, seg):
    size = SEG >> level
    block = reversed_bits(head) >> (4 - level)
    return pl.multiple_of(seg * SEG + block * size, min(size, 128))


def attend_tiles(query, key, value, tile, acc, top):
    key_t = key.T
    for start in range(0, key.shape[1], tile):
        scores = dotg(key_t[start : start + tile], query, 1, 0)
        here = jnp.max(scores, axis=0, keepdims=True)
        new_top = here if top is None else jnp.maximum(top, here)
        probs = jnp.exp2(scores - new_top).astype(BF16)
        part = dotg(value[:, start : start + tile], probs, 1, 0)
        acc = part if top is None else acc * jnp.exp2(top - new_top) + part
        top = new_top
    return acc, top


def local_forward(nseg, q_ref, k_ref, v_ref, keep_ref, o_ref, l_ref, m_ref, qa, ka, va):
    head = pl.program_id(0)
    length = nseg * SEG
    qa[...] = join(q_ref[0], query_rows(head, length))
    va[...] = join(v_ref[0], value_rows(length))
    ka[0] = join(k_ref[0], key_rows(head, 0, 4, length, keep_ref[...]))
    if nseg == 2:
        ka[1] = join(k_ref[0], key_rows(head, 1, 4, length, keep_ref[...]))
    for seg in range(nseg):
        lanes = slice(seg * SEG, (seg + 1) * SEG)
        acc, top = attend_tiles(qa[:, lanes], ka[0, :, lanes], va[:, lanes], 256, None, None)
        o_ref[:, lanes] = acc[:HEAD_DIM]
        l_ref[0, :, lanes] = acc[HEAD_DIM : HEAD_DIM + 1]
        m_ref[0, :, lanes] = top
    if nseg == 2:
        for seg in range(2):
            mine = pl.ds(kept_start(head, 1, seg), SEG // 2)
            other = pl.ds(kept_start(head, 1, 1 - seg), SEG // 2)
            merge_level(qa[:, mine], ka[1, :, other], va[:, other], mine, o_ref, l_ref, m_ref)


def merge_level(query, key, value, mine, o_ref, l_ref, m_ref):
    acc = jnp.concatenate([o_ref[:, mine], jnp.broadcast_to(l_ref[0, :, mine], (16, query.shape[1]))])
    acc, top = attend_tiles(query, key, value, 256, acc, m_ref[0, :, mine])
    o_ref[:, mine] = acc[:HEAD_DIM]
    l_ref[0, :, mine] = acc[HEAD_DIM : HEAD_DIM + 1]
    m_ref[0, :, mine] = top


def remote_keys(head, level, pack, nseg):
    k_ref, v_ref, mask_ref = pack
    length = k_ref.shape[1]
    row = lax.broadcasted_iota(jnp.int32, (16, length), 0)
    keep = jnp.sum(jnp.where(row == head, mask_ref[...].astype(F32), 0.0), axis=0, keepdims=True)
    key = join(k_ref[...], key_rows(head, level, 4 - level, length, keep))
    return key, join(v_ref[...], value_rows(length))


def remote_plan(first):
    return [(level,) for level in range(first, 3)] + [(3, 4)]


def remote_forward(nseg, first, q_ref, keep_ref, o_in, l_in, m_in, *refs):
    head = pl.program_id(0)
    levels = range(first, BRANCHES)
    packs = {level: refs[3 * i : 3 * i + 3] for i, level in enumerate(levels)}
    att_ref, lse_ref, o_ref, l_ref, m_ref, qa = refs[3 * len(levels) :]
    length = nseg * SEG
    qa[...] = join(q_ref[0], query_rows(head, length))
    o_ref[...] = o_in[...]
    l_ref[...] = l_in[...]
    m_ref[...] = m_in[...]
    for group in remote_plan(first):
        pairs = [remote_keys(head, level, packs[level], nseg) for level in group]
        key = jnp.concatenate([pair[0] for pair in pairs], axis=1)
        value = jnp.concatenate([pair[1] for pair in pairs], axis=1)
        for seg in range(nseg):
            mine = pl.ds(kept_start(head, group[0], seg), SEG >> group[0])
            merge_level(qa[:, mine], key, value, mine, o_ref, l_ref, m_ref)
    weight = keep_ref[...] / l_ref[0]
    att_ref[...] = (o_ref[...] * weight).astype(BF16)
    lse_ref[0] = m_ref[0] + jnp.log2(l_ref[0])


def back_tile(query_t, grad_t, query, grad, key, value, dq, dk_ref, dv_ref, lanes, first):
    scores = dotg(query_t, key, 1, 0)
    slope = dotg(grad_t, value, 1, 0)
    probs = jnp.exp2(scores)
    dscore = (probs * slope).astype(BF16)
    probs = probs.astype(BF16)
    part = dotg(key[:HEAD_DIM], dscore, 1, 1)
    dq = part if dq is None else dq + part
    dv = dotg(grad[:HEAD_DIM], probs, 1, 0)
    dk = dotg(query[:HEAD_DIM], dscore, 1, 0)
    if first:
        dv_ref[:, lanes] = dv
        dk_ref[:, lanes] = dk
    else:
        dv_ref[:, lanes] += dv
        dk_ref[:, lanes] += dk
    return dq


def grad_rows(grad, slope):
    length = grad.shape[1]
    row = lax.broadcasted_iota(jnp.int32, (16, length), 0)
    high = (-slope).astype(BF16).astype(F32)
    low = -slope - high
    extra = jnp.where(row == 0, high, jnp.where(row == 1, low, 0.0)).astype(BF16)
    return join(grad, extra)


def back_pair(query, grad, key_ref, value_ref, key_lanes, tile, dk_ref, dv_ref, start_lane, fresh):
    out = []
    for start in range(0, query.shape[1], tile):
        size = min(tile, query.shape[1])
        q_tile, g_tile = query[:, start : start + size], grad[:, start : start + size]
        q_t, g_t = q_tile.T, g_tile.T
        dq = None
        for lanes in key_lanes:
            dq = back_tile(
                q_t, g_t, q_tile, g_tile, key_ref[:, lanes], value_ref[:, lanes], dq,
                dk_ref, dv_ref, lanes, fresh and start == 0,
            )
        out.append(dq)
    return jnp.concatenate(out, axis=1) if len(out) > 1 else out[0]


DQ_SCALE = HEAD_DIM ** (-0.5)
DK_SCALE = math.log(2.0)


def neg_total(lse, keep):
    return jnp.where(keep > 0.5, -lse, NEG)


def local_backward(nseg, first, q_ref, k_ref, v_ref, g_ref, lse_ref, slope_ref, keep_ref, dqr_ref, out_ref, qa, ga, ka, va, dk, dv):
    head = pl.program_id(0)
    length = nseg * SEG
    keep = keep_ref[...]
    qa[...] = join(q_ref[0], query_rows(head, length, neg_total(lse_ref[0], keep)))
    ga[...] = grad_rows(g_ref[...], slope_ref[0])
    va[...] = join(v_ref[0], value_rows(length))
    ka[0] = join(k_ref[0], key_rows(head, 0, 4, length, keep))
    if nseg == 2:
        ka[1] = join(k_ref[0], key_rows(head, 1, 4, length, keep))
    for seg in range(nseg):
        lanes = slice(seg * SEG, (seg + 1) * SEG)
        tiles = [slice(seg * SEG + 256 * i, seg * SEG + 256 * (i + 1)) for i in range(4)]
        dq = back_pair(qa[:, lanes], ga[:, lanes], ka.at[0], va, tiles, 256, dk, dv, 0, True)
        out_ref[0, :, lanes] = dq * DQ_SCALE
    if nseg == 2:
        for seg in range(2):
            mine = pl.ds(kept_start(head, 1, seg), SEG // 2)
            base = kept_start(head, 1, 1 - seg)
            tiles = [pl.ds(pl.multiple_of(base + 256 * i, 256), 256) for i in range(2)]
            dq = back_pair(qa[:, mine], ga[:, mine], ka.at[1], va, tiles, 256, dk, dv, 0, False)
            out_ref[0, :, mine] += dq * DQ_SCALE
    size = SEG >> first
    for seg in range(nseg):
        mine = pl.ds(kept_start(head, first, seg), size)
        out_ref[0, :, mine] += dqr_ref[:, seg * size : (seg + 1) * size]
    out_ref[1] = dk[...] * DK_SCALE
    out_ref[2] = dv[...]


def remote_backward(nseg, first, q_ref, g_ref, lse_ref, slope_ref, keep_ref, *refs):
    head = pl.program_id(0)
    levels = range(first, BRANCHES)
    n = len(levels)
    packs = {level: refs[3 * i : 3 * i + 3] for i, level in enumerate(levels)}
    dqr_ref = refs[3 * n]
    outs = {level: refs[3 * n + 1 + i] for i, level in enumerate(levels)}
    qa, ga, ka, va, dk, dv = refs[4 * n + 1 :]
    length = nseg * SEG
    qa[...] = join(q_ref[0], query_rows(head, length, neg_total(lse_ref[0], keep_ref[...])))
    ga[...] = grad_rows(g_ref[...], slope_ref[0])
    full = SEG >> first
    for group in remote_plan(first):
        for i, level in enumerate(group):
            key, value = remote_keys(head, level, packs[level], nseg)
            ka[:, i * 512 : (i + 1) * 512] = key
            va[:, i * 512 : (i + 1) * 512] = value
        size = SEG >> group[0]
        mine = [pl.ds(kept_start(head, group[0], seg), size) for seg in range(nseg)]
        query = jnp.concatenate([qa[:, m] for m in mine], axis=1)
        grad = jnp.concatenate([ga[:, m] for m in mine], axis=1)
        tiles = [slice(256 * i, 256 * (i + 1)) for i in range(2 * len(group))]
        dq = back_pair(query, grad, ka, va, tiles, 256, dk, dv, 0, True) * DQ_SCALE
        for seg in range(nseg):
            piece = dq[:, seg * size : (seg + 1) * size]
            if group[0] == first:
                dqr_ref[:, seg * full : (seg + 1) * full] = piece
            else:
                inner = (reversed_bits(head) >> (4 - group[0])) & ((1 << (group[0] - first)) - 1)
                lanes = pl.ds(pl.multiple_of(seg * full + inner * size, 128), size)
                dqr_ref[:, lanes] += piece
        for i, level in enumerate(group):
            lanes = slice(i * 512, (i + 1) * 512)
            outs[level][0] = (dk[:, lanes] * DK_SCALE).astype(BF16)
            outs[level][1] = dv[:, lanes].astype(BF16)


def row_block(length):
    return pl.BlockSpec((1, 1, length), lambda h: (h, 0, 0))


def head_block(length):
    return pl.BlockSpec((HEAD_DIM, length), lambda h: (h, 0))


def part_block(part, length):
    return pl.BlockSpec((1, HEAD_DIM, length), lambda h: (part, h, 0))


def keep_block(length):
    return pl.BlockSpec((1, length), lambda h: (0, 0))


def pack_specs(length):
    return [
        pl.BlockSpec((HEAD_DIM, length), lambda h: (h, 0)),
        pl.BlockSpec((HEAD_DIM, length), lambda h: (HEADS + h, 0)),
        pl.BlockSpec((16, length), lambda h: (2 * D // 16, 0)),
    ]


PARAMS = pltpu.CompilerParams(vmem_limit_bytes=VMEM_LIMIT)


def shape(dims, dtype):
    return jax.ShapeDtypeStruct(dims, dtype)


def call_local_forward(nseg, qkv, keep):
    length = nseg * SEG
    return pl.pallas_call(
        functools.partial(local_forward, nseg),
        grid=(HEADS,),
        in_specs=[part_block(0, length), part_block(1, length), part_block(2, length), keep_block(length)],
        out_specs=[head_block(length), row_block(length), row_block(length)],
        out_shape=[shape((D, length), F32), shape((HEADS, 1, length), F32), shape((HEADS, 1, length), F32)],
        scratch_shapes=[
            pltpu.VMEM((64, length), BF16),
            pltpu.VMEM((nseg, 64, length), BF16),
            pltpu.VMEM((64, length), BF16),
        ],
        compiler_params=PARAMS,
        name="local_forward",
    )(qkv, qkv, qkv, keep)


def call_remote_forward(nseg, first, qkv, keep, o_part, l_part, m_part, packs):
    length = nseg * SEG
    args, specs = [], []
    for pack in packs:
        args += [pack] * 3
        specs += pack_specs(pack.shape[1])
    return pl.pallas_call(
        functools.partial(remote_forward, nseg, first),
        grid=(HEADS,),
        in_specs=[part_block(0, length), keep_block(length), head_block(length), row_block(length), row_block(length)]
        + specs,
        out_specs=[head_block(length), row_block(length)],
        out_shape=[shape((D, length), BF16), shape((HEADS, 1, length), F32)],
        scratch_shapes=[
            pltpu.VMEM((HEAD_DIM, length), F32),
            pltpu.VMEM((1, 1, length), F32),
            pltpu.VMEM((1, 1, length), F32),
            pltpu.VMEM((64, length), BF16),
        ],
        compiler_params=PARAMS,
        name="remote_forward",
    )(qkv, keep, o_part, l_part, m_part, *args)


def call_remote_backward(nseg, first, qkv, grad, lse, slope, keep, packs):
    length = nseg * SEG
    args, specs = [], []
    for pack in packs:
        args += [pack] * 3
        specs += pack_specs(pack.shape[1])
    kept = nseg * (SEG >> first)
    return pl.pallas_call(
        functools.partial(remote_backward, nseg, first),
        grid=(HEADS,),
        in_specs=[part_block(0, length), head_block(length), row_block(length), row_block(length), keep_block(length)]
        + specs,
        out_specs=[head_block(kept)]
        + [pl.BlockSpec((2, HEAD_DIM, pack.shape[1]), lambda h: (0, h, 0)) for pack in packs],
        out_shape=[shape((D, kept), F32)] + [shape((2, D, pack.shape[1]), BF16) for pack in packs],
        scratch_shapes=[
            pltpu.VMEM((64, length), BF16),
            pltpu.VMEM((64, length), BF16),
            pltpu.VMEM((64, 1024), BF16),
            pltpu.VMEM((64, 1024), BF16),
            pltpu.VMEM((HEAD_DIM, 1024), F32),
            pltpu.VMEM((HEAD_DIM, 1024), F32),
        ],
        compiler_params=PARAMS,
        name="remote_backward",
    )(qkv, grad, lse, slope, keep, *args)


def call_local_backward(nseg, first, qkv, grad, lse, slope, keep, dq_remote):
    length = nseg * SEG
    return pl.pallas_call(
        functools.partial(local_backward, nseg, first),
        grid=(HEADS,),
        in_specs=[part_block(0, length), part_block(1, length), part_block(2, length), head_block(length),
                  row_block(length), row_block(length), keep_block(length), head_block(dq_remote.shape[1])],
        out_specs=pl.BlockSpec((3, HEAD_DIM, length), lambda h: (0, h, 0)),
        out_shape=shape((3, D, length), F32),
        scratch_shapes=[
            pltpu.VMEM((64, length), BF16),
            pltpu.VMEM((64, length), BF16),
            pltpu.VMEM((nseg, 64, length), BF16),
            pltpu.VMEM((64, length), BF16),
            pltpu.VMEM((HEAD_DIM, length), F32),
            pltpu.VMEM((HEAD_DIM, length), F32),
        ],
        compiler_params=PARAMS,
        name="local_backward",
    )(qkv, qkv, qkv, grad, lse, slope, keep, dq_remote)


def pack_kernel(nseg, first, kv_ref, keep_ref, *outs):
    for i, level in enumerate(range(first, BRANCHES)):
        size = SEG >> level
        for head in range(HEADS):
            start = (reversed_bits(head) >> (4 - level)) * size
            for part in range(2):
                src = pl.ds((part + 1) * D + head * HEAD_DIM, HEAD_DIM)
                dst = pl.ds(part * D + head * HEAD_DIM, HEAD_DIM)
                for seg in range(nseg):
                    outs[i][dst, seg * size : (seg + 1) * size] = kv_ref[
                        src, seg * SEG + start : seg * SEG + start + size
                    ]
        rows = []
        for head in range(HEADS):
            start = (reversed_bits(head) >> (4 - level)) * size
            rows.append(
                jnp.concatenate([keep_ref[:, seg * SEG + start : seg * SEG + start + size] for seg in range(nseg)], axis=1)
            )
        outs[i][2 * D :, :] = jnp.concatenate(rows, axis=0).astype(BF16)


def call_pack(nseg, first, qkv, keep):
    return pl.pallas_call(
        functools.partial(pack_kernel, nseg, first),
        out_shape=[shape((2 * D + 16, nseg * (SEG >> level)), BF16) for level in range(first, BRANCHES)],
        compiler_params=PARAMS,
        name="pack",
    )(qkv.reshape(3 * D, nseg * SEG), keep)


def exchange(array, distance):
    size = lax.axis_size("seq")
    return lax.ppermute(array, "seq", [(i, i ^ distance) for i in range(size)])


def fetch_level(pack, group):
    pieces = exchange(pack, group)
    step = 1
    while step < group:
        pieces = jnp.concatenate([pieces, exchange(pieces, step)], axis=-1)
        step *= 2
    return pieces


def return_level(grads, group):
    step = group // 2
    while step >= 1:
        half = grads.shape[-1] // 2
        other = exchange(grads[..., half:], step)
        grads = (grads[..., :half].astype(F32) + other.astype(F32)).astype(BF16)
        step //= 2
    return exchange(grads, group)


def spread_level(grads, level, nseg):
    size = SEG >> level
    shaped = grads.astype(F32).reshape(2, HEADS, HEAD_DIM, nseg, 1, size)
    head = jnp.arange(HEADS, dtype=jnp.int32)
    block = reversed_bits(head) >> (4 - level)
    hit = block[:, None] == jnp.arange(1 << level, dtype=jnp.int32)[None, :]
    full = jnp.where(hit[None, :, None, None, :, None], shaped, 0.0)
    return full.reshape(2, D, nseg * SEG)


def scatter_sum(term):
    part = lax.psum_scatter(term.astype(BF16), "fsdp", scatter_dimension=0, tiled=True)
    piece = lax.psum_scatter(part, "seq", scatter_dimension=0, tiled=True)
    return lax.all_gather(piece, "seq", axis=0, tiled=True).astype(F32)


def per_device(
    tokens,
    first_gain,
    first_shift,
    project_in,
    project_out,
    second_gain,
    second_shift,
    up_weight,
    down_weight,
    valid_mask,
    cotangent,
):
    length = tokens.shape[1]
    nseg = length // SEG
    first = nseg.bit_length()

    def gather(weight):
        return lax.all_gather(weight, "fsdp", axis=0, tiled=True)

    weight_in = gather(project_in)
    small = gather(jnp.stack([first_gain, first_shift, second_gain, second_shift], axis=1)).astype(F32)
    gain_attend, shift_attend, gain_feed, shift_feed = (small[:, i] for i in range(4))
    weight_out = gather(project_out)
    weight_up = gather(up_weight)
    weight_down = gather(down_weight)

    stream = reorder(tokens[0]).astype(F32)
    keep = reorder(valid_mask[0][:, None])[:, 0].astype(F32)[None, :]
    normed_in, unit_first, inverse_first = normalize(stream, gain_attend, shift_attend)
    inner = normed_in.astype(BF16)
    column_scale = jnp.where(jnp.arange(3 * D) < D, QUERY_SCALE, 1.0).astype(F32)
    qkv = (dotg(weight_in, inner, 0, 1) * column_scale[:, None]).astype(BF16).reshape(3, D, length)

    sends = call_pack(nseg, first, qkv, keep)
    packs = [
        fetch_level(send, (SEG << (level - 1)) // length)
        for level, send in zip(range(first, BRANCHES), sends)
    ]
    o_part, l_part, m_part = call_local_forward(nseg, qkv, keep)
    attended, lse = call_remote_forward(nseg, first, qkv, keep, o_part, l_part, m_part, packs)

    middle = stream + dotg(attended, weight_out, 0, 0)
    normed_mid, unit_second, inverse_second = normalize(middle, gain_feed, shift_feed)
    hidden = normed_mid.astype(BF16)
    upper = jnp.dot(hidden, weight_up, preferred_element_type=F32)
    active = (0.5 * upper * (1.0 + lax.erf(upper * ROOT_HALF))).astype(BF16)
    final = middle + jnp.dot(active, weight_down, preferred_element_type=F32)
    mixed = restore(final.astype(BF16))[None]

    grad_final = reorder(cotangent[0])
    grad_down = dotg(active, grad_final, 0, 0)
    grad_active = dotg(grad_final, weight_down, 1, 1)
    slope = (
        0.5 * (1.0 + lax.erf(upper * ROOT_HALF))
        + upper * jnp.exp(-0.5 * upper * upper) * INV_ROOT_TWO_PI
    )
    grad_upper = (grad_active * slope).astype(BF16)
    grad_up = dotg(hidden, grad_upper, 0, 0)
    grad_hidden = dotg(grad_upper, weight_up, 1, 1)
    grad_mid_norm, grad_gain_feed, grad_shift_feed = normalize_back(
        grad_hidden, unit_second, inverse_second, gain_feed
    )
    grad_middle = grad_final.astype(F32) + grad_mid_norm
    grad_branch = grad_middle.astype(BF16)
    grad_out_proj = dotg(attended, grad_branch, 1, 0)
    grad_merged = (dotg(weight_out, grad_branch, 1, 1) * keep).astype(BF16)
    along = jnp.sum(
        (grad_merged.astype(F32) * attended.astype(F32)).reshape(HEADS, HEAD_DIM, length), axis=1
    )[:, None, :]

    dq_remote, *sent = call_remote_backward(nseg, first, qkv, grad_merged, lse, along, keep, packs)
    returned = [
        return_level(part, (SEG << (level - 1)) // length)
        for level, part in zip(range(first, BRANCHES), sent)
    ]
    local = call_local_backward(nseg, first, qkv, grad_merged, lse, along, keep, dq_remote)
    key_value = local[1:]
    for level, part in zip(range(first, BRANCHES), returned):
        key_value = key_value + spread_level(part, level, nseg)
    grad_mixed = jnp.concatenate([local[:1], key_value], axis=0).astype(BF16).reshape(3 * D, length)

    grad_in = dotg(inner, grad_mixed, 0, 1)
    grad_inner = dotg(grad_mixed, weight_in, 0, 1)
    grad_in_norm, grad_gain_attend, grad_shift_attend = normalize_back(
        grad_inner, unit_first, inverse_first, gain_attend
    )
    tokens_back = restore(grad_middle + grad_in_norm)[None]

    vectors = jnp.stack([grad_gain_attend, grad_shift_attend, grad_gain_feed, grad_shift_feed], axis=1)
    vectors = scatter_sum(vectors)
    return (
        mixed,
        tokens_back,
        vectors[:, 0],
        vectors[:, 1],
        scatter_sum(grad_in),
        scatter_sum(grad_out_proj),
        vectors[:, 2],
        vectors[:, 3],
        scatter_sum(grad_up),
        scatter_sum(grad_down),
    )


def solution(mesh):
    in_specs = (
        P("fsdp", "seq", None),
        P("fsdp"),
        P("fsdp"),
        P("fsdp", None),
        P("fsdp", None),
        P("fsdp"),
        P("fsdp"),
        P("fsdp", None),
        P("fsdp", None),
        P("fsdp", "seq"),
        P("fsdp", "seq", None),
    )
    out_specs = (
        P("fsdp", "seq", None),
        P("fsdp", "seq", None),
        P("fsdp"),
        P("fsdp"),
        P("fsdp", None),
        P("fsdp", None),
        P("fsdp"),
        P("fsdp"),
        P("fsdp", None),
        P("fsdp", None),
    )
    return jax.shard_map(
        per_device, mesh=mesh, in_specs=in_specs, out_specs=out_specs, check_vma=False
    )
```

time: 4630 us -> 1180 us (0.25)
  matrix products: 2750 us -> 159 us
  local copies, waits for them, and re-layouts: 979 us -> 181 us
  other arithmetic: 439 us -> 79.6 us
  Pallas kernels: 0 us -> 314 us
  waiting for transfers between devices: 68.5 us -> 289 us
  blocking collectives: 292 us -> 106 us
    dot_general x446 -> x12, matrix products: 2750 us -> 159 us  [the longest x10 125 us: dotg(): lax.dot_general(left, right, (((left_dim,), (right_dim,)), ((), ())), pre...]
    pallas_call x0 -> x5, Pallas kernels: none -> 314 us  [the longest x1 145 us: call_local_backward(): pl.pallas_call(functools.partial(local_backward, nseg, first), grid=(HEAD...]
    psum x1 -> x0, blocking collectives: 279 us -> none  [per_device(): lax.psum((shards[0], shards[1], shards[2], shards[3], shards[4], shards[5...]
    dynamic_update_slice x14 -> x0, local copies, waits for them, and re-layouts: 274 us -> none  [the longest x8 237 us: attend_backward(): lax.map(segment, (query_b, keys, values, keeping, lse_b, grad_b, slope_b))]
    select_n x42 -> x0, local copies, waits for them, and re-layouts: 204 us -> none  [the longest x32 185 us: spread_rows(): jnp.where(head_pick(ratio, columns)[None], chosen[:, None, :], jnp.asarra...]
    reduce_sum x87 -> x1, other arithmetic: 202 us -> 3.77 us  [per_device(): jnp.sum((grad_merged.astype(F32) * attended.astype(F32)).reshape(HEADS, H...]
    reduce_scatter x4 -> x8, waiting for transfers between devices: 41.7 us -> 185 us  [the longest x4 165 us: scatter_sum(): piece = lax.psum_scatter(part, 'seq', scatter_dimension=0, tiled=True)]
    select_n x43 -> x1, other arithmetic: 98.3 us -> 0.01 us  [per_device(): jnp.where(jnp.arange(3 * D) < D, QUERY_SCALE, 1.0).astype(F32)]
  transfers between devices with their start and end apart: 38 -> 27, of which waited for: 3 -> 11; matrix products, arithmetic and copies ran while one was open for 26% -> 35% of each run, Pallas kernels for 0% -> 27%
where the time goes in v1:
time: 1180 us; the launch traced here: 1160 us
  Pallas kernels  314 us (27%)
  waiting for transfers between devices  289 us (24%)
  local copies, waits for them, and re-layouts  181 us (15%)
  matrix products  159 us (13%)
  blocking collectives  106 us (9%)
  other arithmetic  79.6 us (7%)
  starting transfers between devices  17.8 us (2%)
  between operations  15.5 us (1%)
    reduce_scatter x4, waiting for transfers between devices, scatter_sum(): piece = lax.psum_scatter(part, 'seq', scatter_dimension=0, tiled=True)  165 us
    pallas_call x1, Pallas kernels, call_local_backward(): pl.pallas_call(functools.partial(local_backward, nseg, first), grid=(HEAD...  145 us
    dot_general x10, matrix products, dotg(): lax.dot_general(left, right, (((left_dim,), (right_dim,)), ((), ())), pre...  125 us
    broadcast_in_dim x15, local copies, waits for them, and re-layouts, spread_level(): full = jnp.where(hit[None, :, None, None, :, None], shaped, 0.0)  99 us
    all_gather x3, blocking collectives, scatter_sum(): return lax.all_gather(piece, 'seq', axis=0, tiled=True).astype(F32)  80.5 us
    pallas_call x1, Pallas kernels, call_local_forward(): pl.pallas_call(functools.partial(local_forward, nseg), grid=(HEADS,), in_...  75.3 us
    ppermute x12, waiting for transfers between devices, exchange(): return lax.ppermute(array, 'seq', [(i, i ^ distance) for i in range(size)])  50.8 us
    all_gather x2, waiting for transfers between devices, scatter_sum(): return lax.all_gather(piece, 'seq', axis=0, tiled=True).astype(F32)  49.6 us
  transfers between devices with their start and end apart: 27, of which 11 were waited for; matrix products, arithmetic and copies ran while one was open for 35% of the time, Pallas kernels for 27%

profile of v1, /device:TPU:0, one launch (start us, length us, event | category | flops | bytes accessed | tf_op | source)
XLA Modules:
  0.0 1162.8 jit_solution(1373816997830604533)
XLA Ops:
  12.1 6.1 all-gather
  20.9 7.8 reshape.269
  28.7 9.3 copy.52
  41.5 7.1 multiply_reduce_fusion.5
  53.2 12.0 %multiply_convert_fusion.1 = bf16[2048,2304]{0,1:T(8,128)(2,1)} fusion(bf16[2048,768]{1,0:T(8,128)(2,1)S(1)} %add_convert_fusion.3, bf16[768,2304]{1,0:T(8,128)(2,1)} %all-gather.9.cloned.1.call-done, f32[2304]{0:T(1024)S(1)} %fusion.16), kind=kOutput, calls=%fused_computation.10 | convolution fusion | flops 7257194496 | bytes 16131072 | tf_op jit(solution)/shard_map/dot_general | solution.py:32
  65.2 5.6 pack.1
  75.5 16.9 %collective-permute-done.3 = bf16[1552,128]{1,0:T(8,128)(2,1)S(1)} collective-permute-done((bf16[1552,128]{1,0:T(8,128)(2,1)}, bf16[1552,128]{1,0:T(8,128)(2,1)S(1)}, u32[]{:S(2)}, u32[]{:S(2)}) %collective-permute-start.3) | collective-permute-done | bytes 397344 | tf_op jit(solution)/shard_map/ppermute | solution.py:488
  94.5 10.1 collective-permute-done.4
  106.4 7.3 reshape_squeeze.4
  118.6 75.3 %local_forward.1 = (f32[768,2048]{1,0:T(8,128)}, f32[16,1,2048]{2,1,0:T(1,128)}, f32[16,1,2048]{2,1,0:T(1,128)}) custom-call(bf16[3,768,2048]{2,1,0:T(8,128)(2,1)} %bitcast.89, bf16[3,768,2048]{2,1,0:T(8,128)(2,1)} %bitcast.90, bf16[3,768,2048]{2,1,0:T(8,128)(2,1)} %bitcast.91, f32[1,2048]{1,0:T(1,128)} %convert_element_type.173.keep_ref), custom_call_target="tpu_custom_call" | custom-call | tf_op jit(solution)/shard_map/local_forward/pallas_call | solution.py:366
  196.9 14.7 %collective-permute-done.2 = bf16[1552,256]{1,0:T(8,128)(2,1)S(1)} collective-permute-done((bf16[1552,256]{1,0:T(8,128)(2,1)S(1)}, bf16[1552,256]{1,0:T(8,128)(2,1)S(1)}, u32[]{:S(2)}, u32[]{:S(2)}) %collective-permute-start.2) | collective-permute-done | bytes 794656 | tf_op jit(solution)/shard_map/ppermute | solution.py:488
  213.4 48.0 %remote_forward.1 = (bf16[768,2048]{1,0:T(8,128)(2,1)}, f32[16,1,2048]{2,1,0:T(1,128)}) custom-call(bf16[3,768,2048]{2,1,0:T(8,128)(2,1)} %bitcast.92, f32[1,2048]{1,0:T(1,128)} %convert_element_type.173.keep_ref, f32[768,2048]{1,0:T(8,128)} %get-tuple-element.22.o_in, f32[16,1,2048]{2,1,0:T(1,128)} %get-tuple-element.23.l_in, ...), custom_call_target="tpu_custom_call" | custom-call | tf_op jit(solution)/shard_map/remote_forward/pallas_call | solution.py:388
  261.4 7.2 fusion.26
  272.1 18.5 %multiply_convert_fusion = (bf16[2048,3072]{1,0:T(8,128)(2,1)S(1)}, f32[2048,3072]{1,0:T(8,128)}) fusion(bf16[768,3072]{1,0:T(8,128)(2,1)} %all-gather.13.cloned.1.call-done, f32[2048,768]{1,0:T(8,128)} %copy-done.5, f32[768]{0:T(1024)S(1)} %get-tuple-element.43, f32[768]{0:T(1024)S(1)} %get-tuple-element.42, f32[2048]{0:T(1024)S(1)} %add_rsqrt_fusion.1, ...), kind=kOutput, calls=%fused_computation.7 | convolution fusion | flops 9702998016 | bytes 48781312 | tf_op jit(solution)/shard_map/dot_general | solution.py:571
  295.0 11.7 %convolution_convert_fusion = bf16[3072,768]{1,0:T(8,128)(2,1)} fusion(bf16[2048,3072]{1,0:T(8,128)(2,1)S(1)} %get-tuple-element.52, bf16[2048,768]{1,0:T(8,128)(2,1)S(1)} %bitcast.108), kind=kOutput, calls=%fused_computation.36 | convolution fusion | flops 9666035712 | bytes 20447232 | tf_op jit(solution)/shard_map/dot_general | solution.py:32
  306.9 22.0 %fusion.5 = bf16[2048,3072]{1,0:T(8,128)(2,1)S(1)} fusion(f32[2048,3072]{1,0:T(8,128)} %get-tuple-element.53, bf16[2048,768]{1,0:T(8,128)(2,1)} %bitcast.107, bf16[3072,768]{1,0:T(8,128)(2,1)} %all-gather.15.cloned.1.call-done), kind=kOutput, calls=%fused_computation.6 | convolution fusion | flops 9726590976 | bytes 45613056 | tf_op jit(solution)/shard_map/dot_general | solution.py:32
  333.4 14.0 %convolution_convert_fusion.1 = bf16[768,3072]{1,0:T(8,128)(2,1)} fusion(bf16[2048,3072]{1,0:T(8,128)(2,1)S(1)} %fusion.5, f32[2048,768]{1,0:T(8,128)S(1)} %bitcast.103, f32[768]{0:T(1024)S(1)} %get-tuple-element.43, f32[768]{0:T(1024)S(1)} %get-tuple-element.42, f32[2048]{0:T(1024)S(1)} %add_rsqrt_fusion.1, f32[2048]{0:T(1024)S(1)} %broadcast_multiply_fusion.5), kind=kOutput, calls=%fused_computation.37 | convolution fusion | flops 9673900032 | bytes 23615488 | tf_op jit(solution)/shard_map/dot_general | solution.py:32
  347.6 19.4 %multiply_reduce_fusion = (bf16[768]{0:T(1024)(128)(2,1)S(1)}, f32[2048]{0:T(1024)S(1)}, f32[2048]{0:T(1024)S(1)}, bf16[768]{0:T(1024)(128)(2,1)S(1)}, f32[2048,768]{1,0:T(8,128)}) fusion(f32[2048,768]{1,0:T(8,128)} %copy-done.5, f32[2048]{0:T(1024)S(1)} %add_rsqrt_fusion.1, f32[2048]{0:T(1024)S(1)} %broadcast_multiply_fusion.5, ...), kind=kOutput, calls=%fused_computation.20 | convolution fusion | flops 9677826048 | bytes 29923328 | tf_op jit(solution)/shard_map/dot_general | solution.py:32
  367.1 5.5 multiply_add_fusion.1
  372.6 5.7 convert_multiply_fusion
  382.9 39.5 %remote_backward.1 = (f32[768,512]{1,0:T(8,128)}, bf16[2,768,512]{2,1,0:T(8,128)(2,1)}, bf16[2,768,512]{2,1,0:T(8,128)(2,1)}, bf16[2,768,512]{2,1,0:T(8,128)(2,1)}) custom-call(bf16[3,768,2048]{2,1,0:T(8,128)(2,1)} %bitcast.93, bf16[768,2048]{1,0:T(8,128)(2,1)} %get-tuple-element.56.g_ref, f32[16,1,2048]{2,1,0:T(1,128)} %get-tuple-element.29.lse_ref, ...), custom_call_target="tpu_custom_call" | custom-call | tf_op jit(solution)/shard_map/remote_backward/pallas_call | solution.py:413
  432.9 9.0 collective-permute-done.9
  454.7 9.0 broadcast_in_dim.138
  463.7 145.4 %local_backward.1 = f32[3,768,2048]{2,1,0:T(8,128)} custom-call(bf16[3,768,2048]{2,1,0:T(8,128)(2,1)} %bitcast.94, bf16[3,768,2048]{2,1,0:T(8,128)(2,1)} %bitcast.95, bf16[3,768,2048]{2,1,0:T(8,128)(2,1)} %bitcast.96, bf16[768,2048]{1,0:T(8,128)(2,1)} %get-tuple-element.56.g_ref, f32[16,1,2048]{2,1,0:T(1,128)} %get-tuple-element.29.lse_ref, ...), custom_call_target="tpu_custom_call" | custom-call | tf_op jit(solution)/shard_map/local_backward/pallas_call | solution.py:436
  628.3 5.9 broadcast_in_dim.127
  634.2 15.8 %broadcast_in_dim.128 = f32[2,768,2048]{2,1,0:T(8,128)} reshape(f32[2,16,48,2,4,256]{5,4,3,2,1,0:T(4,128)} %broadcast_in_dim.127) | data formatting | bytes 25165824 | tf_op jit(solution)/shard_map/jit(_where)/broadcast_in_dim | solution.py:516
  657.5 13.7 %broadcast_in_dim.136 = f32[2,768,2048]{2,1,0:T(8,128)} reshape(f32[2,16,48,2,8,128]{5,4,3,2,1,0:T(8,128)} %broadcast_in_dim.135) | data formatting | bytes 25165824 | tf_op jit(solution)/shard_map/jit(_where)/broadcast_in_dim | solution.py:516
  673.3 8.6 broadcast_in_dim.142
  681.9 21.8 %broadcast_in_dim.143 = f32[2,768,2048]{2,1,0:T(8,128)} reshape(f32[2,16,48,2,16,64]{5,4,3,2,1,0:T(8,128)} %broadcast_in_dim.142) | data formatting | bytes 25165824 | tf_op jit(solution)/shard_map/jit(_where)/broadcast_in_dim | solution.py:516
  703.7 21.9 %fusion.7 = bf16[2,768,2048]{2,1,0:T(8,128)(2,1)} fusion(f32[3,768,2048]{2,1,0:T(8,128)} %local_backward.1, f32[2,768,2048]{2,1,0:T(8,128)} %broadcast_in_dim.143, f32[2,768,2048]{2,1,0:T(8,128)} %broadcast_in_dim.136, f32[2,768,2048]{2,1,0:T(8,128)} %broadcast_in_dim.128, pred[768,2048]{1,0:T(8,128)(4,1)} %broadcast_in_dim.138, ...), kind=kLoop, calls=%fused_computation.13 | loop fusion | flops 22020096 | bytes 61341696 | tf_op jit(solution)/shard_map/add | solution.py:605
  725.6 7.2 maximum_convert_fusion
  732.9 13.5 %convolution_convert_fusion.2 = bf16[768,2304]{1,0:T(8,128)(2,1)} fusion(bf16[2048,768]{1,0:T(8,128)(2,1)} %bitcast.112, bf16[2304,2048]{1,0:T(8,128)(2,1)} %bitcast.109), kind=kOutput, calls=%fused_computation.38 | convolution fusion | flops 7249526784 | bytes 16121856 | tf_op jit(solution)/shard_map/dot_general | solution.py:32
  747.8 16.2 %multiply_reduce_fusion.1 = (bf16[768]{0:T(1024)(128)(2,1)S(1)}, f32[2048]{0:T(1024)S(1)}, f32[2048]{0:T(1024)S(1)}, bf16[768]{0:T(1024)(128)(2,1)S(1)}, f32[2048,768]{1,0:T(8,128)}) fusion(f32[2,64,2,2,2,2,768]{6,1,2,3,4,5,0:T(8,128)} %copy.52, f32[2048]{0:T(1024)S(1)} %copy-done.22, f32[2048]{0:T(1024)S(1)} %copy-done.20, f32[768]{0:T(1024)S(1)} %copy-done.24, ...), kind=kOutput, calls=%fused_computation.21 | convolution fusion | flops 7261906944 | bytes 25597952 | tf_op jit(solution)/shard_map/dot_general | solution.py:32
  765.6 19.8 %reduce-scatter.13.cloned.1.call-done = bf16[192,2304]{1,0:T(8,128)(2,1)} async-done(((bf16[768,2304]{1,0:T(8,128)(2,1)}), bf16[192,2304]{1,0:T(8,128)(2,1)}) %reduce-scatter.13.cloned.1.call-update) | async-done | bytes 884752 | tf_op jit(solution)/shard_map/reduce_scatter | solution.py:521
  786.7 66.2 %reduce-scatter.27.cloned.1.call-done = bf16[96,768]{1,0:T(8,128)(2,1)} async-done(((bf16[768,768]{1,0:T(8,128)(2,1)}), bf16[96,768]{1,0:T(8,128)(2,1)}) %reduce-scatter.27.cloned.1.call-update) | async-done | bytes 147472 | tf_op jit(solution)/shard_map/reduce_scatter | solution.py:522
  852.9 15.6 %add_convert_fusion.1 = bf16[2048,768]{1,0:T(8,128)(2,1)S(1)} fusion(f32[2048,768]{1,0:T(8,128)} %copy-done.5, bf16[2048,3072]{1,0:T(8,128)(2,1)} %copy-done.29, bf16[3072,768]{1,0:T(8,128)(2,1)} %all-gather.15.cloned.1.call-done), kind=kOutput, calls=%fused_computation.28 | convolution fusion | flops 9666822144 | bytes 26738688 | tf_op jit(solution)/shard_map/dot_general | solution.py:573
  874.4 44.8 %reduce-scatter.23.cloned.1.call-done = bf16[24,3072]{1,0:T(8,128)(2,1)} async-done(((bf16[192,3072]{1,0:T(8,128)(2,1)}), bf16[24,3072]{1,0:T(8,128)(2,1)}) %reduce-scatter.23.cloned.1.call-update) | async-done | bytes 147472 | tf_op jit(solution)/shard_map/reduce_scatter | solution.py:522
  919.2 7.6 multiply_add_fusion
  926.8 7.5 copy.59
  934.3 8.5 broadcast_in_dim_reshape.7
  943.6 19.6 %all-reduce = bf16[192,4]{0,1:T(4,128)(2,1)S(1)} all-reduce(bf16[192,4]{0,1:T(4,128)(2,1)S(1)} %copy.63), channel_id=3, replica_groups=mesh['seq'=8,'fsdp'=4] {'seq'}, use_global_device_ids=true, to_apply=%region_14.15.clone | all-reduce | flops 768 | bytes 3072
  963.3 16.3 %all-gather.1 = bf16[8,24,4]{1,2,0:T(4,128)(2,1)S(1)} all-gather(bf16[1,24,4]{1,2,0:T(4,128)(2,1)S(1)} %dynamic-slice_bitcast_fusion), channel_id=1, replica_groups=mesh['seq'=8,'fsdp'=4] {'seq'}, dimensions={0}, use_global_device_ids=true | all-gather | bytes 1728 | tf_op jit(solution)/shard_map/all_gather | solution.py:523
  980.2 22.6 %reduce-scatter.19.cloned.1.call-done = bf16[24,768]{1,0:T(8,128)(2,1)} async-done(((bf16[192,768]{1,0:T(8,128)(2,1)}), bf16[24,768]{1,0:T(8,128)(2,1)}) %reduce-scatter.19.cloned.1.call-update) | async-done | bytes 36880 | tf_op jit(solution)/shard_map/reduce_scatter | solution.py:522
  1002.8 31.3 %all_gather.37 = bf16[192,768]{1,0:T(8,128)(2,1)S(1)} all-gather(bf16[24,768]{1,0:T(8,128)(2,1)} %reduce-scatter.19.cloned.1.call-done), channel_id=1, replica_groups=mesh['seq'=8,'fsdp'=4] {'seq'}, dimensions={0}, use_global_device_ids=true | all-gather | bytes 331776 | tf_op jit(solution)/shard_map/all_gather | solution.py:523
  1035.0 31.4 %reduce-scatter.15.cloned.1.call-done = bf16[24,2304]{1,0:T(8,128)(2,1)} async-done(((bf16[192,2304]{1,0:T(8,128)(2,1)}), bf16[24,2304]{1,0:T(8,128)(2,1)}) %reduce-scatter.15.cloned.1.call-update) | async-done | bytes 110608 | tf_op jit(solution)/shard_map/reduce_scatter | solution.py:522
  1066.5 32.9 %all_gather.36 = bf16[192,2304]{1,0:T(8,128)(2,1)S(1)} all-gather(bf16[24,2304]{1,0:T(8,128)(2,1)} %reduce-scatter.15.cloned.1.call-done), channel_id=1, replica_groups=mesh['seq'=8,'fsdp'=4] {'seq'}, dimensions={0}, use_global_device_ids=true | all-gather | bytes 995328 | tf_op jit(solution)/shard_map/all_gather | solution.py:523
  1100.7 10.3 all-gather.19.cloned.1.call-done
  1113.8 39.3 %all-gather.17.cloned.1.call-done = bf16[192,3072]{1,0:T(8,128)(2,1)} async-done(((bf16[24,3072]{1,0:T(8,128)(2,1)}), bf16[192,3072]{1,0:T(8,128)(2,1)}) %all-gather.17.cloned.1.call-update) | async-done | bytes 1179664 | tf_op jit(solution)/shard_map/all_gather | solution.py:523
  (215 shorter events, 122.0 us)
Async XLA Ops:
  7.2 46.0 %all-gather.9.cloned.1.call-start = ((), (), s32[]{:S(2)}) async-start(), calls=%async_computation.9 | async-start | bytes 4423680 | tf_op jit(solution)/shard_map/all_gather | solution.py:544
  7.9 253.5 %all-gather.11.cloned.1.call-start = ((), (), s32[]{:S(2)}) async-start(), calls=%async_computation.10 | async-start | bytes 1474560 | tf_op jit(solution)/shard_map/all_gather | solution.py:544
  8.7 263.4 %all-gather.13.cloned.1.call-start = ((), (), s32[]{:S(2)}) async-start(), calls=%async_computation.11 | async-start | bytes 5898240 | tf_op jit(solution)/shard_map/all_gather | solution.py:544
  9.4 297.5 %all-gather.15.cloned.1.call-start = ((), (), s32[]{:S(2)}) async-start(), calls=%async_computation.12 | async-start | bytes 5898240 | tf_op jit(solution)/shard_map/all_gather | solution.py:544
  48.7 16.5 %copy-start.21 = (f32[2048]{0:T(1024)}, f32[2048]{0:T(1024)S(1)}, u32[]{:S(2)}) copy-start(f32[2048]{0:T(1024)S(1)} %rsqrt.21) | copy-start | bytes 24580
  48.7 16.4 %copy-start.23 = (f32[768]{0:T(1024)}, f32[768]{0:T(1024)S(1)}, u32[]{:S(2)}) copy-start(f32[768]{0:T(1024)S(1)} %get-tuple-element.45) | copy-start | bytes 9220
  48.7 16.4 %copy-start.25 = (f32[768]{0:T(1024)}, f32[768]{0:T(1024)S(1)}, u32[]{:S(2)}) copy-start(f32[768]{0:T(1024)S(1)} %get-tuple-element.44) | copy-start | bytes 9220
  70.8 21.7 %collective-permute-start.3 = (bf16[1552,128]{1,0:T(8,128)(2,1)}, bf16[1552,128]{1,0:T(8,128)(2,1)S(1)}, u32[]{:S(2)}, u32[]{:S(2)}) collective-permute-start(bf16[1552,128]{1,0:T(8,128)(2,1)} %get-tuple-element.27), channel_id=1, source_target_pairs={{0,16},{4,20},{8,24},{12,28},{16,0},{20,4},{24,8},{28,12},{1,17},{... | collective-permute-start | bytes 1191944 | tf_op jit(solution)/shard_map/ppermute | solution.py:488
  74.0 119.9 %collective-permute-start.1 = (bf16[1552,256]{1,0:T(8,128)(2,1)}, bf16[1552,256]{1,0:T(8,128)(2,1)S(1)}, u32[]{:S(2)}, u32[]{:S(2)}) collective-permute-start(bf16[1552,256]{1,0:T(8,128)(2,1)} %get-tuple-element.26), channel_id=1, source_target_pairs={{0,8},{4,12},{8,0},{12,4},{16,24},{20,28},{24,16},{28,20},{1,9},{5... | collective-permute-start | bytes 2383880 | tf_op jit(solution)/shard_map/ppermute | solution.py:488
  92.5 12.1 %collective-permute-start.4 = (bf16[1552,128]{1,0:T(8,128)(2,1)S(1)}, bf16[1552,128]{1,0:T(8,128)(2,1)S(1)}, u32[]{:S(2)}, u32[]{:S(2)}) collective-permute-start(bf16[1552,128]{1,0:T(8,128)(2,1)S(1)} %collective-permute-done.3), channel_id=1, source_target_pairs={{0,4},{4,0},{8,12},{12,8},{16,20},{20,16},{24,28},{28,24},{1,5},{5... | collective-permute-start | bytes 1191944 | tf_op jit(solution)/shard_map/ppermute | solution.py:488
  94.1 117.7 %collective-permute-start = (bf16[1552,512]{1,0:T(8,128)(2,1)}, bf16[1552,512]{1,0:T(8,128)(2,1)S(1)}, u32[]{:S(2)}, u32[]{:S(2)}) collective-permute-start(bf16[1552,512]{1,0:T(8,128)(2,1)} %get-tuple-element.25), channel_id=1, source_target_pairs={{0,4},{4,0},{8,12},{12,8},{16,20},{20,16},{24,28},{28,24},{1,5},{5... | collective-permute-start | bytes 4767752 | tf_op jit(solution)/shard_map/ppermute | solution.py:488
  105.6 90.1 %collective-permute-start.5 = (bf16[1552,256]{1,0:T(8,128)(2,1)}, bf16[1552,256]{1,0:T(8,128)(2,1)}, u32[]{:S(2)}, u32[]{:S(2)}) collective-permute-start(bf16[1552,256]{1,0:T(8,128)(2,1)} %pad_maximum_fusion), channel_id=1, source_target_pairs={{0,8},{4,12},{8,0},{12,4},{16,24},{20,28},{24,16},{28,20},{1,9},{5... | collective-permute-start | bytes 2383880 | tf_op jit(solution)/shard_map/ppermute | solution.py:488
  106.3 640.1 %reduce-scatter.25.cloned.1.call-start = ((), (), s32[]{:S(2)}) async-start(), calls=%async_computation.20 | async-start | bytes 5898240 | tf_op jit(solution)/shard_map/reduce_scatter | solution.py:521
  193.9 17.7 %collective-permute-start.2 = (bf16[1552,256]{1,0:T(8,128)(2,1)S(1)}, bf16[1552,256]{1,0:T(8,128)(2,1)S(1)}, u32[]{:S(2)}, u32[]{:S(2)}) collective-permute-start(bf16[1552,256]{1,0:T(8,128)(2,1)S(1)} %collective-permute-done.1), channel_id=1, source_target_pairs={{0,4},{4,0},{8,12},{12,8},{16,20},{20,16},{24,28},{28,24},{1,5},{5... | collective-permute-start | bytes 2383880 | tf_op jit(solution)/shard_map/ppermute | solution.py:488
  272.0 23.0 %copy-start.6 = (bf16[2,64,2,2,2,2,768]{6,1,2,3,4,5,0:T(8,128)(2,1)S(1)}, bf16[2,64,2,2,2,2,768]{6,1,2,3,4,5,0:T(8,128)(2,1)}, u32[]{:S(2)}) copy-start(bf16[2,64,2,2,2,2,768]{6,1,2,3,4,5,0:T(8,128)(2,1)} %copy.57) | copy-start | bytes 9437188
  306.8 26.6 %slice-start.4 = ((s8[6291456]{0:T(1024)(128)(4,1)}), s8[2097152]{0:T(1024)(128)(4,1)S(1)}, s32[]{:S(2)}) async-start(s8[6291456]{0:T(1024)(128)(4,1)} %bitcast.102), calls=%async_computation.28 | async-start | bytes 4194304
  306.8 440.4 %reduce-scatter.21.cloned.1.call-start = ((), (), s32[]{:S(2)}) async-start(), calls=%async_computation.17 | async-start | bytes 5898240 | tf_op jit(solution)/shard_map/reduce_scatter | solution.py:521
  306.9 26.5 %slice-start.5 = ((s8[6291456]{0:T(1024)(128)(4,1)}), s8[4194304]{0:T(1024)(128)(4,1)S(1)}, s32[]{:S(2)}) async-start(s8[6291456]{0:T(1024)(128)(4,1)} %bitcast.102), calls=%async_computation.29 | async-start | bytes 8388608
  347.4 19.7 %slice-start.6 = ((s8[6291456]{0:T(1024)(128)(4,1)}), s8[2097152]{0:T(1024)(128)(4,1)S(1)}, s32[]{:S(2)}) async-start(s8[6291456]{0:T(1024)(128)(4,1)} %bitcast.104), calls=%async_computation.30 | async-start | bytes 4194304
  347.4 417.6 %reduce-scatter.17.cloned.1.call-start = ((), (), s32[]{:S(2)}) async-start(), calls=%async_computation.15 | async-start | bytes 1474560 | tf_op jit(solution)/shard_map/reduce_scatter | solution.py:521
  347.6 19.4 %slice-start.7 = ((s8[6291456]{0:T(1024)(128)(4,1)}), s8[4194304]{0:T(1024)(128)(4,1)S(1)}, s32[]{:S(2)}) async-start(s8[6291456]{0:T(1024)(128)(4,1)} %bitcast.104), calls=%async_computation.31 | async-start | bytes 8388608
  347.6 19.4 %copy-start.7 = (bf16[2,64,2,2,2,2,768]{6,1,2,3,4,5,0:T(8,128)(2,1)S(1)}, bf16[2,64,2,2,2,2,768]{6,1,2,3,4,5,0:T(8,128)(2,1)}, u32[]{:S(2)}) copy-start(bf16[2,64,2,2,2,2,768]{6,1,2,3,4,5,0:T(8,128)(2,1)} %copy.57) | copy-start | bytes 9437188
  378.3 46.7 %slice-start = ((s8[6291456]{0:T(1024)(128)(4,1)}), s8[2097152]{0:T(1024)(128)(4,1)S(1)}, s32[]{:S(2)}) async-start(s8[6291456]{0:T(1024)(128)(4,1)} %bitcast.97), calls=%async_computation.24 | async-start | bytes 4194304
  382.9 42.1 %slice-start.1 = ((s8[6291456]{0:T(1024)(128)(4,1)}), s8[4194304]{0:T(1024)(128)(4,1)S(1)}, s32[]{:S(2)}) async-start(s8[6291456]{0:T(1024)(128)(4,1)} %bitcast.97), calls=%async_computation.25 | async-start | bytes 8388608
  382.9 42.1 %copy-start.16 = (f32[2,2,2,2,2,64]{5,4,3,2,1,0:T(2,128)S(1)}, f32[2,2,2,2,2,64]{5,4,3,2,1,0:T(2,128)}, u32[]{:S(2)}) copy-start(f32[2,2,2,2,2,64]{5,4,3,2,1,0:T(2,128)} %copy-done.15) | copy-start | bytes 24580
  382.9 42.1 %copy-start.18 = (f32[2,2,2,2,2,64]{5,4,3,2,1,0:T(2,128)S(1)}, f32[2,2,2,2,2,64]{5,4,3,2,1,0:T(2,128)}, u32[]{:S(2)}) copy-start(f32[2,2,2,2,2,64]{5,4,3,2,1,0:T(2,128)} %copy-done.17) | copy-start | bytes 24580
  382.9 42.1 %copy-start.24 = (f32[768]{0:T(1024)S(1)}, f32[768]{0:T(1024)}, u32[]{:S(2)}) copy-start(f32[768]{0:T(1024)} %copy-done.23) | copy-start | bytes 9220
  382.9 42.1 %copy-start.26 = (f32[768]{0:T(1024)S(1)}, f32[768]{0:T(1024)}, u32[]{:S(2)}) copy-start(f32[768]{0:T(1024)} %copy-done.25) | copy-start | bytes 9220
  422.4 19.5 %copy-start.13 = (bf16[2,768,512]{2,1,0:T(8,128)(2,1)S(1)}, bf16[2,768,512]{2,1,0:T(8,128)(2,1)}, u32[]{:S(2)}) copy-start(bf16[2,768,512]{2,1,0:T(8,128)(2,1)} %get-tuple-element.33) | copy-start | bytes 4718596
  423.8 18.2 %collective-permute-start.9 = (bf16[2,768,256]{2,1,0:T(8,128)(2,1)S(1)}, bf16[2,768,256]{2,1,0:T(8,128)(2,1)S(1)}, u32[]{:S(2)}, u32[]{:S(2)}) collective-permute-start(bf16[2,768,256]{2,1,0:T(8,128)(2,1)S(1)} %slice.57), channel_id=1, source_target_pairs={{0,8},{4,12},{8,0},{12,4},{16,24},{20,28},{24,16},{28,20},{1,9},{5... | collective-permute-start | bytes 2359304 | tf_op jit(solution)/shard_map/ppermute | solution.py:488
  430.8 183.4 %collective-permute-start.7 = (bf16[2,768,256]{2,1,0:T(8,128)(2,1)}, bf16[2,768,256]{2,1,0:T(8,128)(2,1)}, u32[]{:S(2)}, u32[]{:S(2)}) collective-permute-start(bf16[2,768,256]{2,1,0:T(8,128)(2,1)} %slice.55), channel_id=1, source_target_pairs={{0,4},{4,0},{8,12},{12,8},{16,20},{20,16},{24,28},{28,24},{1,5},{5... | collective-permute-start | bytes 2359304 | tf_op jit(solution)/shard_map/ppermute | solution.py:488
  432.3 192.5 %collective-permute-start.6 = (bf16[2,768,512]{2,1,0:T(8,128)(2,1)}, bf16[2,768,512]{2,1,0:T(8,128)(2,1)}, u32[]{:S(2)}, u32[]{:S(2)}) collective-permute-start(bf16[2,768,512]{2,1,0:T(8,128)(2,1)} %get-tuple-element.31), channel_id=1, source_target_pairs={{0,4},{4,0},{8,12},{12,8},{16,20},{20,16},{24,28},{28,24},{1,5},{5... | collective-permute-start | bytes 4718600 | tf_op jit(solution)/shard_map/ppermute | solution.py:488
  442.2 174.5 %collective-permute-start.10 = (bf16[2,768,128]{2,1,0:T(8,128)(2,1)S(1)}, bf16[2,768,128]{2,1,0:T(8,128)(2,1)}, u32[]{:S(2)}, u32[]{:S(2)}) collective-permute-start(bf16[2,768,128]{2,1,0:T(8,128)(2,1)S(1)} %slice.71), channel_id=1, source_target_pairs={{0,4},{4,0},{8,12},{12,8},{16,20},{20,16},{24,28},{28,24},{1,5},{5... | collective-permute-start | bytes 1179656 | tf_op jit(solution)/shard_map/ppermute | solution.py:488
  454.7 166.5 %slice-start.2 = ((s8[6291456]{0:T(1024)(128)(4,1)}), s8[2097152]{0:T(1024)(128)(4,1)S(1)}, s32[]{:S(2)}) async-start(s8[6291456]{0:T(1024)(128)(4,1)} %bitcast.99), calls=%async_computation.26 | async-start | bytes 4194304
  463.7 157.4 %slice-start.3 = ((s8[6291456]{0:T(1024)(128)(4,1)}), s8[4194304]{0:T(1024)(128)(4,1)S(1)}, s32[]{:S(2)}) async-start(s8[6291456]{0:T(1024)(128)(4,1)} %bitcast.99), calls=%async_computation.27 | async-start | bytes 8388608
  616.4 33.6 %collective-permute-start.8 = (bf16[2,768,256]{2,1,0:T(8,128)(2,1)}, bf16[2,768,256]{2,1,0:T(8,128)(2,1)}, u32[]{:S(2)}, u32[]{:S(2)}) collective-permute-start(bf16[2,768,256]{2,1,0:T(8,128)(2,1)} %add_convert_fusion.5), channel_id=1, source_target_pairs={{0,8},{4,12},{8,0},{12,4},{16,24},{20,28},{24,16},{28,20},{1,9},{5... | collective-permute-start | bytes 2359304 | tf_op jit(solution)/shard_map/ppermute | solution.py:488
  617.8 53.4 %collective-permute-start.11 = (bf16[2,768,128]{2,1,0:T(8,128)(2,1)S(1)}, bf16[2,768,128]{2,1,0:T(8,128)(2,1)}, u32[]{:S(2)}, u32[]{:S(2)}) collective-permute-start(bf16[2,768,128]{2,1,0:T(8,128)(2,1)S(1)} %add_convert_fusion.6), channel_id=1, source_target_pairs={{0,16},{4,20},{8,24},{12,28},{16,0},{20,4},{24,8},{28,12},{1,17},{... | collective-permute-start | bytes 1179656 | tf_op jit(solution)/shard_map/ppermute | solution.py:488
  624.8 160.5 %reduce-scatter.13.cloned.1.call-start = ((), (), s32[]{:S(2)}) async-start(), calls=%async_computation.13 | async-start | bytes 4423680 | tf_op jit(solution)/shard_map/reduce_scatter | solution.py:521
  703.7 21.9 %copy-start.8 = (bf16[1,768,2048]{2,1,0:T(8,128)(2,1)S(1)}, bf16[1,768,2048]{2,1,0:T(8,128)(2,1)}, u32[]{:S(2)}) copy-start(bf16[1,768,2048]{2,1,0:T(8,128)(2,1)} %slice.68) | copy-start | bytes 9437188
  732.9 14.9 %copy-start.22 = (f32[2048]{0:T(1024)S(1)}, f32[2048]{0:T(1024)}, u32[]{:S(2)}) copy-start(f32[2048]{0:T(1024)} %copy-done.21) | copy-start | bytes 24580
  746.4 106.4 %reduce-scatter.27.cloned.1.call-start = ((), (), s32[]{:S(2)}) async-start(), calls=%async_computation.21 | async-start | bytes 1327104 | tf_op jit(solution)/shard_map/reduce_scatter | solution.py:522
  747.1 172.0 %reduce-scatter.23.cloned.1.call-start = ((), (), s32[]{:S(2)}) async-start(), calls=%async_computation.18 | async-start | bytes 1327104 | tf_op jit(solution)/shard_map/reduce_scatter | solution.py:522
  747.7 195.0 %reduce-scatter.29.cloned.1.call-start = ((), (), s32[]{:S(2)}) async-start(), calls=%async_computation.23 | async-start | bytes 245760
  747.8 37.6 %copy-start.27 = (u32[32]{0:T(128)S(1)}, u32[32]{0:T(128)}, u32[]{:S(2)}) copy-start(u32[32]{0:T(128)} %constant.46) | copy-start | bytes 388
  764.9 237.9 %reduce-scatter.19.cloned.1.call-start = ((), (), s32[]{:S(2)}) async-start(), calls=%async_computation.16 | async-start | bytes 331776 | tf_op jit(solution)/shard_map/reduce_scatter | solution.py:522
  765.5 300.9 %reduce-scatter.15.cloned.1.call-start = ((), (), s32[]{:S(2)}) async-start(), calls=%async_computation.14 | async-start | bytes 995328 | tf_op jit(solution)/shard_map/reduce_scatter | solution.py:522
  785.4 325.6 %all-gather.19.cloned.1.call-start = ((), (), s32[]{:S(2)}) async-start(), calls=%async_computation.22 | async-start | bytes 1327104 | tf_op jit(solution)/shard_map/all_gather | solution.py:523
  852.8 300.3 %all-gather.17.cloned.1.call-start = ((), (), s32[]{:S(2)}) async-start(), calls=%async_computation.19 | async-start | bytes 1327104 | tf_op jit(solution)/shard_map/all_gather | solution.py:523
  (17 other events, 114.4 us)
Sparse Core Ops, SparseCore 0:
  9.6 33.4 all-gather.8
  44.6 17.4 all-gather.10
  63.7 37.4 all-gather.12
  106.4 38.4 all-gather.14
  306.9 48.7 reduce-scatter.24
  358.2 47.8 reduce-scatter.20
  624.9 24.1 reduce-scatter.16
  746.5 38.7 reduce-scatter.12
  788.7 64.0 reduce-scatter.26
  856.1 63.0 reduce-scatter.22
  922.2 18.7 reduce-scatter.28
  944.1 58.7 reduce-scatter.18
  1006.2 60.1 reduce-scatter.14
  1068.5 42.4 all-gather.18
  1113.0 40.0 all-gather.16

commit v2 on v1

--- a/solution.py
+++ b/solution.py
@@ -52,18 +52,6 @@
         jnp.sum(grad * normed, axis=0),
         jnp.sum(grad, axis=0),
     )
-
-
-def reorder(array):
-    rows, cols = array.shape
-    split = array.reshape(rows // SEG, RUN, 2, 2, 2, 2, cols)
-    return split.transpose(0, 5, 4, 3, 2, 1, 6).reshape(rows, cols)
-
-
-def restore(array):
-    rows, cols = array.shape
-    split = array.reshape(rows // SEG, 2, 2, 2, 2, RUN, cols)
-    return split.transpose(0, 5, 4, 3, 2, 1, 6).reshape(rows, cols)
 
 
 def reversed_bits(head):
@@ -98,6 +86,30 @@
     return out.astype(BF16)
 
 
+def residue_of(rho):
+    return reversed_bits(rho)
+
+
+def local_keep(count, length):
+    lane = lax.broadcasted_iota(jnp.int32, (1, length), 1)
+    rho = lax.rem(lane // RUN, RES)
+    position = lane // SEG * SEG + lax.rem(lane, RUN) * RES + residue_of(rho)
+    return position < count
+
+
+def remote_keep(head, level, nseg, mine, limit, length):
+    size = SEG >> level
+    group = (SEG << (level - 1)) // (nseg * SEG)
+    lane = lax.broadcasted_iota(jnp.int32, (1, length), 1)
+    owner = mine ^ (group + lane // (nseg * size))
+    inside = lax.rem(lane, nseg * size)
+    rho = (reversed_bits(head) >> (4 - level)) * (size // RUN) + lax.rem(inside, size) // RUN
+    position = (
+        owner * (nseg * SEG) + inside // size * SEG + lax.rem(inside, RUN) * RES + residue_of(rho)
+    )
+    return position < limit
+
+
 def weight_of(level, step):
     return math.log2((step - level + 1) / (step - level)) if step > level else 0.0
 
@@ -113,7 +125,7 @@
         weight = jnp.where(row == 8 + step, value - high, weight)
     out = jnp.where(inside, weight, 0.0)
     out = jnp.where((row >= 1) & (row <= 3), 1.0, out)
-    out = jnp.where(row == 0, jnp.where(keep > 0.5, 0.0, NEG), out)
+    out = jnp.where(row == 0, jnp.where(keep, 0.0, NEG), out)
     if level == BRANCHES - 1:
         out = jnp.where(row == 4, 1.0, out)
     return out.astype(BF16)
@@ -147,14 +159,15 @@
     return acc, top
 
 
-def local_forward(nseg, q_ref, k_ref, v_ref, keep_ref, o_ref, l_ref, m_ref, qa, ka, va):
+def local_forward(nseg, mask_ref, q_ref, k_ref, v_ref, o_ref, l_ref, m_ref, qa, ka, va):
     head = pl.program_id(0)
     length = nseg * SEG
+    keep = local_keep(mask_ref[0], length)
     qa[...] = join(q_ref[0], query_rows(head, length))
     va[...] = join(v_ref[0], value_rows(length))
-    ka[0] = join(k_ref[0], key_rows(head, 0, 4, length, keep_ref[...]))
+    ka[0] = join(k_ref[0], key_rows(head, 0, 4, length, keep))
     if nseg == 2:
-        ka[1] = join(k_ref[0], key_rows(head, 1, 4, length, keep_ref[...]))
+        ka[1] = join(k_ref[0], key_rows(head, 1, 4, length, keep))
     for seg in range(nseg):
         lanes = slice(seg * SEG, (seg + 1) * SEG)
         acc, top = attend_tiles(qa[:, lanes], ka[0, :, lanes], va[:, lanes], 256, None, None)
@@ -176,11 +189,10 @@
     m_ref[0, :, mine] = top
 
 
-def remote_keys(head, level, pack, nseg):
-    k_ref, v_ref, mask_ref = pack
+def remote_keys(head, level, pack, nseg, mask_ref):
+    k_ref, v_ref = pack
     length = k_ref.shape[1]
-    row = lax.broadcasted_iota(jnp.int32, (16, length), 0)
-    keep = jnp.sum(jnp.where(row == head, mask_ref[...].astype(F32), 0.0), axis=0, keepdims=True)
+    keep = remote_keep(head, level, nseg, mask_ref[1], mask_ref[2], length)
     key = join(k_ref[...], key_rows(head, level, 4 - level, length, keep))
     return key, join(v_ref[...], value_rows(length))
 
@@ -189,24 +201,24 @@
     return [(level,) for level in range(first, 3)] + [(3, 4)]
 
 
-def remote_forward(nseg, first, q_ref, keep_ref, o_in, l_in, m_in, *refs):
+def remote_forward(nseg, first, mask_ref, q_ref, o_in, l_in, m_in, *refs):
     head = pl.program_id(0)
     levels = range(first, BRANCHES)
-    packs = {level: refs[3 * i : 3 * i + 3] for i, level in enumerate(levels)}
-    att_ref, lse_ref, o_ref, l_ref, m_ref, qa = refs[3 * len(levels) :]
+    packs = {level: refs[2 * i : 2 * i + 2] for i, level in enumerate(levels)}
+    att_ref, lse_ref, o_ref, l_ref, m_ref, qa = refs[2 * len(levels) :]
     length = nseg * SEG
     qa[...] = join(q_ref[0], query_rows(head, length))
     o_ref[...] = o_in[...]
     l_ref[...] = l_in[...]
     m_ref[...] = m_in[...]
     for group in remote_plan(first):
-        pairs = [remote_keys(head, level, packs[level], nseg) for level in group]
+        pairs = [remote_keys(head, level, packs[level], nseg, mask_ref) for level in group]
         key = jnp.concatenate([pair[0] for pair in pairs], axis=1)
         value = jnp.concatenate([pair[1] for pair in pairs], axis=1)
         for seg in range(nseg):
             mine = pl.ds(kept_start(head, group[0], seg), SEG >> group[0])
             merge_level(qa[:, mine], key, value, mine, o_ref, l_ref, m_ref)
-    weight = keep_ref[...] / l_ref[0]
+    weight = jnp.where(local_keep(mask_ref[0], length), 1.0, 0.0) / l_ref[0]
     att_ref[...] = (o_ref[...] * weight).astype(BF16)
     lse_ref[0] = m_ref[0] + jnp.log2(l_ref[0])
 
@@ -260,13 +272,13 @@
 
 
 def neg_total(lse, keep):
-    return jnp.where(keep > 0.5, -lse, NEG)
-
-
-def local_backward(nseg, first, q_ref, k_ref, v_ref, g_ref, lse_ref, slope_ref, keep_ref, dqr_ref, out_ref, qa, ga, ka, va, dk, dv):
+    return jnp.where(keep, -lse, NEG)
+
+
+def local_backward(nseg, first, mask_ref, q_ref, k_ref, v_ref, g_ref, lse_ref, slope_ref, dqr_ref, out_ref, qa, ga, ka, va, dk, dv):
     head = pl.program_id(0)
     length = nseg * SEG
-    keep = keep_ref[...]
+    keep = local_keep(mask_ref[0], length)
     qa[...] = join(q_ref[0], query_rows(head, length, neg_total(lse_ref[0], keep)))
     ga[...] = grad_rows(g_ref[...], slope_ref[0])
     va[...] = join(v_ref[0], value_rows(length))
@@ -293,21 +305,21 @@
     out_ref[2] = dv[...]
 
 
-def remote_backward(nseg, first, q_ref, g_ref, lse_ref, slope_ref, keep_ref, *refs):
+def remote_backward(nseg, first, mask_ref, q_ref, g_ref, lse_ref, slope_ref, *refs):
     head = pl.program_id(0)
     levels = range(first, BRANCHES)
     n = len(levels)
-    packs = {level: refs[3 * i : 3 * i + 3] for i, level in enumerate(levels)}
-    dqr_ref = refs[3 * n]
-    outs = {level: refs[3 * n + 1 + i] for i, level in enumerate(levels)}
-    qa, ga, ka, va, dk, dv = refs[4 * n + 1 :]
-    length = nseg * SEG
-    qa[...] = join(q_ref[0], query_rows(head, length, neg_total(lse_ref[0], keep_ref[...])))
+    packs = {level: refs[2 * i : 2 * i + 2] for i, level in enumerate(levels)}
+    dqr_ref = refs[2 * n]
+    outs = {level: refs[2 * n + 1 + i] for i, level in enumerate(levels)}
+    qa, ga, ka, va, dk, dv = refs[3 * n + 1 :]
+    length = nseg * SEG
+    qa[...] = join(q_ref[0], query_rows(head, length, neg_total(lse_ref[0], local_keep(mask_ref[0], length))))
     ga[...] = grad_rows(g_ref[...], slope_ref[0])
     full = SEG >> first
     for group in remote_plan(first):
         for i, level in enumerate(group):
-            key, value = remote_keys(head, level, packs[level], nseg)
+            key, value = remote_keys(head, level, packs[level], nseg, mask_ref)
             ka[:, i * 512 : (i + 1) * 512] = key
             va[:, i * 512 : (i + 1) * 512] = value
         size = SEG >> group[0]
@@ -342,15 +354,13 @@
     return pl.BlockSpec((1, HEAD_DIM, length), lambda h: (part, h, 0))
 
 
-def keep_block(length):
-    return pl.BlockSpec((1, length), lambda h: (0, 0))
+MASK_BLOCK = pl.BlockSpec(memory_space=pltpu.SMEM)
 
 
 def pack_specs(length):
     return [
         pl.BlockSpec((HEAD_DIM, length), lambda h: (h, 0)),
         pl.BlockSpec((HEAD_DIM, length), lambda h: (HEADS + h, 0)),
-        pl.BlockSpec((16, length), lambda h: (2 * D // 16, 0)),
     ]
 
 
@@ -361,12 +371,16 @@
     return jax.ShapeDtypeStruct(dims, dtype)
 
 
-def call_local_forward(nseg, qkv, keep):
+def cost(seconds):
+    return pl.CostEstimate(flops=int(seconds * 1.1e15), transcendentals=0, bytes_accessed=0)
+
+
+def call_local_forward(nseg, qkv, mask):
     length = nseg * SEG
     return pl.pallas_call(
         functools.partial(local_forward, nseg),
         grid=(HEADS,),
-        in_specs=[part_block(0, length), part_block(1, length), part_block(2, length), keep_block(length)],
+        in_specs=[MASK_BLOCK, part_block(0, length), part_block(1, length), part_block(2, length)],
         out_specs=[head_block(length), row_block(length), row_block(length)],
         out_shape=[shape((D, length), F32), shape((HEADS, 1, length), F32), shape((HEADS, 1, length), F32)],
         scratch_shapes=[
@@ -375,20 +389,21 @@
             pltpu.VMEM((64, length), BF16),
         ],
         compiler_params=PARAMS,
+        cost_estimate=cost(nseg * 37e-6),
         name="local_forward",
-    )(qkv, qkv, qkv, keep)
-
-
-def call_remote_forward(nseg, first, qkv, keep, o_part, l_part, m_part, packs):
+    )(mask, qkv, qkv, qkv)
+
+
+def call_remote_forward(nseg, first, qkv, mask, o_part, l_part, m_part, packs):
     length = nseg * SEG
     args, specs = [], []
     for pack in packs:
-        args += [pack] * 3
+        args += [pack] * 2
         specs += pack_specs(pack.shape[1])
     return pl.pallas_call(
         functools.partial(remote_forward, nseg, first),
         grid=(HEADS,),
-        in_specs=[part_block(0, length), keep_block(length), head_block(length), row_block(length), row_block(length)]
+        in_specs=[MASK_BLOCK, part_block(0, length), head_block(length), row_block(length), row_block(length)]
         + specs,
         out_specs=[head_block(length), row_block(length)],
         out_shape=[shape((D, length), BF16), shape((HEADS, 1, length), F32)],
@@ -399,21 +414,22 @@
             pltpu.VMEM((64, length), BF16),
         ],
         compiler_params=PARAMS,
+        cost_estimate=cost(nseg * 24e-6),
         name="remote_forward",
-    )(qkv, keep, o_part, l_part, m_part, *args)
-
-
-def call_remote_backward(nseg, first, qkv, grad, lse, slope, keep, packs):
+    )(mask, qkv, o_part, l_part, m_part, *args)
+
+
+def call_remote_backward(nseg, first, qkv, grad, lse, slope, mask, packs):
     length = nseg * SEG
     args, specs = [], []
     for pack in packs:
-        args += [pack] * 3
+        args += [pack] * 2
         specs += pack_specs(pack.shape[1])
     kept = nseg * (SEG >> first)
     return pl.pallas_call(
         functools.partial(remote_backward, nseg, first),
         grid=(HEADS,),
-        in_specs=[part_block(0, length), head_block(length), row_block(length), row_block(length), keep_block(length)]
+        in_specs=[MASK_BLOCK, part_block(0, length), head_block(length), row_block(length), row_block(length)]
         + specs,
         out_specs=[head_block(kept)]
         + [pl.BlockSpec((2, HEAD_DIM, pack.shape[1]), lambda h: (0, h, 0)) for pack in packs],
@@ -427,17 +443,18 @@
             pltpu.VMEM((HEAD_DIM, 1024), F32),
         ],
         compiler_params=PARAMS,
+        cost_estimate=cost(nseg * 20e-6),
         name="remote_backward",
-    )(qkv, grad, lse, slope, keep, *args)
-
-
-def call_local_backward(nseg, first, qkv, grad, lse, slope, keep, dq_remote):
+    )(mask, qkv, grad, lse, slope, *args)
+
+
+def call_local_backward(nseg, first, qkv, grad, lse, slope, mask, dq_remote):
     length = nseg * SEG
     return pl.pallas_call(
         functools.partial(local_backward, nseg, first),
         grid=(HEADS,),
-        in_specs=[part_block(0, length), part_block(1, length), part_block(2, length), head_block(length),
-                  row_block(length), row_block(length), keep_block(length), head_block(dq_remote.shape[1])],
+        in_specs=[MASK_BLOCK, part_block(0, length), part_block(1, length), part_block(2, length), head_block(length),
+                  row_block(length), row_block(length), head_block(dq_remote.shape[1])],
         out_specs=pl.BlockSpec((3, HEAD_DIM, length), lambda h: (0, h, 0)),
         out_shape=shape((3, D, length), F32),
         scratch_shapes=[
@@ -449,38 +466,360 @@
             pltpu.VMEM((HEAD_DIM, length), F32),
         ],
         compiler_params=PARAMS,
+        cost_estimate=cost(nseg * 72e-6),
         name="local_backward",
-    )(qkv, qkv, qkv, grad, lse, slope, keep, dq_remote)
-
-
-def pack_kernel(nseg, first, kv_ref, keep_ref, *outs):
-    for i, level in enumerate(range(first, BRANCHES)):
-        size = SEG >> level
-        for head in range(HEADS):
-            start = (reversed_bits(head) >> (4 - level)) * size
-            for part in range(2):
-                src = pl.ds((part + 1) * D + head * HEAD_DIM, HEAD_DIM)
-                dst = pl.ds(part * D + head * HEAD_DIM, HEAD_DIM)
+    )(mask, qkv, qkv, qkv, grad, lse, slope, dq_remote)
+
+
+HALF = D // 2
+
+
+def const_block(dims):
+    return pl.BlockSpec(dims, lambda i: (0,) * len(dims), pipeline_mode=pl.Buffered(1))
+
+
+def rev4(value):
+    return int(reversed_bits(value))
+
+
+TILES = D // 128
+
+
+def put_rows(tiled, start, array):
+    for tile in range(TILES):
+        tiled[tile, start : start + array.shape[0], :] = array[:, tile * 128 : (tile + 1) * 128]
+
+
+def get_rows(tiled, start, size):
+    return jnp.concatenate([tiled[tile, start : start + size, :] for tile in range(TILES)], axis=1)
+
+
+def get_residue(tiled, start):
+    return jnp.concatenate(
+        [tiled[tile, pl.ds(start, RUN, stride=RES), :] for tile in range(TILES)], axis=1
+    )
+
+
+def put_residue(tiled, start, array):
+    for tile in range(TILES):
+        tiled[tile, pl.ds(start, RUN, stride=RES), :] = array[:, tile * 128 : (tile + 1) * 128]
+
+
+def project_kernel(nseg, first, tok_ref, gain_ref, shift_ref, w_ref, qkv_ref, xp_ref, inner_ref, *refs):
+    *packs, xs = refs
+    step = pl.program_id(0)
+
+    @pl.when(step == 0)
+    def _():
+        for seg in range(nseg):
+            put_rows(xs, 0, tok_ref[seg * SEG : (seg + 1) * SEG, :].astype(F32))
+            for pair in range(RES // 2):
+                rows = jnp.concatenate(
+                    [get_residue(xs, rev4(2 * pair + i)) for i in range(2)], axis=0
+                )
+                normed = normalize(rows, gain_ref[...], shift_ref[...])[0].astype(BF16)
+                at = slice(seg * SEG + pair * 2 * RUN, seg * SEG + (pair + 1) * 2 * RUN)
+                xp_ref[at, :] = rows.astype(BF16)
+                inner_ref[:, at] = normed.T
+
+    scale = jnp.where(step < 2, QUERY_SCALE, 1.0)
+    for start in range(0, nseg * SEG, 512):
+        lanes = slice(start, start + 512)
+        qkv_ref[0, :, lanes] = (dotg(w_ref[...], inner_ref[:, lanes], 0, 0) * scale).astype(BF16)
+
+    @pl.when(step >= 2)
+    def _():
+        upper = lax.rem(step, 2) == 1
+        for pack, level in zip(packs, range(first, BRANCHES)):
+            size = SEG >> level
+            for head in range(HEADS // 2):
+                rows = slice(head * HEAD_DIM, (head + 1) * HEAD_DIM)
+                pieces = []
                 for seg in range(nseg):
-                    outs[i][dst, seg * size : (seg + 1) * size] = kv_ref[
-                        src, seg * SEG + start : seg * SEG + start + size
-                    ]
-        rows = []
-        for head in range(HEADS):
-            start = (reversed_bits(head) >> (4 - level)) * size
-            rows.append(
-                jnp.concatenate([keep_ref[:, seg * SEG + start : seg * SEG + start + size] for seg in range(nseg)], axis=1)
-            )
-        outs[i][2 * D :, :] = jnp.concatenate(rows, axis=0).astype(BF16)
-
-
-def call_pack(nseg, first, qkv, keep):
+                    start = seg * SEG + (rev4(head) >> (4 - level)) * size
+                    if level < 4:
+                        pieces.append(qkv_ref[0, rows, start : start + size])
+                    else:
+                        both = qkv_ref[0, rows, start : start + 2 * size]
+                        pieces.append(jnp.where(upper, both[:, size:], both[:, :size]))
+                pack[rows, :] = jnp.concatenate(pieces, axis=1) if nseg > 1 else pieces[0]
+
+
+def call_project(nseg, first, tokens, gain, shift, weight):
+    length = nseg * SEG
+    kept = [nseg * (SEG >> level) for level in range(first, BRANCHES)]
     return pl.pallas_call(
-        functools.partial(pack_kernel, nseg, first),
-        out_shape=[shape((2 * D + 16, nseg * (SEG >> level)), BF16) for level in range(first, BRANCHES)],
+        functools.partial(project_kernel, nseg, first),
+        grid=(6,),
+        in_specs=[
+            const_block((length, D)),
+            const_block((1, D)),
+            const_block((1, D)),
+            pl.BlockSpec((D, HALF), lambda i: (0, i)),
+        ],
+        out_specs=[
+            pl.BlockSpec((1, HALF, length), lambda i: (i // 2, i % 2, 0)),
+            const_block((length, D)),
+            const_block((D, length)),
+        ]
+        + [pl.BlockSpec((HALF, size), lambda i: (jnp.maximum(i - 2, 0), 0)) for size in kept],
+        out_shape=[
+            shape((3, D, length), BF16),
+            shape((length, D), BF16),
+            shape((D, length), BF16),
+        ]
+        + [shape((2 * D, size), BF16) for size in kept],
+        scratch_shapes=[pltpu.VMEM((TILES, SEG, 128), F32)],
         compiler_params=PARAMS,
-        name="pack",
-    )(qkv.reshape(3 * D, nseg * SEG), keep)
+        cost_estimate=cost(nseg * 10e-6),
+        name="project",
+    )(tokens, gain, shift, weight)
+
+
+ROWS = 256
+UP_ROWS = 4 * 192
+STACK = UP_ROWS + 192 + D
+
+
+def feed_kernel(
+    nseg, mask_ref, att_ref, x_ref, cot_ref, wout_ref, up_ref, down_ref, gain_ref, shift_ref,
+    mixed_ref, gmid_ref, gm_ref, along_ref, vec_ref, grads_ref,
+    cs, out_acc, up_acc, down_acc, stage, sems,
+):
+    step = pl.program_id(0)
+    quarter = lax.rem(step, 4)
+    low = (quarter >> 1) | ((quarter & 1) << 1)
+
+    @pl.when(step == 0)
+    def _():
+        out_acc[...] = jnp.zeros_like(out_acc)
+        up_acc[...] = jnp.zeros_like(up_acc)
+        down_acc[...] = jnp.zeros_like(down_acc)
+        vec_ref[...] = jnp.zeros_like(vec_ref)
+
+    @pl.when(quarter == 0)
+    def _():
+        put_rows(cs, 0, cot_ref[...].astype(F32))
+
+    grad = jnp.concatenate([get_residue(cs, rev4(i) + low) for i in range(4)], axis=0)
+    grad_b = grad.astype(BF16)
+    att = att_ref[...]
+    middle = x_ref[...].astype(F32) + dotg(att, wout_ref[...], 0, 0)
+    gain = gain_ref[...]
+    normed, unit, inverse = normalize(middle, gain, shift_ref[...])
+    hidden = normed.astype(BF16)
+    hidden_t = hidden.T
+    final = middle
+    grad_hidden = jnp.zeros((ROWS, D), F32)
+    for start in range(0, 4 * D, D):
+        cols = slice(start, start + D)
+        upper = dotg(hidden, up_ref[:, cols], 1, 0)
+        grad_active = dotg(grad_b, down_ref[cols, :], 1, 1)
+        half = 0.5 * (1.0 + lax.erf(upper * ROOT_HALF))
+        slope = half + upper * jnp.exp(-0.5 * upper * upper) * INV_ROOT_TWO_PI
+        active = (upper * half).astype(BF16)
+        grad_upper = (grad_active * slope).astype(BF16)
+        final = final + dotg(active, down_ref[cols, :], 1, 0)
+        grad_hidden = grad_hidden + dotg(grad_upper, up_ref[:, cols], 1, 1)
+        up_acc[:, cols] += dotg(hidden_t, grad_upper, 1, 0)
+        down_acc[cols, :] += dotg(active, grad_b, 0, 0)
+    for i in range(4):
+        put_residue(cs, rev4(i) + low, final[i * RUN : (i + 1) * RUN])
+
+    @pl.when(quarter == 3)
+    def _():
+        mixed_ref[...] = get_rows(cs, 0, SEG).astype(BF16)
+
+    back, gain_back, shift_back = normalize_back(grad_hidden, unit, inverse, gain)
+    vec_ref[0:1, :] += gain_back[None, :]
+    vec_ref[1:2, :] += shift_back[None, :]
+    grad_middle = grad + back
+    gmid_ref[...] = grad_middle
+    branch = grad_middle.astype(BF16)
+    out_acc[...] += dotg(att, branch, 1, 0)
+    lane = lax.broadcasted_iota(jnp.int32, (1, ROWS), 1)
+    position = step // 4 * SEG + lax.rem(lane, RUN) * RES + residue_of(lane // RUN) + low
+    keep = position < mask_ref[0]
+    merged = jnp.where(keep, dotg(wout_ref[...], branch, 1, 1), 0.0).astype(BF16)
+    gm_ref[...] = merged
+    product = merged.astype(F32) * att.astype(F32)
+    for head in range(HEADS):
+        rows = slice(head * HEAD_DIM, (head + 1) * HEAD_DIM)
+        along_ref[head] = jnp.sum(product[rows], axis=0, keepdims=True)
+
+    @pl.when(step == pl.num_programs(0) - 1)
+    def _():
+        copies = []
+        for owner in range(4):
+            for piece in range(3):
+                count = owner * 3 + piece
+                slot = count % 2
+                if count >= 2:
+                    copies[count - 2].wait()
+                if piece == 0:
+                    rows = slice(owner * 192, (owner + 1) * 192)
+                    for col in range(4):
+                        stage[slot, col * 192 : (col + 1) * 192, :] = up_acc[
+                            rows, col * D : (col + 1) * D
+                        ].astype(BF16)
+                    offset, size = 0, UP_ROWS
+                elif piece == 1:
+                    stage[slot, :192, :] = out_acc[owner * 192 : (owner + 1) * 192, :].astype(BF16)
+                    offset, size = UP_ROWS, 192
+                else:
+                    stage[slot, :D, :] = down_acc[owner * D : (owner + 1) * D, :].astype(BF16)
+                    offset, size = UP_ROWS + 192, D
+                copy = pltpu.make_async_copy(
+                    stage.at[slot, pl.ds(0, size), :],
+                    grads_ref.at[owner, pl.ds(offset, size), :],
+                    sems.at[slot],
+                )
+                copy.start()
+                copies.append(copy)
+        copies[-2].wait()
+        copies[-1].wait()
+
+
+def call_feed(nseg, mask, att, x, cot, wout, up, down, gain, shift):
+    length = nseg * SEG
+    return pl.pallas_call(
+        functools.partial(feed_kernel, nseg),
+        grid=(length // ROWS,),
+        in_specs=[
+            MASK_BLOCK,
+            pl.BlockSpec((D, ROWS), lambda i: (0, i)),
+            pl.BlockSpec((ROWS, D), lambda i: (i, 0)),
+            pl.BlockSpec((SEG, D), lambda i: (i // 4, 0)),
+            const_block((D, D)),
+            const_block((D, 4 * D)),
+            const_block((4 * D, D)),
+            const_block((1, D)),
+            const_block((1, D)),
+        ],
+        out_specs=[
+            pl.BlockSpec((SEG, D), lambda i: (i // 4, 0)),
+            pl.BlockSpec((ROWS, D), lambda i: (i, 0)),
+            pl.BlockSpec((D, ROWS), lambda i: (0, i)),
+            pl.BlockSpec((HEADS, 1, ROWS), lambda i: (0, 0, i)),
+            pl.BlockSpec((2, D), lambda i: (0, 0)),
+            pl.BlockSpec(memory_space=pl.ANY),
+        ],
+        out_shape=[
+            shape((length, D), BF16),
+            shape((length, D), F32),
+            shape((D, length), BF16),
+            shape((HEADS, 1, length), F32),
+            shape((2, D), F32),
+            shape((4, STACK, D), BF16),
+        ],
+        scratch_shapes=[
+            pltpu.VMEM((TILES, SEG, 128), F32),
+            pltpu.VMEM((D, D), F32),
+            pltpu.VMEM((D, 4 * D), F32),
+            pltpu.VMEM((4 * D, D), F32),
+            pltpu.VMEM((2, D, D), BF16),
+            pltpu.SemaphoreType.DMA((2,)),
+        ],
+        compiler_params=pltpu.CompilerParams(vmem_limit_bytes=62 * 1024 * 1024),
+        cost_estimate=cost(nseg * 45e-6),
+        name="feed",
+    )(mask, att, x, cot, wout, up, down, gain, shift)
+
+
+def inner_back_kernel(nseg, first, local_ref, inner_ref, w_ref, x_ref, gmid_ref, gain_ref, *refs):
+    n = BRANCHES - first
+    packs, (grad_in_ref, back_ref, vec_ref), (acc, mixed, order) = refs[:n], refs[n : n + 3], refs[n + 3 :]
+    step = pl.program_id(0)
+    length = nseg * SEG
+
+    @pl.when(step < 2)
+    def _():
+        mixed[...] = local_ref[0].astype(BF16)
+
+    @pl.when(step >= 2)
+    def _():
+        upper = lax.rem(step, 2) == 1
+        for pack, level in zip(packs, range(first, BRANCHES)):
+            size = SEG >> level
+            for head in range(HEADS // 2):
+                rows = slice(head * HEAD_DIM, (head + 1) * HEAD_DIM)
+                for seg in range(nseg):
+                    start = seg * SEG + (rev4(head) >> (4 - level)) * size
+                    piece = pack[0, rows, seg * size : (seg + 1) * size].astype(F32)
+                    if level == 4:
+                        zero = jnp.zeros_like(piece)
+                        piece = jnp.concatenate(
+                            [jnp.where(upper, zero, piece), jnp.where(upper, piece, zero)], axis=1
+                        )
+                    local_ref[0, rows, start : start + piece.shape[1]] += piece
+        mixed[...] = local_ref[0].astype(BF16)
+
+    grad_in_ref[...] = dotg(inner_ref[...], mixed[...], 1, 1).astype(BF16)
+    for start in range(0, length, 512):
+        lanes = slice(start, start + 512)
+        part = dotg(w_ref[...], mixed[:, lanes], 1, 0)
+
+        @pl.when(step == 0)
+        def _():
+            acc[:, lanes] = part
+
+        @pl.when(step > 0)
+        def _():
+            acc[:, lanes] += part
+
+    @pl.when(step == pl.num_programs(0) - 1)
+    def _():
+        gain = gain_ref[...]
+        gain_back = jnp.zeros((1, D), F32)
+        shift_back = jnp.zeros((1, D), F32)
+        for seg in range(nseg):
+            for pair in range(RES // 2):
+                at = slice(seg * SEG + pair * 2 * RUN, seg * SEG + (pair + 1) * 2 * RUN)
+                grad = acc[:, at].T
+                _, unit, inverse = normalize(x_ref[at, :].astype(F32), gain, gain)
+                back, gain_part, shift_part = normalize_back(grad, unit, inverse, gain)
+                gain_back = gain_back + gain_part[None, :]
+                shift_back = shift_back + shift_part[None, :]
+                total = gmid_ref[at, :] + back
+                for i in range(2):
+                    put_residue(order, rev4(2 * pair + i), total[i * RUN : (i + 1) * RUN])
+            back_ref[seg * SEG : (seg + 1) * SEG, :] = get_rows(order, 0, SEG)
+        vec_ref[0:1, :] = gain_back
+        vec_ref[1:2, :] = shift_back
+
+
+def call_inner_back(nseg, first, local, inner, weight, x, gmid, gain, packs):
+    length = nseg * SEG
+    return pl.pallas_call(
+        functools.partial(inner_back_kernel, nseg, first),
+        grid=(6,),
+        in_specs=[
+            pl.BlockSpec((1, HALF, length), lambda i: (i // 2, i % 2, 0)),
+            const_block((D, length)),
+            pl.BlockSpec((D, HALF), lambda i: (0, i)),
+            const_block((length, D)),
+            const_block((length, D)),
+            const_block((1, D)),
+        ]
+        + [
+            pl.BlockSpec((1, HALF, pack.shape[2]), lambda i: (jnp.maximum(i // 2 - 1, 0), i % 2, 0))
+            for pack in packs
+        ],
+        out_specs=[
+            pl.BlockSpec((D, HALF), lambda i: (0, i)),
+            const_block((length, D)),
+            const_block((2, D)),
+        ],
+        out_shape=[shape((D, 3 * D), BF16), shape((length, D), F32), shape((2, D), F32)],
+        scratch_shapes=[
+            pltpu.VMEM((D, length), F32),
+            pltpu.VMEM((HALF, length), BF16),
+            pltpu.VMEM((TILES, SEG, 128), F32),
+        ],
+        compiler_params=PARAMS,
+        cost_estimate=cost(nseg * 15e-6),
+        name="inner_back",
+    )(local, inner, weight, x, gmid, gain, *packs)
 
 
 def exchange(array, distance):
@@ -505,22 +844,6 @@
         grads = (grads[..., :half].astype(F32) + other.astype(F32)).astype(BF16)
         step //= 2
     return exchange(grads, group)
-
-
-def spread_level(grads, level, nseg):
-    size = SEG >> level
-    shaped = grads.astype(F32).reshape(2, HEADS, HEAD_DIM, nseg, 1, size)
-    head = jnp.arange(HEADS, dtype=jnp.int32)
-    block = reversed_bits(head) >> (4 - level)
-    hit = block[:, None] == jnp.arange(1 << level, dtype=jnp.int32)[None, :]
-    full = jnp.where(hit[None, :, None, None, :, None], shaped, 0.0)
-    return full.reshape(2, D, nseg * SEG)
-
-
-def scatter_sum(term):
-    part = lax.psum_scatter(term.astype(BF16), "fsdp", scatter_dimension=0, tiled=True)
-    piece = lax.psum_scatter(part, "seq", scatter_dimension=0, tiled=True)
-    return lax.all_gather(piece, "seq", axis=0, tiled=True).astype(F32)
 
 
 def per_device(
@@ -539,92 +862,63 @@
     length = tokens.shape[1]
     nseg = length // SEG
     first = nseg.bit_length()
+    levels = range(first, BRANCHES)
+    group_of = {level: (SEG << (level - 1)) // length for level in levels}
 
     def gather(weight):
         return lax.all_gather(weight, "fsdp", axis=0, tiled=True)
 
     weight_in = gather(project_in)
     small = gather(jnp.stack([first_gain, first_shift, second_gain, second_shift], axis=1)).astype(F32)
-    gain_attend, shift_attend, gain_feed, shift_feed = (small[:, i] for i in range(4))
+    gain_attend, shift_attend, gain_feed, shift_feed = (small[:, i][None, :] for i in range(4))
     weight_out = gather(project_out)
     weight_up = gather(up_weight)
     weight_down = gather(down_weight)
 
-    stream = reorder(tokens[0]).astype(F32)
-    keep = reorder(valid_mask[0][:, None])[:, 0].astype(F32)[None, :]
-    normed_in, unit_first, inverse_first = normalize(stream, gain_attend, shift_attend)
-    inner = normed_in.astype(BF16)
-    column_scale = jnp.where(jnp.arange(3 * D) < D, QUERY_SCALE, 1.0).astype(F32)
-    qkv = (dotg(weight_in, inner, 0, 1) * column_scale[:, None]).astype(BF16).reshape(3, D, length)
-
-    sends = call_pack(nseg, first, qkv, keep)
-    packs = [
-        fetch_level(send, (SEG << (level - 1)) // length)
-        for level, send in zip(range(first, BRANCHES), sends)
-    ]
-    o_part, l_part, m_part = call_local_forward(nseg, qkv, keep)
-    attended, lse = call_remote_forward(nseg, first, qkv, keep, o_part, l_part, m_part, packs)
-
-    middle = stream + dotg(attended, weight_out, 0, 0)
-    normed_mid, unit_second, inverse_second = normalize(middle, gain_feed, shift_feed)
-    hidden = normed_mid.astype(BF16)
-    upper = jnp.dot(hidden, weight_up, preferred_element_type=F32)
-    active = (0.5 * upper * (1.0 + lax.erf(upper * ROOT_HALF))).astype(BF16)
-    final = middle + jnp.dot(active, weight_down, preferred_element_type=F32)
-    mixed = restore(final.astype(BF16))[None]
-
-    grad_final = reorder(cotangent[0])
-    grad_down = dotg(active, grad_final, 0, 0)
-    grad_active = dotg(grad_final, weight_down, 1, 1)
-    slope = (
-        0.5 * (1.0 + lax.erf(upper * ROOT_HALF))
-        + upper * jnp.exp(-0.5 * upper * upper) * INV_ROOT_TWO_PI
+    block_devices = (RES * SEG) // length
+    place = lax.axis_index("seq")
+    count = jnp.sum(valid_mask[0])
+    counts = lax.all_gather(count.astype(F32), "seq")
+    same = jnp.arange(counts.shape[0], dtype=jnp.int32) // block_devices == place // block_devices
+    limit = jnp.sum(jnp.where(same, counts, 0.0)).astype(jnp.int32)
+    local_mask = count[None]
+    mask = jnp.stack([count, place, limit + place // block_devices * (RES * SEG)])
+
+    qkv, x, inner, *sends = call_project(nseg, first, tokens[0], gain_attend, shift_attend, weight_in)
+    packs = [fetch_level(send, group_of[level]) for level, send in zip(levels, sends)]
+    o_part, l_part, m_part = call_local_forward(nseg, qkv, local_mask)
+    attended, lse = call_remote_forward(nseg, first, qkv, mask, o_part, l_part, m_part, packs)
+
+    mixed, grad_middle, grad_merged, along, feed_vec, feed_grads = call_feed(
+        nseg, local_mask, attended, x, cotangent[0], weight_out, weight_up, weight_down, gain_feed, shift_feed
     )
-    grad_upper = (grad_active * slope).astype(BF16)
-    grad_up = dotg(hidden, grad_upper, 0, 0)
-    grad_hidden = dotg(grad_upper, weight_up, 1, 1)
-    grad_mid_norm, grad_gain_feed, grad_shift_feed = normalize_back(
-        grad_hidden, unit_second, inverse_second, gain_feed
+    feed_part = lax.psum_scatter(feed_grads, "fsdp", scatter_dimension=0, tiled=True)
+    feed_sum = lax.psum(feed_part, "seq")[0]
+
+    dq_remote, *sent = call_remote_backward(nseg, first, qkv, grad_merged, lse, along, mask, packs)
+    returned = [return_level(part, group_of[level]) for level, part in zip(levels, sent)]
+    local = call_local_backward(nseg, first, qkv, grad_merged, lse, along, local_mask, dq_remote)
+    grad_in, tokens_back, attend_vec = call_inner_back(
+        nseg, first, local, inner, weight_in, x, grad_middle, gain_attend, returned
     )
-    grad_middle = grad_final.astype(F32) + grad_mid_norm
-    grad_branch = grad_middle.astype(BF16)
-    grad_out_proj = dotg(attended, grad_branch, 1, 0)
-    grad_merged = (dotg(weight_out, grad_branch, 1, 1) * keep).astype(BF16)
-    along = jnp.sum(
-        (grad_merged.astype(F32) * attended.astype(F32)).reshape(HEADS, HEAD_DIM, length), axis=1
-    )[:, None, :]
-
-    dq_remote, *sent = call_remote_backward(nseg, first, qkv, grad_merged, lse, along, keep, packs)
-    returned = [
-        return_level(part, (SEG << (level - 1)) // length)
-        for level, part in zip(range(first, BRANCHES), sent)
-    ]
-    local = call_local_backward(nseg, first, qkv, grad_merged, lse, along, keep, dq_remote)
-    key_value = local[1:]
-    for level, part in zip(range(first, BRANCHES), returned):
-        key_value = key_value + spread_level(part, level, nseg)
-    grad_mixed = jnp.concatenate([local[:1], key_value], axis=0).astype(BF16).reshape(3 * D, length)
-
-    grad_in = dotg(inner, grad_mixed, 0, 1)
-    grad_inner = dotg(grad_mixed, weight_in, 0, 1)
-    grad_in_norm, grad_gain_attend, grad_shift_attend = normalize_back(
-        grad_inner, unit_first, inverse_first, gain_attend
-    )
-    tokens_back = restore(grad_middle + grad_in_norm)[None]
-
-    vectors = jnp.stack([grad_gain_attend, grad_shift_attend, grad_gain_feed, grad_shift_feed], axis=1)
-    vectors = scatter_sum(vectors)
+    in_part = lax.psum_scatter(grad_in, "fsdp", scatter_dimension=0, tiled=True)
+    in_part, feed_sum = lax.optimization_barrier((in_part, feed_sum))
+    in_sum = lax.psum(in_part, "seq")
+    vectors = lax.psum(jnp.concatenate([attend_vec, feed_vec], axis=0), ("fsdp", "seq"))
+    quarter = D // lax.axis_size("fsdp")
+    vectors = lax.dynamic_slice_in_dim(vectors, lax.axis_index("fsdp") * quarter, quarter, 1)
+    up_rows = feed_sum[:UP_ROWS].reshape(4, 192, D)
     return (
-        mixed,
-        tokens_back,
-        vectors[:, 0],
-        vectors[:, 1],
-        scatter_sum(grad_in),
-        scatter_sum(grad_out_proj),
-        vectors[:, 2],
-        vectors[:, 3],
-        scatter_sum(grad_up),
-        scatter_sum(grad_down),
+        mixed[None],
+        tokens_back[None],
+        vectors[0],
+        vectors[1],
+        in_sum.astype(F32),
+        feed_sum[UP_ROWS : UP_ROWS + 192].astype(F32),
+        vectors[2],
+        vectors[3],
+        jnp.concatenate([up_rows[i] for i in range(4)], axis=1).astype(F32),
+        feed_sum[UP_ROWS + 192 :].astype(F32),
     )
 
 

time: 1180 us -> 874 us (0.74)
  local copies, waits for them, and re-layouts: 181 us -> 5.63 us
  Pallas kernels: 314 us -> 477 us
  matrix products: 159 us -> 0 us
  other arithmetic: 79.6 us -> 14 us
  blocking collectives: 106 us -> 66.5 us
  waiting for transfers between devices: 289 us -> 274 us
    psum x0 -> x2, waiting for transfers between devices: none -> 192 us  [the longest x1 120 us: per_device(): feed_sum = lax.psum(feed_part, 'seq')[0]]
    reduce_scatter x8 -> x2, waiting for transfers between devices: 185 us -> 0.1 us  [the longest x1 0.08 us: per_device(): in_part = lax.psum_scatter(grad_in, 'fsdp', scatter_dimension=0, tiled=True)]
    pallas_call x1 -> x3, Pallas kernels: 5.6 us -> 169 us  [the longest x1 100 us: call_feed(): pl.pallas_call(functools.partial(feed_kernel, nseg), grid=(length // ROWS...]
    dot_general x12 -> x0, matrix products: 159 us -> none  [the longest x10 125 us: dotg(): lax.dot_general(left, right, (((left_dim,), (right_dim,)), ((), ())), pre...]
    broadcast_in_dim x16 -> x0, local copies, waits for them, and re-layouts: 99.7 us -> none  [the longest x15 99 us: spread_level(): full = jnp.where(hit[None, :, None, None, :, None], shaped, 0.0)]
    all_gather x3 -> x0, blocking collectives: 80.5 us -> none  [scatter_sum(): return lax.all_gather(piece, 'seq', axis=0, tiled=True).astype(F32)]
    all_gather x2 -> x0, waiting for transfers between devices: 49.6 us -> none  [scatter_sum(): return lax.all_gather(piece, 'seq', axis=0, tiled=True).astype(F32)]
    psum x0 -> x1, blocking collectives: none -> 39.4 us  [per_device(): lax.psum(jnp.concatenate([attend_vec, feed_vec], axis=0), ('fsdp', 'seq'))]
  transfers between devices with their start and end apart: 27 -> 20, of which waited for: 11 -> 9; matrix products, arithmetic and copies ran while one was open for 35% -> 2% of each run, Pallas kernels for 27% -> 43%
where the time goes in v2:
time: 874 us; the launch traced here: 868 us
  Pallas kernels  477 us (55%)
  waiting for transfers between devices  274 us (31%)
  blocking collectives  66.5 us (8%)
  between operations  16.3 us (2%)
  starting transfers between devices  14.9 us (2%)
  other arithmetic  14 us (2%)
    pallas_call x1, Pallas kernels, call_local_backward(): pl.pallas_call(functools.partial(local_backward, nseg, first), grid=(HEAD...  146 us
    psum x1, waiting for transfers between devices, per_device(): feed_sum = lax.psum(feed_part, 'seq')[0]  120 us
    pallas_call x1, Pallas kernels, call_feed(): pl.pallas_call(functools.partial(feed_kernel, nseg), grid=(length // ROWS...  100 us
    pallas_call x1, Pallas kernels, call_local_forward(): pl.pallas_call(functools.partial(local_forward, nseg), grid=(HEADS,), in_...  76.2 us
    psum x1, waiting for transfers between devices, per_device(): in_sum = lax.psum(in_part, 'seq')  72 us
    ppermute x12, waiting for transfers between devices, exchange(): return lax.ppermute(array, 'seq', [(i, i ^ distance) for i in range(size)])  51.7 us
    pallas_call x1, Pallas kernels, call_inner_back(): pl.pallas_call(functools.partial(inner_back_kernel, nseg, first), grid=(6...  47.7 us
    pallas_call x1, Pallas kernels, call_remote_forward(): pl.pallas_call(functools.partial(remote_forward, nseg, first), grid=(HEAD...  47.5 us
  transfers between devices with their start and end apart: 20, of which 9 were waited for; matrix products, arithmetic and copies ran while one was open for 2% of the time, Pallas kernels for 43%

profile of v2, /device:TPU:0, one launch (start us, length us, event | category | flops | bytes accessed | tf_op | source)
XLA Modules:
  0.0 867.8 jit_solution(16541606909430858836)
XLA Ops:
  7.3 0.7 all-gather.6.cloned.1.call-update
  8.0 0.7 all-gather.8.cloned.1.call-update
  8.7 0.7 all-gather.10.cloned.1.call-update
  9.6 6.1 all-gather
  15.8 0.6 slice_bitcast_fusion
  16.4 26.7 %all-gather.6.cloned.1.call-done.w_ref = bf16[768,2304]{1,0:T(8,128)(2,1)} async-done(((bf16[192,2304]{1,0:T(8,128)(2,1)}), bf16[768,2304]{1,0:T(8,128)(2,1)}) %all-gather.6.cloned.1.call-update) | async-done | bytes 3538960 | tf_op jit(solution)/shard_map/all_gather | solution.py:869
  43.1 20.6 %project.1 = (bf16[3,768,2048]{2,1,0:T(8,128)(2,1)}, bf16[2048,768]{1,0:T(8,128)(2,1)}, bf16[768,2048]{1,0:T(8,128)(2,1)}, bf16[1536,512]{1,0:T(8,128)(2,1)}, bf...) custom-call(bf16[2048,768]{1,0:T(8,128)(2,1)} %bitcast.31, f32[1,768]{1,0:T(1,128)} %get-tuple-element.74.gain_ref, ...), custom_call_target="tpu_custom_call" | custom-call | flops 22000001024 | tf_op jit(solution)/shard_map/project/pallas_call | solution.py:551
  63.7 2.5 collective-permute-start.3
  66.2 18.4 %collective-permute-done.3 = bf16[1536,128]{1,0:T(8,128)(2,1)S(1)} collective-permute-done((bf16[1536,128]{1,0:T(8,128)(2,1)}, bf16[1536,128]{1,0:T(8,128)(2,1)S(1)}, u32[]{:S(2)}, u32[]{:S(2)}) %collective-permute-start.3) | collective-permute-done | bytes 393248 | tf_op jit(solution)/shard_map/ppermute | solution.py:827
  84.6 1.5 collective-permute-start.4
  86.1 0.6 reduce_sum.18
  87.4 0.6 dynamic-slice
  88.0 0.8 dynamic-update-slice
  88.8 21.0 %all-reduce = f32[8]{0:T(128)S(1)} all-reduce(f32[8]{0:T(128)S(1)} %dynamic-update-slice), channel_id=1, replica_groups=mesh['seq'=8,'fsdp'=4] {'seq'}, use_global_device_ids=true, to_apply=%add | all-reduce | flops 8 | bytes 64
  109.8 0.6 fusion
  111.1 1.2 pad_add_fusion.mask_ref
  112.4 2.1 collective-permute-start.5
  114.5 76.2 %local_forward.1 = (f32[768,2048]{1,0:T(8,128)}, f32[16,1,2048]{2,1,0:T(1,128)}, f32[16,1,2048]{2,1,0:T(1,128)}) custom-call(s32[1]{0:T(128)} %bitcast.mask_ref, bf16[3,768,2048]{2,1,0:T(8,128)(2,1)} %get-tuple-element.36.q_ref.k_ref.v_ref, bf16[3,768,2048]{2,1,0:T(8,128)(2,1)} %get-tuple-element.36.q_ref.k_ref.v_ref, ...), custom_call_target="tpu_custom_call" | custom-call | flops 81399996416 | tf_op jit(solution)/shard_map/local_forward/pallas_call | solution.py:380
  190.7 2.1 collective-permute-start.2
  193.1 13.0 %collective-permute-done.2 = bf16[1536,256]{1,0:T(8,128)(2,1)S(1)} collective-permute-done((bf16[1536,256]{1,0:T(8,128)(2,1)S(1)}, bf16[1536,256]{1,0:T(8,128)(2,1)S(1)}, u32[]{:S(2)}, u32[]{:S(2)}) %collective-permute-start.2) | collective-permute-done | bytes 786464 | tf_op jit(solution)/shard_map/ppermute | solution.py:827
  206.2 1.1 copy-done.2
  207.3 47.5 %remote_forward.1 = (bf16[768,2048]{1,0:T(8,128)(2,1)}, f32[16,1,2048]{2,1,0:T(1,128)}) custom-call(s32[3]{0:T(128)} %pad_add_fusion.mask_ref, bf16[3,768,2048]{2,1,0:T(8,128)(2,1)} %get-tuple-element.36.q_ref.k_ref.v_ref, f32[768,2048]{1,0:T(8,128)} %get-tuple-element.37.o_in, f32[16,1,2048]{2,1,0:T(1,128)} %get-tuple-element.38.l_in, ...), custom_call_target="tpu_custom_call" | custom-call | flops 52800000000 | tf_op jit(solution)/shard_map/remote_forward/pallas_call | solution.py:403
  254.9 100.3 %feed.1 = (bf16[2048,768]{1,0:T(8,128)(2,1)}, f32[2048,768]{1,0:T(8,128)}, bf16[768,2048]{1,0:T(8,128)(2,1)}, f32[16,1,2048]{2,1,0:T(1,128)}, f32[2,768]{1,0:T(2,128)}, /*index=5*/bf16[4,1728,768]{2,1,0:T(8,128)(2,1)}) custom-call(s32[1]{0:T(128)} %bitcast.mask_ref, bf16[768,2048]{1,0:T(8,128)(2,1)} %get-tuple-element.43.att_ref, ...), custom_call_target="tpu_custom_call" | custom-call | flops 99000000512 | tf_op jit(solution)/shard_map/feed/pallas_call | solution.py:685
  355.2 39.1 %remote_backward.1 = (f32[768,512]{1,0:T(8,128)}, bf16[2,768,512]{2,1,0:T(8,128)(2,1)}, bf16[2,768,512]{2,1,0:T(8,128)(2,1)}, bf16[2,768,512]{2,1,0:T(8,128)(2,1)}) custom-call(s32[3]{0:T(128)} %pad_add_fusion.mask_ref, bf16[3,768,2048]{2,1,0:T(8,128)(2,1)} %get-tuple-element.36.q_ref.k_ref.v_ref, bf16[768,2048]{1,0:T(8,128)(2,1)} %get-tuple-element.46.g_ref, ...), custom_call_target="tpu_custom_call" | custom-call | flops 44000002048 | tf_op jit(solution)/shard_map/remote_backward/pallas_call | solution.py:429
  394.4 1.3 slice.76
  395.7 0.5 collective-permute-start.9
  396.2 1.8 collective-permute-start.7
  398.0 12.3 %collective-permute-done.9 = bf16[2,768,256]{2,1,0:T(8,128)(2,1)S(1)} collective-permute-done((bf16[2,768,256]{2,1,0:T(8,128)(2,1)S(1)}, bf16[2,768,256]{2,1,0:T(8,128)(2,1)S(1)}, u32[]{:S(2)}, u32[]{:S(2)}) %collective-permute-start.9) | collective-permute-done | bytes 786464 | tf_op jit(solution)/shard_map/ppermute | solution.py:827
  410.3 0.2 add_convert_fusion
  410.6 1.8 collective-permute-start.10
  412.3 0.3 collective-permute-start.6
  412.6 1.8 collective-permute-done.7
  414.4 1.1 add_convert_fusion.1
  415.5 1.1 collective-permute-start.8
  416.6 6.3 collective-permute-done.10
  422.9 0.8 add_convert_fusion.2
  423.7 0.9 collective-permute-start.11
  424.6 145.6 %local_backward.1.local_ref = f32[3,768,2048]{2,1,0:T(8,128)} custom-call(s32[1]{0:T(128)} %bitcast.mask_ref, bf16[3,768,2048]{2,1,0:T(8,128)(2,1)} %get-tuple-element.36.q_ref.k_ref.v_ref, bf16[3,768,2048]{2,1,0:T(8,128)(2,1)} %get-tuple-element.36.q_ref.k_ref.v_ref, bf16[3,768,2048]{2,1,0:T(8,128)(2,1)} %get-tuple-element.36.q_ref.k_ref.v_ref, ...), custom_call_target="tpu_custom_call" | custom-call | flops 158400004096 | tf_op jit(solution)/shard_map/local_backward/pallas_call | solution.py:453
  570.3 47.7 %inner_back.1 = (bf16[768,2304]{1,0:T(8,128)(2,1)}, f32[2048,768]{1,0:T(8,128)}, f32[2,768]{1,0:T(2,128)}) custom-call(f32[3,768,2048]{2,1,0:T(8,128)} %local_backward.1.local_ref, bf16[768,2048]{1,0:T(8,128)(2,1)} %get-tuple-element.50.inner_ref, bf16[768,2304]{1,0:T(8,128)(2,1)} %all-gather.6.cloned.1.call-done.w_ref, ...), custom_call_target="tpu_custom_call" | custom-call | flops 32999999488 | tf_op jit(solution)/shard_map/inner_back/pallas_call | solution.py:793
  618.1 0.7 all-reduce.4.cloned.1.call-update
  618.9 39.4 %psum.21 = f32[4,768]{1,0:T(4,128)S(1)} all-reduce(f32[4,768]{1,0:T(4,128)S(1)} %pad_maximum_fusion.1), channel_id=1, replica_groups=mesh['seq'=8,'fsdp'=4] {'fsdp','seq'}, use_global_device_ids=true, to_apply=%region_2.3 | all-reduce | flops 3072 | bytes 24576 | tf_op jit(solution)/shard_map/psum | solution.py:907
  658.3 0.7 fusion.2
  659.0 120.3 %all-reduce.4.cloned.1.call-done = bf16[1728,768]{1,0:T(8,128)(2,1)} async-done(((bf16[1728,768]{1,0:T(8,128)(2,1)}), bf16[1728,768]{1,0:T(8,128)(2,1)}) %all-reduce.4.cloned.1.call-update) | async-done | bytes 2654224 | tf_op jit(solution)/shard_map/psum | solution.py:896
  779.3 2.3 fusion.1
  781.6 2.8 slice_convert_fusion
  784.4 1.7 maximum_convert_fusion
  786.1 72.0 %all-reduce.6.cloned.1.call-done = bf16[192,2304]{1,0:T(8,128)(2,1)} async-done(((bf16[192,2304]{1,0:T(8,128)(2,1)}), bf16[192,2304]{1,0:T(8,128)(2,1)}) %all-reduce.6.cloned.1.call-update) | async-done | bytes 884752 | tf_op jit(solution)/shard_map/psum | solution.py:906
  858.1 2.5 convert_element_type.60
  (66 shorter events, 1.3 us)
Async XLA Ops:
  7.2 2.3 copy-start.7
  7.2 2.3 copy-start.8
  7.2 2.3 copy-start.9
  7.2 2.3 copy-start.10
  7.2 35.9 %all-gather.6.cloned.1.call-start = ((), (), s32[]{:S(2)}) async-start(), calls=%async_computation.2 | async-start | bytes 4423680 | tf_op jit(solution)/shard_map/all_gather | solution.py:869
  8.0 246.9 %all-gather.8.cloned.1.call-start = ((), (), s32[]{:S(2)}) async-start(), calls=%async_computation.3 | async-start | bytes 1474560 | tf_op jit(solution)/shard_map/all_gather | solution.py:869
  8.7 246.1 %all-gather.10.cloned.1.call-start = ((), (), s32[]{:S(2)}) async-start(), calls=%async_computation.4 | async-start | bytes 5898240 | tf_op jit(solution)/shard_map/all_gather | solution.py:869
  9.4 245.4 %all-gather.12.cloned.1.call-start = ((), (), s32[]{:S(2)}) async-start(), calls=%async_computation.5 | async-start | bytes 5898240 | tf_op jit(solution)/shard_map/all_gather | solution.py:869
  43.1 43.0 %copy-start.4 = (s32[1,2048]{1,0:T(1,128)S(1)}, s32[1,2048]{1,0:T(1,128)}, u32[]{:S(2)}) copy-start(s32[1,2048]{1,0:T(1,128)} %param.20) | copy-start | bytes 24580
  43.1 44.3 %copy-start.11 = (u32[32]{0:T(128)S(1)}, u32[32]{0:T(128)}, u32[]{:S(2)}) copy-start(u32[32]{0:T(128)} %constant.52) | copy-start | bytes 388
  63.7 20.9 %collective-permute-start.3 = (bf16[1536,128]{1,0:T(8,128)(2,1)}, bf16[1536,128]{1,0:T(8,128)(2,1)S(1)}, u32[]{:S(2)}, u32[]{:S(2)}) collective-permute-start(bf16[1536,128]{1,0:T(8,128)(2,1)} %get-tuple-element.42), channel_id=1, source_target_pairs={{0,16},{4,20},{8,24},{12,28},{16,0},{20,4},{24,8},{28,12},{1,17},{... | collective-permute-start | bytes 1179656 | tf_op jit(solution)/shard_map/ppermute | solution.py:827
  84.6 27.8 %collective-permute-start.4 = (bf16[1536,128]{1,0:T(8,128)(2,1)S(1)}, bf16[1536,128]{1,0:T(8,128)(2,1)S(1)}, u32[]{:S(2)}, u32[]{:S(2)}) collective-permute-start(bf16[1536,128]{1,0:T(8,128)(2,1)S(1)} %collective-permute-done.3), channel_id=1, source_target_pairs={{0,4},{4,0},{8,12},{12,8},{16,20},{20,16},{24,28},{28,24},{1,5},{5... | collective-permute-start | bytes 1179656 | tf_op jit(solution)/shard_map/ppermute | solution.py:827
  88.8 529.3 %reduce-scatter.5.cloned.1.call-start = ((), (), s32[]{:S(2)}) async-start(), calls=%async_computation.7 | async-start | bytes 13271040 | tf_op jit(solution)/shard_map/reduce_scatter | solution.py:895
  112.3 78.4 %collective-permute-start.1 = (bf16[1536,256]{1,0:T(8,128)(2,1)}, bf16[1536,256]{1,0:T(8,128)(2,1)S(1)}, u32[]{:S(2)}, u32[]{:S(2)}) collective-permute-start(bf16[1536,256]{1,0:T(8,128)(2,1)} %get-tuple-element.41), channel_id=1, source_target_pairs={{0,8},{4,12},{8,0},{12,4},{16,24},{20,28},{24,16},{28,20},{1,9},{5... | collective-permute-start | bytes 2359304 | tf_op jit(solution)/shard_map/ppermute | solution.py:827
  112.3 93.9 %collective-permute-start = (bf16[1536,512]{1,0:T(8,128)(2,1)}, bf16[1536,512]{1,0:T(8,128)(2,1)}, u32[]{:S(2)}, u32[]{:S(2)}) collective-permute-start(bf16[1536,512]{1,0:T(8,128)(2,1)} %get-tuple-element.40), channel_id=1, source_target_pairs={{0,4},{4,0},{8,12},{12,8},{16,20},{20,16},{24,28},{28,24},{1,5},{5... | collective-permute-start | bytes 4718600 | tf_op jit(solution)/shard_map/ppermute | solution.py:827
  112.4 80.6 %collective-permute-start.5 = (bf16[1536,256]{1,0:T(8,128)(2,1)S(1)}, bf16[1536,256]{1,0:T(8,128)(2,1)S(1)}, u32[]{:S(2)}, u32[]{:S(2)}) collective-permute-start(bf16[1536,256]{1,0:T(8,128)(2,1)S(1)} %pad_maximum_fusion), channel_id=1, source_target_pairs={{0,8},{4,12},{8,0},{12,4},{16,24},{20,28},{24,16},{28,20},{1,9},{5... | collective-permute-start | bytes 2359304 | tf_op jit(solution)/shard_map/ppermute | solution.py:827
  190.7 15.4 %collective-permute-start.2 = (bf16[1536,256]{1,0:T(8,128)(2,1)S(1)}, bf16[1536,256]{1,0:T(8,128)(2,1)S(1)}, u32[]{:S(2)}, u32[]{:S(2)}) collective-permute-start(bf16[1536,256]{1,0:T(8,128)(2,1)S(1)} %collective-permute-done.1), channel_id=1, source_target_pairs={{0,4},{4,0},{8,12},{12,8},{16,20},{20,16},{24,28},{28,24},{1,5},{5... | collective-permute-start | bytes 2359304 | tf_op jit(solution)/shard_map/ppermute | solution.py:827
  193.1 13.1 %copy-start.3 = (bf16[1536,512]{1,0:T(8,128)(2,1)}, bf16[1536,512]{1,0:T(8,128)(2,1)S(1)}, u32[]{:S(2)}) copy-start(bf16[1536,512]{1,0:T(8,128)(2,1)S(1)} %constant_dynamic-update-slice_fusion.2.refs_4_.refs_5_) | copy-start | bytes 4718596
  206.2 1.1 copy-start.2
  355.2 303.9 %reduce-scatter.3.cloned.1.call-start = ((), (), s32[]{:S(2)}) async-start(), calls=%async_computation.6 | async-start | bytes 4423680 | tf_op jit(solution)/shard_map/reduce_scatter | solution.py:904
  394.3 1.8 copy-start
  394.3 16.0 %copy-start.1 = (bf16[2,768,512]{2,1,0:T(8,128)(2,1)S(1)}, bf16[2,768,512]{2,1,0:T(8,128)(2,1)}, u32[]{:S(2)}) copy-start(bf16[2,768,512]{2,1,0:T(8,128)(2,1)} %get-tuple-element.54) | copy-start | bytes 4718596
  395.7 14.6 %collective-permute-start.9 = (bf16[2,768,256]{2,1,0:T(8,128)(2,1)S(1)}, bf16[2,768,256]{2,1,0:T(8,128)(2,1)S(1)}, u32[]{:S(2)}, u32[]{:S(2)}) collective-permute-start(bf16[2,768,256]{2,1,0:T(8,128)(2,1)S(1)} %slice.76), channel_id=1, source_target_pairs={{0,8},{4,12},{8,0},{12,4},{16,24},{20,28},{24,16},{28,20},{1,9},{5... | collective-permute-start | bytes 2359304 | tf_op jit(solution)/shard_map/ppermute | solution.py:827
  396.2 18.2 %collective-permute-start.7 = (bf16[2,768,256]{2,1,0:T(8,128)(2,1)S(1)}, bf16[2,768,256]{2,1,0:T(8,128)(2,1)S(1)}, u32[]{:S(2)}, u32[]{:S(2)}) collective-permute-start(bf16[2,768,256]{2,1,0:T(8,128)(2,1)S(1)} %slice.74), channel_id=1, source_target_pairs={{0,4},{4,0},{8,12},{12,8},{16,20},{20,16},{24,28},{28,24},{1,5},{5... | collective-permute-start | bytes 2359304 | tf_op jit(solution)/shard_map/ppermute | solution.py:827
  410.6 12.3 %collective-permute-start.10 = (bf16[2,768,128]{2,1,0:T(8,128)(2,1)S(1)}, bf16[2,768,128]{2,1,0:T(8,128)(2,1)S(1)}, u32[]{:S(2)}, u32[]{:S(2)}) collective-permute-start(bf16[2,768,128]{2,1,0:T(8,128)(2,1)S(1)} %slice.94), channel_id=1, source_target_pairs={{0,4},{4,0},{8,12},{12,8},{16,20},{20,16},{24,28},{28,24},{1,5},{5... | collective-permute-start | bytes 1179656 | tf_op jit(solution)/shard_map/ppermute | solution.py:827
  412.3 157.9 %collective-permute-start.6 = (bf16[2,768,512]{2,1,0:T(8,128)(2,1)}, bf16[2,768,512]{2,1,0:T(8,128)(2,1)}, u32[]{:S(2)}, u32[]{:S(2)}) collective-permute-start(bf16[2,768,512]{2,1,0:T(8,128)(2,1)} %get-tuple-element.52), channel_id=1, source_target_pairs={{0,4},{4,0},{8,12},{12,8},{16,20},{20,16},{24,28},{28,24},{1,5},{5... | collective-permute-start | bytes 4718600 | tf_op jit(solution)/shard_map/ppermute | solution.py:827
  415.5 154.8 %collective-permute-start.8 = (bf16[2,768,256]{2,1,0:T(8,128)(2,1)}, bf16[2,768,256]{2,1,0:T(8,128)(2,1)}, u32[]{:S(2)}, u32[]{:S(2)}) collective-permute-start(bf16[2,768,256]{2,1,0:T(8,128)(2,1)} %add_convert_fusion.1), channel_id=1, source_target_pairs={{0,8},{4,12},{8,0},{12,4},{16,24},{20,28},{24,16},{28,20},{1,9},{5... | collective-permute-start | bytes 2359304 | tf_op jit(solution)/shard_map/ppermute | solution.py:827
  423.7 146.6 %collective-permute-start.11 = (bf16[2,768,128]{2,1,0:T(8,128)(2,1)}, bf16[2,768,128]{2,1,0:T(8,128)(2,1)}, u32[]{:S(2)}, u32[]{:S(2)}) collective-permute-start(bf16[2,768,128]{2,1,0:T(8,128)(2,1)} %add_convert_fusion.2), channel_id=1, source_target_pairs={{0,16},{4,20},{8,24},{12,28},{16,0},{20,4},{24,8},{28,12},{1,17},{... | collective-permute-start | bytes 1179656 | tf_op jit(solution)/shard_map/ppermute | solution.py:827
  618.0 0.8 copy-start.5
  618.0 0.8 copy-start.6
  618.0 161.3 %all-reduce.4.cloned.1.call-start = ((), (), s32[]{:S(2)}) async-start(), calls=%async_computation.8 | async-start | bytes 5308416 | tf_op jit(solution)/shard_map/psum | solution.py:896
  618.8 239.3 %all-reduce.6.cloned.1.call-start = ((), (), s32[]{:S(2)}) async-start(), calls=%async_computation.9 | async-start | bytes 1769472 | tf_op jit(solution)/shard_map/psum | solution.py:906
Sparse Core Ops, SparseCore 0:
  9.6 33.4 all-gather.5
  44.7 17.4 all-gather.7
  63.7 37.4 all-gather.9
  102.6 37.4 all-gather.11
  355.3 83.6 reduce-scatter.4
  618.1 40.8 reduce-scatter.2
  663.1 116.1 all-reduce.3
  783.2 74.8 all-reduce.5

commit v3 on v2

--- a/solution.py
+++ b/solution.py
@@ -97,17 +97,14 @@
     return position < count
 
 
-def remote_keep(head, level, nseg, mine, limit, length):
+def packed_keep(count, level, nseg):
     size = SEG >> level
-    group = (SEG << (level - 1)) // (nseg * SEG)
-    lane = lax.broadcasted_iota(jnp.int32, (1, length), 1)
-    owner = mine ^ (group + lane // (nseg * size))
-    inside = lax.rem(lane, nseg * size)
-    rho = (reversed_bits(head) >> (4 - level)) * (size // RUN) + lax.rem(inside, size) // RUN
-    position = (
-        owner * (nseg * SEG) + inside // size * SEG + lax.rem(inside, RUN) * RES + residue_of(rho)
-    )
-    return position < limit
+    dims = (HEADS, nseg * size)
+    head = lax.broadcasted_iota(jnp.int32, dims, 0)
+    lane = lax.broadcasted_iota(jnp.int32, dims, 1)
+    rho = (reversed_bits(head) >> (4 - level)) * (size // RUN) + lax.rem(lane, size) // RUN
+    position = lane // size * SEG + lax.rem(lane, RUN) * RES + residue_of(rho)
+    return jnp.where(position < count, 1.0, 0.0).astype(BF16)
 
 
 def weight_of(level, step):
@@ -146,6 +143,269 @@
     return pl.multiple_of(seg * SEG + block * size, min(size, 128))
 
 
+def partner(axis, distance):
+    place = lax.axis_index(axis)
+    return {axis: place + distance * (1 - 2 * lax.rem(lax.div(place, distance), 2))}
+
+
+def seq_bits():
+    return lax.axis_size("seq").bit_length() - 1
+
+
+def meet(peers):
+    barrier = pltpu.get_barrier_semaphore()
+    for axis, distance in peers:
+        pl.semaphore_signal(
+            barrier, inc=1, device_id=partner(axis, distance), device_id_type=pl.DeviceIdType.MESH
+        )
+    pl.semaphore_wait(barrier, len(peers))
+
+
+class Sends:
+    def __init__(self, send_sems, recv_sems):
+        self.send_sems, self.recv_sems, self.made = send_sems, recv_sems, {}
+
+    def copy(self, key, source, target, axis, distance):
+        index = self.made.setdefault(key, len(self.made))
+        return pltpu.make_async_remote_copy(
+            src_ref=source,
+            dst_ref=target,
+            send_sem=self.send_sems.at[index],
+            recv_sem=self.recv_sems.at[index],
+            device_id=partner(axis, distance),
+            device_id_type=pl.DeviceIdType.MESH,
+        )
+
+
+class Gather:
+    def __init__(self, nseg, first, packs, gathered, sends):
+        self.hops, self.distances = [], set()
+        for level, pack, into in zip(range(first, BRANCHES), packs, gathered):
+            group = (SEG << (level - 1)) // (nseg * SEG)
+            hops = [((level, 0), pack, into.at[0], group)]
+            step = 1
+            while step < group:
+                hops.append(((level, step), into.at[pl.ds(0, step)], into.at[pl.ds(step, step)], step))
+                step *= 2
+            self.hops.append([sends.copy(k, a, b, "seq", d) for k, a, b, d in hops])
+            self.distances |= {hop[3] for hop in hops}
+
+    def peers(self):
+        return [("seq", distance) for distance in sorted(self.distances)]
+
+    def start(self):
+        for hops in self.hops:
+            hops[0].start()
+
+    def pass_on(self, turn):
+        for hops in self.hops:
+            if turn < len(hops):
+                hops[turn - 1].wait_recv()
+                hops[turn].start()
+
+    def finish(self):
+        for hops in self.hops:
+            for hop in hops:
+                hop.wait_send()
+            hops[-1].wait_recv()
+
+    def turns(self):
+        return max(len(hops) for hops in self.hops)
+
+
+class Return:
+    def __init__(self, nseg, first, sent, returned, bufs, recvs, local_sems, sends):
+        self.plans = []
+        for i, level in enumerate(range(first, BRANCHES)):
+            group = (SEG << (level - 1)) // (nseg * SEG)
+            plan = []
+            if group == 1:
+                plan.append((None, sends.copy((level, 0), sent[i].at[0], returned[i], "seq", group)))
+                self.plans.append((plan, None))
+                continue
+            buf, recv = bufs.pop(0), recvs.pop(0)
+            step = group // 2
+            load = pltpu.make_async_copy(sent[i].at[pl.ds(0, step)], buf, local_sems.at[i])
+            source, at, add = sent[i].at[pl.ds(step, step)], 0, None
+            while step >= 1:
+                into = recv.at[pl.ds(at, step)]
+                plan.append((add, sends.copy((level, step), source, into, "seq", step)))
+                add = (buf, recv, at, step)
+                at += step
+                step //= 2
+                if step:
+                    source = buf.at[pl.ds(step, step)]
+            plan.append((add, sends.copy((level, 0), buf.at[0], returned[i], "seq", group)))
+            self.plans.append((plan, load))
+
+    def start(self):
+        for plan, load in self.plans:
+            if load is not None:
+                load.start()
+            plan[0][1].start()
+
+    def turn(self, number):
+        for plan, load in self.plans:
+            if number < len(plan):
+                plan[number - 1][1].wait_recv()
+                if number == 1 and load is not None:
+                    load.wait()
+                buf, recv, at, step = plan[number][0]
+                for i in range(step):
+                    buf[i] = (buf[i].astype(F32) + recv[at + i].astype(F32)).astype(BF16)
+                plan[number][1].start()
+
+    def finish(self):
+        for plan, load in self.plans:
+            for _, copy in plan:
+                copy.wait_send()
+            plan[-1][1].wait_recv()
+
+    def turns(self):
+        return max(len(plan) for plan, _ in self.plans)
+
+
+def add_blocks(into, at, other, start, count):
+    unit = max(u for u in range(1, 13) if count % u == 0)
+
+    def body(i, carry):
+        rows = pl.ds(at + i * unit, unit)
+        part = other[pl.ds(start + i * unit, unit)].astype(F32)
+        into[rows] = (into[rows].astype(F32) + part).astype(BF16)
+        return carry
+
+    lax.fori_loop(0, count // unit, body, 0)
+
+
+def copy_blocks(into, other, at, count):
+    unit = max(u for u in range(1, 13) if count % u == 0)
+
+    def body(i, carry):
+        rows = pl.ds(at + i * unit, unit)
+        into[rows] = other[rows]
+        return carry
+
+    lax.fori_loop(0, count // unit, body, 0)
+
+
+class Reduce:
+    def __init__(self, chunks, blocks, source, terms, own, recv_core, recv_x, recv_seq, total, sends, loads=None):
+        self.chunks, self.blocks, self.source, self.terms, self.own = chunks, blocks, source, terms, own
+        self.recv_core, self.recv_x, self.recv_seq, self.total = recv_core, recv_x, recv_seq, total
+        self.sends, self.loads = sends, loads
+        fsdp = lax.axis_index("fsdp")
+        self.core, self.x = lax.rem(fsdp, 2), lax.div(fsdp, 2)
+        self.bits = seq_bits()
+        seq = lax.axis_index("seq")
+        self.low = [0]
+        self.given = []
+        for j in range(self.bits):
+            bit = lax.rem(lax.div(seq, 2**j), 2)
+            half = blocks >> (j + 1)
+            self.given.append(self.low[j] + (1 - bit) * half)
+            self.low.append(self.low[j] + bit * half)
+
+    def peers(self):
+        return [("fsdp", 1), ("fsdp", 2)] + [("seq", 2**j) for j in range(self.bits)]
+
+    def stages(self):
+        return 2 + 2 * self.bits
+
+    def core_copy(self, chunk, xo):
+        rows = pl.ds(chunk * self.blocks, self.blocks)
+        owner = 2 * xo + 1 - self.core
+        return self.sends.copy(
+            ("core", chunk, xo), self.source.at[owner, rows], self.recv_core.at[xo, rows], "fsdp", 1
+        )
+
+    def load_copy(self, chunk, xo):
+        rows = pl.ds(chunk * self.blocks, self.blocks)
+        return pltpu.make_async_copy(
+            self.source.at[2 * xo + self.core, rows], self.terms.at[xo, rows], self.loads.at[2 * chunk + xo]
+        )
+
+    def x_copy(self, chunk):
+        rows = pl.ds(chunk * self.blocks, self.blocks)
+        return self.sends.copy(
+            ("x", chunk), self.terms.at[self.own(1 - self.x), rows], self.recv_x.at[rows], "fsdp", 2
+        )
+
+    def down_copy(self, chunk, j):
+        half = self.blocks >> (j + 1)
+        base = chunk * self.blocks
+        rows = pl.ds(base + self.given[j], half)
+        into = pl.ds(base + self.blocks - (self.blocks >> j), half)
+        return self.sends.copy(
+            ("down", chunk, j), self.terms.at[self.own(self.x), rows], self.recv_seq.at[into], "seq", 2**j
+        )
+
+    def up_copy(self, chunk, j):
+        rows = pl.ds(chunk * self.blocks + self.low[j + 1], self.blocks >> (j + 1))
+        return self.sends.copy(("up", chunk, j), self.total.at[rows], self.total.at[rows], "seq", 2**j)
+
+    def begin(self, chunk):
+        for xo in range(2):
+            if self.loads is not None:
+                self.load_copy(chunk, xo).start()
+            self.core_copy(chunk, xo).start()
+
+    def event(self, stage, chunk):
+        base = chunk * self.blocks
+        if stage == 0:
+            for xo in range(2):
+                self.core_copy(chunk, xo).wait_recv()
+                if self.loads is not None:
+                    self.load_copy(chunk, xo).wait()
+                add_blocks(self.terms.at[self.own(xo)], base, self.recv_core.at[xo], base, self.blocks)
+            self.x_copy(chunk).start()
+        elif stage < 2 + self.bits:
+            j = stage - 2
+            mine = self.terms.at[self.own(self.x)]
+            if stage == 1:
+                self.x_copy(chunk).wait_recv()
+                add_blocks(mine, base, self.recv_x, base, self.blocks)
+            else:
+                self.down_copy(chunk, j).wait_recv()
+                half = self.blocks >> (j + 1)
+                add_blocks(
+                    mine, base + self.low[j + 1], self.recv_seq, base + self.blocks - (self.blocks >> j), half
+                )
+            if j + 1 < self.bits:
+                self.down_copy(chunk, j + 1).start()
+            else:
+                copy_blocks(self.total, mine, base + self.low[self.bits], self.blocks >> self.bits)
+                self.up_copy(chunk, self.bits - 1).start()
+        else:
+            j = 2 * self.bits + 1 - stage
+            self.up_copy(chunk, j).wait_recv()
+            if j:
+                self.up_copy(chunk, j - 1).start()
+
+    def finish(self):
+        for chunk in range(self.chunks):
+            for xo in range(2):
+                self.core_copy(chunk, xo).wait_send()
+            self.x_copy(chunk).wait_send()
+            for j in range(self.bits):
+                self.down_copy(chunk, j).wait_send()
+                self.up_copy(chunk, j).wait_send()
+
+    def copies(self):
+        return self.chunks * (3 + 2 * self.bits)
+
+
+def run_schedule(step, last, events):
+    due = {}
+    for when, call in events:
+        due.setdefault(min(when, last), []).append(call)
+    for when in sorted(due):
+
+        @pl.when(step == when)
+        def _():
+            for call in due[when]:
+                call()
+
+
 def attend_tiles(query, key, value, tile, acc, top):
     key_t = key.T
     for start in range(0, key.shape[1], tile):
@@ -159,9 +419,23 @@
     return acc, top
 
 
-def local_forward(nseg, mask_ref, q_ref, k_ref, v_ref, o_ref, l_ref, m_ref, qa, ka, va):
+def local_forward(nseg, first, mask_ref, q_ref, k_ref, v_ref, *refs):
+    n = BRANCHES - first
+    packs, (o_ref, l_ref, m_ref), gathered = refs[:n], refs[n : n + 3], refs[n + 3 : 2 * n + 3]
+    qa, ka, va, send_sems, recv_sems = refs[2 * n + 3 :]
     head = pl.program_id(0)
     length = nseg * SEG
+    gather = Gather(nseg, first, packs, gathered, Sends(send_sems, recv_sems))
+
+    def begin():
+        meet(gather.peers())
+        gather.start()
+
+    events = [(0, begin)]
+    for turn in range(1, gather.turns()):
+        events.append((2 + 4 * turn, functools.partial(gather.pass_on, turn)))
+    run_schedule(head, HEADS - 1, events)
+
     keep = local_keep(mask_ref[0], length)
     qa[...] = join(q_ref[0], query_rows(head, length))
     va[...] = join(v_ref[0], value_rows(length))
@@ -180,6 +454,8 @@
             other = pl.ds(kept_start(head, 1, 1 - seg), SEG // 2)
             merge_level(qa[:, mine], ka[1, :, other], va[:, other], mine, o_ref, l_ref, m_ref)
 
+    run_schedule(head, HEADS - 1, [(HEADS - 1, gather.finish)])
+
 
 def merge_level(query, key, value, mine, o_ref, l_ref, m_ref):
     acc = jnp.concatenate([o_ref[:, mine], jnp.broadcast_to(l_ref[0, :, mine], (16, query.shape[1]))])
@@ -189,12 +465,16 @@
     m_ref[0, :, mine] = top
 
 
-def remote_keys(head, level, pack, nseg, mask_ref):
-    k_ref, v_ref = pack
-    length = k_ref.shape[1]
-    keep = remote_keep(head, level, nseg, mask_ref[1], mask_ref[2], length)
-    key = join(k_ref[...], key_rows(head, level, 4 - level, length, keep))
-    return key, join(v_ref[...], value_rows(length))
+def remote_keys(head, level, pack):
+    k_ref, v_ref, mask_ref = pack
+    pieces = range(k_ref.shape[0])
+    key, value, mask = (
+        jnp.concatenate([ref[i] for i in pieces], axis=1) for ref in (k_ref, v_ref, mask_ref)
+    )
+    length = key.shape[1]
+    row = lax.broadcasted_iota(jnp.int32, (16, length), 0)
+    keep = jnp.sum(jnp.where(row == head, mask.astype(F32), 0.0), axis=0, keepdims=True) > 0.5
+    return join(key, key_rows(head, level, 4 - level, length, keep)), join(value, value_rows(length))
 
 
 def remote_plan(first):
@@ -204,15 +484,15 @@
 def remote_forward(nseg, first, mask_ref, q_ref, o_in, l_in, m_in, *refs):
     head = pl.program_id(0)
     levels = range(first, BRANCHES)
-    packs = {level: refs[2 * i : 2 * i + 2] for i, level in enumerate(levels)}
-    att_ref, lse_ref, o_ref, l_ref, m_ref, qa = refs[2 * len(levels) :]
+    packs = {level: refs[3 * i : 3 * i + 3] for i, level in enumerate(levels)}
+    att_ref, lse_ref, o_ref, l_ref, m_ref, qa = refs[3 * len(levels) :]
     length = nseg * SEG
     qa[...] = join(q_ref[0], query_rows(head, length))
     o_ref[...] = o_in[...]
     l_ref[...] = l_in[...]
     m_ref[...] = m_in[...]
     for group in remote_plan(first):
-        pairs = [remote_keys(head, level, packs[level], nseg, mask_ref) for level in group]
+        pairs = [remote_keys(head, level, packs[level]) for level in group]
         key = jnp.concatenate([pair[0] for pair in pairs], axis=1)
         value = jnp.concatenate([pair[1] for pair in pairs], axis=1)
         for seg in range(nseg):
@@ -275,9 +555,42 @@
     return jnp.where(keep, -lse, NEG)
 
 
-def local_backward(nseg, first, mask_ref, q_ref, k_ref, v_ref, g_ref, lse_ref, slope_ref, dqr_ref, out_ref, qa, ga, ka, va, dk, dv):
+def local_backward(nseg, first, mask_ref, q_ref, k_ref, v_ref, g_ref, lse_ref, slope_ref, dqr_ref, *refs):
+    n = BRANCHES - first
+    sent, feed_ref, out_ref = refs[:n], refs[n], refs[n + 1]
+    returned, (up_ref, proj_ref, down_ref) = refs[n + 2 : 2 * n + 2], refs[2 * n + 2 : 2 * n + 5]
+    qa, ga, ka, va, dk, dv = refs[2 * n + 5 : 2 * n + 11]
+    rest = list(refs[2 * n + 11 :])
+    back_send, back_recv, back_load, red_send, red_recv, red_load = rest[-6:]
+    terms, recv_core, recv_x, recv_seq, total = rest[-11:-6]
+    bufs, recvs = rest[: (len(rest) - 11) // 2], rest[(len(rest) - 11) // 2 : -11]
     head = pl.program_id(0)
+    last = HEADS - 1
     length = nseg * SEG
+
+    back = Return(nseg, first, sent, returned, bufs, recvs, back_load, Sends(back_send, back_recv))
+    blocks = terms.shape[1] // CHUNKS
+    reduce = Reduce(
+        CHUNKS, blocks, feed_ref, terms, lambda xo: xo, recv_core, recv_x, recv_seq, total,
+        Sends(red_send, red_recv), red_load,
+    )
+
+    def begin():
+        meet(reduce.peers())
+        back.start()
+        for chunk in range(CHUNKS):
+            reduce.begin(chunk)
+
+    events = [(2 * turn, functools.partial(back.turn, turn)) for turn in range(1, back.turns())]
+    for chunk in range(CHUNKS):
+        for stage in range(reduce.stages()):
+            if stage == 0:
+                when = 1 + (chunk + 1) // 2
+            else:
+                when = 3 + 2 * chunk + stage + (stage >= 2) + (stage == reduce.stages() - 1)
+            events.append((when, functools.partial(reduce.event, stage, chunk)))
+    run_schedule(head, last, [(0, begin)] + sorted(events, key=lambda event: event[0]))
+
     keep = local_keep(mask_ref[0], length)
     qa[...] = join(q_ref[0], query_rows(head, length, neg_total(lse_ref[0], keep)))
     ga[...] = grad_rows(g_ref[...], slope_ref[0])
@@ -304,22 +617,38 @@
     out_ref[1] = dk[...] * DK_SCALE
     out_ref[2] = dv[...]
 
+    @pl.when(head == last)
+    def _():
+        back.finish()
+        reduce.finish()
+        for tile in range(TILES):
+            cols = slice(tile * 128, (tile + 1) * 128)
+            for col in range(4):
+                at = col * 72 + tile * 12
+                up_ref[:, col * D + tile * 128 : col * D + (tile + 1) * 128] = rows_of(total, at, 12)
+            proj_ref[:, cols] = rows_of(total, 288 + tile * 12, 12)
+            down_ref[:, cols] = rows_of(total, 360 + tile * 48, 48)
+
+
+def rows_of(total, at, count):
+    return total[at : at + count].astype(F32).reshape(count * 16, 128)
+
 
 def remote_backward(nseg, first, mask_ref, q_ref, g_ref, lse_ref, slope_ref, *refs):
     head = pl.program_id(0)
     levels = range(first, BRANCHES)
     n = len(levels)
-    packs = {level: refs[2 * i : 2 * i + 2] for i, level in enumerate(levels)}
-    dqr_ref = refs[2 * n]
-    outs = {level: refs[2 * n + 1 + i] for i, level in enumerate(levels)}
-    qa, ga, ka, va, dk, dv = refs[3 * n + 1 :]
+    packs = {level: refs[3 * i : 3 * i + 3] for i, level in enumerate(levels)}
+    dqr_ref = refs[3 * n]
+    outs = {level: refs[3 * n + 1 + i] for i, level in enumerate(levels)}
+    qa, ga, ka, va, dk, dv = refs[4 * n + 1 :]
     length = nseg * SEG
     qa[...] = join(q_ref[0], query_rows(head, length, neg_total(lse_ref[0], local_keep(mask_ref[0], length))))
     ga[...] = grad_rows(g_ref[...], slope_ref[0])
     full = SEG >> first
     for group in remote_plan(first):
         for i, level in enumerate(group):
-            key, value = remote_keys(head, level, packs[level], nseg, mask_ref)
+            key, value = remote_keys(head, level, packs[level])
             ka[:, i * 512 : (i + 1) * 512] = key
             va[:, i * 512 : (i + 1) * 512] = value
         size = SEG >> group[0]
@@ -337,9 +666,11 @@
                 lanes = pl.ds(pl.multiple_of(seg * full + inner * size, 128), size)
                 dqr_ref[:, lanes] += piece
         for i, level in enumerate(group):
-            lanes = slice(i * 512, (i + 1) * 512)
-            outs[level][0] = (dk[:, lanes] * DK_SCALE).astype(BF16)
-            outs[level][1] = dv[:, lanes].astype(BF16)
+            pieces, _, _, size = outs[level].shape
+            for piece in range(pieces):
+                lanes = slice(i * 512 + piece * size, i * 512 + (piece + 1) * size)
+                outs[level][piece, 0] = (dk[:, lanes] * DK_SCALE).astype(BF16)
+                outs[level][piece, 1] = dv[:, lanes].astype(BF16)
 
 
 def row_block(length):
@@ -357,11 +688,26 @@
 MASK_BLOCK = pl.BlockSpec(memory_space=pltpu.SMEM)
 
 
-def pack_specs(length):
+def pack_specs(pack):
+    group, _, length = pack.shape
     return [
-        pl.BlockSpec((HEAD_DIM, length), lambda h: (h, 0)),
-        pl.BlockSpec((HEAD_DIM, length), lambda h: (HEADS + h, 0)),
+        pl.BlockSpec((group, HEAD_DIM, length), lambda h: (0, h, 0)),
+        pl.BlockSpec((group, HEAD_DIM, length), lambda h: (0, HEADS + h, 0)),
+        pl.BlockSpec((group, 16, length), lambda h: (0, 2 * D // 16, 0)),
     ]
+
+
+ANY_BLOCK = pl.BlockSpec(memory_space=pl.ANY)
+
+
+def sems(count):
+    return pltpu.SemaphoreType.DMA((count,))
+
+
+def talking(collective_id):
+    return pltpu.CompilerParams(
+        vmem_limit_bytes=VMEM_LIMIT, collective_id=collective_id, has_side_effects=True
+    )
 
 
 PARAMS = pltpu.CompilerParams(vmem_limit_bytes=VMEM_LIMIT)
@@ -375,31 +721,39 @@
     return pl.CostEstimate(flops=int(seconds * 1.1e15), transcendentals=0, bytes_accessed=0)
 
 
-def call_local_forward(nseg, qkv, mask):
+def call_local_forward(nseg, first, qkv, mask, packs):
     length = nseg * SEG
-    return pl.pallas_call(
-        functools.partial(local_forward, nseg),
+    n = len(packs)
+    groups = [(SEG << (level - 1)) // length for level in range(first, BRANCHES)]
+    hops = sum(group.bit_length() for group in groups)
+    o_part, l_part, m_part, *gathered = pl.pallas_call(
+        functools.partial(local_forward, nseg, first),
         grid=(HEADS,),
-        in_specs=[MASK_BLOCK, part_block(0, length), part_block(1, length), part_block(2, length)],
-        out_specs=[head_block(length), row_block(length), row_block(length)],
-        out_shape=[shape((D, length), F32), shape((HEADS, 1, length), F32), shape((HEADS, 1, length), F32)],
+        in_specs=[MASK_BLOCK, part_block(0, length), part_block(1, length), part_block(2, length)]
+        + [ANY_BLOCK] * n,
+        out_specs=[head_block(length), row_block(length), row_block(length)] + [ANY_BLOCK] * n,
+        out_shape=[shape((D, length), F32), shape((HEADS, 1, length), F32), shape((HEADS, 1, length), F32)]
+        + [shape((group,) + pack.shape, BF16) for group, pack in zip(groups, packs)],
         scratch_shapes=[
             pltpu.VMEM((64, length), BF16),
             pltpu.VMEM((nseg, 64, length), BF16),
             pltpu.VMEM((64, length), BF16),
+            sems(hops),
+            sems(hops),
         ],
-        compiler_params=PARAMS,
+        compiler_params=talking(1),
         cost_estimate=cost(nseg * 37e-6),
         name="local_forward",
-    )(mask, qkv, qkv, qkv)
+    )(mask, qkv, qkv, qkv, *packs)
+    return o_part, l_part, m_part, gathered
 
 
 def call_remote_forward(nseg, first, qkv, mask, o_part, l_part, m_part, packs):
     length = nseg * SEG
     args, specs = [], []
     for pack in packs:
-        args += [pack] * 2
-        specs += pack_specs(pack.shape[1])
+        args += [pack] * 3
+        specs += pack_specs(pack)
     return pl.pallas_call(
         functools.partial(remote_forward, nseg, first),
         grid=(HEADS,),
@@ -423,8 +777,8 @@
     length = nseg * SEG
     args, specs = [], []
     for pack in packs:
-        args += [pack] * 2
-        specs += pack_specs(pack.shape[1])
+        args += [pack] * 3
+        specs += pack_specs(pack)
     kept = nseg * (SEG >> first)
     return pl.pallas_call(
         functools.partial(remote_backward, nseg, first),
@@ -432,8 +786,12 @@
         in_specs=[MASK_BLOCK, part_block(0, length), head_block(length), row_block(length), row_block(length)]
         + specs,
         out_specs=[head_block(kept)]
-        + [pl.BlockSpec((2, HEAD_DIM, pack.shape[1]), lambda h: (0, h, 0)) for pack in packs],
-        out_shape=[shape((D, kept), F32)] + [shape((2, D, pack.shape[1]), BF16) for pack in packs],
+        + [
+            pl.BlockSpec((pack.shape[0], 2, HEAD_DIM, pack.shape[2]), lambda h: (0, 0, h, 0))
+            for pack in packs
+        ],
+        out_shape=[shape((D, kept), F32)]
+        + [shape((pack.shape[0], 2, D, pack.shape[2]), BF16) for pack in packs],
         scratch_shapes=[
             pltpu.VMEM((64, length), BF16),
             pltpu.VMEM((64, length), BF16),
@@ -448,15 +806,40 @@
     )(mask, qkv, grad, lse, slope, *args)
 
 
-def call_local_backward(nseg, first, qkv, grad, lse, slope, mask, dq_remote):
+CHUNKS = 3
+FEED_BLOCKS = (4 * D + D + 4 * D) * D // (4 * 16 * 128)
+IN_BLOCKS = 3 * D * D // (4 * 16 * 128)
+
+
+def padded(blocks):
+    unit = CHUNKS * lax.axis_size("seq")
+    return (blocks + unit - 1) // unit * unit
+
+
+def reduce_copies():
+    return CHUNKS * (3 + 2 * seq_bits())
+
+
+def call_local_backward(nseg, first, qkv, grad, lse, slope, mask, dq_remote, sent, feed_grads):
     length = nseg * SEG
-    return pl.pallas_call(
+    n = len(sent)
+    groups = [part.shape[0] for part in sent]
+    hops = sum(group.bit_length() for group in groups)
+    blocks = feed_grads.shape[1]
+    bufs = [pltpu.VMEM((g // 2,) + part.shape[1:], BF16) for g, part in zip(groups, sent) if g > 1]
+    recvs = [pltpu.VMEM((g - 1,) + part.shape[1:], BF16) for g, part in zip(groups, sent) if g > 1]
+    local, *rest = pl.pallas_call(
         functools.partial(local_backward, nseg, first),
         grid=(HEADS,),
         in_specs=[MASK_BLOCK, part_block(0, length), part_block(1, length), part_block(2, length), head_block(length),
-                  row_block(length), row_block(length), head_block(dq_remote.shape[1])],
-        out_specs=pl.BlockSpec((3, HEAD_DIM, length), lambda h: (0, h, 0)),
-        out_shape=shape((3, D, length), F32),
+                  row_block(length), row_block(length), head_block(dq_remote.shape[1])]
+        + [ANY_BLOCK] * (n + 1),
+        out_specs=[pl.BlockSpec((3, HEAD_DIM, length), lambda h: (0, h, 0))]
+        + [ANY_BLOCK] * n
+        + [const_block((192, 4 * D)), const_block((192, D)), const_block((D, D))],
+        out_shape=[shape((3, D, length), F32)]
+        + [shape(part.shape[1:], BF16) for part in sent]
+        + [shape((192, 4 * D), F32), shape((192, D), F32), shape((D, D), F32)],
         scratch_shapes=[
             pltpu.VMEM((64, length), BF16),
             pltpu.VMEM((64, length), BF16),
@@ -464,11 +847,27 @@
             pltpu.VMEM((64, length), BF16),
             pltpu.VMEM((HEAD_DIM, length), F32),
             pltpu.VMEM((HEAD_DIM, length), F32),
+        ]
+        + bufs
+        + recvs
+        + [
+            pltpu.VMEM((2, blocks, 16, 128), BF16),
+            pltpu.VMEM((2, blocks, 16, 128), BF16),
+            pltpu.VMEM((blocks, 16, 128), BF16),
+            pltpu.VMEM((blocks, 16, 128), BF16),
+            pltpu.VMEM((blocks, 16, 128), BF16),
+            sems(hops),
+            sems(hops),
+            sems(n),
+            sems(reduce_copies()),
+            sems(reduce_copies()),
+            sems(2 * CHUNKS),
         ],
-        compiler_params=PARAMS,
+        compiler_params=talking(2),
         cost_estimate=cost(nseg * 72e-6),
         name="local_backward",
-    )(mask, qkv, qkv, qkv, grad, lse, slope, dq_remote)
+    )(mask, qkv, qkv, qkv, grad, lse, slope, dq_remote, *sent, feed_grads)
+    return local, rest[:n], rest[n:]
 
 
 HALF = D // 2
@@ -505,7 +904,7 @@
         tiled[tile, pl.ds(start, RUN, stride=RES), :] = array[:, tile * 128 : (tile + 1) * 128]
 
 
-def project_kernel(nseg, first, tok_ref, gain_ref, shift_ref, w_ref, qkv_ref, xp_ref, inner_ref, *refs):
+def project_kernel(nseg, first, mask_ref, tok_ref, gain_ref, shift_ref, w_ref, qkv_ref, xp_ref, inner_ref, *refs):
     *packs, xs = refs
     step = pl.program_id(0)
 
@@ -521,6 +920,8 @@
                 at = slice(seg * SEG + pair * 2 * RUN, seg * SEG + (pair + 1) * 2 * RUN)
                 xp_ref[at, :] = rows.astype(BF16)
                 inner_ref[:, at] = normed.T
+        for pack, level in zip(packs, range(first, BRANCHES)):
+            pack[2 * D :, :] = packed_keep(mask_ref[0], level, nseg)
 
     scale = jnp.where(step < 2, QUERY_SCALE, 1.0)
     for start in range(0, nseg * SEG, 512):
@@ -542,16 +943,18 @@
                     else:
                         both = qkv_ref[0, rows, start : start + 2 * size]
                         pieces.append(jnp.where(upper, both[:, size:], both[:, :size]))
-                pack[rows, :] = jnp.concatenate(pieces, axis=1) if nseg > 1 else pieces[0]
-
-
-def call_project(nseg, first, tokens, gain, shift, weight):
+                into = pl.ds(pl.multiple_of((step - 2) * HALF + head * HEAD_DIM, 16), HEAD_DIM)
+                pack[into, :] = jnp.concatenate(pieces, axis=1) if nseg > 1 else pieces[0]
+
+
+def call_project(nseg, first, mask, tokens, gain, shift, weight):
     length = nseg * SEG
     kept = [nseg * (SEG >> level) for level in range(first, BRANCHES)]
     return pl.pallas_call(
         functools.partial(project_kernel, nseg, first),
         grid=(6,),
         in_specs=[
+            MASK_BLOCK,
             const_block((length, D)),
             const_block((1, D)),
             const_block((1, D)),
@@ -562,23 +965,26 @@
             const_block((length, D)),
             const_block((D, length)),
         ]
-        + [pl.BlockSpec((HALF, size), lambda i: (jnp.maximum(i - 2, 0), 0)) for size in kept],
+        + [const_block((2 * D + 16, size)) for size in kept],
         out_shape=[
             shape((3, D, length), BF16),
             shape((length, D), BF16),
             shape((D, length), BF16),
         ]
-        + [shape((2 * D, size), BF16) for size in kept],
+        + [shape((2 * D + 16, size), BF16) for size in kept],
         scratch_shapes=[pltpu.VMEM((TILES, SEG, 128), F32)],
         compiler_params=PARAMS,
         cost_estimate=cost(nseg * 10e-6),
         name="project",
-    )(tokens, gain, shift, weight)
+    )(mask, tokens, gain, shift, weight)
 
 
 ROWS = 256
-UP_ROWS = 4 * 192
-STACK = UP_ROWS + 192 + D
+
+
+def blocks_of(ref, rows, col):
+    part = ref[rows, col * 128 : (col + 1) * 128].astype(BF16)
+    return part.reshape(part.shape[0] // 16, 16, 128)
 
 
 def feed_kernel(
@@ -657,21 +1063,20 @@
                 if count >= 2:
                     copies[count - 2].wait()
                 if piece == 0:
-                    rows = slice(owner * 192, (owner + 1) * 192)
-                    for col in range(4):
-                        stage[slot, col * 192 : (col + 1) * 192, :] = up_acc[
-                            rows, col * D : (col + 1) * D
-                        ].astype(BF16)
-                    offset, size = 0, UP_ROWS
+                    rows, offset, size = slice(owner * 192, (owner + 1) * 192), 0, 288
+                    for col in range(4 * TILES):
+                        stage[slot, col * 12 : (col + 1) * 12] = blocks_of(up_acc, rows, col)
                 elif piece == 1:
-                    stage[slot, :192, :] = out_acc[owner * 192 : (owner + 1) * 192, :].astype(BF16)
-                    offset, size = UP_ROWS, 192
+                    rows, offset, size = slice(owner * 192, (owner + 1) * 192), 288, 72
+                    for col in range(TILES):
+                        stage[slot, col * 12 : (col + 1) * 12] = blocks_of(out_acc, rows, col)
                 else:
-                    stage[slot, :D, :] = down_acc[owner * D : (owner + 1) * D, :].astype(BF16)
-                    offset, size = UP_ROWS + 192, D
+                    rows, offset, size = slice(owner * D, (owner + 1) * D), 360, 288
+                    for col in range(TILES):
+                        stage[slot, col * 48 : (col + 1) * 48] = blocks_of(down_acc, rows, col)
                 copy = pltpu.make_async_copy(
-                    stage.at[slot, pl.ds(0, size), :],
-                    grads_ref.at[owner, pl.ds(offset, size), :],
+                    stage.at[slot, pl.ds(0, size)],
+                    grads_ref.at[owner, pl.ds(offset, size)],
                     sems.at[slot],
                 )
                 copy.start()
@@ -710,14 +1115,14 @@
             shape((D, length), BF16),
             shape((HEADS, 1, length), F32),
             shape((2, D), F32),
-            shape((4, STACK, D), BF16),
+            shape((4, padded(FEED_BLOCKS), 16, 128), BF16),
         ],
         scratch_shapes=[
             pltpu.VMEM((TILES, SEG, 128), F32),
             pltpu.VMEM((D, D), F32),
             pltpu.VMEM((D, 4 * D), F32),
             pltpu.VMEM((4 * D, D), F32),
-            pltpu.VMEM((2, D, D), BF16),
+            pltpu.VMEM((2, 288, 16, 128), BF16),
             pltpu.SemaphoreType.DMA((2,)),
         ],
         compiler_params=pltpu.CompilerParams(vmem_limit_bytes=62 * 1024 * 1024),
@@ -726,17 +1131,48 @@
     )(mask, att, x, cot, wout, up, down, gain, shift)
 
 
-def inner_back_kernel(nseg, first, local_ref, inner_ref, w_ref, x_ref, gmid_ref, gain_ref, *refs):
+STEPS = 6
+
+
+def inner_back_kernel(nseg, first, local_ref, inner_ref, w_ref, x_ref, gmid_ref, gain_ref, feed_vec_ref, *refs):
     n = BRANCHES - first
-    packs, (grad_in_ref, back_ref, vec_ref), (acc, mixed, order) = refs[:n], refs[n : n + 3], refs[n + 3 :]
+    packs, (weight_ref, back_ref, vec_ref) = refs[:n], refs[n : n + 3]
+    acc, mixed, order, terms, recv_core, recv_x, recv_seq, total, vecs, vec_recv = refs[n + 3 : n + 13]
+    red_send, red_recv, vec_send, vec_recv_sems = refs[n + 13 :]
     step = pl.program_id(0)
+    last = pl.num_programs(0) - 1
     length = nseg * SEG
+    end = STEPS + length // ROWS
+    blocks = terms.shape[1] // CHUNKS
+    core = lax.rem(lax.axis_index("fsdp"), 2)
+    reduce = Reduce(
+        CHUNKS, blocks, terms, terms, lambda xo: 2 * xo + core, recv_core, recv_x, recv_seq, total,
+        Sends(red_send, red_recv),
+    )
+    vec_sends = Sends(vec_send, vec_recv_sems)
+
+    def vec_copy(i):
+        return vec_sends.copy(i, vecs.at[i], vec_recv.at[i], *reduce.peers()[i])
+
+    def vec_event(i):
+        vec_copy(i).wait_recv()
+        vecs[i + 1] = vecs[i] + vec_recv[i]
+        if i + 1 < len(reduce.peers()):
+            vec_copy(i + 1).start()
+
+    def vec_start():
+        vec_copy(0).start()
+
+    @pl.when(step == 0)
+    def _():
+        meet(reduce.peers())
+        vecs[0] = jnp.concatenate([jnp.zeros((2, D), F32), feed_vec_ref[...], jnp.zeros((4, D), F32)], axis=0)
 
     @pl.when(step < 2)
     def _():
         mixed[...] = local_ref[0].astype(BF16)
 
-    @pl.when(step >= 2)
+    @pl.when((step >= 2) & (step < STEPS))
     def _():
         upper = lax.rem(step, 2) == 1
         for pack, level in zip(packs, range(first, BRANCHES)):
@@ -754,96 +1190,127 @@
                     local_ref[0, rows, start : start + piece.shape[1]] += piece
         mixed[...] = local_ref[0].astype(BF16)
 
-    grad_in_ref[...] = dotg(inner_ref[...], mixed[...], 1, 1).astype(BF16)
-    for start in range(0, length, 512):
-        lanes = slice(start, start + 512)
-        part = dotg(w_ref[...], mixed[:, lanes], 1, 0)
-
-        @pl.when(step == 0)
+    @pl.when(step < STEPS)
+    def _():
+        grad_in = dotg(inner_ref[...], mixed[...], 1, 1).astype(BF16)
+        base = lax.div(step, 2) * blocks + lax.rem(step, 2) * 36
+        for col in range(3):
+            part = grad_in[:, col * 128 : (col + 1) * 128].reshape(4, 12, 16, 128)
+            for owner in range(4):
+                terms[owner, pl.ds(base + col * 12, 12)] = part[owner]
+        for start in range(0, length, 512):
+            lanes = slice(start, start + 512)
+            part = dotg(w_ref[...], mixed[:, lanes], 1, 0)
+
+            @pl.when(step == 0)
+            def _():
+                acc[:, lanes] = part
+
+            @pl.when(step > 0)
+            def _():
+                acc[:, lanes] += part
+
+    events = []
+    for chunk in range(CHUNKS):
+        begin = 2 * chunk + 1
+        events.append((begin, functools.partial(reduce.begin, chunk)))
+        for stage in range(reduce.stages()):
+            when = begin + 1 + stage + (1 if stage else 0) + max(0, stage - 1 - chunk)
+            events.append((when, functools.partial(reduce.event, stage, chunk)))
+    events.append((end - 1, vec_start))
+    for i in range(len(reduce.peers())):
+        events.append((end + i, functools.partial(vec_event, i)))
+    events.sort(key=lambda event: event[0])
+
+    @pl.when((step >= STEPS) & (step < end))
+    def _():
+        turn = step - STEPS
+        quarter = lax.rem(turn, 4)
+        low = (quarter >> 1) | ((quarter & 1) << 1)
+        gain = gain_ref[...]
+        grad = acc[:, pl.ds(pl.multiple_of(turn * ROWS, ROWS), ROWS)].T
+        _, unit, inverse = normalize(x_ref[...].astype(F32), gain, gain)
+        back, gain_part, shift_part = normalize_back(grad, unit, inverse, gain)
+        vecs[0, 0:1, :] += gain_part[None, :]
+        vecs[0, 1:2, :] += shift_part[None, :]
+        total_back = gmid_ref[...] + back
+        for i in range(4):
+            put_residue(order, rev4(i) + low, total_back[i * RUN : (i + 1) * RUN])
+
+        @pl.when(quarter == 3)
         def _():
-            acc[:, lanes] = part
-
-        @pl.when(step > 0)
-        def _():
-            acc[:, lanes] += part
-
-    @pl.when(step == pl.num_programs(0) - 1)
+            back_ref[...] = get_rows(order, 0, SEG)
+
+    run_schedule(step, last, events)
+
+    @pl.when(step == last)
     def _():
-        gain = gain_ref[...]
-        gain_back = jnp.zeros((1, D), F32)
-        shift_back = jnp.zeros((1, D), F32)
-        for seg in range(nseg):
-            for pair in range(RES // 2):
-                at = slice(seg * SEG + pair * 2 * RUN, seg * SEG + (pair + 1) * 2 * RUN)
-                grad = acc[:, at].T
-                _, unit, inverse = normalize(x_ref[at, :].astype(F32), gain, gain)
-                back, gain_part, shift_part = normalize_back(grad, unit, inverse, gain)
-                gain_back = gain_back + gain_part[None, :]
-                shift_back = shift_back + shift_part[None, :]
-                total = gmid_ref[at, :] + back
-                for i in range(2):
-                    put_residue(order, rev4(2 * pair + i), total[i * RUN : (i + 1) * RUN])
-            back_ref[seg * SEG : (seg + 1) * SEG, :] = get_rows(order, 0, SEG)
-        vec_ref[0:1, :] = gain_back
-        vec_ref[1:2, :] = shift_back
-
-
-def call_inner_back(nseg, first, local, inner, weight, x, gmid, gain, packs):
+        reduce.finish()
+        for i in range(len(reduce.peers())):
+            vec_copy(i).wait_send()
+        vec_ref[...] = vecs[len(reduce.peers())]
+        for part in range(STEPS):
+            for col in range(3):
+                at = part // 2 * blocks + part % 2 * 36 + col * 12
+                weight_ref[:, part * HALF + col * 128 : part * HALF + (col + 1) * 128] = rows_of(total, at, 12)
+
+
+def call_inner_back(nseg, first, local, inner, weight, x, gmid, gain, feed_vec, packs):
     length = nseg * SEG
+    turns = length // ROWS
+    blocks = padded(IN_BLOCKS)
+    if blocks // CHUNKS < 72:
+        raise ValueError("blocks")
+    peers = 2 + seq_bits()
+
+    def at(i):
+        return jnp.minimum(i, STEPS - 1)
+
+    def turn(i):
+        return jnp.clip(i - STEPS, 0, turns - 1)
+
     return pl.pallas_call(
         functools.partial(inner_back_kernel, nseg, first),
-        grid=(6,),
+        grid=(STEPS + turns + 1,),
         in_specs=[
-            pl.BlockSpec((1, HALF, length), lambda i: (i // 2, i % 2, 0)),
+            pl.BlockSpec((1, HALF, length), lambda i: (at(i) // 2, at(i) % 2, 0)),
             const_block((D, length)),
-            pl.BlockSpec((D, HALF), lambda i: (0, i)),
-            const_block((length, D)),
-            const_block((length, D)),
+            pl.BlockSpec((D, HALF), lambda i: (0, at(i))),
+            pl.BlockSpec((ROWS, D), lambda i: (turn(i), 0)),
+            pl.BlockSpec((ROWS, D), lambda i: (turn(i), 0)),
             const_block((1, D)),
+            const_block((2, D)),
         ]
         + [
-            pl.BlockSpec((1, HALF, pack.shape[2]), lambda i: (jnp.maximum(i // 2 - 1, 0), i % 2, 0))
+            pl.BlockSpec((1, HALF, pack.shape[2]), lambda i: (jnp.maximum(at(i) // 2 - 1, 0), at(i) % 2, 0))
             for pack in packs
         ],
         out_specs=[
-            pl.BlockSpec((D, HALF), lambda i: (0, i)),
-            const_block((length, D)),
-            const_block((2, D)),
+            const_block((192, 3 * D)),
+            pl.BlockSpec((SEG, D), lambda i: (turn(i) // 4, 0)),
+            const_block((8, D)),
         ],
-        out_shape=[shape((D, 3 * D), BF16), shape((length, D), F32), shape((2, D), F32)],
+        out_shape=[shape((192, 3 * D), F32), shape((length, D), F32), shape((8, D), F32)],
         scratch_shapes=[
             pltpu.VMEM((D, length), F32),
             pltpu.VMEM((HALF, length), BF16),
             pltpu.VMEM((TILES, SEG, 128), F32),
+            pltpu.VMEM((4, blocks, 16, 128), BF16),
+            pltpu.VMEM((2, blocks, 16, 128), BF16),
+            pltpu.VMEM((blocks, 16, 128), BF16),
+            pltpu.VMEM((blocks, 16, 128), BF16),
+            pltpu.VMEM((blocks, 16, 128), BF16),
+            pltpu.VMEM((peers + 1, 8, D), F32),
+            pltpu.VMEM((peers, 8, D), F32),
+            sems(reduce_copies()),
+            sems(reduce_copies()),
+            sems(peers),
+            sems(peers),
         ],
-        compiler_params=PARAMS,
+        compiler_params=talking(3),
         cost_estimate=cost(nseg * 15e-6),
         name="inner_back",
-    )(local, inner, weight, x, gmid, gain, *packs)
-
-
-def exchange(array, distance):
-    size = lax.axis_size("seq")
-    return lax.ppermute(array, "seq", [(i, i ^ distance) for i in range(size)])
-
-
-def fetch_level(pack, group):
-    pieces = exchange(pack, group)
-    step = 1
-    while step < group:
-        pieces = jnp.concatenate([pieces, exchange(pieces, step)], axis=-1)
-        step *= 2
-    return pieces
-
-
-def return_level(grads, group):
-    step = group // 2
-    while step >= 1:
-        half = grads.shape[-1] // 2
-        other = exchange(grads[..., half:], step)
-        grads = (grads[..., :half].astype(F32) + other.astype(F32)).astype(BF16)
-        step //= 2
-    return exchange(grads, group)
+    )(local, inner, weight, x, gmid, gain, feed_vec, *packs)
 
 
 def per_device(
@@ -862,8 +1329,6 @@
     length = tokens.shape[1]
     nseg = length // SEG
     first = nseg.bit_length()
-    levels = range(first, BRANCHES)
-    group_of = {level: (SEG << (level - 1)) // length for level in levels}
 
     def gather(weight):
         return lax.all_gather(weight, "fsdp", axis=0, tiled=True)
@@ -875,50 +1340,36 @@
     weight_up = gather(up_weight)
     weight_down = gather(down_weight)
 
-    block_devices = (RES * SEG) // length
-    place = lax.axis_index("seq")
-    count = jnp.sum(valid_mask[0])
-    counts = lax.all_gather(count.astype(F32), "seq")
-    same = jnp.arange(counts.shape[0], dtype=jnp.int32) // block_devices == place // block_devices
-    limit = jnp.sum(jnp.where(same, counts, 0.0)).astype(jnp.int32)
-    local_mask = count[None]
-    mask = jnp.stack([count, place, limit + place // block_devices * (RES * SEG)])
-
-    qkv, x, inner, *sends = call_project(nseg, first, tokens[0], gain_attend, shift_attend, weight_in)
-    packs = [fetch_level(send, group_of[level]) for level, send in zip(levels, sends)]
-    o_part, l_part, m_part = call_local_forward(nseg, qkv, local_mask)
-    attended, lse = call_remote_forward(nseg, first, qkv, mask, o_part, l_part, m_part, packs)
+    mask = jnp.sum(valid_mask[0])[None]
+
+    qkv, x, inner, *packs = call_project(nseg, first, mask, tokens[0], gain_attend, shift_attend, weight_in)
+    o_part, l_part, m_part, gathered = call_local_forward(nseg, first, qkv, mask, packs)
+    attended, lse = call_remote_forward(nseg, first, qkv, mask, o_part, l_part, m_part, gathered)
 
     mixed, grad_middle, grad_merged, along, feed_vec, feed_grads = call_feed(
-        nseg, local_mask, attended, x, cotangent[0], weight_out, weight_up, weight_down, gain_feed, shift_feed
+        nseg, mask, attended, x, cotangent[0], weight_out, weight_up, weight_down, gain_feed, shift_feed
     )
-    feed_part = lax.psum_scatter(feed_grads, "fsdp", scatter_dimension=0, tiled=True)
-    feed_sum = lax.psum(feed_part, "seq")[0]
-
-    dq_remote, *sent = call_remote_backward(nseg, first, qkv, grad_merged, lse, along, mask, packs)
-    returned = [return_level(part, group_of[level]) for level, part in zip(levels, sent)]
-    local = call_local_backward(nseg, first, qkv, grad_merged, lse, along, local_mask, dq_remote)
-    grad_in, tokens_back, attend_vec = call_inner_back(
-        nseg, first, local, inner, weight_in, x, grad_middle, gain_attend, returned
+
+    dq_remote, *sent = call_remote_backward(nseg, first, qkv, grad_merged, lse, along, mask, gathered)
+    local, returned, (grad_up, grad_out, grad_down) = call_local_backward(
+        nseg, first, qkv, grad_merged, lse, along, mask, dq_remote, sent, feed_grads
     )
-    in_part = lax.psum_scatter(grad_in, "fsdp", scatter_dimension=0, tiled=True)
-    in_part, feed_sum = lax.optimization_barrier((in_part, feed_sum))
-    in_sum = lax.psum(in_part, "seq")
-    vectors = lax.psum(jnp.concatenate([attend_vec, feed_vec], axis=0), ("fsdp", "seq"))
+    grad_in, tokens_back, vectors = call_inner_back(
+        nseg, first, local, inner, weight_in, x, grad_middle, gain_attend, feed_vec, returned
+    )
     quarter = D // lax.axis_size("fsdp")
     vectors = lax.dynamic_slice_in_dim(vectors, lax.axis_index("fsdp") * quarter, quarter, 1)
-    up_rows = feed_sum[:UP_ROWS].reshape(4, 192, D)
     return (
         mixed[None],
         tokens_back[None],
         vectors[0],
         vectors[1],
-        in_sum.astype(F32),
-        feed_sum[UP_ROWS : UP_ROWS + 192].astype(F32),
+        grad_in,
+        grad_out,
         vectors[2],
         vectors[3],
-        jnp.concatenate([up_rows[i] for i in range(4)], axis=1).astype(F32),
-        feed_sum[UP_ROWS + 192 :].astype(F32),
+        grad_up,
+        grad_down,
     )
 
 

time: 874 us -> 650 us (0.74)
  waiting for transfers between devices: 274 us -> 28.2 us
  Pallas kernels: 477 us -> 576 us
  blocking collectives: 66.5 us -> 6.11 us
  starting transfers between devices: 14.9 us -> 0.15 us
  other arithmetic: 14 us -> 0.66 us
  local copies, waits for them, and re-layouts: 5.63 us -> 14.9 us
    psum x2 -> x0, waiting for transfers between devices: 192 us -> none  [the longest x1 120 us: per_device(): feed_sum = lax.psum(feed_part, 'seq')[0]]
    ppermute x12 -> x0, waiting for transfers between devices: 51.7 us -> none  [exchange(): return lax.ppermute(array, 'seq', [(i, i ^ distance) for i in range(size)])]
    pallas_call x2, Pallas kernels: 124 us -> 174 us  [the longest x1 95.3 us: call_local_forward(): pl.pallas_call(functools.partial(local_forward, nseg, first), grid=(HEADS...]
    pallas_call x1, Pallas kernels: 146 us -> 190 us  [call_local_backward(): pl.pallas_call(functools.partial(local_backward, nseg, first), grid=(HEAD...]
    psum x1 -> x0, blocking collectives: 39.4 us -> none  [per_device(): lax.psum(jnp.concatenate([attend_vec, feed_vec], axis=0), ('fsdp', 'seq'))]
    unnamed x1 -> x0, blocking collectives: 21 us -> none
    ppermute x12 -> x0, starting transfers between devices: 14.6 us -> none  [exchange(): return lax.ppermute(array, 'seq', [(i, i ^ distance) for i in range(size)])]
    unnamed x30 -> x23, local copies, waits for them, and re-layouts: 2.73 us -> 12.6 us
  transfers between devices with their start and end apart: 20 -> 4, of which waited for: 9 -> 1; matrix products, arithmetic and copies ran while one was open for 2% -> 0% of each run, Pallas kernels for 43% -> 26%
where the time goes in v3:
time: 650 us; the launch traced here: 641 us
  Pallas kernels  576 us (89%)
  waiting for transfers between devices  28.2 us (4%)
  local copies, waits for them, and re-layouts  14.9 us (2%)
  between operations  14.4 us (2%)
    pallas_call x1, Pallas kernels, call_local_backward(): pl.pallas_call(functools.partial(local_backward, nseg, first), grid=(HEAD...  190 us
    pallas_call x1, Pallas kernels, call_feed(): pl.pallas_call(functools.partial(feed_kernel, nseg), grid=(length // ROWS...  100 us
    pallas_call x1, Pallas kernels, call_local_forward(): pl.pallas_call(functools.partial(local_forward, nseg, first), grid=(HEADS...  95.3 us
    pallas_call x1, Pallas kernels, call_inner_back(): pl.pallas_call(functools.partial(inner_back_kernel, nseg, first), grid=(S...  79.1 us
    pallas_call x1, Pallas kernels, call_remote_forward(): pl.pallas_call(functools.partial(remote_forward, nseg, first), grid=(HEAD...  48.9 us
    pallas_call x1, Pallas kernels, call_remote_backward(): pl.pallas_call(functools.partial(remote_backward, nseg, first), grid=(HEA...  40.9 us
    all_gather x4, waiting for transfers between devices, gather(): return lax.all_gather(weight, 'fsdp', axis=0, tiled=True)  25.6 us
    pallas_call x1, Pallas kernels, call_project(): pl.pallas_call(functools.partial(project_kernel, nseg, first), grid=(6,),...  21.8 us
  transfers between devices with their start and end apart: 4, of which 1 were waited for; matrix products, arithmetic and copies ran while one was open for 0% of the time, Pallas kernels for 26%

profile of v3, /device:TPU:0, one launch (start us, length us, event | category | flops | bytes accessed | tf_op | source)
XLA Modules:
  0.0 640.6 jit_solution(8605962255352802231)
XLA Ops:
  7.2 0.0 copy-start.5
  7.2 0.0 copy-start.6
  7.2 0.0 copy-start.7
  7.2 0.0 copy-start.8
  7.2 0.0 copy-start.4
  7.2 0.0 all-gather.6.cloned.1.call-start
  7.3 0.7 all-gather.6.cloned.1.call-update
  8.0 0.0 all-gather.8.cloned.1.call-start
  8.0 0.7 all-gather.8.cloned.1.call-update
  8.7 0.0 all-gather.10.cloned.1.call-start
  8.8 0.7 all-gather.10.cloned.1.call-update
  9.4 0.0 all-gather.12.cloned.1.call-start
  9.5 0.5 all-gather.12.cloned.1.call-update
  10.0 0.0 copy-done.5
  10.0 0.0 copy-done.6
  10.1 0.0 copy-done.7
  10.1 0.0 copy-done.8
  10.1 6.1 all-gather
  16.2 0.1 reshape.22
  16.3 0.6 slice_bitcast_fusion
  16.9 0.0 copy-done.4
  17.0 0.6 reduce_sum.9
  17.6 25.5 %all-gather.6.cloned.1.call-done.w_ref = bf16[768,2304]{1,0:T(8,128)(2,1)} async-done(((bf16[192,2304]{1,0:T(8,128)(2,1)}), bf16[768,2304]{1,0:T(8,128)(2,1)}) %all-gather.6.cloned.1.call-update) | async-done | bytes 3538960 | tf_op jit(solution)/shard_map/all_gather | solution.py:1334
  43.1 21.8 %project.1 = (bf16[3,768,2048]{2,1,0:T(8,128)(2,1)}, bf16[2048,768]{1,0:T(8,128)(2,1)}, bf16[768,2048]{1,0:T(8,128)(2,1)}, bf16[1552,512]{1,0:T(8,128)(2,1)}, bf...) custom-call(s32[1]{0:T(128)} %bitcast.mask_ref, bf16[2048,768]{1,0:T(8,128)(2,1)} %bitcast.26, ...), custom_call_target="tpu_custom_call" | custom-call | flops 22000001024 | tf_op jit(solution)/shard_map/project/pallas_call | solution.py:953
  64.9 95.3 %local_forward.1 = (f32[768,2048]{1,0:T(8,128)}, f32[16,1,2048]{2,1,0:T(1,128)}, f32[16,1,2048]{2,1,0:T(1,128)}, bf16[1,1552,512]{2,1,0:T(8,128)(2,1)}, bf16[2,1...) custom-call(s32[1]{0:T(128)} %bitcast.mask_ref, bf16[3,768,2048]{2,1,0:T(8,128)(2,1)} %get-tuple-element.44.q_ref.k_ref.v_ref, ...), custom_call_target="tpu_custom_call" | custom-call | flops 81399996416 | tf_op jit(solution)/shard_map/local_forward/pallas_call | solution.py:729
  160.2 48.9 %remote_forward.1 = (bf16[768,2048]{1,0:T(8,128)(2,1)}, f32[16,1,2048]{2,1,0:T(1,128)}) custom-call(s32[1]{0:T(128)} %bitcast.mask_ref, bf16[3,768,2048]{2,1,0:T(8,128)(2,1)} %get-tuple-element.44.q_ref.k_ref.v_ref, f32[768,2048]{1,0:T(8,128)} %get-tuple-element.48.o_in, f32[16,1,2048]{2,1,0:T(1,128)} %get-tuple-element.49.l_in, ...), custom_call_target="tpu_custom_call" | custom-call | flops 52800000000 | tf_op jit(solution)/shard_map/remote_forward/pallas_call | solution.py:757
  209.1 0.0 all-gather.8.cloned.1.call-done.wout_ref
  209.2 0.0 all-gather.10.cloned.1.call-done.up_ref
  209.2 0.0 all-gather.12.cloned.1.call-done.down_ref
  209.2 100.4 %feed.1 = (bf16[2048,768]{1,0:T(8,128)(2,1)}, f32[2048,768]{1,0:T(8,128)}, bf16[768,2048]{1,0:T(8,128)(2,1)}, f32[16,1,2048]{2,1,0:T(1,128)}, f32[2,768]{1,0:T(2,128)}, /*index=5*/bf16[4,648,16,128]{3,2,1,0:T(8,128)(2,1)}) custom-call(s32[1]{0:T(128)} %bitcast.mask_ref, bf16[768,2048]{1,0:T(8,128)(2,1)} %get-tuple-element.54.att_ref, ...), custom_call_target="tpu_custom_call" | custom-call | flops 99000000512 | tf_op jit(solution)/shard_map/feed/pallas_call | solution.py:1090
  309.6 40.9 %remote_backward.1 = (f32[768,512]{1,0:T(8,128)}, bf16[1,2,768,512]{3,2,1,0:T(8,128)(2,1)}, bf16[2,2,768,256]{3,2,1,0:T(8,128)(2,1)}, bf16[4,2,768,128]{3,2,1,0:T(8,128)(2,1)}) custom-call(s32[1]{0:T(128)} %bitcast.mask_ref, bf16[3,768,2048]{2,1,0:T(8,128)(2,1)} %get-tuple-element.44.q_ref.k_ref.v_ref, bf16[768,2048]{1,0:T(8,128)(2,1)} %get-tuple-element.57.g_ref, ...), custom_call_target="tpu_custom_call" | custom-call | flops 44000002048 | tf_op jit(solution)/shard_map/remote_backward/pallas_call | solution.py:783
  350.5 189.8 %local_backward.1 = (f32[3,768,2048]{2,1,0:T(8,128)}, bf16[2,768,512]{2,1,0:T(8,128)(2,1)}, bf16[2,768,256]{2,1,0:T(8,128)(2,1)}, bf16[2,768,128]{2,1,0:T(8,128)...) custom-call(s32[1]{0:T(128)} %bitcast.mask_ref, ...), custom_call_target="tpu_custom_call" | custom-call | flops 158400004096 | tf_op jit(solution)/shard_map/local_backward/pallas_call | solution.py:831
  540.4 79.1 %inner_back.1 = (f32[192,2304]{1,0:T(8,128)}, f32[2048,768]{1,0:T(8,128)}, f32[8,768]{1,0:T(8,128)}) custom-call(f32[3,768,2048]{2,1,0:T(8,128)} %get-tuple-element.65.local_ref, bf16[768,2048]{1,0:T(8,128)(2,1)} %get-tuple-element.66.inner_ref, bf16[768,2304]{1,0:T(8,128)(2,1)} %all-gather.6.cloned.1.call-done.w_ref, ...), custom_call_target="tpu_custom_call" | custom-call | flops 32999999488 | tf_op jit(solution)/shard_map/inner_back/pallas_call | solution.py:1272
  619.5 1.5 fusion
  621.0 0.0 copy-start.2
  621.0 6.0 copy.28
  627.1 0.0 copy-done.2
  627.1 0.0 copy-start.3
  627.1 0.0 copy-start.1
  627.1 1.2 copy.29
  628.3 0.2 copy-done.3
  628.5 0.8 copy.30
  629.3 0.4 copy-done.1
  629.7 0.0 copy-start
  629.7 1.4 copy.31
  631.1 1.1 copy-done
  632.3 1.4 copy.32
  (6 shorter events, 0.0 us)
Async XLA Ops:
  7.2 2.9 copy-start.5
  7.2 2.9 copy-start.6
  7.2 2.9 copy-start.7
  7.2 2.9 copy-start.8
  7.2 9.7 %copy-start.4 = (s32[1,2048]{1,0:T(1,128)S(1)}, s32[1,2048]{1,0:T(1,128)}, u32[]{:S(2)}) copy-start(s32[1,2048]{1,0:T(1,128)} %param.20) | copy-start | bytes 24580
  7.2 35.9 %all-gather.6.cloned.1.call-start = ((), (), s32[]{:S(2)}) async-start(), calls=%async_computation | async-start | bytes 4423680 | tf_op jit(solution)/shard_map/all_gather | solution.py:1334
  8.0 201.2 %all-gather.8.cloned.1.call-start = ((), (), s32[]{:S(2)}) async-start(), calls=%async_computation.1 | async-start | bytes 1474560 | tf_op jit(solution)/shard_map/all_gather | solution.py:1334
  8.7 200.5 %all-gather.10.cloned.1.call-start = ((), (), s32[]{:S(2)}) async-start(), calls=%async_computation.2 | async-start | bytes 5898240 | tf_op jit(solution)/shard_map/all_gather | solution.py:1334
  9.4 199.8 %all-gather.12.cloned.1.call-start = ((), (), s32[]{:S(2)}) async-start(), calls=%async_computation.3 | async-start | bytes 5898240 | tf_op jit(solution)/shard_map/all_gather | solution.py:1334
  621.0 6.0 copy-start.2
  627.1 1.4 copy-start.3
  627.1 2.7 copy-start.1
  629.7 2.5 copy-start
Sparse Core Ops, SparseCore 0:
  9.6 33.4 all-gather.5
  44.7 17.4 all-gather.7
  63.8 37.4 all-gather.9
  102.7 37.4 all-gather.11

commit v4 on v3

--- a/solution.py
+++ b/solution.py
@@ -406,17 +406,55 @@
                 call()
 
 
-def attend_tiles(query, key, value, tile, acc, top):
-    key_t = key.T
-    for start in range(0, key.shape[1], tile):
-        scores = dotg(key_t[start : start + tile], query, 1, 0)
-        here = jnp.max(scores, axis=0, keepdims=True)
-        new_top = here if top is None else jnp.maximum(top, here)
-        probs = jnp.exp2(scores - new_top).astype(BF16)
-        part = dotg(value[:, start : start + tile], probs, 1, 0)
-        acc = part if top is None else acc * jnp.exp2(top - new_top) + part
-        top = new_top
-    return acc, top
+FRONT = 3
+KEY_TILE = 128
+
+
+class State:
+    def __init__(self, query, acc=None, top=None):
+        self.query, self.acc, self.top = query, acc, top
+
+
+def attend(items):
+    items = list(items)
+    ready = []
+    for turn in range(len(items) + FRONT):
+        if turn < len(items):
+            state, key, _ = items[turn]
+            ready.append(dotg(key, state.query, 1, 0))
+        if turn >= FRONT:
+            state, _, value = items[turn - FRONT]
+            scores, ready[turn - FRONT] = ready[turn - FRONT], None
+            top = jnp.max(scores, axis=0, keepdims=True)
+            if state.top is not None:
+                top = jnp.maximum(top, state.top)
+            probs = jnp.exp2(scores - top).astype(BF16)
+            part = dotg(value, probs, 1, 0)
+            state.acc = part if state.top is None else state.acc * jnp.exp2(state.top - top) + part
+            state.top = top
+
+
+def key_items(state, key_t, value):
+    size = key_t.shape[0]
+    tile = min(KEY_TILE, size)
+    for start in range(0, size, tile):
+        yield state, key_t[start : start + tile], value[:, start : start + tile]
+
+
+def load_state(query, mine, o_ref, l_ref, m_ref):
+    acc = [jnp.concatenate([o_ref[:, at], jnp.broadcast_to(l_ref[0, :, at], (16, at.size))]) for at in mine]
+    top = [m_ref[0, :, at] for at in mine]
+    return State(query, jnp.concatenate(acc, axis=1), jnp.concatenate(top, axis=1))
+
+
+def store_state(state, mine, o_ref, l_ref, m_ref):
+    start = 0
+    for at in mine:
+        lanes = slice(start, start + at.size)
+        o_ref[:, at] = state.acc[:HEAD_DIM, lanes]
+        l_ref[0, :, at] = state.acc[HEAD_DIM : HEAD_DIM + 1, lanes]
+        m_ref[0, :, at] = state.top[:, lanes]
+        start += at.size
 
 
 def local_forward(nseg, first, mask_ref, q_ref, k_ref, v_ref, *refs):
@@ -435,34 +473,45 @@
     for turn in range(1, gather.turns()):
         events.append((2 + 4 * turn, functools.partial(gather.pass_on, turn)))
     run_schedule(head, HEADS - 1, events)
-
+    local_forward_core(nseg, mask_ref, q_ref, k_ref, v_ref, o_ref, l_ref, m_ref, qa, ka, va)
+    run_schedule(head, HEADS - 1, [(HEADS - 1, gather.finish)])
+
+
+def local_forward_scratch(nseg):
+    length = nseg * SEG
+    return [
+        pltpu.VMEM((64, length), BF16),
+        pltpu.VMEM((nseg, 64, length), BF16),
+        pltpu.VMEM((64, length), BF16),
+    ]
+
+
+def local_forward_core(nseg, mask_ref, q_ref, k_ref, v_ref, o_ref, l_ref, m_ref, qa, ka, va):
+    head = pl.program_id(0)
+    length = nseg * SEG
     keep = local_keep(mask_ref[0], length)
     qa[...] = join(q_ref[0], query_rows(head, length))
     va[...] = join(v_ref[0], value_rows(length))
     ka[0] = join(k_ref[0], key_rows(head, 0, 4, length, keep))
     if nseg == 2:
         ka[1] = join(k_ref[0], key_rows(head, 1, 4, length, keep))
+    states, items = [], []
     for seg in range(nseg):
         lanes = slice(seg * SEG, (seg + 1) * SEG)
-        acc, top = attend_tiles(qa[:, lanes], ka[0, :, lanes], va[:, lanes], 256, None, None)
-        o_ref[:, lanes] = acc[:HEAD_DIM]
-        l_ref[0, :, lanes] = acc[HEAD_DIM : HEAD_DIM + 1]
-        m_ref[0, :, lanes] = top
+        states.append(State(qa[:, lanes]))
+        items += key_items(states[-1], ka[0, :, lanes].T, va[:, lanes])
+    attend(items)
+    for seg in range(nseg):
+        store_state(states[seg], [pl.ds(seg * SEG, SEG)], o_ref, l_ref, m_ref)
     if nseg == 2:
+        kept = [pl.ds(kept_start(head, 1, seg), SEG // 2) for seg in range(2)]
+        states = [load_state(qa[:, at], [at], o_ref, l_ref, m_ref) for at in kept]
+        items = []
         for seg in range(2):
-            mine = pl.ds(kept_start(head, 1, seg), SEG // 2)
-            other = pl.ds(kept_start(head, 1, 1 - seg), SEG // 2)
-            merge_level(qa[:, mine], ka[1, :, other], va[:, other], mine, o_ref, l_ref, m_ref)
-
-    run_schedule(head, HEADS - 1, [(HEADS - 1, gather.finish)])
-
-
-def merge_level(query, key, value, mine, o_ref, l_ref, m_ref):
-    acc = jnp.concatenate([o_ref[:, mine], jnp.broadcast_to(l_ref[0, :, mine], (16, query.shape[1]))])
-    acc, top = attend_tiles(query, key, value, 256, acc, m_ref[0, :, mine])
-    o_ref[:, mine] = acc[:HEAD_DIM]
-    l_ref[0, :, mine] = acc[HEAD_DIM : HEAD_DIM + 1]
-    m_ref[0, :, mine] = top
+            items += key_items(states[seg], ka[1, :, kept[1 - seg]].T, va[:, kept[1 - seg]])
+        attend(items)
+        for seg in range(2):
+            store_state(states[seg], [kept[seg]], o_ref, l_ref, m_ref)
 
 
 def remote_keys(head, level, pack):
@@ -495,31 +544,14 @@
         pairs = [remote_keys(head, level, packs[level]) for level in group]
         key = jnp.concatenate([pair[0] for pair in pairs], axis=1)
         value = jnp.concatenate([pair[1] for pair in pairs], axis=1)
-        for seg in range(nseg):
-            mine = pl.ds(kept_start(head, group[0], seg), SEG >> group[0])
-            merge_level(qa[:, mine], key, value, mine, o_ref, l_ref, m_ref)
+        mine = [pl.ds(kept_start(head, group[0], seg), SEG >> group[0]) for seg in range(nseg)]
+        query = jnp.concatenate([qa[:, at] for at in mine], axis=1)
+        state = load_state(query, mine, o_ref, l_ref, m_ref)
+        attend(key_items(state, key.T, value))
+        store_state(state, mine, o_ref, l_ref, m_ref)
     weight = jnp.where(local_keep(mask_ref[0], length), 1.0, 0.0) / l_ref[0]
     att_ref[...] = (o_ref[...] * weight).astype(BF16)
     lse_ref[0] = m_ref[0] + jnp.log2(l_ref[0])
-
-
-def back_tile(query_t, grad_t, query, grad, key, value, dq, dk_ref, dv_ref, lanes, first):
-    scores = dotg(query_t, key, 1, 0)
-    slope = dotg(grad_t, value, 1, 0)
-    probs = jnp.exp2(scores)
-    dscore = (probs * slope).astype(BF16)
-    probs = probs.astype(BF16)
-    part = dotg(key[:HEAD_DIM], dscore, 1, 1)
-    dq = part if dq is None else dq + part
-    dv = dotg(grad[:HEAD_DIM], probs, 1, 0)
-    dk = dotg(query[:HEAD_DIM], dscore, 1, 0)
-    if first:
-        dv_ref[:, lanes] = dv
-        dk_ref[:, lanes] = dk
-    else:
-        dv_ref[:, lanes] += dv
-        dk_ref[:, lanes] += dk
-    return dq
 
 
 def grad_rows(grad, slope):
@@ -531,20 +563,60 @@
     return join(grad, extra)
 
 
-def back_pair(query, grad, key_ref, value_ref, key_lanes, tile, dk_ref, dv_ref, start_lane, fresh):
-    out = []
-    for start in range(0, query.shape[1], tile):
-        size = min(tile, query.shape[1])
-        q_tile, g_tile = query[:, start : start + size], grad[:, start : start + size]
-        q_t, g_t = q_tile.T, g_tile.T
-        dq = None
-        for lanes in key_lanes:
-            dq = back_tile(
-                q_t, g_t, q_tile, g_tile, key_ref[:, lanes], value_ref[:, lanes], dq,
-                dk_ref, dv_ref, lanes, fresh and start == 0,
-            )
-        out.append(dq)
-    return jnp.concatenate(out, axis=1) if len(out) > 1 else out[0]
+AHEAD = 2
+QUERY_TILE = 256
+BACK_KEYS = 256
+
+
+class Side:
+    def __init__(self, query, grad):
+        self.query, self.grad = query[:HEAD_DIM], grad[:HEAD_DIM]
+        self.query_t, self.grad_t = query.T, grad.T
+        self.dq = None
+
+
+def attend_back(items, dk_ref, dv_ref, written):
+    items = list(items)
+    ready = []
+    for turn in range(len(items) + AHEAD):
+        if turn < len(items):
+            side, key, value, _, _ = items[turn]
+            ready.append((dotg(side.query_t, key, 1, 0), dotg(side.grad_t, value, 1, 0)))
+        if turn >= AHEAD:
+            side, key, _, lanes, name = items[turn - AHEAD]
+            scores, slope = ready[turn - AHEAD]
+            ready[turn - AHEAD] = None
+            probs = jnp.exp2(scores)
+            dscore = (probs * slope).astype(BF16)
+            dv = dotg(side.grad, probs.astype(BF16), 1, 0)
+            dk = dotg(side.query, dscore, 1, 0)
+            part = dotg(key[:HEAD_DIM], dscore, 1, 1)
+            side.dq = part if side.dq is None else side.dq + part
+            if name in written:
+                dv_ref[:, lanes] += dv
+                dk_ref[:, lanes] += dk
+            else:
+                written.add(name)
+                dv_ref[:, lanes] = dv
+                dk_ref[:, lanes] = dk
+
+
+def sides_of(query, grad):
+    tile = min(QUERY_TILE, query.shape[1])
+    return [
+        Side(query[:, start : start + tile], grad[:, start : start + tile])
+        for start in range(0, query.shape[1], tile)
+    ]
+
+
+def pairs(sides, key_ref, value_ref, tiles):
+    return [
+        (side, key_ref[:, lanes], value_ref[:, lanes], lanes, name) for side in sides for name, lanes in tiles
+    ]
+
+
+def joined(sides):
+    return jnp.concatenate([side.dq for side in sides], axis=1) if len(sides) > 1 else sides[0].dq
 
 
 DQ_SCALE = HEAD_DIM ** (-0.5)
@@ -590,32 +662,10 @@
                 when = 3 + 2 * chunk + stage + (stage >= 2) + (stage == reduce.stages() - 1)
             events.append((when, functools.partial(reduce.event, stage, chunk)))
     run_schedule(head, last, [(0, begin)] + sorted(events, key=lambda event: event[0]))
-
-    keep = local_keep(mask_ref[0], length)
-    qa[...] = join(q_ref[0], query_rows(head, length, neg_total(lse_ref[0], keep)))
-    ga[...] = grad_rows(g_ref[...], slope_ref[0])
-    va[...] = join(v_ref[0], value_rows(length))
-    ka[0] = join(k_ref[0], key_rows(head, 0, 4, length, keep))
-    if nseg == 2:
-        ka[1] = join(k_ref[0], key_rows(head, 1, 4, length, keep))
-    for seg in range(nseg):
-        lanes = slice(seg * SEG, (seg + 1) * SEG)
-        tiles = [slice(seg * SEG + 256 * i, seg * SEG + 256 * (i + 1)) for i in range(4)]
-        dq = back_pair(qa[:, lanes], ga[:, lanes], ka.at[0], va, tiles, 256, dk, dv, 0, True)
-        out_ref[0, :, lanes] = dq * DQ_SCALE
-    if nseg == 2:
-        for seg in range(2):
-            mine = pl.ds(kept_start(head, 1, seg), SEG // 2)
-            base = kept_start(head, 1, 1 - seg)
-            tiles = [pl.ds(pl.multiple_of(base + 256 * i, 256), 256) for i in range(2)]
-            dq = back_pair(qa[:, mine], ga[:, mine], ka.at[1], va, tiles, 256, dk, dv, 0, False)
-            out_ref[0, :, mine] += dq * DQ_SCALE
-    size = SEG >> first
-    for seg in range(nseg):
-        mine = pl.ds(kept_start(head, first, seg), size)
-        out_ref[0, :, mine] += dqr_ref[:, seg * size : (seg + 1) * size]
-    out_ref[1] = dk[...] * DK_SCALE
-    out_ref[2] = dv[...]
+    local_backward_core(
+        nseg, first, mask_ref, q_ref, k_ref, v_ref, g_ref, lse_ref, slope_ref, dqr_ref, out_ref,
+        qa, ga, ka, va, dk, dv,
+    )
 
     @pl.when(head == last)
     def _():
@@ -628,6 +678,65 @@
                 up_ref[:, col * D + tile * 128 : col * D + (tile + 1) * 128] = rows_of(total, at, 12)
             proj_ref[:, cols] = rows_of(total, 288 + tile * 12, 12)
             down_ref[:, cols] = rows_of(total, 360 + tile * 48, 48)
+
+
+def local_backward_scratch(nseg):
+    length = nseg * SEG
+    return [
+        pltpu.VMEM((64, length), BF16),
+        pltpu.VMEM((64, length), BF16),
+        pltpu.VMEM((nseg, 64, length), BF16),
+        pltpu.VMEM((64, length), BF16),
+        pltpu.VMEM((HEAD_DIM, length), F32),
+        pltpu.VMEM((HEAD_DIM, length), F32),
+    ]
+
+
+def local_backward_core(
+    nseg, first, mask_ref, q_ref, k_ref, v_ref, g_ref, lse_ref, slope_ref, dqr_ref, out_ref,
+    qa, ga, ka, va, dk, dv,
+):
+    head = pl.program_id(0)
+    length = nseg * SEG
+    keep = local_keep(mask_ref[0], length)
+    qa[...] = join(q_ref[0], query_rows(head, length, neg_total(lse_ref[0], keep)))
+    ga[...] = grad_rows(g_ref[...], slope_ref[0])
+    va[...] = join(v_ref[0], value_rows(length))
+    ka[0] = join(k_ref[0], key_rows(head, 0, 4, length, keep))
+    if nseg == 2:
+        ka[1] = join(k_ref[0], key_rows(head, 1, 4, length, keep))
+    items, sides, written = [], [], set()
+    for seg in range(nseg):
+        lanes = slice(seg * SEG, (seg + 1) * SEG)
+        tiles = [
+            ((seg, i), slice(seg * SEG + BACK_KEYS * i, seg * SEG + BACK_KEYS * (i + 1)))
+            for i in range(SEG // BACK_KEYS)
+        ]
+        sides.append(sides_of(qa[:, lanes], ga[:, lanes]))
+        items += pairs(sides[-1], ka.at[0], va, tiles)
+    attend_back(items, dk, dv, written)
+    for seg in range(nseg):
+        out_ref[0, :, seg * SEG : (seg + 1) * SEG] = joined(sides[seg]) * DQ_SCALE
+    if nseg == 2:
+        items, sides = [], []
+        kept = [pl.ds(kept_start(head, 1, seg), SEG // 2) for seg in range(2)]
+        for seg in range(2):
+            base = kept_start(head, 1, 1 - seg)
+            tile = min(BACK_KEYS, SEG // 2)
+            tiles = [
+                ((seg, i), pl.ds(pl.multiple_of(base + tile * i, tile), tile)) for i in range(SEG // 2 // tile)
+            ]
+            sides.append(sides_of(qa[:, kept[seg]], ga[:, kept[seg]]))
+            items += pairs(sides[-1], ka.at[1], va, tiles)
+        attend_back(items, dk, dv, set(item[4] for item in items))
+        for seg in range(2):
+            out_ref[0, :, kept[seg]] += joined(sides[seg]) * DQ_SCALE
+    size = SEG >> first
+    for seg in range(nseg):
+        mine = pl.ds(kept_start(head, first, seg), size)
+        out_ref[0, :, mine] += dqr_ref[:, seg * size : (seg + 1) * size]
+    out_ref[1] = dk[...] * DK_SCALE
+    out_ref[2] = dv[...]
 
 
 def rows_of(total, at, count):
@@ -655,8 +764,11 @@
         mine = [pl.ds(kept_start(head, group[0], seg), size) for seg in range(nseg)]
         query = jnp.concatenate([qa[:, m] for m in mine], axis=1)
         grad = jnp.concatenate([ga[:, m] for m in mine], axis=1)
-        tiles = [slice(256 * i, 256 * (i + 1)) for i in range(2 * len(group))]
-        dq = back_pair(query, grad, ka, va, tiles, 256, dk, dv, 0, True) * DQ_SCALE
+        tile = min(BACK_KEYS, 512)
+        tiles = [(i, slice(tile * i, tile * (i + 1))) for i in range(512 // tile * len(group))]
+        sides = sides_of(query, grad)
+        attend_back(pairs(sides, ka, va, tiles), dk, dv, set())
+        dq = joined(sides) * DQ_SCALE
         for seg in range(nseg):
             piece = dq[:, seg * size : (seg + 1) * size]
             if group[0] == first:
@@ -734,10 +846,8 @@
         out_specs=[head_block(length), row_block(length), row_block(length)] + [ANY_BLOCK] * n,
         out_shape=[shape((D, length), F32), shape((HEADS, 1, length), F32), shape((HEADS, 1, length), F32)]
         + [shape((group,) + pack.shape, BF16) for group, pack in zip(groups, packs)],
-        scratch_shapes=[
-            pltpu.VMEM((64, length), BF16),
-            pltpu.VMEM((nseg, 64, length), BF16),
-            pltpu.VMEM((64, length), BF16),
+        scratch_shapes=local_forward_scratch(nseg)
+        + [
             sems(hops),
             sems(hops),
         ],
@@ -840,14 +950,7 @@
         out_shape=[shape((3, D, length), F32)]
         + [shape(part.shape[1:], BF16) for part in sent]
         + [shape((192, 4 * D), F32), shape((192, D), F32), shape((D, D), F32)],
-        scratch_shapes=[
-            pltpu.VMEM((64, length), BF16),
-            pltpu.VMEM((64, length), BF16),
-            pltpu.VMEM((nseg, 64, length), BF16),
-            pltpu.VMEM((64, length), BF16),
-            pltpu.VMEM((HEAD_DIM, length), F32),
-            pltpu.VMEM((HEAD_DIM, length), F32),
-        ]
+        scratch_shapes=local_backward_scratch(nseg)
         + bufs
         + recvs
         + [
@@ -904,29 +1007,102 @@
         tiled[tile, pl.ds(start, RUN, stride=RES), :] = array[:, tile * 128 : (tile + 1) * 128]
 
 
-def project_kernel(nseg, first, mask_ref, tok_ref, gain_ref, shift_ref, w_ref, qkv_ref, xp_ref, inner_ref, *refs):
-    *packs, xs = refs
+COLUMN_CHUNKS = 3
+
+
+def project_kernel(nseg, first, mask_ref, tok_ref, *refs):
+    n = BRANCHES - first
+    vectors, w_ref = refs[:4], refs[4]
+    qkv_ref, xp_ref, inner_ref, weight_ref, gains_ref = refs[5:10]
+    packs = refs[10 : 10 + n]
+    xs, weight, gains, vec_send, vec_recv, w_send, w_recv, w_load, w_store = refs[10 + n :]
     step = pl.program_id(0)
+    last = pl.num_programs(0) - 1
+    me = lax.axis_index("fsdp")
+    sibling = me + 1 - 2 * lax.rem(me, 2)
+    across = lax.rem(me + 2, 4)
+    sends = Sends(w_send, w_recv)
+
+    def send(source, target, key, other):
+        index = sends.made.setdefault(key, len(sends.made))
+        return pltpu.make_async_remote_copy(
+            src_ref=source, dst_ref=target, send_sem=w_send.at[index], recv_sem=w_recv.at[index],
+            device_id={"fsdp": other}, device_id_type=pl.DeviceIdType.MESH,
+        )
+
+    def chunk_copies(chunk):
+        cols = pl.ds(chunk * D, D)
+        mine = w_ref.at[:, cols]
+        load = pltpu.make_async_copy(mine, weight.at[me, :, cols], w_load.at[chunk])
+        core = send(mine, weight.at[me, :, cols], ("core", chunk), sibling)
+        x = send(mine, weight.at[me, :, cols], ("x", chunk), across)
+        handed = weight.at[across, :, cols]
+        return load, core, x, send(handed, handed, ("hand", chunk), sibling)
+
+    def vec_copies():
+        return [
+            pltpu.make_async_remote_copy(
+                src_ref=gains.at[me], dst_ref=gains.at[me], send_sem=vec_send.at[i], recv_sem=vec_recv.at[i],
+                device_id={"fsdp": other}, device_id_type=pl.DeviceIdType.MESH,
+            )
+            for i, other in enumerate((sibling, across, 3 - me))
+        ]
+
+    store = pltpu.make_async_copy(weight, weight_ref, w_store.at[0])
 
     @pl.when(step == 0)
     def _():
+        barrier = pltpu.get_barrier_semaphore()
+        for other in (sibling, across, 3 - me):
+            pl.semaphore_signal(
+                barrier, inc=1, device_id={"fsdp": other}, device_id_type=pl.DeviceIdType.MESH
+            )
+        for i, vector in enumerate(vectors):
+            gains[me, i : i + 1, :192] = vector[...].astype(F32)
+        pl.semaphore_wait(barrier, 3)
+        for copy in vec_copies():
+            copy.start()
+        for chunk in range(COLUMN_CHUNKS):
+            for copy in chunk_copies(chunk)[:3]:
+                copy.start()
+        for copy in vec_copies():
+            copy.wait_recv()
+        full = [
+            jnp.concatenate([gains[owner, i : i + 1, :192] for owner in range(4)], axis=1) for i in range(4)
+        ]
+        gains_ref[...] = jnp.concatenate(full + [jnp.zeros((4, D), F32)], axis=0)
         for seg in range(nseg):
             put_rows(xs, 0, tok_ref[seg * SEG : (seg + 1) * SEG, :].astype(F32))
             for pair in range(RES // 2):
-                rows = jnp.concatenate(
-                    [get_residue(xs, rev4(2 * pair + i)) for i in range(2)], axis=0
-                )
-                normed = normalize(rows, gain_ref[...], shift_ref[...])[0].astype(BF16)
+                rows = jnp.concatenate([get_residue(xs, rev4(2 * pair + i)) for i in range(2)], axis=0)
+                normed = normalize(rows, full[0], full[1])[0].astype(BF16)
                 at = slice(seg * SEG + pair * 2 * RUN, seg * SEG + (pair + 1) * 2 * RUN)
                 xp_ref[at, :] = rows.astype(BF16)
                 inner_ref[:, at] = normed.T
         for pack, level in zip(packs, range(first, BRANCHES)):
             pack[2 * D :, :] = packed_keep(mask_ref[0], level, nseg)
 
+    for chunk in range(COLUMN_CHUNKS):
+
+        @pl.when(step == 2 * chunk)
+        def _():
+            load, core, x, hand = chunk_copies(chunk)
+            x.wait_recv()
+            hand.start()
+            load.wait()
+            core.wait_recv()
+            hand.wait_recv()
+
+    @pl.when(step == 4)
+    def _():
+        store.start()
+
+    cols = pl.ds(pl.multiple_of(step * HALF, HALF), HALF)
+    block = jnp.concatenate([weight[owner, :, cols] for owner in range(4)], axis=0)
     scale = jnp.where(step < 2, QUERY_SCALE, 1.0)
     for start in range(0, nseg * SEG, 512):
         lanes = slice(start, start + 512)
-        qkv_ref[0, :, lanes] = (dotg(w_ref[...], inner_ref[:, lanes], 0, 0) * scale).astype(BF16)
+        qkv_ref[0, :, lanes] = (dotg(block, inner_ref[:, lanes], 0, 0) * scale).astype(BF16)
 
     @pl.when(step >= 2)
     def _():
@@ -946,37 +1122,54 @@
                 into = pl.ds(pl.multiple_of((step - 2) * HALF + head * HEAD_DIM, 16), HEAD_DIM)
                 pack[into, :] = jnp.concatenate(pieces, axis=1) if nseg > 1 else pieces[0]
 
-
-def call_project(nseg, first, mask, tokens, gain, shift, weight):
+    @pl.when(step == last)
+    def _():
+        for copy in vec_copies():
+            copy.wait_send()
+        for chunk in range(COLUMN_CHUNKS):
+            for copy in chunk_copies(chunk)[1:]:
+                copy.wait_send()
+        store.wait()
+
+
+def call_project(nseg, first, mask, tokens, vectors, weight):
     length = nseg * SEG
     kept = [nseg * (SEG >> level) for level in range(first, BRANCHES)]
     return pl.pallas_call(
         functools.partial(project_kernel, nseg, first),
         grid=(6,),
-        in_specs=[
-            MASK_BLOCK,
-            const_block((length, D)),
-            const_block((1, D)),
-            const_block((1, D)),
-            pl.BlockSpec((D, HALF), lambda i: (0, i)),
-        ],
+        in_specs=[MASK_BLOCK, const_block((length, D))] + [const_block((1, 192))] * 4 + [ANY_BLOCK],
         out_specs=[
             pl.BlockSpec((1, HALF, length), lambda i: (i // 2, i % 2, 0)),
             const_block((length, D)),
             const_block((D, length)),
+            ANY_BLOCK,
+            const_block((8, D)),
         ]
         + [const_block((2 * D + 16, size)) for size in kept],
         out_shape=[
             shape((3, D, length), BF16),
             shape((length, D), BF16),
             shape((D, length), BF16),
+            shape((4, 192, 3 * D), BF16),
+            shape((8, D), F32),
         ]
         + [shape((2 * D + 16, size), BF16) for size in kept],
-        scratch_shapes=[pltpu.VMEM((TILES, SEG, 128), F32)],
-        compiler_params=PARAMS,
+        scratch_shapes=[
+            pltpu.VMEM((TILES, SEG, 128), F32),
+            pltpu.VMEM((4, 192, 3 * D), BF16),
+            pltpu.VMEM((4, 8, 256), F32),
+            sems(3),
+            sems(3),
+            sems(3 * COLUMN_CHUNKS),
+            sems(3 * COLUMN_CHUNKS),
+            sems(COLUMN_CHUNKS),
+            sems(1),
+        ],
+        compiler_params=talking(4),
         cost_estimate=cost(nseg * 10e-6),
         name="project",
-    )(mask, tokens, gain, shift, weight)
+    )(mask, tokens, *vectors, weight)
 
 
 ROWS = 256
@@ -988,7 +1181,7 @@
 
 
 def feed_kernel(
-    nseg, mask_ref, att_ref, x_ref, cot_ref, wout_ref, up_ref, down_ref, gain_ref, shift_ref,
+    nseg, mask_ref, att_ref, x_ref, cot_ref, wout_ref, up_ref, down_ref, gains_ref,
     mixed_ref, gmid_ref, gm_ref, along_ref, vec_ref, grads_ref,
     cs, out_acc, up_acc, down_acc, stage, sems,
 ):
@@ -1011,8 +1204,8 @@
     grad_b = grad.astype(BF16)
     att = att_ref[...]
     middle = x_ref[...].astype(F32) + dotg(att, wout_ref[...], 0, 0)
-    gain = gain_ref[...]
-    normed, unit, inverse = normalize(middle, gain, shift_ref[...])
+    gain = gains_ref[2:3, :]
+    normed, unit, inverse = normalize(middle, gain, gains_ref[3:4, :])
     hidden = normed.astype(BF16)
     hidden_t = hidden.T
     final = middle
@@ -1085,7 +1278,7 @@
         copies[-1].wait()
 
 
-def call_feed(nseg, mask, att, x, cot, wout, up, down, gain, shift):
+def call_feed(nseg, mask, att, x, cot, wout, up, down, gains):
     length = nseg * SEG
     return pl.pallas_call(
         functools.partial(feed_kernel, nseg),
@@ -1098,8 +1291,7 @@
             const_block((D, D)),
             const_block((D, 4 * D)),
             const_block((4 * D, D)),
-            const_block((1, D)),
-            const_block((1, D)),
+            const_block((8, D)),
         ],
         out_specs=[
             pl.BlockSpec((SEG, D), lambda i: (i // 4, 0)),
@@ -1128,7 +1320,7 @@
         compiler_params=pltpu.CompilerParams(vmem_limit_bytes=62 * 1024 * 1024),
         cost_estimate=cost(nseg * 45e-6),
         name="feed",
-    )(mask, att, x, cot, wout, up, down, gain, shift)
+    )(mask, att, x, cot, wout, up, down, gains)
 
 
 STEPS = 6
@@ -1227,7 +1419,7 @@
         turn = step - STEPS
         quarter = lax.rem(turn, 4)
         low = (quarter >> 1) | ((quarter & 1) << 1)
-        gain = gain_ref[...]
+        gain = gain_ref[0:1, :]
         grad = acc[:, pl.ds(pl.multiple_of(turn * ROWS, ROWS), ROWS)].T
         _, unit, inverse = normalize(x_ref[...].astype(F32), gain, gain)
         back, gain_part, shift_part = normalize_back(grad, unit, inverse, gain)
@@ -1278,7 +1470,7 @@
             pl.BlockSpec((D, HALF), lambda i: (0, at(i))),
             pl.BlockSpec((ROWS, D), lambda i: (turn(i), 0)),
             pl.BlockSpec((ROWS, D), lambda i: (turn(i), 0)),
-            const_block((1, D)),
+            const_block((8, D)),
             const_block((2, D)),
         ]
         + [
@@ -1333,21 +1525,20 @@
     def gather(weight):
         return lax.all_gather(weight, "fsdp", axis=0, tiled=True)
 
-    weight_in = gather(project_in)
-    small = gather(jnp.stack([first_gain, first_shift, second_gain, second_shift], axis=1)).astype(F32)
-    gain_attend, shift_attend, gain_feed, shift_feed = (small[:, i][None, :] for i in range(4))
     weight_out = gather(project_out)
     weight_up = gather(up_weight)
     weight_down = gather(down_weight)
 
     mask = jnp.sum(valid_mask[0])[None]
 
-    qkv, x, inner, *packs = call_project(nseg, first, mask, tokens[0], gain_attend, shift_attend, weight_in)
+    vectors = [vector[None, :] for vector in (first_gain, first_shift, second_gain, second_shift)]
+    qkv, x, inner, weight_in, gains, *packs = call_project(nseg, first, mask, tokens[0], vectors, project_in)
+    weight_in = weight_in.reshape(D, 3 * D)
     o_part, l_part, m_part, gathered = call_local_forward(nseg, first, qkv, mask, packs)
     attended, lse = call_remote_forward(nseg, first, qkv, mask, o_part, l_part, m_part, gathered)
 
     mixed, grad_middle, grad_merged, along, feed_vec, feed_grads = call_feed(
-        nseg, mask, attended, x, cotangent[0], weight_out, weight_up, weight_down, gain_feed, shift_feed
+        nseg, mask, attended, x, cotangent[0], weight_out, weight_up, weight_down, gains
     )
 
     dq_remote, *sent = call_remote_backward(nseg, first, qkv, grad_merged, lse, along, mask, gathered)
@@ -1355,7 +1546,7 @@
         nseg, first, qkv, grad_merged, lse, along, mask, dq_remote, sent, feed_grads
     )
     grad_in, tokens_back, vectors = call_inner_back(
-        nseg, first, local, inner, weight_in, x, grad_middle, gain_attend, feed_vec, returned
+        nseg, first, local, inner, weight_in, x, grad_middle, gains, feed_vec, returned
     )
     quarter = D // lax.axis_size("fsdp")
     vectors = lax.dynamic_slice_in_dim(vectors, lax.axis_index("fsdp") * quarter, quarter, 1)

time: 650 us -> 557 us (0.86)
  Pallas kernels: 576 us -> 514 us
  waiting for transfers between devices: 28.2 us -> 2.12 us
    pallas_call x1, Pallas kernels: 190 us -> 157 us  [call_local_backward(): pl.pallas_call(functools.partial(local_backward, nseg, first), grid=(HEAD...]
    pallas_call x1, Pallas kernels: 48.9 us -> 22.9 us  [call_remote_forward(): pl.pallas_call(functools.partial(remote_forward, nseg, first), grid=(HEAD...]
    all_gather x4 -> x3, waiting for transfers between devices: 25.6 us -> 0.06 us  [gather(): return lax.all_gather(weight, 'fsdp', axis=0, tiled=True)]
    pallas_call x1, Pallas kernels: 21.8 us -> 41.3 us  [call_project(): pl.pallas_call(functools.partial(project_kernel, nseg, first), grid=(6,),...]
    pallas_call x1, Pallas kernels: 40.9 us -> 28 us  [call_remote_backward(): pl.pallas_call(functools.partial(remote_backward, nseg, first), grid=(HEA...]
    pallas_call x1, Pallas kernels: 95.3 us -> 87.8 us  [call_local_forward(): pl.pallas_call(functools.partial(local_forward, nseg, first), grid=(HEADS...]
  transfers between devices with their start and end apart: 4 -> 3, of which waited for: 1 -> 0; matrix products, arithmetic and copies ran while one was open for 0% -> 1% of each run, Pallas kernels for 26% -> 28%
where the time goes in v4:
time: 557 us; the launch traced here: 548 us
  Pallas kernels  514 us (92%)
  local copies, waits for them, and re-layouts  16.4 us (3%)
  between operations  14.3 us (3%)
    pallas_call x1, Pallas kernels, call_local_backward(): pl.pallas_call(functools.partial(local_backward, nseg, first), grid=(HEAD...  157 us
    pallas_call x1, Pallas kernels, call_feed(): pl.pallas_call(functools.partial(feed_kernel, nseg), grid=(length // ROWS...  100 us
    pallas_call x1, Pallas kernels, call_local_forward(): pl.pallas_call(functools.partial(local_forward, nseg, first), grid=(HEADS...  87.8 us
    pallas_call x1, Pallas kernels, call_inner_back(): pl.pallas_call(functools.partial(inner_back_kernel, nseg, first), grid=(S...  77.6 us
    pallas_call x1, Pallas kernels, call_project(): pl.pallas_call(functools.partial(project_kernel, nseg, first), grid=(6,),...  41.3 us
    pallas_call x1, Pallas kernels, call_remote_backward(): pl.pallas_call(functools.partial(remote_backward, nseg, first), grid=(HEA...  28 us
    pallas_call x1, Pallas kernels, call_remote_forward(): pl.pallas_call(functools.partial(remote_forward, nseg, first), grid=(HEAD...  22.9 us
    unnamed x23, local copies, waits for them, and re-layouts  12.6 us
  transfers between devices with their start and end apart: 3, of which 0 were waited for; matrix products, arithmetic and copies ran while one was open for 1% of the time, Pallas kernels for 28%

profile of v4, /device:TPU:0, one launch (start us, length us, event | category | flops | bytes accessed | tf_op | source)
XLA Modules:
  0.0 548.1 jit_solution(7860905728574345393)
XLA Ops:
  7.2 0.0 copy-start.5
  7.2 0.0 copy-start.6
  7.2 0.0 copy-start.7
  7.2 0.0 copy-start.8
  7.2 0.0 copy-start.4
  7.2 0.0 all-gather.4.cloned.1.call-start
  7.3 0.7 all-gather.4.cloned.1.call-update
  8.0 0.0 all-gather.6.cloned.1.call-start
  8.0 0.7 all-gather.6.cloned.1.call-update
  8.7 0.0 all-gather.8.cloned.1.call-start
  8.8 0.7 all-gather.8.cloned.1.call-update
  9.4 0.0 copy-done.5
  9.5 0.6 broadcast_in_dim.22.refs_0_
  10.0 0.0 copy-done.6
  10.0 0.6 broadcast_in_dim.23.refs_1_
  10.6 0.0 copy-done.7
  10.6 0.6 broadcast_in_dim.24.refs_2_
  11.2 0.0 copy-done.8
  11.2 0.6 broadcast_in_dim.25.refs_3_
  11.7 0.0 copy-done.4
  11.7 0.7 reduce_sum.9
  12.4 41.3 %project.1 = (bf16[3,768,2048]{2,1,0:T(8,128)(2,1)}, bf16[2048,768]{1,0:T(8,128)(2,1)}, bf16[768,2048]{1,0:T(8,128)(2,1)}, bf16[4,192,2304]{2,1,0:T(8,128)(2,1)}...) custom-call(s32[1]{0:T(128)} %bitcast.mask_ref, ...), custom_call_target="tpu_custom_call" | custom-call | flops 22000001024 | tf_op jit(solution)/shard_map/project/pallas_call | solution.py:1138
  53.7 87.8 %local_forward.1 = (f32[768,2048]{1,0:T(8,128)}, f32[16,1,2048]{2,1,0:T(1,128)}, f32[16,1,2048]{2,1,0:T(1,128)}, bf16[1,1552,512]{2,1,0:T(8,128)(2,1)}, bf16[2,1...) custom-call(s32[1]{0:T(128)} %bitcast.mask_ref, bf16[3,768,2048]{2,1,0:T(8,128)(2,1)} %get-tuple-element.46.q_ref.k_ref.v_ref, ...), custom_call_target="tpu_custom_call" | custom-call | flops 81399996416 | tf_op jit(solution)/shard_map/local_forward/pallas_call | solution.py:841
  141.5 22.9 %remote_forward.1 = (bf16[768,2048]{1,0:T(8,128)(2,1)}, f32[16,1,2048]{2,1,0:T(1,128)}) custom-call(s32[1]{0:T(128)} %bitcast.mask_ref, bf16[3,768,2048]{2,1,0:T(8,128)(2,1)} %get-tuple-element.46.q_ref.k_ref.v_ref, f32[768,2048]{1,0:T(8,128)} %get-tuple-element.50.o_in, f32[16,1,2048]{2,1,0:T(1,128)} %get-tuple-element.51.l_in, ...), custom_call_target="tpu_custom_call" | custom-call | flops 52800000000 | tf_op jit(solution)/shard_map/remote_forward/pallas_call | solution.py:867
  164.3 0.0 all-gather.4.cloned.1.call-done.wout_ref
  164.4 0.0 all-gather.6.cloned.1.call-done.up_ref
  164.4 0.0 all-gather.8.cloned.1.call-done.down_ref
  164.4 100.4 %feed.1 = (bf16[2048,768]{1,0:T(8,128)(2,1)}, f32[2048,768]{1,0:T(8,128)}, bf16[768,2048]{1,0:T(8,128)(2,1)}, f32[16,1,2048]{2,1,0:T(1,128)}, f32[2,768]{1,0:T(2,128)}, /*index=5*/bf16[4,648,16,128]{3,2,1,0:T(8,128)(2,1)}) custom-call(s32[1]{0:T(128)} %bitcast.mask_ref, bf16[768,2048]{1,0:T(8,128)(2,1)} %get-tuple-element.56.att_ref, ...), custom_call_target="tpu_custom_call" | custom-call | flops 99000000512 | tf_op jit(solution)/shard_map/feed/pallas_call | solution.py:1283
  264.8 28.0 %remote_backward.1 = (f32[768,512]{1,0:T(8,128)}, bf16[1,2,768,512]{3,2,1,0:T(8,128)(2,1)}, bf16[2,2,768,256]{3,2,1,0:T(8,128)(2,1)}, bf16[4,2,768,128]{3,2,1,0:T(8,128)(2,1)}) custom-call(s32[1]{0:T(128)} %bitcast.mask_ref, bf16[3,768,2048]{2,1,0:T(8,128)(2,1)} %get-tuple-element.46.q_ref.k_ref.v_ref, bf16[768,2048]{1,0:T(8,128)(2,1)} %get-tuple-element.60.g_ref, ...), custom_call_target="tpu_custom_call" | custom-call | flops 44000002048 | tf_op jit(solution)/shard_map/remote_backward/pallas_call | solution.py:893
  292.8 156.6 %local_backward.1 = (f32[3,768,2048]{2,1,0:T(8,128)}, bf16[2,768,512]{2,1,0:T(8,128)(2,1)}, bf16[2,768,256]{2,1,0:T(8,128)(2,1)}, bf16[2,768,128]{2,1,0:T(8,128)...) custom-call(s32[1]{0:T(128)} %bitcast.mask_ref, ...), custom_call_target="tpu_custom_call" | custom-call | flops 158400004096 | tf_op jit(solution)/shard_map/local_backward/pallas_call | solution.py:941
  449.4 77.6 %inner_back.1 = (f32[192,2304]{1,0:T(8,128)}, f32[2048,768]{1,0:T(8,128)}, f32[8,768]{1,0:T(8,128)}) custom-call(f32[3,768,2048]{2,1,0:T(8,128)} %get-tuple-element.68.local_ref, bf16[768,2048]{1,0:T(8,128)(2,1)} %get-tuple-element.69.inner_ref, bf16[768,2304]{1,0:T(8,128)(2,1)} %bitcast.17, bf16[2048,768]{1,0:T(8,128)(2,1)} %get-tuple-element.57.x_ref, ...), custom_call_target="tpu_custom_call" | custom-call | flops 32999999488 | tf_op jit(solution)/shard_map/inner_back/pallas_call | solution.py:1464
  527.0 1.5 fusion
  528.5 0.0 copy-start.2
  528.5 6.0 %copy.26 = f32[1,2048,768]{2,1,0:T(8,128)} copy(f32[1,2048,768]{2,1,0:T(8,128)} %bitcast.10) | data formatting | bytes 12582912
  534.6 0.0 copy-done.2
  534.6 0.0 copy-start.3
  534.6 0.0 copy-start.1
  534.6 1.2 copy.27
  535.8 0.2 copy-done.3
  536.0 0.8 copy.28
  536.8 0.4 copy-done.1
  537.2 0.0 copy-start
  537.2 1.4 copy.29
  538.6 1.1 copy-done
  539.7 1.4 copy.30
Async XLA Ops:
  7.2 2.3 copy-start.5
  7.2 2.8 copy-start.6
  7.2 3.4 copy-start.7
  7.2 4.0 copy-start.8
  7.2 4.5 copy-start.4
  7.2 157.1 %all-gather.4.cloned.1.call-start = ((), (), s32[]{:S(2)}) async-start(), calls=%async_computation | async-start | bytes 1474560 | tf_op jit(solution)/shard_map/all_gather | solution.py:1526
  8.0 156.4 %all-gather.6.cloned.1.call-start = ((), (), s32[]{:S(2)}) async-start(), calls=%async_computation.1 | async-start | bytes 5898240 | tf_op jit(solution)/shard_map/all_gather | solution.py:1526
  8.7 155.7 %all-gather.8.cloned.1.call-start = ((), (), s32[]{:S(2)}) async-start(), calls=%async_computation.2 | async-start | bytes 5898240 | tf_op jit(solution)/shard_map/all_gather | solution.py:1526
  528.5 6.0 %copy-start.2 = (f32[192,2304]{1,0:T(8,128)S(1)}, f32[192,2304]{1,0:T(8,128)}, u32[]{:S(2)}) copy-start(f32[192,2304]{1,0:T(8,128)} %get-tuple-element.100) | copy-start | bytes 5308420
  534.6 1.4 copy-start.3
  534.6 2.7 copy-start.1
  537.2 2.5 copy-start
Sparse Core Ops, SparseCore 0:
  9.6 26.5 all-gather.3
  37.8 37.4 all-gather.5
  76.9 37.4 all-gather.7

commit v5 on v4

--- a/solution.py
+++ b/solution.py
@@ -194,14 +194,13 @@
         return [("seq", distance) for distance in sorted(self.distances)]
 
     def start(self):
-        for hops in self.hops:
+        for hops in reversed(self.hops):
             hops[0].start()
 
-    def pass_on(self, turn):
-        for hops in self.hops:
-            if turn < len(hops):
-                hops[turn - 1].wait_recv()
-                hops[turn].start()
+    def pass_on(self, index, turn):
+        hops = self.hops[index]
+        hops[turn - 1].wait_recv()
+        hops[turn].start()
 
     def finish(self):
         for hops in self.hops:
@@ -210,7 +209,12 @@
             hops[-1].wait_recv()
 
     def turns(self):
-        return max(len(hops) for hops in self.hops)
+        events = []
+        for index, hops in reversed(list(enumerate(self.hops))):
+            for turn in range(1, len(hops)):
+                when = 4 * turn + (2 if turn > 1 else 0) + (len(self.hops) - 1 - index)
+                events.append((when, functools.partial(self.pass_on, index, turn)))
+        return events
 
 
 class Return:
@@ -238,14 +242,15 @@
             plan.append((add, sends.copy((level, 0), buf.at[0], returned[i], "seq", group)))
             self.plans.append((plan, load))
 
-    def start(self):
-        for plan, load in self.plans:
-            if load is not None:
-                load.start()
-            plan[0][1].start()
+    def start(self, direct):
+        for plan, load in reversed(self.plans):
+            if direct == (load is None):
+                if load is not None:
+                    load.start()
+                plan[0][1].start()
 
     def turn(self, number):
-        for plan, load in self.plans:
+        for plan, load in reversed(self.plans):
             if number < len(plan):
                 plan[number - 1][1].wait_recv()
                 if number == 1 and load is not None:
@@ -277,39 +282,49 @@
     lax.fori_loop(0, count // unit, body, 0)
 
 
-def copy_blocks(into, other, at, count):
+def copy_blocks(into, at, other, start, count):
     unit = max(u for u in range(1, 13) if count % u == 0)
 
     def body(i, carry):
-        rows = pl.ds(at + i * unit, unit)
-        into[rows] = other[rows]
+        into[pl.ds(at + i * unit, unit)] = other[pl.ds(start + i * unit, unit)]
         return carry
 
     lax.fori_loop(0, count // unit, body, 0)
 
 
+def halving(blocks, order):
+    seq = lax.axis_index("seq")
+    low, given = [0], []
+    for j, distance in enumerate(order):
+        bit = lax.rem(lax.div(seq, distance), 2)
+        half = blocks >> (j + 1)
+        given.append(low[j] + (1 - bit) * half)
+        low.append(low[j] + bit * half)
+    return low, given
+
+
+def orders():
+    plain = [2**j for j in range(seq_bits())]
+    return [plain] * (CHUNKS - 1) + [plain[1:] + plain[:1]]
+
+
+def all_peers():
+    return [("fsdp", 1), ("fsdp", 2)] + [("seq", 2**j) for j in range(seq_bits())]
+
+
 class Reduce:
-    def __init__(self, chunks, blocks, source, terms, own, recv_core, recv_x, recv_seq, total, sends, loads=None):
-        self.chunks, self.blocks, self.source, self.terms, self.own = chunks, blocks, source, terms, own
-        self.recv_core, self.recv_x, self.recv_seq, self.total = recv_core, recv_x, recv_seq, total
+    def __init__(self, blocks, source, terms, own, recv_core, recv_x, recv_seq, sends, done, loads=None):
+        self.blocks, self.source, self.terms, self.own, self.done = blocks, source, terms, own, done
+        self.recv_core, self.recv_x, self.recv_seq = recv_core, recv_x, recv_seq
         self.sends, self.loads = sends, loads
         fsdp = lax.axis_index("fsdp")
         self.core, self.x = lax.rem(fsdp, 2), lax.div(fsdp, 2)
         self.bits = seq_bits()
-        seq = lax.axis_index("seq")
-        self.low = [0]
-        self.given = []
-        for j in range(self.bits):
-            bit = lax.rem(lax.div(seq, 2**j), 2)
-            half = blocks >> (j + 1)
-            self.given.append(self.low[j] + (1 - bit) * half)
-            self.low.append(self.low[j] + bit * half)
-
-    def peers(self):
-        return [("fsdp", 1), ("fsdp", 2)] + [("seq", 2**j) for j in range(self.bits)]
+        self.orders = orders()
+        self.halves = [halving(blocks, order) for order in self.orders]
 
     def stages(self):
-        return 2 + 2 * self.bits
+        return 2 + self.bits
 
     def core_copy(self, chunk, xo):
         rows = pl.ds(chunk * self.blocks, self.blocks)
@@ -333,15 +348,12 @@
     def down_copy(self, chunk, j):
         half = self.blocks >> (j + 1)
         base = chunk * self.blocks
-        rows = pl.ds(base + self.given[j], half)
+        rows = pl.ds(base + self.halves[chunk][1][j], half)
         into = pl.ds(base + self.blocks - (self.blocks >> j), half)
         return self.sends.copy(
-            ("down", chunk, j), self.terms.at[self.own(self.x), rows], self.recv_seq.at[into], "seq", 2**j
+            ("down", chunk, j), self.terms.at[self.own(self.x), rows], self.recv_seq.at[into], "seq",
+            self.orders[chunk][j],
         )
-
-    def up_copy(self, chunk, j):
-        rows = pl.ds(chunk * self.blocks + self.low[j + 1], self.blocks >> (j + 1))
-        return self.sends.copy(("up", chunk, j), self.total.at[rows], self.total.at[rows], "seq", 2**j)
 
     def begin(self, chunk):
         for xo in range(2):
@@ -351,6 +363,8 @@
 
     def event(self, stage, chunk):
         base = chunk * self.blocks
+        low = self.halves[chunk][0]
+        mine = self.terms.at[self.own(self.x)]
         if stage == 0:
             for xo in range(2):
                 self.core_copy(chunk, xo).wait_recv()
@@ -358,40 +372,59 @@
                     self.load_copy(chunk, xo).wait()
                 add_blocks(self.terms.at[self.own(xo)], base, self.recv_core.at[xo], base, self.blocks)
             self.x_copy(chunk).start()
-        elif stage < 2 + self.bits:
-            j = stage - 2
-            mine = self.terms.at[self.own(self.x)]
-            if stage == 1:
-                self.x_copy(chunk).wait_recv()
-                add_blocks(mine, base, self.recv_x, base, self.blocks)
-            else:
-                self.down_copy(chunk, j).wait_recv()
-                half = self.blocks >> (j + 1)
-                add_blocks(
-                    mine, base + self.low[j + 1], self.recv_seq, base + self.blocks - (self.blocks >> j), half
-                )
-            if j + 1 < self.bits:
-                self.down_copy(chunk, j + 1).start()
-            else:
-                copy_blocks(self.total, mine, base + self.low[self.bits], self.blocks >> self.bits)
-                self.up_copy(chunk, self.bits - 1).start()
+            return
+        j = stage - 2
+        if stage == 1:
+            self.x_copy(chunk).wait_recv()
+            add_blocks(mine, base, self.recv_x, base, self.blocks)
         else:
-            j = 2 * self.bits + 1 - stage
-            self.up_copy(chunk, j).wait_recv()
-            if j:
-                self.up_copy(chunk, j - 1).start()
+            self.down_copy(chunk, j).wait_recv()
+            half = self.blocks >> (j + 1)
+            add_blocks(mine, base + low[j + 1], self.recv_seq, base + self.blocks - (self.blocks >> j), half)
+        if j + 1 < self.bits:
+            self.down_copy(chunk, j + 1).start()
+        else:
+            self.done(chunk, mine, base + low[self.bits])
 
     def finish(self):
-        for chunk in range(self.chunks):
+        for chunk in range(CHUNKS):
             for xo in range(2):
                 self.core_copy(chunk, xo).wait_send()
             self.x_copy(chunk).wait_send()
             for j in range(self.bits):
                 self.down_copy(chunk, j).wait_send()
-                self.up_copy(chunk, j).wait_send()
-
-    def copies(self):
-        return self.chunks * (3 + 2 * self.bits)
+
+
+class Spread:
+    def __init__(self, blocks, total, sends):
+        self.blocks, self.total, self.sends = blocks, total, sends
+        self.bits = seq_bits()
+        self.orders = orders()
+        self.lows = [halving(blocks, order)[0] for order in self.orders]
+
+    def stages(self):
+        return self.bits
+
+    def copy(self, chunk, j):
+        rows = pl.ds(chunk * self.blocks + self.lows[chunk][j + 1], self.blocks >> (j + 1))
+        here = self.total.at[rows]
+        return self.sends.copy((chunk, j), here, here, "seq", self.orders[chunk][j])
+
+    def begin(self, chunk, ref, start):
+        size = self.blocks >> self.bits
+        copy_blocks(self.total, chunk * self.blocks + self.lows[chunk][self.bits], ref, start, size)
+        self.copy(chunk, self.bits - 1).start()
+
+    def event(self, stage, chunk):
+        j = self.bits - 1 - stage
+        self.copy(chunk, j).wait_recv()
+        if j:
+            self.copy(chunk, j - 1).start()
+
+    def finish(self):
+        for chunk in range(CHUNKS):
+            for j in range(self.bits):
+                self.copy(chunk, j).wait_send()
 
 
 def run_schedule(step, last, events):
@@ -469,10 +502,7 @@
         meet(gather.peers())
         gather.start()
 
-    events = [(0, begin)]
-    for turn in range(1, gather.turns()):
-        events.append((2 + 4 * turn, functools.partial(gather.pass_on, turn)))
-    run_schedule(head, HEADS - 1, events)
+    run_schedule(head, HEADS - 1, [(0, begin)] + sorted(gather.turns(), key=lambda event: event[0]))
     local_forward_core(nseg, mask_ref, q_ref, k_ref, v_ref, o_ref, l_ref, m_ref, qa, ka, va)
     run_schedule(head, HEADS - 1, [(HEADS - 1, gather.finish)])
 
@@ -630,36 +660,34 @@
 def local_backward(nseg, first, mask_ref, q_ref, k_ref, v_ref, g_ref, lse_ref, slope_ref, dqr_ref, *refs):
     n = BRANCHES - first
     sent, feed_ref, out_ref = refs[:n], refs[n], refs[n + 1]
-    returned, (up_ref, proj_ref, down_ref) = refs[n + 2 : 2 * n + 2], refs[2 * n + 2 : 2 * n + 5]
-    qa, ga, ka, va, dk, dv = refs[2 * n + 5 : 2 * n + 11]
-    rest = list(refs[2 * n + 11 :])
+    returned, piece_ref = refs[n + 2 : 2 * n + 2], refs[2 * n + 2]
+    qa, ga, ka, va, dk, dv = refs[2 * n + 3 : 2 * n + 9]
+    rest = list(refs[2 * n + 9 :])
     back_send, back_recv, back_load, red_send, red_recv, red_load = rest[-6:]
-    terms, recv_core, recv_x, recv_seq, total = rest[-11:-6]
-    bufs, recvs = rest[: (len(rest) - 11) // 2], rest[(len(rest) - 11) // 2 : -11]
+    terms, recv_core, recv_x, recv_seq = rest[-10:-6]
+    bufs, recvs = rest[: (len(rest) - 10) // 2], rest[(len(rest) - 10) // 2 : -10]
     head = pl.program_id(0)
     last = HEADS - 1
-    length = nseg * SEG
 
     back = Return(nseg, first, sent, returned, bufs, recvs, back_load, Sends(back_send, back_recv))
     blocks = terms.shape[1] // CHUNKS
     reduce = Reduce(
-        CHUNKS, blocks, feed_ref, terms, lambda xo: xo, recv_core, recv_x, recv_seq, total,
-        Sends(red_send, red_recv), red_load,
+        blocks, feed_ref, terms, lambda xo: xo, recv_core, recv_x, recv_seq, Sends(red_send, red_recv),
+        lambda chunk, ref, start: copy_blocks(piece_ref.at[chunk], 0, ref, start, blocks >> seq_bits()),
+        red_load,
     )
 
     def begin():
-        meet(reduce.peers())
-        back.start()
+        meet(all_peers())
+        back.start(False)
         for chunk in range(CHUNKS):
             reduce.begin(chunk)
 
-    events = [(2 * turn, functools.partial(back.turn, turn)) for turn in range(1, back.turns())]
+    events = [(3 * turn, functools.partial(back.turn, turn)) for turn in range(1, back.turns())]
+    events.append((8, functools.partial(back.start, True)))
     for chunk in range(CHUNKS):
         for stage in range(reduce.stages()):
-            if stage == 0:
-                when = 1 + (chunk + 1) // 2
-            else:
-                when = 3 + 2 * chunk + stage + (stage >= 2) + (stage == reduce.stages() - 1)
+            when = 1 + (chunk + 1) // 2 if stage == 0 else 4 + 3 * chunk + 2 * (stage - 1)
             events.append((when, functools.partial(reduce.event, stage, chunk)))
     run_schedule(head, last, [(0, begin)] + sorted(events, key=lambda event: event[0]))
     local_backward_core(
@@ -671,13 +699,6 @@
     def _():
         back.finish()
         reduce.finish()
-        for tile in range(TILES):
-            cols = slice(tile * 128, (tile + 1) * 128)
-            for col in range(4):
-                at = col * 72 + tile * 12
-                up_ref[:, col * D + tile * 128 : col * D + (tile + 1) * 128] = rows_of(total, at, 12)
-            proj_ref[:, cols] = rows_of(total, 288 + tile * 12, 12)
-            down_ref[:, cols] = rows_of(total, 360 + tile * 48, 48)
 
 
 def local_backward_scratch(nseg):
@@ -740,7 +761,7 @@
 
 
 def rows_of(total, at, count):
-    return total[at : at + count].astype(F32).reshape(count * 16, 128)
+    return total[at : at + count].reshape(count * 16, 128)
 
 
 def remote_backward(nseg, first, mask_ref, q_ref, g_ref, lse_ref, slope_ref, *refs):
@@ -816,9 +837,9 @@
     return pltpu.SemaphoreType.DMA((count,))
 
 
-def talking(collective_id):
+def talking(collective_id, mebibytes=56):
     return pltpu.CompilerParams(
-        vmem_limit_bytes=VMEM_LIMIT, collective_id=collective_id, has_side_effects=True
+        vmem_limit_bytes=mebibytes * 1024 * 1024, collective_id=collective_id, has_side_effects=True
     )
 
 
@@ -927,7 +948,7 @@
 
 
 def reduce_copies():
-    return CHUNKS * (3 + 2 * seq_bits())
+    return CHUNKS * (3 + seq_bits())
 
 
 def call_local_backward(nseg, first, qkv, grad, lse, slope, mask, dq_remote, sent, feed_grads):
@@ -936,6 +957,7 @@
     groups = [part.shape[0] for part in sent]
     hops = sum(group.bit_length() for group in groups)
     blocks = feed_grads.shape[1]
+    piece = (CHUNKS, blocks // CHUNKS >> seq_bits(), 16, 128)
     bufs = [pltpu.VMEM((g // 2,) + part.shape[1:], BF16) for g, part in zip(groups, sent) if g > 1]
     recvs = [pltpu.VMEM((g - 1,) + part.shape[1:], BF16) for g, part in zip(groups, sent) if g > 1]
     local, *rest = pl.pallas_call(
@@ -946,17 +968,16 @@
         + [ANY_BLOCK] * (n + 1),
         out_specs=[pl.BlockSpec((3, HEAD_DIM, length), lambda h: (0, h, 0))]
         + [ANY_BLOCK] * n
-        + [const_block((192, 4 * D)), const_block((192, D)), const_block((D, D))],
+        + [const_block(piece)],
         out_shape=[shape((3, D, length), F32)]
         + [shape(part.shape[1:], BF16) for part in sent]
-        + [shape((192, 4 * D), F32), shape((192, D), F32), shape((D, D), F32)],
+        + [shape(piece, BF16)],
         scratch_shapes=local_backward_scratch(nseg)
         + bufs
         + recvs
         + [
             pltpu.VMEM((2, blocks, 16, 128), BF16),
             pltpu.VMEM((2, blocks, 16, 128), BF16),
-            pltpu.VMEM((blocks, 16, 128), BF16),
             pltpu.VMEM((blocks, 16, 128), BF16),
             pltpu.VMEM((blocks, 16, 128), BF16),
             sems(hops),
@@ -970,7 +991,7 @@
         cost_estimate=cost(nseg * 72e-6),
         name="local_backward",
     )(mask, qkv, qkv, qkv, grad, lse, slope, dq_remote, *sent, feed_grads)
-    return local, rest[:n], rest[n:]
+    return local, rest[:n], rest[n]
 
 
 HALF = D // 2
@@ -1326,30 +1347,36 @@
 STEPS = 6
 
 
-def inner_back_kernel(nseg, first, local_ref, inner_ref, w_ref, x_ref, gmid_ref, gain_ref, feed_vec_ref, *refs):
+def inner_back_kernel(
+    nseg, first, local_ref, inner_ref, w_ref, x_ref, gmid_ref, gain_ref, feed_vec_ref, piece_ref, *refs
+):
     n = BRANCHES - first
-    packs, (weight_ref, back_ref, vec_ref) = refs[:n], refs[n : n + 3]
-    acc, mixed, order, terms, recv_core, recv_x, recv_seq, total, vecs, vec_recv = refs[n + 3 : n + 13]
-    red_send, red_recv, vec_send, vec_recv_sems = refs[n + 13 :]
+    packs, (weight_ref, back_ref, vec_ref, up_ref, proj_ref, down_ref) = refs[:n], refs[n : n + 6]
+    acc, mixed, order, terms, recv_core, recv_x, recv_seq, total, feed_total, vecs, vec_recv = refs[n + 6 : n + 17]
+    red_send, red_recv, in_send, in_recv, feed_send, feed_recv, vec_send, vec_recv_sems = refs[n + 17 :]
     step = pl.program_id(0)
     last = pl.num_programs(0) - 1
     length = nseg * SEG
-    end = STEPS + length // ROWS
+    turns = length // ROWS
+    end = STEPS + turns
     blocks = terms.shape[1] // CHUNKS
     core = lax.rem(lax.axis_index("fsdp"), 2)
+    spread = Spread(blocks, total, Sends(in_send, in_recv))
     reduce = Reduce(
-        CHUNKS, blocks, terms, terms, lambda xo: 2 * xo + core, recv_core, recv_x, recv_seq, total,
-        Sends(red_send, red_recv),
+        blocks, terms, terms, lambda xo: 2 * xo + core, recv_core, recv_x, recv_seq, Sends(red_send, red_recv),
+        spread.begin,
     )
+    feed_spread = Spread(feed_total.shape[0] // CHUNKS, feed_total, Sends(feed_send, feed_recv))
     vec_sends = Sends(vec_send, vec_recv_sems)
+    peers = all_peers()
 
     def vec_copy(i):
-        return vec_sends.copy(i, vecs.at[i], vec_recv.at[i], *reduce.peers()[i])
+        return vec_sends.copy(i, vecs.at[i], vec_recv.at[i], *peers[i])
 
     def vec_event(i):
         vec_copy(i).wait_recv()
         vecs[i + 1] = vecs[i] + vec_recv[i]
-        if i + 1 < len(reduce.peers()):
+        if i + 1 < len(peers):
             vec_copy(i + 1).start()
 
     def vec_start():
@@ -1357,12 +1384,10 @@
 
     @pl.when(step == 0)
     def _():
-        meet(reduce.peers())
+        meet(peers)
         vecs[0] = jnp.concatenate([jnp.zeros((2, D), F32), feed_vec_ref[...], jnp.zeros((4, D), F32)], axis=0)
-
-    @pl.when(step < 2)
-    def _():
-        mixed[...] = local_ref[0].astype(BF16)
+        for chunk in reversed(range(CHUNKS)):
+            feed_spread.begin(chunk, piece_ref.at[chunk], 0)
 
     @pl.when((step >= 2) & (step < STEPS))
     def _():
@@ -1380,47 +1405,34 @@
                             [jnp.where(upper, zero, piece), jnp.where(upper, piece, zero)], axis=1
                         )
                     local_ref[0, rows, start : start + piece.shape[1]] += piece
-        mixed[...] = local_ref[0].astype(BF16)
 
     @pl.when(step < STEPS)
     def _():
-        grad_in = dotg(inner_ref[...], mixed[...], 1, 1).astype(BF16)
+        block = local_ref[0].astype(BF16)
+        mixed[pl.ds(pl.multiple_of(step * HALF, HALF), HALF), :] = block
         base = lax.div(step, 2) * blocks + lax.rem(step, 2) * 36
+        grad_in = dotg(block, inner_ref[...], 1, 1).T.astype(BF16)
         for col in range(3):
             part = grad_in[:, col * 128 : (col + 1) * 128].reshape(4, 12, 16, 128)
             for owner in range(4):
                 terms[owner, pl.ds(base + col * 12, 12)] = part[owner]
-        for start in range(0, length, 512):
-            lanes = slice(start, start + 512)
-            part = dotg(w_ref[...], mixed[:, lanes], 1, 0)
-
-            @pl.when(step == 0)
-            def _():
-                acc[:, lanes] = part
-
-            @pl.when(step > 0)
-            def _():
-                acc[:, lanes] += part
-
-    events = []
-    for chunk in range(CHUNKS):
-        begin = 2 * chunk + 1
-        events.append((begin, functools.partial(reduce.begin, chunk)))
-        for stage in range(reduce.stages()):
-            when = begin + 1 + stage + (1 if stage else 0) + max(0, stage - 1 - chunk)
-            events.append((when, functools.partial(reduce.event, stage, chunk)))
-    events.append((end - 1, vec_start))
-    for i in range(len(reduce.peers())):
-        events.append((end + i, functools.partial(vec_event, i)))
-    events.sort(key=lambda event: event[0])
+
+    def inner_grad(turn):
+        lanes = pl.ds(pl.multiple_of(turn * ROWS, ROWS), ROWS)
+        acc[lax.rem(turn, 2)] = dotg(w_ref[...], mixed[:, lanes], 1, 0)
+
+    @pl.when(step == STEPS - 1)
+    def _():
+        inner_grad(step - (STEPS - 1))
 
     @pl.when((step >= STEPS) & (step < end))
     def _():
         turn = step - STEPS
+        inner_grad(lax.rem(turn + 1, turns))
         quarter = lax.rem(turn, 4)
         low = (quarter >> 1) | ((quarter & 1) << 1)
         gain = gain_ref[0:1, :]
-        grad = acc[:, pl.ds(pl.multiple_of(turn * ROWS, ROWS), ROWS)].T
+        grad = acc[lax.rem(turn, 2)].T
         _, unit, inverse = normalize(x_ref[...].astype(F32), gain, gain)
         back, gain_part, shift_part = normalize_back(grad, unit, inverse, gain)
         vecs[0, 0:1, :] += gain_part[None, :]
@@ -1433,27 +1445,57 @@
         def _():
             back_ref[...] = get_rows(order, 0, SEG)
 
-    run_schedule(step, last, events)
+    events = []
+    for chunk in range(CHUNKS):
+        for stage in range(feed_spread.stages()):
+            events.append((1 + stage, functools.partial(feed_spread.event, stage, chunk)))
+    for chunk in range(CHUNKS):
+        begin = 2 * chunk + 1
+        events.append((begin, functools.partial(reduce.begin, chunk)))
+        for stage in range(reduce.stages()):
+            when = begin + 1 + (0 if stage == 0 else 3 * chunk + 2 * stage)
+            events.append((when, functools.partial(reduce.event, stage, chunk)))
+        for stage in range(spread.stages()):
+            when = begin + 2 * reduce.stages() + 3 * chunk + 2 * stage
+            events.append((when, functools.partial(spread.event, stage, chunk)))
+    events.append((end - 1, vec_start))
+    for i in range(len(peers)):
+        events.append((end + i, functools.partial(vec_event, i)))
+    run_schedule(step, last, sorted(events, key=lambda event: event[0]))
+
+    @pl.when(step == end - 2)
+    def _():
+        for tile in range(TILES):
+            cols = slice(tile * 128, (tile + 1) * 128)
+            for col in range(4):
+                at = col * 72 + tile * 12
+                up_ref[:, col * D + tile * 128 : col * D + (tile + 1) * 128] = rows_of(feed_total, at, 12)
+            proj_ref[:, cols] = rows_of(feed_total, 288 + tile * 12, 12)
+            down_ref[:, cols] = rows_of(feed_total, 360 + tile * 48, 48)
 
     @pl.when(step == last)
     def _():
         reduce.finish()
-        for i in range(len(reduce.peers())):
+        spread.finish()
+        feed_spread.finish()
+        for i in range(len(peers)):
             vec_copy(i).wait_send()
-        vec_ref[...] = vecs[len(reduce.peers())]
+        vec_ref[...] = vecs[len(peers)]
         for part in range(STEPS):
             for col in range(3):
                 at = part // 2 * blocks + part % 2 * 36 + col * 12
                 weight_ref[:, part * HALF + col * 128 : part * HALF + (col + 1) * 128] = rows_of(total, at, 12)
 
 
-def call_inner_back(nseg, first, local, inner, weight, x, gmid, gain, feed_vec, packs):
+def call_inner_back(nseg, first, local, inner, weight, x, gmid, gain, feed_vec, pieces, packs):
     length = nseg * SEG
     turns = length // ROWS
     blocks = padded(IN_BLOCKS)
     if blocks // CHUNKS < 72:
         raise ValueError("blocks")
-    peers = 2 + seq_bits()
+    bits = seq_bits()
+    peers = 2 + bits
+    feed_blocks = CHUNKS * (pieces.shape[1] << bits)
 
     def at(i):
         return jnp.minimum(i, STEPS - 1)
@@ -1467,11 +1509,12 @@
         in_specs=[
             pl.BlockSpec((1, HALF, length), lambda i: (at(i) // 2, at(i) % 2, 0)),
             const_block((D, length)),
-            pl.BlockSpec((D, HALF), lambda i: (0, at(i))),
+            const_block((D, 3 * D)),
             pl.BlockSpec((ROWS, D), lambda i: (turn(i), 0)),
             pl.BlockSpec((ROWS, D), lambda i: (turn(i), 0)),
             const_block((8, D)),
             const_block((2, D)),
+            const_block(pieces.shape),
         ]
         + [
             pl.BlockSpec((1, HALF, pack.shape[2]), lambda i: (jnp.maximum(at(i) // 2 - 1, 0), at(i) % 2, 0))
@@ -1481,28 +1524,43 @@
             const_block((192, 3 * D)),
             pl.BlockSpec((SEG, D), lambda i: (turn(i) // 4, 0)),
             const_block((8, D)),
+            const_block((192, 4 * D)),
+            const_block((192, D)),
+            const_block((D, D)),
         ],
-        out_shape=[shape((192, 3 * D), F32), shape((length, D), F32), shape((8, D), F32)],
+        out_shape=[
+            shape((192, 3 * D), BF16),
+            shape((length, D), F32),
+            shape((8, D), F32),
+            shape((192, 4 * D), BF16),
+            shape((192, D), BF16),
+            shape((D, D), BF16),
+        ],
         scratch_shapes=[
-            pltpu.VMEM((D, length), F32),
-            pltpu.VMEM((HALF, length), BF16),
+            pltpu.VMEM((2, D, ROWS), F32),
+            pltpu.VMEM((3 * D, length), BF16),
             pltpu.VMEM((TILES, SEG, 128), F32),
             pltpu.VMEM((4, blocks, 16, 128), BF16),
             pltpu.VMEM((2, blocks, 16, 128), BF16),
             pltpu.VMEM((blocks, 16, 128), BF16),
             pltpu.VMEM((blocks, 16, 128), BF16),
             pltpu.VMEM((blocks, 16, 128), BF16),
+            pltpu.VMEM((feed_blocks, 16, 128), BF16),
             pltpu.VMEM((peers + 1, 8, D), F32),
             pltpu.VMEM((peers, 8, D), F32),
             sems(reduce_copies()),
             sems(reduce_copies()),
+            sems(CHUNKS * bits),
+            sems(CHUNKS * bits),
+            sems(CHUNKS * bits),
+            sems(CHUNKS * bits),
             sems(peers),
             sems(peers),
         ],
-        compiler_params=talking(3),
+        compiler_params=talking(3, 60),
         cost_estimate=cost(nseg * 15e-6),
         name="inner_back",
-    )(local, inner, weight, x, gmid, gain, feed_vec, *packs)
+    )(local, inner, weight, x, gmid, gain, feed_vec, pieces, *packs)
 
 
 def per_device(
@@ -1525,15 +1583,13 @@
     def gather(weight):
         return lax.all_gather(weight, "fsdp", axis=0, tiled=True)
 
-    weight_out = gather(project_out)
-    weight_up = gather(up_weight)
-    weight_down = gather(down_weight)
-
     mask = jnp.sum(valid_mask[0])[None]
 
     vectors = [vector[None, :] for vector in (first_gain, first_shift, second_gain, second_shift)]
     qkv, x, inner, weight_in, gains, *packs = call_project(nseg, first, mask, tokens[0], vectors, project_in)
     weight_in = weight_in.reshape(D, 3 * D)
+    _, *shards = lax.optimization_barrier((gains, project_out, up_weight, down_weight))
+    weight_out, weight_up, weight_down = (gather(shard) for shard in shards)
     o_part, l_part, m_part, gathered = call_local_forward(nseg, first, qkv, mask, packs)
     attended, lse = call_remote_forward(nseg, first, qkv, mask, o_part, l_part, m_part, gathered)
 
@@ -1542,11 +1598,11 @@
     )
 
     dq_remote, *sent = call_remote_backward(nseg, first, qkv, grad_merged, lse, along, mask, gathered)
-    local, returned, (grad_up, grad_out, grad_down) = call_local_backward(
+    local, returned, pieces = call_local_backward(
         nseg, first, qkv, grad_merged, lse, along, mask, dq_remote, sent, feed_grads
     )
-    grad_in, tokens_back, vectors = call_inner_back(
-        nseg, first, local, inner, weight_in, x, grad_middle, gains, feed_vec, returned
+    grad_in, tokens_back, vectors, grad_up, grad_out, grad_down = call_inner_back(
+        nseg, first, local, inner, weight_in, x, grad_middle, gains, feed_vec, pieces, returned
     )
     quarter = D // lax.axis_size("fsdp")
     vectors = lax.dynamic_slice_in_dim(vectors, lax.axis_index("fsdp") * quarter, quarter, 1)
@@ -1555,12 +1611,12 @@
         tokens_back[None],
         vectors[0],
         vectors[1],
-        grad_in,
-        grad_out,
+        grad_in.astype(F32),
+        grad_out.astype(F32),
         vectors[2],
         vectors[3],
-        grad_up,
-        grad_down,
+        grad_up.astype(F32),
+        grad_down.astype(F32),
     )
 
 

time: 557 us -> 514 us (0.923)
  Pallas kernels: 514 us -> 471 us
  other arithmetic: 0.68 us -> 8.24 us
  local copies, waits for them, and re-layouts: 16.4 us -> 9.1 us
    pallas_call x1, Pallas kernels: 157 us -> 107 us  [call_local_backward(): pl.pallas_call(functools.partial(local_backward, nseg, first), grid=(HEAD...]
    pallas_call x1, Pallas kernels: 77.6 us -> 106 us  [call_inner_back(): pl.pallas_call(functools.partial(inner_back_kernel, nseg, first), grid=(S...]
    pallas_call x1, Pallas kernels: 87.8 us -> 70.8 us  [call_local_forward(): pl.pallas_call(functools.partial(local_forward, nseg, first), grid=(HEADS...]
    unnamed x23 -> x9, local copies, waits for them, and re-layouts: 12.6 us -> 2.72 us
    convert_element_type x0 -> x4, other arithmetic: none -> 6.83 us  [the longest x1 3.08 us: per_device(): grad_up.astype(F32)]
    pallas_call x1, Pallas kernels: 41.3 us -> 35.3 us  [call_project(): pl.pallas_call(functools.partial(project_kernel, nseg, first), grid=(6,),...]
  transfers between devices with their start and end apart: 3 -> 3, of which waited for: 0 -> 1; matrix products, arithmetic and copies ran while one was open for 1% -> 0% of each run, Pallas kernels for 28% -> 19%
where the time goes in v5:
time: 514 us; the launch traced here: 506 us
  Pallas kernels  471 us (92%)
  between operations  14.3 us (3%)
  local copies, waits for them, and re-layouts  9.1 us (2%)
  other arithmetic  8.24 us (2%)
    pallas_call x1, Pallas kernels, call_local_backward(): pl.pallas_call(functools.partial(local_backward, nseg, first), grid=(HEAD...  107 us
    pallas_call x1, Pallas kernels, call_inner_back(): pl.pallas_call(functools.partial(inner_back_kernel, nseg, first), grid=(S...  106 us
    pallas_call x1, Pallas kernels, call_feed(): pl.pallas_call(functools.partial(feed_kernel, nseg), grid=(length // ROWS...  100 us
    pallas_call x1, Pallas kernels, call_local_forward(): pl.pallas_call(functools.partial(local_forward, nseg, first), grid=(HEADS...  70.8 us
    pallas_call x1, Pallas kernels, call_project(): pl.pallas_call(functools.partial(project_kernel, nseg, first), grid=(6,),...  35.3 us
    pallas_call x1, Pallas kernels, call_remote_backward(): pl.pallas_call(functools.partial(remote_backward, nseg, first), grid=(HEA...  28.1 us
    pallas_call x1, Pallas kernels, call_remote_forward(): pl.pallas_call(functools.partial(remote_forward, nseg, first), grid=(HEAD...  22.9 us
  transfers between devices with their start and end apart: 3, of which 1 were waited for; matrix products, arithmetic and copies ran while one was open for 0% of the time, Pallas kernels for 19%

profile of v5, /device:TPU:0, one launch (start us, length us, event | category | flops | bytes accessed | tf_op | source)
XLA Modules:
  0.0 505.8 jit_solution(8246708557343953371)
XLA Ops:
  7.2 0.0 all-gather.4.cloned.1.call-start
  7.2 1.2 broadcast_in_dim.22.refs_0_
  8.4 1.2 broadcast_in_dim.23.refs_1_
  9.7 1.2 broadcast_in_dim.24.refs_2_
  10.9 1.2 broadcast_in_dim.25.refs_3_
  12.1 1.4 reduce_sum.9
  13.5 35.3 %project.1 = (bf16[3,768,2048]{2,1,0:T(8,128)(2,1)}, bf16[2048,768]{1,0:T(8,128)(2,1)}, bf16[768,2048]{1,0:T(8,128)(2,1)}, bf16[4,192,2304]{2,1,0:T(8,128)(2,1)}...) custom-call(s32[1]{0:T(128)} %bitcast.mask_ref, ...), custom_call_target="tpu_custom_call" | custom-call | flops 22000001024 | tf_op jit(solution)/shard_map/project/pallas_call | solution.py:1159
  48.8 0.0 all-gather.4.cloned.1.call-update
  48.8 0.0 all-gather.6.cloned.1.call-start
  48.9 0.7 all-gather.6.cloned.1.call-update
  49.6 0.0 all-gather.8.cloned.1.call-start
  49.6 0.7 all-gather.8.cloned.1.call-update
  50.3 70.8 %local_forward.1 = (f32[768,2048]{1,0:T(8,128)}, f32[16,1,2048]{2,1,0:T(1,128)}, f32[16,1,2048]{2,1,0:T(1,128)}, bf16[1,1552,512]{2,1,0:T(8,128)(2,1)}, bf16[2,1...) custom-call(s32[1]{0:T(128)} %bitcast.mask_ref, bf16[3,768,2048]{2,1,0:T(8,128)(2,1)} %get-tuple-element.50.q_ref.k_ref.v_ref, ...), custom_call_target="tpu_custom_call" | custom-call | flops 81399996416 | tf_op jit(solution)/shard_map/local_forward/pallas_call | solution.py:862
  121.1 22.9 %remote_forward.1 = (bf16[768,2048]{1,0:T(8,128)(2,1)}, f32[16,1,2048]{2,1,0:T(1,128)}) custom-call(s32[1]{0:T(128)} %bitcast.mask_ref, bf16[3,768,2048]{2,1,0:T(8,128)(2,1)} %get-tuple-element.50.q_ref.k_ref.v_ref, f32[768,2048]{1,0:T(8,128)} %get-tuple-element.54.o_in, f32[16,1,2048]{2,1,0:T(1,128)} %get-tuple-element.55.l_in, ...), custom_call_target="tpu_custom_call" | custom-call | flops 52800000000 | tf_op jit(solution)/shard_map/remote_forward/pallas_call | solution.py:888
  144.0 0.0 all-gather.4.cloned.1.call-done.wout_ref
  144.1 0.0 all-gather.6.cloned.1.call-done.up_ref
  144.1 2.1 all-gather.8.cloned.1.call-done.down_ref
  146.2 100.4 %feed.1 = (bf16[2048,768]{1,0:T(8,128)(2,1)}, f32[2048,768]{1,0:T(8,128)}, bf16[768,2048]{1,0:T(8,128)(2,1)}, f32[16,1,2048]{2,1,0:T(1,128)}, f32[2,768]{1,0:T(2,128)}, /*index=5*/bf16[4,648,16,128]{3,2,1,0:T(8,128)(2,1)}) custom-call(s32[1]{0:T(128)} %bitcast.mask_ref, bf16[768,2048]{1,0:T(8,128)(2,1)} %get-tuple-element.60.att_ref, ...), custom_call_target="tpu_custom_call" | custom-call | flops 99000000512 | tf_op jit(solution)/shard_map/feed/pallas_call | solution.py:1304
  246.6 28.1 %remote_backward.1 = (f32[768,512]{1,0:T(8,128)}, bf16[1,2,768,512]{3,2,1,0:T(8,128)(2,1)}, bf16[2,2,768,256]{3,2,1,0:T(8,128)(2,1)}, bf16[4,2,768,128]{3,2,1,0:T(8,128)(2,1)}) custom-call(s32[1]{0:T(128)} %bitcast.mask_ref, bf16[3,768,2048]{2,1,0:T(8,128)(2,1)} %get-tuple-element.50.q_ref.k_ref.v_ref, bf16[768,2048]{1,0:T(8,128)(2,1)} %get-tuple-element.67.g_ref, ...), custom_call_target="tpu_custom_call" | custom-call | flops 44000002048 | tf_op jit(solution)/shard_map/remote_backward/pallas_call | solution.py:914
  274.7 107.4 %local_backward.1 = (f32[3,768,2048]{2,1,0:T(8,128)}, bf16[2,768,512]{2,1,0:T(8,128)(2,1)}, bf16[2,768,256]{2,1,0:T(8,128)(2,1)}, bf16[2,768,128]{2,1,0:T(8,128)(2,1)}, bf16[3,27,16,128]{3,2,1,0:T(8,128)(2,1)}) custom-call(s32[1]{0:T(128)} %bitcast.mask_ref, bf16[3,768,2048]{2,1,0:T(8,128)(2,1)} %get-tuple-element.50.q_ref.k_ref.v_ref, ...), custom_call_target="tpu_custom_call" | custom-call | flops 158400004096 | tf_op jit(solution)/shard_map/local_backward/pallas_call | solution.py:963
  382.1 105.7 %inner_back.1 = (bf16[192,2304]{1,0:T(8,128)(2,1)}, f32[2048,768]{1,0:T(8,128)}, f32[8,768]{1,0:T(8,128)}, bf16[192,3072]{1,0:T(8,128)(2,1)}, bf16[192,768]{1,0:T(8,128)(2,1)}, /*index=5*/bf16[768,768]{1,0:T(8,128)(2,1)}) custom-call(f32[3,768,2048]{2,1,0:T(8,128)} %get-tuple-element.75.local_ref, bf16[768,2048]{1,0:T(8,128)(2,1)} %get-tuple-element.76.inner_ref, ...), custom_call_target="tpu_custom_call" | custom-call | flops 32999999488 | tf_op jit(solution)/shard_map/inner_back/pallas_call | solution.py:1506
  487.8 0.0 copy-start.1
  487.8 0.0 copy-start.2
  487.8 3.1 convert_element_type.14
  490.9 0.0 copy-start.3
  490.9 0.0 copy-done.1
  490.9 0.0 copy-start
  490.9 1.6 convert_element_type.15
  492.5 0.0 copy-done.2
  492.5 1.3 convert_element_type.12
  493.8 0.0 copy-done.3
  493.8 0.9 convert_element_type.13
  494.6 1.5 fusion
  496.1 0.0 copy-done
  496.1 2.7 copy.22
Async XLA Ops:
  7.2 136.9 %all-gather.4.cloned.1.call-start = ((), (), s32[]{:S(2)}) async-start(), calls=%async_computation | async-start | bytes 1474560 | tf_op jit(solution)/shard_map/all_gather | solution.py:1584
  48.8 95.2 %all-gather.6.cloned.1.call-start = ((), (), s32[]{:S(2)}) async-start(), calls=%async_computation.1 | async-start | bytes 5898240 | tf_op jit(solution)/shard_map/all_gather | solution.py:1584
  49.6 96.6 %all-gather.8.cloned.1.call-start = ((), (), s32[]{:S(2)}) async-start(), calls=%async_computation.2 | async-start | bytes 5898240 | tf_op jit(solution)/shard_map/all_gather | solution.py:1584
  487.8 3.1 copy-start.1
  487.8 4.7 copy-start.2
  490.9 2.9 copy-start.3
  490.9 5.3 %copy-start = (f32[2048,768]{1,0:T(8,128)S(1)}, f32[2048,768]{1,0:T(8,128)}, u32[]{:S(2)}) copy-start(f32[2048,768]{1,0:T(8,128)} %get-tuple-element.84) | copy-start | bytes 18874372
Sparse Core Ops, SparseCore 0:
  48.9 19.0 all-gather.3
  69.6 37.4 all-gather.5
  108.7 37.4 all-gather.7

commit v6 on v5

--- a/solution.py
+++ b/solution.py
@@ -215,6 +215,40 @@
                 when = 4 * turn + (2 if turn > 1 else 0) + (len(self.hops) - 1 - index)
                 events.append((when, functools.partial(self.pass_on, index, turn)))
         return events
+
+
+class Shards:
+    def __init__(self, shards, whole, sends, loads):
+        self.copies = []
+        me = lax.axis_index("fsdp")
+        other = lax.rem(me + 2, 4)
+        for i, (shard, into) in enumerate(zip(shards, whole)):
+            self.copies.append(
+                (
+                    pltpu.make_async_copy(shard, into.at[me], loads.at[i]),
+                    sends.copy((i, "core"), shard, into.at[me], "fsdp", 1),
+                    sends.copy((i, "x"), shard, into.at[me], "fsdp", 2),
+                    sends.copy((i, "hand"), into.at[other], into.at[other], "fsdp", 1),
+                )
+            )
+
+    def start(self):
+        for load, core, x, _ in self.copies:
+            load.start()
+            core.start()
+            x.start()
+
+    def hand(self, i):
+        _, _, x, hand = self.copies[i]
+        x.wait_recv()
+        hand.start()
+
+    def finish(self):
+        for load, core, x, hand in self.copies:
+            load.wait()
+            core.wait()
+            x.wait_send()
+            hand.wait()
 
 
 class Return:
@@ -303,24 +337,31 @@
     return low, given
 
 
-def orders():
+def feed_orders():
     plain = [2**j for j in range(seq_bits())]
     return [plain] * (CHUNKS - 1) + [plain[1:] + plain[:1]]
 
 
+def inner_orders():
+    plain = [2**j for j in range(seq_bits())]
+    return [plain] * (CHUNKS - 1) + [[plain[1], plain[0]] + plain[2:]]
+
+
 def all_peers():
     return [("fsdp", 1), ("fsdp", 2)] + [("seq", 2**j) for j in range(seq_bits())]
 
 
 class Reduce:
-    def __init__(self, blocks, source, terms, own, recv_core, recv_x, recv_seq, sends, done, loads=None):
+    def __init__(
+        self, orders, blocks, source, terms, own, recv_core, recv_x, recv_seq, sends, done, loads=None
+    ):
         self.blocks, self.source, self.terms, self.own, self.done = blocks, source, terms, own, done
         self.recv_core, self.recv_x, self.recv_seq = recv_core, recv_x, recv_seq
         self.sends, self.loads = sends, loads
         fsdp = lax.axis_index("fsdp")
         self.core, self.x = lax.rem(fsdp, 2), lax.div(fsdp, 2)
         self.bits = seq_bits()
-        self.orders = orders()
+        self.orders = orders
         self.halves = [halving(blocks, order) for order in self.orders]
 
     def stages(self):
@@ -396,10 +437,10 @@
 
 
 class Spread:
-    def __init__(self, blocks, total, sends):
+    def __init__(self, orders, blocks, total, sends):
         self.blocks, self.total, self.sends = blocks, total, sends
         self.bits = seq_bits()
-        self.orders = orders()
+        self.orders = orders
         self.lows = [halving(blocks, order)[0] for order in self.orders]
 
     def stages(self):
@@ -492,19 +533,27 @@
 
 def local_forward(nseg, first, mask_ref, q_ref, k_ref, v_ref, *refs):
     n = BRANCHES - first
-    packs, (o_ref, l_ref, m_ref), gathered = refs[:n], refs[n : n + 3], refs[n + 3 : 2 * n + 3]
-    qa, ka, va, send_sems, recv_sems = refs[2 * n + 3 :]
+    packs, shards, (o_ref, l_ref, m_ref) = refs[:n], refs[n : n + 3], refs[n + 3 : n + 6]
+    gathered, whole = refs[n + 6 : 2 * n + 6], refs[2 * n + 6 : 2 * n + 9]
+    qa, ka, va, send_sems, recv_sems, shard_send, shard_recv, shard_load = refs[2 * n + 9 :]
     head = pl.program_id(0)
-    length = nseg * SEG
     gather = Gather(nseg, first, packs, gathered, Sends(send_sems, recv_sems))
+    fetch = Shards(shards, whole, Sends(shard_send, shard_recv), shard_load)
 
     def begin():
-        meet(gather.peers())
+        meet(gather.peers() + [("fsdp", 1), ("fsdp", 2)])
         gather.start()
-
-    run_schedule(head, HEADS - 1, [(0, begin)] + sorted(gather.turns(), key=lambda event: event[0]))
+        fetch.start()
+
+    def finish():
+        gather.finish()
+        fetch.hand(2)
+        fetch.finish()
+
+    hands = [(3, functools.partial(fetch.hand, 0)), (10, functools.partial(fetch.hand, 1))]
+    run_schedule(head, HEADS - 1, [(0, begin)] + sorted(gather.turns() + hands, key=lambda event: event[0]))
     local_forward_core(nseg, mask_ref, q_ref, k_ref, v_ref, o_ref, l_ref, m_ref, qa, ka, va)
-    run_schedule(head, HEADS - 1, [(HEADS - 1, gather.finish)])
+    run_schedule(head, HEADS - 1, [(HEADS - 1, finish)])
 
 
 def local_forward_scratch(nseg):
@@ -672,7 +721,7 @@
     back = Return(nseg, first, sent, returned, bufs, recvs, back_load, Sends(back_send, back_recv))
     blocks = terms.shape[1] // CHUNKS
     reduce = Reduce(
-        blocks, feed_ref, terms, lambda xo: xo, recv_core, recv_x, recv_seq, Sends(red_send, red_recv),
+        feed_orders(), blocks, feed_ref, terms, lambda xo: xo, recv_core, recv_x, recv_seq, Sends(red_send, red_recv),
         lambda chunk, ref, start: copy_blocks(piece_ref.at[chunk], 0, ref, start, blocks >> seq_bits()),
         red_load,
     )
@@ -854,29 +903,34 @@
     return pl.CostEstimate(flops=int(seconds * 1.1e15), transcendentals=0, bytes_accessed=0)
 
 
-def call_local_forward(nseg, first, qkv, mask, packs):
+def call_local_forward(nseg, first, qkv, mask, packs, shards):
     length = nseg * SEG
     n = len(packs)
     groups = [(SEG << (level - 1)) // length for level in range(first, BRANCHES)]
     hops = sum(group.bit_length() for group in groups)
-    o_part, l_part, m_part, *gathered = pl.pallas_call(
+    o_part, l_part, m_part, *rest = pl.pallas_call(
         functools.partial(local_forward, nseg, first),
         grid=(HEADS,),
         in_specs=[MASK_BLOCK, part_block(0, length), part_block(1, length), part_block(2, length)]
-        + [ANY_BLOCK] * n,
-        out_specs=[head_block(length), row_block(length), row_block(length)] + [ANY_BLOCK] * n,
+        + [ANY_BLOCK] * (n + 3),
+        out_specs=[head_block(length), row_block(length), row_block(length)] + [ANY_BLOCK] * (n + 3),
         out_shape=[shape((D, length), F32), shape((HEADS, 1, length), F32), shape((HEADS, 1, length), F32)]
-        + [shape((group,) + pack.shape, BF16) for group, pack in zip(groups, packs)],
+        + [shape((group,) + pack.shape, BF16) for group, pack in zip(groups, packs)]
+        + [shape((4,) + shard.shape, BF16) for shard in shards],
         scratch_shapes=local_forward_scratch(nseg)
         + [
             sems(hops),
             sems(hops),
+            sems(9),
+            sems(9),
+            sems(3),
         ],
         compiler_params=talking(1),
         cost_estimate=cost(nseg * 37e-6),
         name="local_forward",
-    )(mask, qkv, qkv, qkv, *packs)
-    return o_part, l_part, m_part, gathered
+    )(mask, qkv, qkv, qkv, *packs, *shards)
+    whole = [weight.reshape(4 * weight.shape[1], weight.shape[2]) for weight in rest[n:]]
+    return o_part, l_part, m_part, rest[:n], whole
 
 
 def call_remote_forward(nseg, first, qkv, mask, o_part, l_part, m_part, packs):
@@ -1079,7 +1133,7 @@
                 barrier, inc=1, device_id={"fsdp": other}, device_id_type=pl.DeviceIdType.MESH
             )
         for i, vector in enumerate(vectors):
-            gains[me, i : i + 1, :192] = vector[...].astype(F32)
+            gains[me, i : i + 1, :192] = vector[...].astype(F32).reshape(1, 192)
         pl.semaphore_wait(barrier, 3)
         for copy in vec_copies():
             copy.start()
@@ -1159,7 +1213,7 @@
     return pl.pallas_call(
         functools.partial(project_kernel, nseg, first),
         grid=(6,),
-        in_specs=[MASK_BLOCK, const_block((length, D))] + [const_block((1, 192))] * 4 + [ANY_BLOCK],
+        in_specs=[MASK_BLOCK, const_block((length, D))] + [const_block((192,))] * 4 + [ANY_BLOCK],
         out_specs=[
             pl.BlockSpec((1, HALF, length), lambda i: (i // 2, i % 2, 0)),
             const_block((length, D)),
@@ -1345,6 +1399,19 @@
 
 
 STEPS = 6
+INNER_TABLE = (
+    (1, "start", 0, 0), (1, "feed", 2, 0), (1, "feed", 1, 0), (2, "feed", 0, 0),
+    (2, "reduce", 0, 0), (3, "start", 1, 0), (4, "feed", 2, 1), (4, "feed", 1, 1),
+    (4, "reduce", 1, 0), (4, "reduce", 0, 1), (4, "feed", 0, 1), (5, "start", 2, 0),
+    (8, "reduce", 1, 1), (8, "reduce", 2, 0), (8, "feed", 2, 2), (8, "feed", 1, 2),
+    (9, "reduce", 0, 2), (12, "reduce", 0, 3), (13, "vec_start", 0, 0), (13, "reduce", 2, 1),
+    (14, "feed", 0, 2), (14, "reduce", 0, 4), (14, "vec", 0, 0), (14, "reduce", 1, 2),
+    (14, "vec", 0, 1), (14, "reduce", 2, 2), (14, "vec", 0, 2), (14, "spread", 0, 0),
+    (14, "reduce", 1, 3), (14, "vec", 0, 3), (14, "reduce", 2, 3), (14, "spread", 0, 1),
+    (14, "reduce", 1, 4), (14, "vec", 0, 4), (14, "reduce", 2, 4), (14, "spread", 0, 2),
+    (14, "spread", 1, 0), (14, "spread", 2, 0), (14, "spread", 1, 1), (14, "spread", 2, 1),
+    (14, "spread", 1, 2), (14, "spread", 2, 2),
+)
 
 
 def inner_back_kernel(
@@ -1361,12 +1428,12 @@
     end = STEPS + turns
     blocks = terms.shape[1] // CHUNKS
     core = lax.rem(lax.axis_index("fsdp"), 2)
-    spread = Spread(blocks, total, Sends(in_send, in_recv))
+    spread = Spread(inner_orders(), blocks, total, Sends(in_send, in_recv))
     reduce = Reduce(
-        blocks, terms, terms, lambda xo: 2 * xo + core, recv_core, recv_x, recv_seq, Sends(red_send, red_recv),
+        inner_orders(), blocks, terms, terms, lambda xo: 2 * xo + core, recv_core, recv_x, recv_seq, Sends(red_send, red_recv),
         spread.begin,
     )
-    feed_spread = Spread(feed_total.shape[0] // CHUNKS, feed_total, Sends(feed_send, feed_recv))
+    feed_spread = Spread(feed_orders(), feed_total.shape[0] // CHUNKS, feed_total, Sends(feed_send, feed_recv))
     vec_sends = Sends(vec_send, vec_recv_sems)
     peers = all_peers()
 
@@ -1445,25 +1512,35 @@
         def _():
             back_ref[...] = get_rows(order, 0, SEG)
 
-    events = []
-    for chunk in range(CHUNKS):
-        for stage in range(feed_spread.stages()):
-            events.append((1 + stage, functools.partial(feed_spread.event, stage, chunk)))
-    for chunk in range(CHUNKS):
-        begin = 2 * chunk + 1
-        events.append((begin, functools.partial(reduce.begin, chunk)))
-        for stage in range(reduce.stages()):
-            when = begin + 1 + (0 if stage == 0 else 3 * chunk + 2 * stage)
-            events.append((when, functools.partial(reduce.event, stage, chunk)))
-        for stage in range(spread.stages()):
-            when = begin + 2 * reduce.stages() + 3 * chunk + 2 * stage
-            events.append((when, functools.partial(spread.event, stage, chunk)))
-    events.append((end - 1, vec_start))
-    for i in range(len(peers)):
-        events.append((end + i, functools.partial(vec_event, i)))
-    run_schedule(step, last, sorted(events, key=lambda event: event[0]))
-
-    @pl.when(step == end - 2)
+    calls = {
+        "start": lambda chunk, stage: reduce.begin(chunk),
+        "reduce": lambda chunk, stage: reduce.event(stage, chunk),
+        "spread": lambda chunk, stage: spread.event(stage, chunk),
+        "feed": lambda chunk, stage: feed_spread.event(stage, chunk),
+        "vec_start": lambda chunk, stage: vec_start(),
+        "vec": lambda chunk, stage: vec_event(stage),
+    }
+    if seq_bits() == 3 and turns == 8:
+        table = INNER_TABLE
+    else:
+        table = []
+        for chunk in range(CHUNKS):
+            begin = 2 * chunk + 1
+            late = begin + 2 * reduce.stages() + 3 * chunk
+            table += [(1 + 2 * stage, "feed", chunk, stage) for stage in range(feed_spread.stages())]
+            table += [(begin, "start", chunk, 0), (begin + 1, "reduce", chunk, 0)]
+            table += [
+                (begin + 1 + 3 * chunk + 2 * stage, "reduce", chunk, stage)
+                for stage in range(1, reduce.stages())
+            ]
+            table += [(late + 2 * stage, "spread", chunk, stage) for stage in range(spread.stages())]
+        table += [(end - 1, "vec_start", 0, 0)]
+        table += [(end + stage, "vec", 0, stage) for stage in range(len(peers))]
+        table.sort(key=lambda event: event[0])
+    events = [(when, functools.partial(calls[name], chunk, stage)) for when, name, chunk, stage in table]
+    run_schedule(step, last, events)
+
+    @pl.when(step == last)
     def _():
         for tile in range(TILES):
             cols = slice(tile * 128, (tile + 1) * 128)
@@ -1580,17 +1657,14 @@
     nseg = length // SEG
     first = nseg.bit_length()
 
-    def gather(weight):
-        return lax.all_gather(weight, "fsdp", axis=0, tiled=True)
-
     mask = jnp.sum(valid_mask[0])[None]
 
-    vectors = [vector[None, :] for vector in (first_gain, first_shift, second_gain, second_shift)]
+    vectors = [first_gain, first_shift, second_gain, second_shift]
     qkv, x, inner, weight_in, gains, *packs = call_project(nseg, first, mask, tokens[0], vectors, project_in)
     weight_in = weight_in.reshape(D, 3 * D)
-    _, *shards = lax.optimization_barrier((gains, project_out, up_weight, down_weight))
-    weight_out, weight_up, weight_down = (gather(shard) for shard in shards)
-    o_part, l_part, m_part, gathered = call_local_forward(nseg, first, qkv, mask, packs)
+    o_part, l_part, m_part, gathered, (weight_out, weight_up, weight_down) = call_local_forward(
+        nseg, first, qkv, mask, packs, (project_out, up_weight, down_weight)
+    )
     attended, lse = call_remote_forward(nseg, first, qkv, mask, o_part, l_part, m_part, gathered)
 
     mixed, grad_middle, grad_merged, along, feed_vec, feed_grads = call_feed(

time: 514 us -> 491 us (0.955)
  between operations: 14.3 us -> 1.15 us
    pallas_call x1, Pallas kernels: 106 us -> 84.8 us  [call_inner_back(): pl.pallas_call(functools.partial(inner_back_kernel, nseg, first), grid=(S...]
    pallas_call x1, Pallas kernels: 70.8 us -> 86.8 us  [call_local_forward(): pl.pallas_call(functools.partial(local_forward, nseg, first), grid=(HEADS...]
  transfers between devices with their start and end apart: 3 -> 0, of which waited for: 1 -> 0; matrix products, arithmetic and copies ran while one was open for 0% -> 0% of each run, Pallas kernels for 19% -> 0%
where the time goes in v6:
time: 491 us; the launch traced here: 483 us
  Pallas kernels  466 us (95%)
  other arithmetic  8.19 us (2%)
  local copies, waits for them, and re-layouts  7.41 us (2%)
    pallas_call x1, Pallas kernels, call_local_backward(): pl.pallas_call(functools.partial(local_backward, nseg, first), grid=(HEAD...  108 us
    pallas_call x1, Pallas kernels, call_feed(): pl.pallas_call(functools.partial(feed_kernel, nseg), grid=(length // ROWS...  100 us
    pallas_call x1, Pallas kernels, call_local_forward(): pl.pallas_call(functools.partial(local_forward, nseg, first), grid=(HEADS...  86.8 us
    pallas_call x1, Pallas kernels, call_inner_back(): pl.pallas_call(functools.partial(inner_back_kernel, nseg, first), grid=(S...  84.8 us
    pallas_call x1, Pallas kernels, call_project(): pl.pallas_call(functools.partial(project_kernel, nseg, first), grid=(6,),...  35.2 us
    pallas_call x1, Pallas kernels, call_remote_backward(): pl.pallas_call(functools.partial(remote_backward, nseg, first), grid=(HEA...  28 us
    pallas_call x1, Pallas kernels, call_remote_forward(): pl.pallas_call(functools.partial(remote_forward, nseg, first), grid=(HEAD...  22.9 us

profile of v6, /device:TPU:0, one launch (start us, length us, event | category | flops | bytes accessed | tf_op | source)
XLA Modules:
  0.0 483.0 jit_solution(6180140956572417582)
XLA Ops:
  0.6 1.4 reduce_sum.9
  2.0 35.2 %project.1 = (bf16[3,768,2048]{2,1,0:T(8,128)(2,1)}, bf16[2048,768]{1,0:T(8,128)(2,1)}, bf16[768,2048]{1,0:T(8,128)(2,1)}, bf16[4,192,2304]{2,1,0:T(8,128)(2,1)}...) custom-call(s32[1]{0:T(128)} %bitcast.mask_ref, ...), custom_call_target="tpu_custom_call" | custom-call | flops 22000001024 | tf_op jit(solution)/shard_map/project/pallas_call | solution.py:1213
  37.2 86.8 %local_forward.1 = (f32[768,2048]{1,0:T(8,128)}, f32[16,1,2048]{2,1,0:T(1,128)}, f32[16,1,2048]{2,1,0:T(1,128)}, bf16[1,1552,512]{2,1,0:T(8,128)(2,1)}, bf16[2,1...) custom-call(s32[1]{0:T(128)} %bitcast.mask_ref, ...), custom_call_target="tpu_custom_call" | custom-call | flops 81399996416 | tf_op jit(solution)/shard_map/local_forward/pallas_call | solution.py:911
  124.0 22.9 %remote_forward.1 = (bf16[768,2048]{1,0:T(8,128)(2,1)}, f32[16,1,2048]{2,1,0:T(1,128)}) custom-call(s32[1]{0:T(128)} %bitcast.mask_ref, bf16[3,768,2048]{2,1,0:T(8,128)(2,1)} %get-tuple-element.50.q_ref.k_ref.v_ref, f32[768,2048]{1,0:T(8,128)} %get-tuple-element.54.o_in, f32[16,1,2048]{2,1,0:T(1,128)} %get-tuple-element.55.l_in, ...), custom_call_target="tpu_custom_call" | custom-call | flops 52800000000 | tf_op jit(solution)/shard_map/remote_forward/pallas_call | solution.py:942
  147.0 100.4 %feed.1 = (bf16[2048,768]{1,0:T(8,128)(2,1)}, f32[2048,768]{1,0:T(8,128)}, bf16[768,2048]{1,0:T(8,128)(2,1)}, f32[16,1,2048]{2,1,0:T(1,128)}, f32[2,768]{1,0:T(2,128)}, /*index=5*/bf16[4,648,16,128]{3,2,1,0:T(8,128)(2,1)}) custom-call(s32[1]{0:T(128)} %bitcast.mask_ref, bf16[768,2048]{1,0:T(8,128)(2,1)} %get-tuple-element.60.att_ref, ...), custom_call_target="tpu_custom_call" | custom-call | flops 99000000512 | tf_op jit(solution)/shard_map/feed/pallas_call | solution.py:1358
  247.3 28.0 %remote_backward.1 = (f32[768,512]{1,0:T(8,128)}, bf16[1,2,768,512]{3,2,1,0:T(8,128)(2,1)}, bf16[2,2,768,256]{3,2,1,0:T(8,128)(2,1)}, bf16[4,2,768,128]{3,2,1,0:T(8,128)(2,1)}) custom-call(s32[1]{0:T(128)} %bitcast.mask_ref, bf16[3,768,2048]{2,1,0:T(8,128)(2,1)} %get-tuple-element.50.q_ref.k_ref.v_ref, bf16[768,2048]{1,0:T(8,128)(2,1)} %get-tuple-element.67.g_ref, ...), custom_call_target="tpu_custom_call" | custom-call | flops 44000002048 | tf_op jit(solution)/shard_map/remote_backward/pallas_call | solution.py:968
  275.3 108.1 %local_backward.1 = (f32[3,768,2048]{2,1,0:T(8,128)}, bf16[2,768,512]{2,1,0:T(8,128)(2,1)}, bf16[2,768,256]{2,1,0:T(8,128)(2,1)}, bf16[2,768,128]{2,1,0:T(8,128)(2,1)}, bf16[3,27,16,128]{3,2,1,0:T(8,128)(2,1)}) custom-call(s32[1]{0:T(128)} %bitcast.mask_ref, bf16[3,768,2048]{2,1,0:T(8,128)(2,1)} %get-tuple-element.50.q_ref.k_ref.v_ref, ...), custom_call_target="tpu_custom_call" | custom-call | flops 158400004096 | tf_op jit(solution)/shard_map/local_backward/pallas_call | solution.py:1017
  383.5 84.8 %inner_back.1 = (bf16[192,2304]{1,0:T(8,128)(2,1)}, f32[2048,768]{1,0:T(8,128)}, f32[8,768]{1,0:T(8,128)}, bf16[192,3072]{1,0:T(8,128)(2,1)}, bf16[192,768]{1,0:T(8,128)(2,1)}, /*index=5*/bf16[768,768]{1,0:T(8,128)(2,1)}) custom-call(f32[3,768,2048]{2,1,0:T(8,128)} %get-tuple-element.75.local_ref, bf16[768,2048]{1,0:T(8,128)(2,1)} %get-tuple-element.76.inner_ref, ...), custom_call_target="tpu_custom_call" | custom-call | flops 32999999488 | tf_op jit(solution)/shard_map/inner_back/pallas_call | solution.py:1583
  468.3 0.0 copy-start
  468.3 0.0 copy-start.1
  468.3 3.1 convert_element_type.14
  471.4 0.0 copy-start.2
  471.4 0.0 copy-done
  471.4 1.6 convert_element_type.15
  473.0 0.0 copy-done.1
  473.0 1.3 convert_element_type.12
  474.3 0.0 copy-done.2
  474.3 0.9 convert_element_type.13
  475.2 1.5 fusion
  476.7 5.9 %copy.22 = f32[1,2048,768]{2,1,0:T(8,128)} copy(f32[1,2048,768]{2,1,0:T(8,128)} %bitcast.13) | data formatting | bytes 12582912
Async XLA Ops:
  468.3 3.1 copy-start
  468.3 4.7 copy-start.1
  471.4 2.9 copy-start.2

commit v7 on v6

--- a/solution.py
+++ b/solution.py
@@ -182,7 +182,8 @@
         self.hops, self.distances = [], set()
         for level, pack, into in zip(range(first, BRANCHES), packs, gathered):
             group = (SEG << (level - 1)) // (nseg * SEG)
-            hops = [((level, 0), pack, into.at[0], group)]
+            source = pack if pack.shape[0] == into.shape[1] else pack.at[pl.ds(D, D + 16)]
+            hops = [((level, 0), source, into.at[0], group)]
             step = 1
             while step < group:
                 hops.append(((level, step), into.at[pl.ds(0, step)], into.at[pl.ds(step, step)], step))
@@ -232,16 +233,19 @@
                 )
             )
 
-    def start(self):
-        for load, core, x, _ in self.copies:
+    def start(self, count):
+        for i, (load, core, x, _) in enumerate(self.copies):
             load.start()
             core.start()
-            x.start()
+            if i < count:
+                x.start()
 
     def hand(self, i):
         _, _, x, hand = self.copies[i]
         x.wait_recv()
         hand.start()
+        if i + 1 < len(self.copies):
+            self.copies[i + 1][2].start()
 
     def finish(self):
         for load, core, x, hand in self.copies:
@@ -533,9 +537,9 @@
 
 def local_forward(nseg, first, mask_ref, q_ref, k_ref, v_ref, *refs):
     n = BRANCHES - first
-    packs, shards, (o_ref, l_ref, m_ref) = refs[:n], refs[n : n + 3], refs[n + 3 : n + 6]
-    gathered, whole = refs[n + 6 : 2 * n + 6], refs[2 * n + 6 : 2 * n + 9]
-    qa, ka, va, send_sems, recv_sems, shard_send, shard_recv, shard_load = refs[2 * n + 9 :]
+    packs, shards, (o_ref, l_ref, m_ref) = refs[:n], refs[n : n + 2], refs[n + 2 : n + 5]
+    gathered, whole = refs[n + 5 : 2 * n + 5], refs[2 * n + 5 : 2 * n + 7]
+    qa, ka, va, send_sems, recv_sems, shard_send, shard_recv, shard_load = refs[2 * n + 7 :]
     head = pl.program_id(0)
     gather = Gather(nseg, first, packs, gathered, Sends(send_sems, recv_sems))
     fetch = Shards(shards, whole, Sends(shard_send, shard_recv), shard_load)
@@ -543,14 +547,14 @@
     def begin():
         meet(gather.peers() + [("fsdp", 1), ("fsdp", 2)])
         gather.start()
-        fetch.start()
+        fetch.start(1)
 
     def finish():
         gather.finish()
-        fetch.hand(2)
+        fetch.hand(1)
         fetch.finish()
 
-    hands = [(3, functools.partial(fetch.hand, 0)), (10, functools.partial(fetch.hand, 1))]
+    hands = [(9, functools.partial(fetch.hand, 0))]
     run_schedule(head, HEADS - 1, [(0, begin)] + sorted(gather.turns() + hands, key=lambda event: event[0]))
     local_forward_core(nseg, mask_ref, q_ref, k_ref, v_ref, o_ref, l_ref, m_ref, qa, ka, va)
     run_schedule(head, HEADS - 1, [(HEADS - 1, finish)])
@@ -870,13 +874,18 @@
 MASK_BLOCK = pl.BlockSpec(memory_space=pltpu.SMEM)
 
 
-def pack_specs(pack):
-    group, _, length = pack.shape
-    return [
-        pl.BlockSpec((group, HEAD_DIM, length), lambda h: (0, h, 0)),
-        pl.BlockSpec((group, HEAD_DIM, length), lambda h: (0, HEADS + h, 0)),
-        pl.BlockSpec((group, 16, length), lambda h: (0, 2 * D // 16, 0)),
-    ]
+def pack_args(keys, packs):
+    args, specs = [], []
+    for i, pack in enumerate(packs):
+        group, _, length = pack.shape
+        ahead = 0 if i == 0 else HEADS
+        args += [keys if i == 0 else pack, pack, pack]
+        specs += [
+            pl.BlockSpec((group, HEAD_DIM, length), lambda h: (0, h, 0)),
+            pl.BlockSpec((group, HEAD_DIM, length), lambda h, ahead=ahead: (0, ahead + h, 0)),
+            pl.BlockSpec((group, 16, length), lambda h, ahead=ahead: (0, (ahead + HEADS) * 3, 0)),
+        ]
+    return args, specs
 
 
 ANY_BLOCK = pl.BlockSpec(memory_space=pl.ANY)
@@ -912,18 +921,21 @@
         functools.partial(local_forward, nseg, first),
         grid=(HEADS,),
         in_specs=[MASK_BLOCK, part_block(0, length), part_block(1, length), part_block(2, length)]
-        + [ANY_BLOCK] * (n + 3),
-        out_specs=[head_block(length), row_block(length), row_block(length)] + [ANY_BLOCK] * (n + 3),
+        + [ANY_BLOCK] * (n + 2),
+        out_specs=[head_block(length), row_block(length), row_block(length)] + [ANY_BLOCK] * (n + 2),
         out_shape=[shape((D, length), F32), shape((HEADS, 1, length), F32), shape((HEADS, 1, length), F32)]
-        + [shape((group,) + pack.shape, BF16) for group, pack in zip(groups, packs)]
+        + [
+            shape((group, D + 16 if i == 0 else pack.shape[0], pack.shape[1]), BF16)
+            for i, (group, pack) in enumerate(zip(groups, packs))
+        ]
         + [shape((4,) + shard.shape, BF16) for shard in shards],
         scratch_shapes=local_forward_scratch(nseg)
         + [
             sems(hops),
             sems(hops),
-            sems(9),
-            sems(9),
-            sems(3),
+            sems(6),
+            sems(6),
+            sems(2),
         ],
         compiler_params=talking(1),
         cost_estimate=cost(nseg * 37e-6),
@@ -933,12 +945,9 @@
     return o_part, l_part, m_part, rest[:n], whole
 
 
-def call_remote_forward(nseg, first, qkv, mask, o_part, l_part, m_part, packs):
+def call_remote_forward(nseg, first, qkv, mask, o_part, l_part, m_part, keys, packs):
     length = nseg * SEG
-    args, specs = [], []
-    for pack in packs:
-        args += [pack] * 3
-        specs += pack_specs(pack)
+    args, specs = pack_args(keys, packs)
     return pl.pallas_call(
         functools.partial(remote_forward, nseg, first),
         grid=(HEADS,),
@@ -958,12 +967,9 @@
     )(mask, qkv, o_part, l_part, m_part, *args)
 
 
-def call_remote_backward(nseg, first, qkv, grad, lse, slope, mask, packs):
+def call_remote_backward(nseg, first, qkv, grad, lse, slope, mask, keys, packs):
     length = nseg * SEG
-    args, specs = [], []
-    for pack in packs:
-        args += [pack] * 3
-        specs += pack_specs(pack)
+    args, specs = pack_args(keys, packs)
     kept = nseg * (SEG >> first)
     return pl.pallas_call(
         functools.partial(remote_backward, nseg, first),
@@ -1087,10 +1093,11 @@
 
 def project_kernel(nseg, first, mask_ref, tok_ref, *refs):
     n = BRANCHES - first
-    vectors, w_ref = refs[:4], refs[4]
-    qkv_ref, xp_ref, inner_ref, weight_ref, gains_ref = refs[5:10]
-    packs = refs[10 : 10 + n]
-    xs, weight, gains, vec_send, vec_recv, w_send, w_recv, w_load, w_store = refs[10 + n :]
+    vectors, w_ref, out_ref = refs[:4], refs[4], refs[5]
+    qkv_ref, xp_ref, inner_ref, weight_ref, gains_ref, whole_ref, keys_ref = refs[6:13]
+    packs = refs[13 : 13 + n]
+    xs, weight, gains, key_pack, vec_send, vec_recv, w_send, w_recv, w_load, w_store = refs[13 + n : 23 + n]
+    key_send, key_recv, out_send, out_recv, out_load = refs[23 + n :]
     step = pl.program_id(0)
     last = pl.num_programs(0) - 1
     me = lax.axis_index("fsdp")
@@ -1124,6 +1131,8 @@
         ]
 
     store = pltpu.make_async_copy(weight, weight_ref, w_store.at[0])
+    fetch = Shards([out_ref], [whole_ref], Sends(out_send, out_recv), out_load)
+    ahead = Sends(key_send, key_recv).copy(0, key_pack, keys_ref, "seq", 1)
 
     @pl.when(step == 0)
     def _():
@@ -1132,14 +1141,18 @@
             pl.semaphore_signal(
                 barrier, inc=1, device_id={"fsdp": other}, device_id_type=pl.DeviceIdType.MESH
             )
+        pl.semaphore_signal(
+            barrier, inc=1, device_id=partner("seq", 1), device_id_type=pl.DeviceIdType.MESH
+        )
         for i, vector in enumerate(vectors):
             gains[me, i : i + 1, :192] = vector[...].astype(F32).reshape(1, 192)
-        pl.semaphore_wait(barrier, 3)
+        pl.semaphore_wait(barrier, 4)
         for copy in vec_copies():
             copy.start()
-        for chunk in range(COLUMN_CHUNKS):
-            for copy in chunk_copies(chunk)[:3]:
+        for turn in range(COLUMN_CHUNKS):
+            for copy in chunk_copies((turn + 1) % COLUMN_CHUNKS)[: 3 if turn == 0 else 2]:
                 copy.start()
+        fetch.start(1)
         for copy in vec_copies():
             copy.wait_recv()
         full = [
@@ -1157,29 +1170,36 @@
         for pack, level in zip(packs, range(first, BRANCHES)):
             pack[2 * D :, :] = packed_keep(mask_ref[0], level, nseg)
 
-    for chunk in range(COLUMN_CHUNKS):
-
-        @pl.when(step == 2 * chunk)
+    for turn in range(COLUMN_CHUNKS):
+
+        @pl.when(step == 2 * turn)
         def _():
-            load, core, x, hand = chunk_copies(chunk)
+            load, core, x, hand = chunk_copies((turn + 1) % COLUMN_CHUNKS)
             x.wait_recv()
             hand.start()
+            if turn + 1 < COLUMN_CHUNKS:
+                chunk_copies((turn + 2) % COLUMN_CHUNKS)[2].start()
             load.wait()
             core.wait_recv()
             hand.wait_recv()
 
+    @pl.when(step == 2)
+    def _():
+        fetch.hand(0)
+
     @pl.when(step == 4)
     def _():
         store.start()
 
-    cols = pl.ds(pl.multiple_of(step * HALF, HALF), HALF)
+    where = lax.rem(step + 2, 6)
+    cols = pl.ds(pl.multiple_of(where * HALF, HALF), HALF)
     block = jnp.concatenate([weight[owner, :, cols] for owner in range(4)], axis=0)
-    scale = jnp.where(step < 2, QUERY_SCALE, 1.0)
+    scale = jnp.where(step >= 4, QUERY_SCALE, 1.0)
     for start in range(0, nseg * SEG, 512):
         lanes = slice(start, start + 512)
         qkv_ref[0, :, lanes] = (dotg(block, inner_ref[:, lanes], 0, 0) * scale).astype(BF16)
 
-    @pl.when(step >= 2)
+    @pl.when(step < 4)
     def _():
         upper = lax.rem(step, 2) == 1
         for pack, level in zip(packs, range(first, BRANCHES)):
@@ -1194,8 +1214,13 @@
                     else:
                         both = qkv_ref[0, rows, start : start + 2 * size]
                         pieces.append(jnp.where(upper, both[:, size:], both[:, :size]))
-                into = pl.ds(pl.multiple_of((step - 2) * HALF + head * HEAD_DIM, 16), HEAD_DIM)
+                into = pl.ds(pl.multiple_of(step * HALF + head * HEAD_DIM, 16), HEAD_DIM)
                 pack[into, :] = jnp.concatenate(pieces, axis=1) if nseg > 1 else pieces[0]
+
+    @pl.when(step == 1)
+    def _():
+        key_pack[...] = packs[0][:D, :]
+        ahead.start()
 
     @pl.when(step == last)
     def _():
@@ -1205,21 +1230,25 @@
             for copy in chunk_copies(chunk)[1:]:
                 copy.wait_send()
         store.wait()
-
-
-def call_project(nseg, first, mask, tokens, vectors, weight):
+        fetch.finish()
+        ahead.wait()
+
+
+def call_project(nseg, first, mask, tokens, vectors, weight, weight_out):
     length = nseg * SEG
     kept = [nseg * (SEG >> level) for level in range(first, BRANCHES)]
     return pl.pallas_call(
         functools.partial(project_kernel, nseg, first),
         grid=(6,),
-        in_specs=[MASK_BLOCK, const_block((length, D))] + [const_block((192,))] * 4 + [ANY_BLOCK],
+        in_specs=[MASK_BLOCK, const_block((length, D))] + [const_block((192,))] * 4 + [ANY_BLOCK] * 2,
         out_specs=[
-            pl.BlockSpec((1, HALF, length), lambda i: (i // 2, i % 2, 0)),
+            pl.BlockSpec((1, HALF, length), lambda i: ((i + 2) % 6 // 2, i % 2, 0)),
             const_block((length, D)),
             const_block((D, length)),
             ANY_BLOCK,
             const_block((8, D)),
+            ANY_BLOCK,
+            ANY_BLOCK,
         ]
         + [const_block((2 * D + 16, size)) for size in kept],
         out_shape=[
@@ -1228,23 +1257,31 @@
             shape((D, length), BF16),
             shape((4, 192, 3 * D), BF16),
             shape((8, D), F32),
+            shape((4, 192, D), BF16),
+            shape((D, kept[0]), BF16),
         ]
         + [shape((2 * D + 16, size), BF16) for size in kept],
         scratch_shapes=[
             pltpu.VMEM((TILES, SEG, 128), F32),
             pltpu.VMEM((4, 192, 3 * D), BF16),
             pltpu.VMEM((4, 8, 256), F32),
+            pltpu.VMEM((D, kept[0]), BF16),
             sems(3),
             sems(3),
             sems(3 * COLUMN_CHUNKS),
             sems(3 * COLUMN_CHUNKS),
             sems(COLUMN_CHUNKS),
             sems(1),
+            sems(1),
+            sems(1),
+            sems(3),
+            sems(3),
+            sems(1),
         ],
         compiler_params=talking(4),
         cost_estimate=cost(nseg * 10e-6),
         name="project",
-    )(mask, tokens, *vectors, weight)
+    )(mask, tokens, *vectors, weight, weight_out)
 
 
 ROWS = 256
@@ -1660,18 +1697,21 @@
     mask = jnp.sum(valid_mask[0])[None]
 
     vectors = [first_gain, first_shift, second_gain, second_shift]
-    qkv, x, inner, weight_in, gains, *packs = call_project(nseg, first, mask, tokens[0], vectors, project_in)
+    qkv, x, inner, weight_in, gains, weight_out, keys, *packs = call_project(
+        nseg, first, mask, tokens[0], vectors, project_in, project_out
+    )
+    weight_out, keys = weight_out.reshape(D, D), keys[None]
     weight_in = weight_in.reshape(D, 3 * D)
-    o_part, l_part, m_part, gathered, (weight_out, weight_up, weight_down) = call_local_forward(
-        nseg, first, qkv, mask, packs, (project_out, up_weight, down_weight)
+    o_part, l_part, m_part, gathered, (weight_up, weight_down) = call_local_forward(
+        nseg, first, qkv, mask, packs, (up_weight, down_weight)
     )
-    attended, lse = call_remote_forward(nseg, first, qkv, mask, o_part, l_part, m_part, gathered)
+    attended, lse = call_remote_forward(nseg, first, qkv, mask, o_part, l_part, m_part, keys, gathered)
 
     mixed, grad_middle, grad_merged, along, feed_vec, feed_grads = call_feed(
         nseg, mask, attended, x, cotangent[0], weight_out, weight_up, weight_down, gains
     )
 
-    dq_remote, *sent = call_remote_backward(nseg, first, qkv, grad_merged, lse, along, mask, gathered)
+    dq_remote, *sent = call_remote_backward(nseg, first, qkv, grad_merged, lse, along, mask, keys, gathered)
     local, returned, pieces = call_local_backward(
         nseg, first, qkv, grad_merged, lse, along, mask, dq_remote, sent, feed_grads
     )

time: 491 us -> 491 us (level)
    pallas_call x1, Pallas kernels: 86.8 us -> 77.9 us  [call_local_forward(): pl.pallas_call(functools.partial(local_forward, nseg, first), grid=(HEADS...]
    pallas_call x1, Pallas kernels: 35.2 us -> 42.9 us  [call_project(): pl.pallas_call(functools.partial(project_kernel, nseg, first), grid=(6,),...]
where the time goes in v7:
time: 491 us; the launch traced here: 482 us
  Pallas kernels  466 us (95%)
  other arithmetic  8.19 us (2%)
  local copies, waits for them, and re-layouts  7.41 us (2%)
    pallas_call x1, Pallas kernels, call_local_backward(): pl.pallas_call(functools.partial(local_backward, nseg, first), grid=(HEAD...  108 us
    pallas_call x1, Pallas kernels, call_feed(): pl.pallas_call(functools.partial(feed_kernel, nseg), grid=(length // ROWS...  100 us
    pallas_call x1, Pallas kernels, call_inner_back(): pl.pallas_call(functools.partial(inner_back_kernel, nseg, first), grid=(S...  85.5 us
    pallas_call x1, Pallas kernels, call_local_forward(): pl.pallas_call(functools.partial(local_forward, nseg, first), grid=(HEADS...  77.9 us
    pallas_call x1, Pallas kernels, call_project(): pl.pallas_call(functools.partial(project_kernel, nseg, first), grid=(6,),...  42.9 us
    pallas_call x1, Pallas kernels, call_remote_backward(): pl.pallas_call(functools.partial(remote_backward, nseg, first), grid=(HEA...  28 us
    pallas_call x1, Pallas kernels, call_remote_forward(): pl.pallas_call(functools.partial(remote_forward, nseg, first), grid=(HEAD...  22.9 us

profile of v7, /device:TPU:0, one launch (start us, length us, event | category | flops | bytes accessed | tf_op | source)
XLA Modules:
  0.0 482.3 jit_solution(2225341840333116503)
XLA Ops:
  0.6 1.4 reduce_sum.9
  2.0 42.9 %project.1 = (bf16[3,768,2048]{2,1,0:T(8,128)(2,1)}, bf16[2048,768]{1,0:T(8,128)(2,1)}, bf16[768,2048]{1,0:T(8,128)(2,1)}, bf16[4,192,2304]{2,1,0:T(8,128)(2,1)}...) custom-call(s32[1]{0:T(128)} %bitcast.mask_ref, ...), custom_call_target="tpu_custom_call" | custom-call | flops 22000001024 | tf_op jit(solution)/shard_map/project/pallas_call | solution.py:1240
  44.9 77.9 %local_forward.1 = (f32[768,2048]{1,0:T(8,128)}, f32[16,1,2048]{2,1,0:T(1,128)}, f32[16,1,2048]{2,1,0:T(1,128)}, bf16[1,784,512]{2,1,0:T(8,128)(2,1)}, bf16[2,15...) custom-call(s32[1]{0:T(128)} %bitcast.mask_ref, ...), custom_call_target="tpu_custom_call" | custom-call | flops 81399996416 | tf_op jit(solution)/shard_map/local_forward/pallas_call | solution.py:920
  122.9 22.9 %remote_forward.1 = (bf16[768,2048]{1,0:T(8,128)(2,1)}, f32[16,1,2048]{2,1,0:T(1,128)}) custom-call(s32[1]{0:T(128)} %bitcast.mask_ref, bf16[3,768,2048]{2,1,0:T(8,128)(2,1)} %get-tuple-element.51.q_ref.k_ref.v_ref, f32[768,2048]{1,0:T(8,128)} %get-tuple-element.55.o_in, f32[16,1,2048]{2,1,0:T(1,128)} %get-tuple-element.56.l_in, ...), custom_call_target="tpu_custom_call" | custom-call | flops 52800000000 | tf_op jit(solution)/shard_map/remote_forward/pallas_call | solution.py:951
  145.8 100.4 %feed.1 = (bf16[2048,768]{1,0:T(8,128)(2,1)}, f32[2048,768]{1,0:T(8,128)}, bf16[768,2048]{1,0:T(8,128)(2,1)}, f32[16,1,2048]{2,1,0:T(1,128)}, f32[2,768]{1,0:T(2,128)}, /*index=5*/bf16[4,648,16,128]{3,2,1,0:T(8,128)(2,1)}) custom-call(s32[1]{0:T(128)} %bitcast.mask_ref, bf16[768,2048]{1,0:T(8,128)(2,1)} %get-tuple-element.62.att_ref, ...), custom_call_target="tpu_custom_call" | custom-call | flops 99000000512 | tf_op jit(solution)/shard_map/feed/pallas_call | solution.py:1395
  246.2 28.0 %remote_backward.1 = (f32[768,512]{1,0:T(8,128)}, bf16[1,2,768,512]{3,2,1,0:T(8,128)(2,1)}, bf16[2,2,768,256]{3,2,1,0:T(8,128)(2,1)}, bf16[4,2,768,128]{3,2,1,0:T(8,128)(2,1)}) custom-call(s32[1]{0:T(128)} %bitcast.mask_ref, bf16[3,768,2048]{2,1,0:T(8,128)(2,1)} %get-tuple-element.51.q_ref.k_ref.v_ref, bf16[768,2048]{1,0:T(8,128)(2,1)} %get-tuple-element.69.g_ref, ...), custom_call_target="tpu_custom_call" | custom-call | flops 44000002048 | tf_op jit(solution)/shard_map/remote_backward/pallas_call | solution.py:974
  274.2 107.9 %local_backward.1 = (f32[3,768,2048]{2,1,0:T(8,128)}, bf16[2,768,512]{2,1,0:T(8,128)(2,1)}, bf16[2,768,256]{2,1,0:T(8,128)(2,1)}, bf16[2,768,128]{2,1,0:T(8,128)(2,1)}, bf16[3,27,16,128]{3,2,1,0:T(8,128)(2,1)}) custom-call(s32[1]{0:T(128)} %bitcast.mask_ref, bf16[3,768,2048]{2,1,0:T(8,128)(2,1)} %get-tuple-element.51.q_ref.k_ref.v_ref, ...), custom_call_target="tpu_custom_call" | custom-call | flops 158400004096 | tf_op jit(solution)/shard_map/local_backward/pallas_call | solution.py:1023
  382.1 85.5 %inner_back.1 = (bf16[192,2304]{1,0:T(8,128)(2,1)}, f32[2048,768]{1,0:T(8,128)}, f32[8,768]{1,0:T(8,128)}, bf16[192,3072]{1,0:T(8,128)(2,1)}, bf16[192,768]{1,0:T(8,128)(2,1)}, /*index=5*/bf16[768,768]{1,0:T(8,128)(2,1)}) custom-call(f32[3,768,2048]{2,1,0:T(8,128)} %get-tuple-element.77.local_ref, bf16[768,2048]{1,0:T(8,128)(2,1)} %get-tuple-element.78.inner_ref, ...), custom_call_target="tpu_custom_call" | custom-call | flops 32999999488 | tf_op jit(solution)/shard_map/inner_back/pallas_call | solution.py:1620
  467.6 0.0 copy-start
  467.6 0.0 copy-start.1
  467.6 3.1 convert_element_type.14
  470.7 0.0 copy-start.2
  470.7 0.0 copy-done
  470.7 1.6 convert_element_type.15
  472.3 0.0 copy-done.1
  472.3 1.3 convert_element_type.12
  473.6 0.0 copy-done.2
  473.6 0.9 convert_element_type.13
  474.5 1.5 fusion
  476.0 5.9 %copy.22 = f32[1,2048,768]{2,1,0:T(8,128)} copy(f32[1,2048,768]{2,1,0:T(8,128)} %bitcast.14) | data formatting | bytes 12582912
Async XLA Ops:
  467.6 3.1 copy-start
  467.6 4.7 copy-start.1
  470.7 2.9 copy-start.2

commit v8 on v7

--- a/solution.py
+++ b/solution.py
@@ -213,17 +213,21 @@
         events = []
         for index, hops in reversed(list(enumerate(self.hops))):
             for turn in range(1, len(hops)):
-                when = 4 * turn + (2 if turn > 1 else 0) + (len(self.hops) - 1 - index)
+                when = 5 + 3 * (turn - 1) + (len(self.hops) - 1 - index)
                 events.append((when, functools.partial(self.pass_on, index, turn)))
         return events
 
 
 class Shards:
-    def __init__(self, shards, whole, sends, loads):
+    def __init__(self, shards, whole, stages, sends, loads):
         self.copies = []
+        self.staged = [
+            pltpu.make_async_copy(shard, stage, loads.at[i])
+            for i, (shard, stage) in enumerate(zip(shards, stages))
+        ]
         me = lax.axis_index("fsdp")
         other = lax.rem(me + 2, 4)
-        for i, (shard, into) in enumerate(zip(shards, whole)):
+        for i, (shard, into) in enumerate(zip(stages, whole)):
             self.copies.append(
                 (
                     pltpu.make_async_copy(shard, into.at[me], loads.at[i]),
@@ -234,7 +238,10 @@
             )
 
     def start(self, count):
+        for staged in self.staged:
+            staged.start()
         for i, (load, core, x, _) in enumerate(self.copies):
+            self.staged[i].wait()
             load.start()
             core.start()
             if i < count:
@@ -535,14 +542,18 @@
         start += at.size
 
 
+DOWN_FIRST = 384
+
+
 def local_forward(nseg, first, mask_ref, q_ref, k_ref, v_ref, *refs):
     n = BRANCHES - first
     packs, shards, (o_ref, l_ref, m_ref) = refs[:n], refs[n : n + 2], refs[n + 2 : n + 5]
     gathered, whole = refs[n + 5 : 2 * n + 5], refs[2 * n + 5 : 2 * n + 7]
-    qa, ka, va, send_sems, recv_sems, shard_send, shard_recv, shard_load = refs[2 * n + 7 :]
+    qa, ka, va, send_sems, recv_sems, up_stage, down_stage, shard_send, shard_recv, shard_load = refs[2 * n + 7 :]
     head = pl.program_id(0)
     gather = Gather(nseg, first, packs, gathered, Sends(send_sems, recv_sems))
-    fetch = Shards(shards, whole, Sends(shard_send, shard_recv), shard_load)
+    pieces = [shards[0], shards[1].at[pl.ds(0, DOWN_FIRST)]]
+    fetch = Shards(pieces, whole, [up_stage, down_stage], Sends(shard_send, shard_recv), shard_load)
 
     def begin():
         meet(gather.peers() + [("fsdp", 1), ("fsdp", 2)])
@@ -551,10 +562,9 @@
 
     def finish():
         gather.finish()
-        fetch.hand(1)
         fetch.finish()
 
-    hands = [(9, functools.partial(fetch.hand, 0))]
+    hands = [(9, functools.partial(fetch.hand, 0)), (14, functools.partial(fetch.hand, 1))]
     run_schedule(head, HEADS - 1, [(0, begin)] + sorted(gather.turns() + hands, key=lambda event: event[0]))
     local_forward_core(nseg, mask_ref, q_ref, k_ref, v_ref, o_ref, l_ref, m_ref, qa, ka, va)
     run_schedule(head, HEADS - 1, [(HEADS - 1, finish)])
@@ -617,7 +627,18 @@
     head = pl.program_id(0)
     levels = range(first, BRANCHES)
     packs = {level: refs[3 * i : 3 * i + 3] for i, level in enumerate(levels)}
-    att_ref, lse_ref, o_ref, l_ref, m_ref, qa = refs[3 * len(levels) :]
+    shard_ref, att_ref, lse_ref, whole_ref, o_ref, l_ref, m_ref, qa, stage, *shard_sems = refs[
+        3 * len(levels) :
+    ]
+    shard_send, shard_recv, shard_load = shard_sems
+    piece = shard_ref.at[pl.ds(DOWN_FIRST, D - DOWN_FIRST)]
+    fetch = Shards([piece], [whole_ref], [stage], Sends(shard_send, shard_recv), shard_load)
+
+    def begin():
+        meet([("fsdp", 1), ("fsdp", 2)])
+        fetch.start(1)
+
+    run_schedule(head, HEADS - 1, [(0, begin), (12, functools.partial(fetch.hand, 0))])
     length = nseg * SEG
     qa[...] = join(q_ref[0], query_rows(head, length))
     o_ref[...] = o_in[...]
@@ -635,6 +656,7 @@
     weight = jnp.where(local_keep(mask_ref[0], length), 1.0, 0.0) / l_ref[0]
     att_ref[...] = (o_ref[...] * weight).astype(BF16)
     lse_ref[0] = m_ref[0] + jnp.log2(l_ref[0])
+    run_schedule(head, HEADS - 1, [(HEADS - 1, fetch.finish)])
 
 
 def grad_rows(grad, slope):
@@ -917,6 +939,7 @@
     n = len(packs)
     groups = [(SEG << (level - 1)) // length for level in range(first, BRANCHES)]
     hops = sum(group.bit_length() for group in groups)
+    pieces = [shards[0].shape, (DOWN_FIRST, D)]
     o_part, l_part, m_part, *rest = pl.pallas_call(
         functools.partial(local_forward, nseg, first),
         grid=(HEADS,),
@@ -928,11 +951,14 @@
             shape((group, D + 16 if i == 0 else pack.shape[0], pack.shape[1]), BF16)
             for i, (group, pack) in enumerate(zip(groups, packs))
         ]
-        + [shape((4,) + shard.shape, BF16) for shard in shards],
+        + [shape((4,) + piece, BF16) for piece in pieces],
         scratch_shapes=local_forward_scratch(nseg)
         + [
             sems(hops),
             sems(hops),
+        ]
+        + [pltpu.VMEM(piece, BF16) for piece in pieces]
+        + [
             sems(6),
             sems(6),
             sems(2),
@@ -941,30 +967,39 @@
         cost_estimate=cost(nseg * 37e-6),
         name="local_forward",
     )(mask, qkv, qkv, qkv, *packs, *shards)
-    whole = [weight.reshape(4 * weight.shape[1], weight.shape[2]) for weight in rest[n:]]
-    return o_part, l_part, m_part, rest[:n], whole
-
-
-def call_remote_forward(nseg, first, qkv, mask, o_part, l_part, m_part, keys, packs):
+    whole_up, down_first = rest[n:]
+    return o_part, l_part, m_part, rest[:n], whole_up.reshape(D, 4 * D), down_first
+
+
+def call_remote_forward(nseg, first, qkv, mask, o_part, l_part, m_part, keys, packs, shard):
     length = nseg * SEG
     args, specs = pack_args(keys, packs)
     return pl.pallas_call(
         functools.partial(remote_forward, nseg, first),
         grid=(HEADS,),
         in_specs=[MASK_BLOCK, part_block(0, length), head_block(length), row_block(length), row_block(length)]
-        + specs,
-        out_specs=[head_block(length), row_block(length)],
-        out_shape=[shape((D, length), BF16), shape((HEADS, 1, length), F32)],
+        + specs
+        + [ANY_BLOCK],
+        out_specs=[head_block(length), row_block(length), ANY_BLOCK],
+        out_shape=[
+            shape((D, length), BF16),
+            shape((HEADS, 1, length), F32),
+            shape((4, D - DOWN_FIRST, D), BF16),
+        ],
         scratch_shapes=[
             pltpu.VMEM((HEAD_DIM, length), F32),
             pltpu.VMEM((1, 1, length), F32),
             pltpu.VMEM((1, 1, length), F32),
             pltpu.VMEM((64, length), BF16),
+            pltpu.VMEM((D - DOWN_FIRST, D), BF16),
+            sems(3),
+            sems(3),
+            sems(1),
         ],
-        compiler_params=PARAMS,
+        compiler_params=talking(5),
         cost_estimate=cost(nseg * 24e-6),
         name="remote_forward",
-    )(mask, qkv, o_part, l_part, m_part, *args)
+    )(mask, qkv, o_part, l_part, m_part, *args, shard)
 
 
 def call_remote_backward(nseg, first, qkv, grad, lse, slope, mask, keys, packs):
@@ -1097,7 +1132,7 @@
     qkv_ref, xp_ref, inner_ref, weight_ref, gains_ref, whole_ref, keys_ref = refs[6:13]
     packs = refs[13 : 13 + n]
     xs, weight, gains, key_pack, vec_send, vec_recv, w_send, w_recv, w_load, w_store = refs[13 + n : 23 + n]
-    key_send, key_recv, out_send, out_recv, out_load = refs[23 + n :]
+    key_send, key_recv, out_stage, out_send, out_recv, out_load = refs[23 + n :]
     step = pl.program_id(0)
     last = pl.num_programs(0) - 1
     me = lax.axis_index("fsdp")
@@ -1131,7 +1166,7 @@
         ]
 
     store = pltpu.make_async_copy(weight, weight_ref, w_store.at[0])
-    fetch = Shards([out_ref], [whole_ref], Sends(out_send, out_recv), out_load)
+    fetch = Shards([out_ref], [whole_ref], [out_stage], Sends(out_send, out_recv), out_load)
     ahead = Sends(key_send, key_recv).copy(0, key_pack, keys_ref, "seq", 1)
 
     @pl.when(step == 0)
@@ -1274,6 +1309,7 @@
             sems(1),
             sems(1),
             sems(1),
+            pltpu.VMEM((192, D), BF16),
             sems(3),
             sems(3),
             sems(1),
@@ -1293,7 +1329,7 @@
 
 
 def feed_kernel(
-    nseg, mask_ref, att_ref, x_ref, cot_ref, wout_ref, up_ref, down_ref, gains_ref,
+    nseg, mask_ref, att_ref, x_ref, cot_ref, wout_ref, up_ref, down_a, down_b, gains_ref,
     mixed_ref, gmid_ref, gm_ref, along_ref, vec_ref, grads_ref,
     cs, out_acc, up_acc, down_acc, stage, sems,
 ):
@@ -1325,12 +1361,13 @@
     for start in range(0, 4 * D, D):
         cols = slice(start, start + D)
         upper = dotg(hidden, up_ref[:, cols], 1, 0)
-        grad_active = dotg(grad_b, down_ref[cols, :], 1, 1)
+        down = jnp.concatenate([down_a[start // D], down_b[start // D]], axis=0)
+        grad_active = dotg(grad_b, down, 1, 1)
         half = 0.5 * (1.0 + lax.erf(upper * ROOT_HALF))
         slope = half + upper * jnp.exp(-0.5 * upper * upper) * INV_ROOT_TWO_PI
         active = (upper * half).astype(BF16)
         grad_upper = (grad_active * slope).astype(BF16)
-        final = final + dotg(active, down_ref[cols, :], 1, 0)
+        final = final + dotg(active, down, 1, 0)
         grad_hidden = grad_hidden + dotg(grad_upper, up_ref[:, cols], 1, 1)
         up_acc[:, cols] += dotg(hidden_t, grad_upper, 1, 0)
         down_acc[cols, :] += dotg(active, grad_b, 0, 0)
@@ -1390,7 +1427,7 @@
         copies[-1].wait()
 
 
-def call_feed(nseg, mask, att, x, cot, wout, up, down, gains):
+def call_feed(nseg, mask, att, x, cot, wout, up, down_a, down_b, gains):
     length = nseg * SEG
     return pl.pallas_call(
         functools.partial(feed_kernel, nseg),
@@ -1402,7 +1439,8 @@
             pl.BlockSpec((SEG, D), lambda i: (i // 4, 0)),
             const_block((D, D)),
             const_block((D, 4 * D)),
-            const_block((4 * D, D)),
+            const_block((4, DOWN_FIRST, D)),
+            const_block((4, D - DOWN_FIRST, D)),
             const_block((8, D)),
         ],
         out_specs=[
@@ -1432,7 +1470,7 @@
         compiler_params=pltpu.CompilerParams(vmem_limit_bytes=62 * 1024 * 1024),
         cost_estimate=cost(nseg * 45e-6),
         name="feed",
-    )(mask, att, x, cot, wout, up, down, gains)
+    )(mask, att, x, cot, wout, up, down_a, down_b, gains)
 
 
 STEPS = 6
@@ -1702,13 +1740,15 @@
     )
     weight_out, keys = weight_out.reshape(D, D), keys[None]
     weight_in = weight_in.reshape(D, 3 * D)
-    o_part, l_part, m_part, gathered, (weight_up, weight_down) = call_local_forward(
+    o_part, l_part, m_part, gathered, weight_up, down_first = call_local_forward(
         nseg, first, qkv, mask, packs, (up_weight, down_weight)
     )
-    attended, lse = call_remote_forward(nseg, first, qkv, mask, o_part, l_part, m_part, keys, gathered)
+    attended, lse, down_second = call_remote_forward(
+        nseg, first, qkv, mask, o_part, l_part, m_part, keys, gathered, down_weight
+    )
 
     mixed, grad_middle, grad_merged, along, feed_vec, feed_grads = call_feed(
-        nseg, mask, attended, x, cotangent[0], weight_out, weight_up, weight_down, gains
+        nseg, mask, attended, x, cotangent[0], weight_out, weight_up, down_first, down_second, gains
     )
 
     dq_remote, *sent = call_remote_backward(nseg, first, qkv, grad_merged, lse, along, mask, keys, gathered)

time: 491 us -> 479 us (0.976)
  Pallas kernels: 466 us -> 454 us
    pallas_call x1, Pallas kernels: 77.9 us -> 66.2 us  [call_local_forward(): pl.pallas_call(functools.partial(local_forward, nseg, first), grid=(HEADS...]
where the time goes in v8:
time: 479 us; the launch traced here: 470 us
  Pallas kernels  454 us (95%)
  other arithmetic  8.14 us (2%)
  local copies, waits for them, and re-layouts  7.41 us (2%)
    pallas_call x1, Pallas kernels, call_local_backward(): pl.pallas_call(functools.partial(local_backward, nseg, first), grid=(HEAD...  106 us
    pallas_call x1, Pallas kernels, call_feed(): pl.pallas_call(functools.partial(feed_kernel, nseg), grid=(length // ROWS...  100 us
    pallas_call x1, Pallas kernels, call_inner_back(): pl.pallas_call(functools.partial(inner_back_kernel, nseg, first), grid=(S...  84.5 us
    pallas_call x1, Pallas kernels, call_local_forward(): pl.pallas_call(functools.partial(local_forward, nseg, first), grid=(HEADS...  66.2 us
    pallas_call x1, Pallas kernels, call_project(): pl.pallas_call(functools.partial(project_kernel, nseg, first), grid=(6,),...  42.8 us
    pallas_call x1, Pallas kernels, call_remote_backward(): pl.pallas_call(functools.partial(remote_backward, nseg, first), grid=(HEA...  28.1 us
    pallas_call x1, Pallas kernels, call_remote_forward(): pl.pallas_call(functools.partial(remote_forward, nseg, first), grid=(HEAD...  25.7 us

profile of v8, /device:TPU:0, one launch (start us, length us, event | category | flops | bytes accessed | tf_op | source)
XLA Modules:
  0.0 470.3 jit_solution(2786438709586464685)
XLA Ops:
  0.6 1.4 reduce_sum.9
  2.0 42.8 %project.1 = (bf16[3,768,2048]{2,1,0:T(8,128)(2,1)}, bf16[2048,768]{1,0:T(8,128)(2,1)}, bf16[768,2048]{1,0:T(8,128)(2,1)}, bf16[4,192,2304]{2,1,0:T(8,128)(2,1)}...) custom-call(s32[1]{0:T(128)} %bitcast.mask_ref, ...), custom_call_target="tpu_custom_call" | custom-call | flops 22000001024 | tf_op jit(solution)/shard_map/project/pallas_call | solution.py:1275
  44.8 66.2 %local_forward.1 = (f32[768,2048]{1,0:T(8,128)}, f32[16,1,2048]{2,1,0:T(1,128)}, f32[16,1,2048]{2,1,0:T(1,128)}, bf16[1,784,512]{2,1,0:T(8,128)(2,1)}, bf16[2,15...) custom-call(s32[1]{0:T(128)} %bitcast.mask_ref, ...), custom_call_target="tpu_custom_call" | custom-call | flops 81399996416 | tf_op jit(solution)/shard_map/local_forward/pallas_call | solution.py:943
  111.0 25.7 %remote_forward.1 = (bf16[768,2048]{1,0:T(8,128)(2,1)}, f32[16,1,2048]{2,1,0:T(1,128)}, bf16[4,384,768]{2,1,0:T(8,128)(2,1)}) custom-call(s32[1]{0:T(128)} %bitcast.mask_ref, bf16[3,768,2048]{2,1,0:T(8,128)(2,1)} %get-tuple-element.52.q_ref.k_ref.v_ref, f32[768,2048]{1,0:T(8,128)} %get-tuple-element.56.o_in, f32[16,1,2048]{2,1,0:T(1,128)} %get-tuple-element.57.l_in, ...), custom_call_target="tpu_custom_call" | custom-call | flops 52800000000 | tf_op jit(solution)/shard_map/remote_forward/pallas_call | solution.py:977
  136.7 100.3 %feed.1 = (bf16[2048,768]{1,0:T(8,128)(2,1)}, f32[2048,768]{1,0:T(8,128)}, bf16[768,2048]{1,0:T(8,128)(2,1)}, f32[16,1,2048]{2,1,0:T(1,128)}, f32[2,768]{1,0:T(2,128)}, /*index=5*/bf16[4,648,16,128]{3,2,1,0:T(8,128)(2,1)}) custom-call(s32[1]{0:T(128)} %bitcast.mask_ref, bf16[768,2048]{1,0:T(8,128)(2,1)} %get-tuple-element.63.att_ref, ...), custom_call_target="tpu_custom_call" | custom-call | flops 99000000512 | tf_op jit(solution)/shard_map/feed/pallas_call | solution.py:1432
  237.1 28.1 %remote_backward.1 = (f32[768,512]{1,0:T(8,128)}, bf16[1,2,768,512]{3,2,1,0:T(8,128)(2,1)}, bf16[2,2,768,256]{3,2,1,0:T(8,128)(2,1)}, bf16[4,2,768,128]{3,2,1,0:T(8,128)(2,1)}) custom-call(s32[1]{0:T(128)} %bitcast.mask_ref, bf16[3,768,2048]{2,1,0:T(8,128)(2,1)} %get-tuple-element.52.q_ref.k_ref.v_ref, bf16[768,2048]{1,0:T(8,128)(2,1)} %get-tuple-element.71.g_ref, ...), custom_call_target="tpu_custom_call" | custom-call | flops 44000002048 | tf_op jit(solution)/shard_map/remote_backward/pallas_call | solution.py:1009
  265.1 106.1 %local_backward.1 = (f32[3,768,2048]{2,1,0:T(8,128)}, bf16[2,768,512]{2,1,0:T(8,128)(2,1)}, bf16[2,768,256]{2,1,0:T(8,128)(2,1)}, bf16[2,768,128]{2,1,0:T(8,128)(2,1)}, bf16[3,27,16,128]{3,2,1,0:T(8,128)(2,1)}) custom-call(s32[1]{0:T(128)} %bitcast.mask_ref, bf16[3,768,2048]{2,1,0:T(8,128)(2,1)} %get-tuple-element.52.q_ref.k_ref.v_ref, ...), custom_call_target="tpu_custom_call" | custom-call | flops 158400004096 | tf_op jit(solution)/shard_map/local_backward/pallas_call | solution.py:1058
  371.2 84.5 %inner_back.1 = (bf16[192,2304]{1,0:T(8,128)(2,1)}, f32[2048,768]{1,0:T(8,128)}, f32[8,768]{1,0:T(8,128)}, bf16[192,3072]{1,0:T(8,128)(2,1)}, bf16[192,768]{1,0:T(8,128)(2,1)}, /*index=5*/bf16[768,768]{1,0:T(8,128)(2,1)}) custom-call(f32[3,768,2048]{2,1,0:T(8,128)} %get-tuple-element.79.local_ref, bf16[768,2048]{1,0:T(8,128)(2,1)} %get-tuple-element.80.inner_ref, ...), custom_call_target="tpu_custom_call" | custom-call | flops 32999999488 | tf_op jit(solution)/shard_map/inner_back/pallas_call | solution.py:1658
  455.7 0.0 copy-start
  455.7 3.0 convert_element_type.14
  458.7 0.0 copy-start.1
  458.7 0.0 copy-done
  458.8 0.0 copy-start.2
  458.8 1.6 convert_element_type.15
  460.3 0.0 copy-done.1
  460.3 1.3 convert_element_type.12
  461.7 0.0 copy-done.2
  461.7 0.9 convert_element_type.13
  462.5 1.5 fusion
  464.0 5.9 %copy.22 = f32[1,2048,768]{2,1,0:T(8,128)} copy(f32[1,2048,768]{2,1,0:T(8,128)} %bitcast.13) | data formatting | bytes 12582912
Async XLA Ops:
  455.7 3.0 copy-start
  458.7 1.6 copy-start.1
  458.8 2.9 copy-start.2

commit v9 on v8

--- a/solution.py
+++ b/solution.py
@@ -213,14 +213,14 @@
         events = []
         for index, hops in reversed(list(enumerate(self.hops))):
             for turn in range(1, len(hops)):
-                when = 5 + 3 * (turn - 1) + (len(self.hops) - 1 - index)
+                when = 6 + 3 * (turn - 1) + 2 * (len(self.hops) - 1 - index)
                 events.append((when, functools.partial(self.pass_on, index, turn)))
         return events
 
 
 class Shards:
-    def __init__(self, shards, whole, stages, sends, loads):
-        self.copies = []
+    def __init__(self, shards, whole, stages, sends, loads, started=1):
+        self.copies, self.started = [], started
         self.staged = [
             pltpu.make_async_copy(shard, stage, loads.at[i])
             for i, (shard, stage) in enumerate(zip(shards, stages))
@@ -237,21 +237,21 @@
                 )
             )
 
-    def start(self, count):
+    def start(self):
         for staged in self.staged:
             staged.start()
         for i, (load, core, x, _) in enumerate(self.copies):
             self.staged[i].wait()
             load.start()
             core.start()
-            if i < count:
+            if i < self.started:
                 x.start()
 
     def hand(self, i):
         _, _, x, hand = self.copies[i]
         x.wait_recv()
         hand.start()
-        if i + 1 < len(self.copies):
+        if self.started <= i + 1 < len(self.copies):
             self.copies[i + 1][2].start()
 
     def finish(self):
@@ -547,24 +547,24 @@
 
 def local_forward(nseg, first, mask_ref, q_ref, k_ref, v_ref, *refs):
     n = BRANCHES - first
-    packs, shards, (o_ref, l_ref, m_ref) = refs[:n], refs[n : n + 2], refs[n + 2 : n + 5]
-    gathered, whole = refs[n + 5 : 2 * n + 5], refs[2 * n + 5 : 2 * n + 7]
-    qa, ka, va, send_sems, recv_sems, up_stage, down_stage, shard_send, shard_recv, shard_load = refs[2 * n + 7 :]
+    packs, shards, (o_ref, l_ref, m_ref) = refs[:n], refs[n : n + 3], refs[n + 3 : n + 6]
+    gathered, whole = refs[n + 6 : 2 * n + 6], refs[2 * n + 6 : 2 * n + 9]
+    qa, ka, va, send_sems, recv_sems, *stages, shard_send, shard_recv, shard_load = refs[2 * n + 9 :]
     head = pl.program_id(0)
     gather = Gather(nseg, first, packs, gathered, Sends(send_sems, recv_sems))
-    pieces = [shards[0], shards[1].at[pl.ds(0, DOWN_FIRST)]]
-    fetch = Shards(pieces, whole, [up_stage, down_stage], Sends(shard_send, shard_recv), shard_load)
+    pieces = [shards[0], shards[1], shards[2].at[pl.ds(0, DOWN_FIRST)]]
+    fetch = Shards(pieces, whole, stages, Sends(shard_send, shard_recv), shard_load, 2)
 
     def begin():
         meet(gather.peers() + [("fsdp", 1), ("fsdp", 2)])
         gather.start()
-        fetch.start(1)
+        fetch.start()
 
     def finish():
         gather.finish()
         fetch.finish()
 
-    hands = [(9, functools.partial(fetch.hand, 0)), (14, functools.partial(fetch.hand, 1))]
+    hands = [(when, functools.partial(fetch.hand, i)) for i, when in enumerate((11, 11, 15))]
     run_schedule(head, HEADS - 1, [(0, begin)] + sorted(gather.turns() + hands, key=lambda event: event[0]))
     local_forward_core(nseg, mask_ref, q_ref, k_ref, v_ref, o_ref, l_ref, m_ref, qa, ka, va)
     run_schedule(head, HEADS - 1, [(HEADS - 1, finish)])
@@ -636,7 +636,7 @@
 
     def begin():
         meet([("fsdp", 1), ("fsdp", 2)])
-        fetch.start(1)
+        fetch.start()
 
     run_schedule(head, HEADS - 1, [(0, begin), (12, functools.partial(fetch.hand, 0))])
     length = nseg * SEG
@@ -939,13 +939,13 @@
     n = len(packs)
     groups = [(SEG << (level - 1)) // length for level in range(first, BRANCHES)]
     hops = sum(group.bit_length() for group in groups)
-    pieces = [shards[0].shape, (DOWN_FIRST, D)]
+    pieces = [shards[0].shape, shards[1].shape, (DOWN_FIRST, D)]
     o_part, l_part, m_part, *rest = pl.pallas_call(
         functools.partial(local_forward, nseg, first),
         grid=(HEADS,),
         in_specs=[MASK_BLOCK, part_block(0, length), part_block(1, length), part_block(2, length)]
-        + [ANY_BLOCK] * (n + 2),
-        out_specs=[head_block(length), row_block(length), row_block(length)] + [ANY_BLOCK] * (n + 2),
+        + [ANY_BLOCK] * (n + 3),
+        out_specs=[head_block(length), row_block(length), row_block(length)] + [ANY_BLOCK] * (n + 3),
         out_shape=[shape((D, length), F32), shape((HEADS, 1, length), F32), shape((HEADS, 1, length), F32)]
         + [
             shape((group, D + 16 if i == 0 else pack.shape[0], pack.shape[1]), BF16)
@@ -959,16 +959,18 @@
         ]
         + [pltpu.VMEM(piece, BF16) for piece in pieces]
         + [
-            sems(6),
-            sems(6),
-            sems(2),
+            sems(9),
+            sems(9),
+            sems(3),
         ],
         compiler_params=talking(1),
         cost_estimate=cost(nseg * 37e-6),
         name="local_forward",
     )(mask, qkv, qkv, qkv, *packs, *shards)
-    whole_up, down_first = rest[n:]
-    return o_part, l_part, m_part, rest[:n], whole_up.reshape(D, 4 * D), down_first
+    whole_out, whole_up, down_first = rest[n:]
+    return (
+        o_part, l_part, m_part, rest[:n], whole_out.reshape(D, D), whole_up.reshape(D, 4 * D), down_first
+    )
 
 
 def call_remote_forward(nseg, first, qkv, mask, o_part, l_part, m_part, keys, packs, shard):
@@ -1128,11 +1130,11 @@
 
 def project_kernel(nseg, first, mask_ref, tok_ref, *refs):
     n = BRANCHES - first
-    vectors, w_ref, out_ref = refs[:4], refs[4], refs[5]
-    qkv_ref, xp_ref, inner_ref, weight_ref, gains_ref, whole_ref, keys_ref = refs[6:13]
-    packs = refs[13 : 13 + n]
-    xs, weight, gains, key_pack, vec_send, vec_recv, w_send, w_recv, w_load, w_store = refs[13 + n : 23 + n]
-    key_send, key_recv, out_stage, out_send, out_recv, out_load = refs[23 + n :]
+    vectors, w_ref = refs[:4], refs[4]
+    qkv_ref, xp_ref, inner_ref, weight_ref, gains_ref, keys_ref = refs[5:11]
+    packs = refs[11 : 11 + n]
+    xs, weight, gains, key_pack, vec_send, vec_recv, w_send, w_recv, w_load, w_store = refs[11 + n : 21 + n]
+    key_send, key_recv = refs[21 + n :]
     step = pl.program_id(0)
     last = pl.num_programs(0) - 1
     me = lax.axis_index("fsdp")
@@ -1166,8 +1168,12 @@
         ]
 
     store = pltpu.make_async_copy(weight, weight_ref, w_store.at[0])
-    fetch = Shards([out_ref], [whole_ref], [out_stage], Sends(out_send, out_recv), out_load)
-    ahead = Sends(key_send, key_recv).copy(0, key_pack, keys_ref, "seq", 1)
+    key_sends = Sends(key_send, key_recv)
+
+    def ahead(half):
+        rows = pl.ds(half * HALF, HALF)
+        return key_sends.copy(half, key_pack.at[rows], keys_ref.at[rows], "seq", 1)
+
 
     @pl.when(step == 0)
     def _():
@@ -1187,7 +1193,6 @@
         for turn in range(COLUMN_CHUNKS):
             for copy in chunk_copies((turn + 1) % COLUMN_CHUNKS)[: 3 if turn == 0 else 2]:
                 copy.start()
-        fetch.start(1)
         for copy in vec_copies():
             copy.wait_recv()
         full = [
@@ -1217,10 +1222,6 @@
             load.wait()
             core.wait_recv()
             hand.wait_recv()
-
-    @pl.when(step == 2)
-    def _():
-        fetch.hand(0)
 
     @pl.when(step == 4)
     def _():
@@ -1252,10 +1253,13 @@
                 into = pl.ds(pl.multiple_of(step * HALF + head * HEAD_DIM, 16), HEAD_DIM)
                 pack[into, :] = jnp.concatenate(pieces, axis=1) if nseg > 1 else pieces[0]
 
-    @pl.when(step == 1)
-    def _():
-        key_pack[...] = packs[0][:D, :]
-        ahead.start()
+    for half in range(2):
+
+        @pl.when(step == half)
+        def _():
+            rows = slice(half * HALF, (half + 1) * HALF)
+            key_pack[rows, :] = packs[0][rows, :]
+            ahead(half).start()
 
     @pl.when(step == last)
     def _():
@@ -1265,24 +1269,23 @@
             for copy in chunk_copies(chunk)[1:]:
                 copy.wait_send()
         store.wait()
-        fetch.finish()
-        ahead.wait()
-
-
-def call_project(nseg, first, mask, tokens, vectors, weight, weight_out):
+        for half in range(2):
+            ahead(half).wait()
+
+
+def call_project(nseg, first, mask, tokens, vectors, weight):
     length = nseg * SEG
     kept = [nseg * (SEG >> level) for level in range(first, BRANCHES)]
     return pl.pallas_call(
         functools.partial(project_kernel, nseg, first),
         grid=(6,),
-        in_specs=[MASK_BLOCK, const_block((length, D))] + [const_block((192,))] * 4 + [ANY_BLOCK] * 2,
+        in_specs=[MASK_BLOCK, const_block((length, D))] + [const_block((192,))] * 4 + [ANY_BLOCK],
         out_specs=[
             pl.BlockSpec((1, HALF, length), lambda i: ((i + 2) % 6 // 2, i % 2, 0)),
             const_block((length, D)),
             const_block((D, length)),
             ANY_BLOCK,
             const_block((8, D)),
-            ANY_BLOCK,
             ANY_BLOCK,
         ]
         + [const_block((2 * D + 16, size)) for size in kept],
@@ -1292,7 +1295,6 @@
             shape((D, length), BF16),
             shape((4, 192, 3 * D), BF16),
             shape((8, D), F32),
-            shape((4, 192, D), BF16),
             shape((D, kept[0]), BF16),
         ]
         + [shape((2 * D + 16, size), BF16) for size in kept],
@@ -1307,17 +1309,13 @@
             sems(3 * COLUMN_CHUNKS),
             sems(COLUMN_CHUNKS),
             sems(1),
-            sems(1),
-            sems(1),
-            pltpu.VMEM((192, D), BF16),
-            sems(3),
-            sems(3),
-            sems(1),
+            sems(2),
+            sems(2),
         ],
         compiler_params=talking(4),
         cost_estimate=cost(nseg * 10e-6),
         name="project",
-    )(mask, tokens, *vectors, weight, weight_out)
+    )(mask, tokens, *vectors, weight)
 
 
 ROWS = 256
@@ -1735,13 +1733,13 @@
     mask = jnp.sum(valid_mask[0])[None]
 
     vectors = [first_gain, first_shift, second_gain, second_shift]
-    qkv, x, inner, weight_in, gains, weight_out, keys, *packs = call_project(
-        nseg, first, mask, tokens[0], vectors, project_in, project_out
+    qkv, x, inner, weight_in, gains, keys, *packs = call_project(
+        nseg, first, mask, tokens[0], vectors, project_in
     )
-    weight_out, keys = weight_out.reshape(D, D), keys[None]
+    keys = keys[None]
     weight_in = weight_in.reshape(D, 3 * D)
-    o_part, l_part, m_part, gathered, weight_up, down_first = call_local_forward(
-        nseg, first, qkv, mask, packs, (up_weight, down_weight)
+    o_part, l_part, m_part, gathered, weight_out, weight_up, down_first = call_local_forward(
+        nseg, first, qkv, mask, packs, (project_out, up_weight, down_weight)
     )
     attended, lse, down_second = call_remote_forward(
         nseg, first, qkv, mask, o_part, l_part, m_part, keys, gathered, down_weight

time: 479 us -> 470 us (0.981)
  Pallas kernels: 454 us -> 445 us
    pallas_call x1, Pallas kernels: 66.2 us -> 60.8 us  [call_local_forward(): pl.pallas_call(functools.partial(local_forward, nseg, first), grid=(HEADS...]
where the time goes in v9:
time: 470 us; the launch traced here: 462 us
  Pallas kernels  445 us (95%)
  other arithmetic  8.14 us (2%)
  local copies, waits for them, and re-layouts  7.41 us (2%)
    pallas_call x1, Pallas kernels, call_local_backward(): pl.pallas_call(functools.partial(local_backward, nseg, first), grid=(HEAD...  105 us
    pallas_call x1, Pallas kernels, call_feed(): pl.pallas_call(functools.partial(feed_kernel, nseg), grid=(length // ROWS...  100 us
    pallas_call x1, Pallas kernels, call_inner_back(): pl.pallas_call(functools.partial(inner_back_kernel, nseg, first), grid=(S...  84.7 us
    pallas_call x1, Pallas kernels, call_local_forward(): pl.pallas_call(functools.partial(local_forward, nseg, first), grid=(HEADS...  60.8 us
    pallas_call x1, Pallas kernels, call_project(): pl.pallas_call(functools.partial(project_kernel, nseg, first), grid=(6,),...  40.4 us
    pallas_call x1, Pallas kernels, call_remote_backward(): pl.pallas_call(functools.partial(remote_backward, nseg, first), grid=(HEA...  28.1 us
    pallas_call x1, Pallas kernels, call_remote_forward(): pl.pallas_call(functools.partial(remote_forward, nseg, first), grid=(HEAD...  26.1 us

profile of v9, /device:TPU:0, one launch (start us, length us, event | category | flops | bytes accessed | tf_op | source)
XLA Modules:
  0.0 462.0 jit_solution(11517294001310647395)
XLA Ops:
  0.6 1.4 reduce_sum.9
  2.0 40.4 %project.1 = (bf16[3,768,2048]{2,1,0:T(8,128)(2,1)}, bf16[2048,768]{1,0:T(8,128)(2,1)}, bf16[768,2048]{1,0:T(8,128)(2,1)}, bf16[4,192,2304]{2,1,0:T(8,128)(2,1)}...) custom-call(s32[1]{0:T(128)} %bitcast.mask_ref, ...), custom_call_target="tpu_custom_call" | custom-call | flops 22000001024 | tf_op jit(solution)/shard_map/project/pallas_call | solution.py:1279
  42.4 60.8 %local_forward.1 = (f32[768,2048]{1,0:T(8,128)}, f32[16,1,2048]{2,1,0:T(1,128)}, f32[16,1,2048]{2,1,0:T(1,128)}, bf16[1,784,512]{2,1,0:T(8,128)(2,1)}, bf16[2,15...) custom-call(s32[1]{0:T(128)} %bitcast.mask_ref, ...), custom_call_target="tpu_custom_call" | custom-call | flops 81399996416 | tf_op jit(solution)/shard_map/local_forward/pallas_call | solution.py:943
  103.3 26.1 %remote_forward.1 = (bf16[768,2048]{1,0:T(8,128)(2,1)}, f32[16,1,2048]{2,1,0:T(1,128)}, bf16[4,384,768]{2,1,0:T(8,128)(2,1)}) custom-call(s32[1]{0:T(128)} %bitcast.mask_ref, bf16[3,768,2048]{2,1,0:T(8,128)(2,1)} %get-tuple-element.52.q_ref.k_ref.v_ref, f32[768,2048]{1,0:T(8,128)} %get-tuple-element.56.o_in, f32[16,1,2048]{2,1,0:T(1,128)} %get-tuple-element.57.l_in, ...), custom_call_target="tpu_custom_call" | custom-call | flops 52800000000 | tf_op jit(solution)/shard_map/remote_forward/pallas_call | solution.py:979
  129.4 100.3 %feed.1 = (bf16[2048,768]{1,0:T(8,128)(2,1)}, f32[2048,768]{1,0:T(8,128)}, bf16[768,2048]{1,0:T(8,128)(2,1)}, f32[16,1,2048]{2,1,0:T(1,128)}, f32[2,768]{1,0:T(2,128)}, /*index=5*/bf16[4,648,16,128]{3,2,1,0:T(8,128)(2,1)}) custom-call(s32[1]{0:T(128)} %bitcast.mask_ref, bf16[768,2048]{1,0:T(8,128)(2,1)} %get-tuple-element.63.att_ref, ...), custom_call_target="tpu_custom_call" | custom-call | flops 99000000512 | tf_op jit(solution)/shard_map/feed/pallas_call | solution.py:1430
  229.8 28.1 %remote_backward.1 = (f32[768,512]{1,0:T(8,128)}, bf16[1,2,768,512]{3,2,1,0:T(8,128)(2,1)}, bf16[2,2,768,256]{3,2,1,0:T(8,128)(2,1)}, bf16[4,2,768,128]{3,2,1,0:T(8,128)(2,1)}) custom-call(s32[1]{0:T(128)} %bitcast.mask_ref, bf16[3,768,2048]{2,1,0:T(8,128)(2,1)} %get-tuple-element.52.q_ref.k_ref.v_ref, bf16[768,2048]{1,0:T(8,128)(2,1)} %get-tuple-element.71.g_ref, ...), custom_call_target="tpu_custom_call" | custom-call | flops 44000002048 | tf_op jit(solution)/shard_map/remote_backward/pallas_call | solution.py:1011
  257.8 104.8 %local_backward.1 = (f32[3,768,2048]{2,1,0:T(8,128)}, bf16[2,768,512]{2,1,0:T(8,128)(2,1)}, bf16[2,768,256]{2,1,0:T(8,128)(2,1)}, bf16[2,768,128]{2,1,0:T(8,128)(2,1)}, bf16[3,27,16,128]{3,2,1,0:T(8,128)(2,1)}) custom-call(s32[1]{0:T(128)} %bitcast.mask_ref, bf16[3,768,2048]{2,1,0:T(8,128)(2,1)} %get-tuple-element.52.q_ref.k_ref.v_ref, ...), custom_call_target="tpu_custom_call" | custom-call | flops 158400004096 | tf_op jit(solution)/shard_map/local_backward/pallas_call | solution.py:1060
  362.6 84.7 %inner_back.1 = (bf16[192,2304]{1,0:T(8,128)(2,1)}, f32[2048,768]{1,0:T(8,128)}, f32[8,768]{1,0:T(8,128)}, bf16[192,3072]{1,0:T(8,128)(2,1)}, bf16[192,768]{1,0:T(8,128)(2,1)}, /*index=5*/bf16[768,768]{1,0:T(8,128)(2,1)}) custom-call(f32[3,768,2048]{2,1,0:T(8,128)} %get-tuple-element.79.local_ref, bf16[768,2048]{1,0:T(8,128)(2,1)} %get-tuple-element.80.inner_ref, ...), custom_call_target="tpu_custom_call" | custom-call | flops 32999999488 | tf_op jit(solution)/shard_map/inner_back/pallas_call | solution.py:1656
  447.4 0.0 copy-start
  447.4 3.0 convert_element_type.14
  450.4 0.0 copy-start.1
  450.4 0.0 copy-done
  450.4 0.0 copy-start.2
  450.4 1.6 convert_element_type.15
  452.0 0.0 copy-done.1
  452.0 1.3 convert_element_type.12
  453.3 0.0 copy-done.2
  453.3 0.9 convert_element_type.13
  454.2 1.5 fusion
  455.7 5.9 %copy.22 = f32[1,2048,768]{2,1,0:T(8,128)} copy(f32[1,2048,768]{2,1,0:T(8,128)} %bitcast.13) | data formatting | bytes 12582912
Async XLA Ops:
  447.4 3.0 copy-start
  450.4 1.6 copy-start.1
  450.4 2.9 copy-start.2

commit v10 on v9

--- a/solution.py
+++ b/solution.py
@@ -759,7 +759,7 @@
             reduce.begin(chunk)
 
     events = [(3 * turn, functools.partial(back.turn, turn)) for turn in range(1, back.turns())]
-    events.append((8, functools.partial(back.start, True)))
+    events.append((9, functools.partial(back.start, True)))
     for chunk in range(CHUNKS):
         for stage in range(reduce.stages()):
             when = 1 + (chunk + 1) // 2 if stage == 0 else 4 + 3 * chunk + 2 * (stage - 1)
@@ -1473,17 +1473,48 @@
 
 STEPS = 6
 INNER_TABLE = (
-    (1, "start", 0, 0), (1, "feed", 2, 0), (1, "feed", 1, 0), (2, "feed", 0, 0),
-    (2, "reduce", 0, 0), (3, "start", 1, 0), (4, "feed", 2, 1), (4, "feed", 1, 1),
-    (4, "reduce", 1, 0), (4, "reduce", 0, 1), (4, "feed", 0, 1), (5, "start", 2, 0),
-    (8, "reduce", 1, 1), (8, "reduce", 2, 0), (8, "feed", 2, 2), (8, "feed", 1, 2),
-    (9, "reduce", 0, 2), (12, "reduce", 0, 3), (13, "vec_start", 0, 0), (13, "reduce", 2, 1),
-    (14, "feed", 0, 2), (14, "reduce", 0, 4), (14, "vec", 0, 0), (14, "reduce", 1, 2),
-    (14, "vec", 0, 1), (14, "reduce", 2, 2), (14, "vec", 0, 2), (14, "spread", 0, 0),
-    (14, "reduce", 1, 3), (14, "vec", 0, 3), (14, "reduce", 2, 3), (14, "spread", 0, 1),
-    (14, "reduce", 1, 4), (14, "vec", 0, 4), (14, "reduce", 2, 4), (14, "spread", 0, 2),
-    (14, "spread", 1, 0), (14, "spread", 2, 0), (14, "spread", 1, 1), (14, "spread", 2, 1),
-    (14, "spread", 1, 2), (14, "spread", 2, 2),
+    (1, "start", 0, 0),
+    (1, "feed", 2, 0),
+    (1, "feed", 1, 0),
+    (2, "feed", 0, 0),
+    (2, "reduce", 0, 0),
+    (3, "start", 1, 0),
+    (4, "reduce", 1, 0),
+    (5, "reduce", 0, 1),
+    (5, "start", 2, 0),
+    (6, "feed", 2, 1),
+    (6, "feed", 1, 1),
+    (6, "feed", 0, 1),
+    (6, "reduce", 2, 0),
+    (8, "reduce", 1, 1),
+    (9, "reduce", 0, 2),
+    (11, "feed", 2, 2),
+    (11, "feed", 1, 2),
+    (12, "reduce", 0, 3),
+    (13, "vec_start", 0, 0),
+    (13, "reduce", 2, 1),
+    (14, "feed", 0, 2),
+    (14, "reduce", 0, 4),
+    (14, "vec", 0, 0),
+    (14, "reduce", 1, 2),
+    (14, "vec", 0, 1),
+    (14, "reduce", 2, 2),
+    (14, "vec", 0, 2),
+    (14, "spread", 0, 0),
+    (14, "reduce", 1, 3),
+    (14, "vec", 0, 3),
+    (14, "reduce", 2, 3),
+    (14, "spread", 0, 1),
+    (14, "reduce", 1, 4),
+    (14, "vec", 0, 4),
+    (14, "reduce", 2, 4),
+    (14, "spread", 0, 2),
+    (14, "spread", 1, 0),
+    (14, "spread", 2, 0),
+    (14, "spread", 1, 1),
+    (14, "spread", 2, 1),
+    (14, "spread", 1, 2),
+    (14, "spread", 2, 2),
 )
 
 

time: 470 us -> 468 us (level)
  no operation moved by 1% of the time
where the time goes in v10:
time: 468 us; the launch traced here: 460 us
  Pallas kernels  443 us (95%)
  other arithmetic  8.14 us (2%)
  local copies, waits for them, and re-layouts  7.41 us (2%)
    pallas_call x1, Pallas kernels, call_local_backward(): pl.pallas_call(functools.partial(local_backward, nseg, first), grid=(HEAD...  105 us
    pallas_call x1, Pallas kernels, call_feed(): pl.pallas_call(functools.partial(feed_kernel, nseg), grid=(length // ROWS...  100 us
    pallas_call x1, Pallas kernels, call_inner_back(): pl.pallas_call(functools.partial(inner_back_kernel, nseg, first), grid=(S...  82.8 us
    pallas_call x1, Pallas kernels, call_local_forward(): pl.pallas_call(functools.partial(local_forward, nseg, first), grid=(HEADS...  60.8 us
    pallas_call x1, Pallas kernels, call_project(): pl.pallas_call(functools.partial(project_kernel, nseg, first), grid=(6,),...  40.4 us
    pallas_call x1, Pallas kernels, call_remote_backward(): pl.pallas_call(functools.partial(remote_backward, nseg, first), grid=(HEA...  28.1 us
    pallas_call x1, Pallas kernels, call_remote_forward(): pl.pallas_call(functools.partial(remote_forward, nseg, first), grid=(HEAD...  26.1 us

profile of v10, /device:TPU:0, one launch (start us, length us, event | category | flops | bytes accessed | tf_op | source)
XLA Modules:
  0.0 460.1 jit_solution(7830677698977974460)
XLA Ops:
  0.6 1.4 reduce_sum.9
  2.0 40.4 %project.1 = (bf16[3,768,2048]{2,1,0:T(8,128)(2,1)}, bf16[2048,768]{1,0:T(8,128)(2,1)}, bf16[768,2048]{1,0:T(8,128)(2,1)}, bf16[4,192,2304]{2,1,0:T(8,128)(2,1)}...) custom-call(s32[1]{0:T(128)} %bitcast.mask_ref, ...), custom_call_target="tpu_custom_call" | custom-call | flops 22000001024 | tf_op jit(solution)/shard_map/project/pallas_call | solution.py:1279
  42.4 60.8 %local_forward.1 = (f32[768,2048]{1,0:T(8,128)}, f32[16,1,2048]{2,1,0:T(1,128)}, f32[16,1,2048]{2,1,0:T(1,128)}, bf16[1,784,512]{2,1,0:T(8,128)(2,1)}, bf16[2,15...) custom-call(s32[1]{0:T(128)} %bitcast.mask_ref, ...), custom_call_target="tpu_custom_call" | custom-call | flops 81399996416 | tf_op jit(solution)/shard_map/local_forward/pallas_call | solution.py:943
  103.3 26.1 %remote_forward.1 = (bf16[768,2048]{1,0:T(8,128)(2,1)}, f32[16,1,2048]{2,1,0:T(1,128)}, bf16[4,384,768]{2,1,0:T(8,128)(2,1)}) custom-call(s32[1]{0:T(128)} %bitcast.mask_ref, bf16[3,768,2048]{2,1,0:T(8,128)(2,1)} %get-tuple-element.52.q_ref.k_ref.v_ref, f32[768,2048]{1,0:T(8,128)} %get-tuple-element.56.o_in, f32[16,1,2048]{2,1,0:T(1,128)} %get-tuple-element.57.l_in, ...), custom_call_target="tpu_custom_call" | custom-call | flops 52800000000 | tf_op jit(solution)/shard_map/remote_forward/pallas_call | solution.py:979
  129.4 100.3 %feed.1 = (bf16[2048,768]{1,0:T(8,128)(2,1)}, f32[2048,768]{1,0:T(8,128)}, bf16[768,2048]{1,0:T(8,128)(2,1)}, f32[16,1,2048]{2,1,0:T(1,128)}, f32[2,768]{1,0:T(2,128)}, /*index=5*/bf16[4,648,16,128]{3,2,1,0:T(8,128)(2,1)}) custom-call(s32[1]{0:T(128)} %bitcast.mask_ref, bf16[768,2048]{1,0:T(8,128)(2,1)} %get-tuple-element.63.att_ref, ...), custom_call_target="tpu_custom_call" | custom-call | flops 99000000512 | tf_op jit(solution)/shard_map/feed/pallas_call | solution.py:1430
  229.8 28.1 %remote_backward.1 = (f32[768,512]{1,0:T(8,128)}, bf16[1,2,768,512]{3,2,1,0:T(8,128)(2,1)}, bf16[2,2,768,256]{3,2,1,0:T(8,128)(2,1)}, bf16[4,2,768,128]{3,2,1,0:T(8,128)(2,1)}) custom-call(s32[1]{0:T(128)} %bitcast.mask_ref, bf16[3,768,2048]{2,1,0:T(8,128)(2,1)} %get-tuple-element.52.q_ref.k_ref.v_ref, bf16[768,2048]{1,0:T(8,128)(2,1)} %get-tuple-element.71.g_ref, ...), custom_call_target="tpu_custom_call" | custom-call | flops 44000002048 | tf_op jit(solution)/shard_map/remote_backward/pallas_call | solution.py:1011
  257.8 104.8 %local_backward.1 = (f32[3,768,2048]{2,1,0:T(8,128)}, bf16[2,768,512]{2,1,0:T(8,128)(2,1)}, bf16[2,768,256]{2,1,0:T(8,128)(2,1)}, bf16[2,768,128]{2,1,0:T(8,128)(2,1)}, bf16[3,27,16,128]{3,2,1,0:T(8,128)(2,1)}) custom-call(s32[1]{0:T(128)} %bitcast.mask_ref, bf16[3,768,2048]{2,1,0:T(8,128)(2,1)} %get-tuple-element.52.q_ref.k_ref.v_ref, ...), custom_call_target="tpu_custom_call" | custom-call | flops 158400004096 | tf_op jit(solution)/shard_map/local_backward/pallas_call | solution.py:1060
  362.6 82.8 %inner_back.1 = (bf16[192,2304]{1,0:T(8,128)(2,1)}, f32[2048,768]{1,0:T(8,128)}, f32[8,768]{1,0:T(8,128)}, bf16[192,3072]{1,0:T(8,128)(2,1)}, bf16[192,768]{1,0:T(8,128)(2,1)}, /*index=5*/bf16[768,768]{1,0:T(8,128)(2,1)}) custom-call(f32[3,768,2048]{2,1,0:T(8,128)} %get-tuple-element.79.local_ref, bf16[768,2048]{1,0:T(8,128)(2,1)} %get-tuple-element.80.inner_ref, ...), custom_call_target="tpu_custom_call" | custom-call | flops 32999999488 | tf_op jit(solution)/shard_map/inner_back/pallas_call | solution.py:1687
  445.5 0.0 copy-start
  445.5 3.0 convert_element_type.14
  448.5 0.0 copy-start.1
  448.5 0.0 copy-done
  448.5 0.0 copy-start.2
  448.5 1.6 convert_element_type.15
  450.1 0.0 copy-done.1
  450.1 1.3 convert_element_type.12
  451.4 0.0 copy-done.2
  451.4 0.9 convert_element_type.13
  452.3 1.5 fusion
  453.8 5.9 %copy.22 = f32[1,2048,768]{2,1,0:T(8,128)} copy(f32[1,2048,768]{2,1,0:T(8,128)} %bitcast.13) | data formatting | bytes 12582912
Async XLA Ops:
  445.5 3.0 copy-start
  448.5 1.6 copy-start.1
  448.5 2.9 copy-start.2
